TPU v7x, 32 devices: a whole 2x2x4 slice. The times are simulated.
32 devices in a mesh: fsdp: 4 (over x, core), ctx: 4 (over z), tp: 2 (over y).
Axes of the slice: x: 2, y: 2, z: 4, core: 2. Of those that a mesh axis runs over, the one named last changes fastest.
Arguments:
- earlier: bfloat16 [8, 8, 1024, 2048], P(None, 'fsdp', 'ctx'), may hold values from -6 to 6
- mix_in: float32 [32, 8, 1024], P(None, 'fsdp', 'ctx'), may hold values from -3 to 3
- lengths: int32 [8], P('fsdp'), may hold values from 256 to 1024, as said below
- w_query: bfloat16 [2048, 2048], P(('fsdp', 'ctx'), 'tp'), may hold values from -0.125 to 0.125
- w_key: bfloat16 [2048, 2048], P(('fsdp', 'ctx'), 'tp'), may hold values from -0.125 to 0.125
- w_value: bfloat16 [2048, 2048], P(('fsdp', 'ctx'), 'tp'), may hold values from -0.125 to 0.125
- w_proj: bfloat16 [2048, 2048], P('tp', ('fsdp', 'ctx')), may hold values from -2 to 2
- w_up: bfloat16 [2048, 8192], P(('fsdp', 'ctx'), 'tp'), may hold values from -0.125 to 0.125
- w_down: bfloat16 [8192, 2048], P('tp', ('fsdp', 'ctx')), may hold values from -0.0625 to 0.0625
- first_gain: bfloat16 [2048], P(('fsdp', 'ctx')), may hold values from 0.099609375 to 1.8984375
- first_shift: bfloat16 [2048], P(('fsdp', 'ctx')), may hold values from -3 to 3
- second_gain: bfloat16 [2048], P(('fsdp', 'ctx')), may hold values from 0.099609375 to 1.8984375
- second_shift: bfloat16 [2048], P(('fsdp', 'ctx')), may hold values from -3 to 3
- mixer_in: bfloat16 [2048, 36], P(('fsdp', 'ctx')), may hold values from -0.125 to 0.125
- mixer_out: float32 [36, 36], replicated, may hold values from -1 to 1
- mixer_bias: float32 [36], replicated, may hold values from -3 to 3
- grad_out: bfloat16 [8, 1024, 2048], P('fsdp', 'ctx'), may hold values from -6 to 6
- grad_mix: float32 [36, 8, 1024], P(None, 'fsdp', 'ctx'), may hold values from -12 to 12
Outputs:
- output: bfloat16 [8, 1024, 2048], P('fsdp', 'ctx')
- mix_out: float32 [36, 8, 1024], P(None, 'fsdp', 'ctx')
- grad_earlier: bfloat16 [8, 8, 1024, 2048], P(None, 'fsdp', 'ctx')
- grad_mix_in: float32 [32, 8, 1024], P(None, 'fsdp', 'ctx')
- grad_query: float32 [2048, 2048], P(('fsdp', 'ctx'), 'tp')
- grad_key: float32 [2048, 2048], P(('fsdp', 'ctx'), 'tp')
- grad_value: float32 [2048, 2048], P(('fsdp', 'ctx'), 'tp')
- grad_proj: float32 [2048, 2048], P('tp', ('fsdp', 'ctx'))
- grad_up: float32 [2048, 8192], P(('fsdp', 'ctx'), 'tp')
- grad_down: float32 [8192, 2048], P('tp', ('fsdp', 'ctx'))
- grad_first_gain: float32 [2048], P(('fsdp', 'ctx'))
- grad_first_shift: float32 [2048], P(('fsdp', 'ctx'))
- grad_second_gain: float32 [2048], P(('fsdp', 'ctx'))
- grad_second_shift: float32 [2048], P(('fsdp', 'ctx'))
- grad_mixer_in: float32 [2048, 36], P(('fsdp', 'ctx'))
- grad_mixer_out: float32 [36, 36], replicated
- grad_mixer_bias: float32 [36], replicated
Inputs may be any that keep to these rules, and one draw needn't show every extreme that they name: `lengths`: every row is used from slot 0; some row uses all 1024 slots and some row uses a quarter of them.
All inputs are finite; a program needn't handle non-finite values.
Results may differ from a plain program's by a relative error of at most 0.012.
Values may be sent and summed in bfloat16 or wider, within the bound.
No kernel may reach another device: no remote copies, remote signals or barrier semaphores. Data moves between devices by JAX's collectives and lax.ppermute only.
A program may use at most 960 MiB of HBM per device.

v0:
```python
from functools import partial
import math

import jax
import jax.numpy as jnp
from jax import lax
from jax.sharding import PartitionSpec as P

HD = 128
ROT = 32
STREAMS = 4
MIXW = 36


EPSILON = 1e-05
RMS_EPSILON = 1e-06
HIGHEST = lax.Precision.HIGHEST
NEGATIVE = -1e30


def layer_norm(values, gain, shift):
    center = values - jnp.mean(values, axis=-1, keepdims=True)
    spread = jnp.mean(center * center, axis=-1, keepdims=True)
    return center * lax.rsqrt(spread + EPSILON) * gain + shift


def rotate(values, positions):
    half = ROT // 2
    frequency = 10000.0 ** (-2.0 * jnp.arange(half, dtype=jnp.float32) / ROT)
    angles = positions.astype(jnp.float32)[:, None] * frequency[None, :]
    cosine = jnp.cos(angles)[:, None, :]
    sine = jnp.sin(angles)[:, None, :]
    first = values[..., :half]
    second = values[..., half:ROT]
    return jnp.concatenate(
        [first * cosine - second * sine, second * cosine + first * sine, values[..., ROT:]], axis=-1
    )


def activate(values):
    return jax.nn.gelu(values, approximate=False)


def mixer(final, weight_in, weight_out, bias):
    normed = final * lax.rsqrt(jnp.mean(final * final, axis=-1, keepdims=True) + RMS_EPSILON)
    hidden = activate(
        jnp.dot(normed, weight_in, precision=HIGHEST, preferred_element_type=jnp.float32)
    )
    return jnp.dot(hidden, weight_out, precision=HIGHEST, preferred_element_type=jnp.float32) + bias


def product(form, left, right):
    return jnp.einsum(form, left, right, preferred_element_type=jnp.float32)


def gather_weights(
    w_query,
    w_key,
    w_value,
    w_up,
    mixer_in,
    first_gain,
    first_shift,
    second_gain,
    second_shift,
    w_proj,
    w_down,
):
    front = (
        lax.all_gather(w_query, ("fsdp", "ctx"), axis=0, tiled=True),
        lax.all_gather(w_key, ("fsdp", "ctx"), axis=0, tiled=True),
        lax.all_gather(w_value, ("fsdp", "ctx"), axis=0, tiled=True),
        lax.all_gather(w_up, ("fsdp", "ctx"), axis=0, tiled=True),
        lax.all_gather(mixer_in, ("fsdp", "ctx"), axis=0, tiled=True),
        lax.all_gather(first_gain, ("fsdp", "ctx"), axis=0, tiled=True),
        lax.all_gather(first_shift, ("fsdp", "ctx"), axis=0, tiled=True),
        lax.all_gather(second_gain, ("fsdp", "ctx"), axis=0, tiled=True),
        lax.all_gather(second_shift, ("fsdp", "ctx"), axis=0, tiled=True),
    )
    behind = (
        lax.all_gather(w_proj, ("fsdp", "ctx"), axis=1, tiled=True),
        lax.all_gather(w_down, ("fsdp", "ctx"), axis=1, tiled=True),
    )
    return tuple(front) + tuple(behind)


def masked_scores(query_rot, keys, slots, key_slots, length):
    scores = product("shd,thd->hst", query_rot, keys) * (1.0 / math.sqrt(HD))
    allowed = (key_slots[None, :] <= slots[:, None]) & (key_slots[None, :] < length)
    return (jnp.where(allowed[None], scores, NEGATIVE), allowed)


def body(
    earlier,
    mix_in,
    lengths,
    w_query,
    w_key,
    w_value,
    w_proj,
    w_up,
    w_down,
    first_gain,
    first_shift,
    second_gain,
    second_shift,
    mixer_in,
    mixer_out,
    mixer_bias,
    grad_out,
    grad_mix,
):
    count_prev = earlier.shape[0]
    micro_count = earlier.shape[1]
    seq_local = earlier.shape[2]
    width = earlier.shape[3]
    tokens = micro_count * seq_local
    heads_local = w_query.shape[1] // HD
    width_local = heads_local * HD
    seq_total = seq_local * lax.axis_size("ctx")
    slots = lax.axis_index("ctx") * seq_local + jnp.arange(seq_local, dtype=jnp.int32)
    positions = jnp.tile(slots, micro_count)
    key_slots = jnp.arange(seq_total, dtype=jnp.int32)
    scale = 1.0 / math.sqrt(HD)
    rope_here = partial(rotate, positions=positions)
    gathered = gather_weights(
        w_query,
        w_key,
        w_value,
        w_up,
        mixer_in,
        first_gain,
        first_shift,
        second_gain,
        second_shift,
        w_proj,
        w_down,
    )
    (
        full_query,
        full_key,
        full_value,
        full_up,
        full_mixer,
        gain_first,
        shift_first,
        gain_second,
        shift_second,
        full_proj,
        full_down,
    ) = gathered
    gain_first = gain_first.astype(jnp.float32)
    shift_first = shift_first.astype(jnp.float32)
    gain_second = gain_second.astype(jnp.float32)
    shift_second = shift_second.astype(jnp.float32)
    valid = (slots[None, :] < lengths[:, None]).astype(jnp.float32).reshape(tokens)
    inputs = earlier.reshape(count_prev, tokens, width)
    coeff = mix_in.reshape(STREAMS, count_prev, tokens)
    streams = coeff[:, 0, :, None] * inputs[0].astype(jnp.float32)[None]
    for prev_index in range(1, count_prev):
        streams = (
            streams + coeff[:, prev_index, :, None] * inputs[prev_index].astype(jnp.float32)[None]
        )
    query_in = layer_norm(streams[0], gain_first, shift_first).astype(jnp.bfloat16)
    key_in = layer_norm(streams[1], gain_first, shift_first).astype(jnp.bfloat16)
    value_in = layer_norm(streams[2], gain_first, shift_first).astype(jnp.bfloat16)
    query_pre = jnp.dot(query_in, full_query, preferred_element_type=jnp.float32).reshape(
        tokens, heads_local, HD
    )
    key_pre = jnp.dot(key_in, full_key, preferred_element_type=jnp.float32).reshape(
        tokens, heads_local, HD
    )
    query_rot = rope_here(query_pre).astype(jnp.bfloat16)
    key_rot = rope_here(key_pre).astype(jnp.bfloat16)
    value_own = jnp.dot(value_in, full_value, preferred_element_type=jnp.float32).astype(
        jnp.bfloat16
    )
    keys_all, values_all = (
        lax.all_gather(
            key_rot.reshape(micro_count, seq_local, width_local), "ctx", axis=1, tiled=True
        ),
        lax.all_gather(
            value_own.reshape(micro_count, seq_local, width_local), "ctx", axis=1, tiled=True
        ),
    )
    query_rows = query_rot.reshape(micro_count, seq_local, heads_local, HD)
    attended_rows, logsums = ([], [])
    for batch_index in range(micro_count):
        keys_three = keys_all[batch_index].reshape(seq_total, heads_local, HD)
        values_three = values_all[batch_index].reshape(seq_total, heads_local, HD)
        masked, allowed = masked_scores(
            query_rows[batch_index], keys_three, slots, key_slots, lengths[batch_index]
        )
        top = jnp.max(masked, axis=-1, keepdims=True)
        expo = jnp.exp(masked - top)
        total = jnp.sum(expo, axis=-1, keepdims=True)
        logsums.append(top + jnp.log(total))
        probs_b = (expo / total).astype(jnp.bfloat16)
        attended_rows.append(
            product("hst,thd->shd", probs_b, values_three).reshape(seq_local, width_local)
        )
    attended = jnp.concatenate(attended_rows, axis=0).astype(jnp.bfloat16)
    branch = lax.psum(jnp.dot(attended, full_proj, preferred_element_type=jnp.float32), "tp")
    residual = streams[3] + branch
    normed = layer_norm(residual, gain_second, shift_second).astype(jnp.bfloat16)
    upward = jnp.dot(normed, full_up, preferred_element_type=jnp.float32)
    active = activate(upward).astype(jnp.bfloat16)
    downward = lax.psum(jnp.dot(active, full_down, preferred_element_type=jnp.float32), "tp")
    final = residual + downward
    output = final.astype(jnp.bfloat16).reshape(micro_count, seq_local, width)
    mixer_full = full_mixer.astype(jnp.float32)
    mix_value, mix_pull = jax.vjp(mixer, final, mixer_full, mixer_out, mixer_bias)
    mix_out = mix_value.T.reshape(MIXW, micro_count, seq_local)
    mix_cotangent = (grad_mix.reshape(MIXW, tokens) * valid[None]).T
    grad_final_mix, grad_mixer_first, grad_mixer_second, grad_mixer_shift = mix_pull(mix_cotangent)
    grad_final = (
        grad_out.reshape(tokens, width).astype(jnp.float32) * valid[:, None] + grad_final_mix
    )
    grad_down_b = grad_final.astype(jnp.bfloat16)
    grad_down_w = product("tf,td->fd", active, grad_down_b)
    grad_active = product("td,fd->tf", grad_down_b, full_down)
    unused_up, gelu_pull = jax.vjp(activate, upward)
    grad_upward_b = gelu_pull(grad_active)[0].astype(jnp.bfloat16)
    grad_up_w = product("tc,tf->cf", normed, grad_upward_b)
    grad_normed = lax.psum(product("tf,cf->tc", grad_upward_b, full_up), "tp")
    unused_norm, norm_pull = jax.vjp(layer_norm, residual, gain_second, shift_second)
    grad_residual_norm, grad_gain_second, grad_shift_second = norm_pull(grad_normed)
    grad_residual = grad_final + grad_residual_norm
    grad_branch_b = grad_residual.astype(jnp.bfloat16)
    grad_proj_w = product("te,td->ed", attended, grad_branch_b)
    grad_attended = (
        product("td,ed->te", grad_branch_b, full_proj)
        .astype(jnp.bfloat16)
        .reshape(micro_count, seq_local, heads_local, HD)
    )
    query_parts, key_parts, value_parts = ([], [], [])
    for batch_index in range(micro_count):
        keys_three = keys_all[batch_index].reshape(seq_total, heads_local, HD)
        values_three = values_all[batch_index].reshape(seq_total, heads_local, HD)
        masked_again, allowed_again = masked_scores(
            query_rows[batch_index], keys_three, slots, key_slots, lengths[batch_index]
        )
        probs = jnp.where(allowed_again[None], jnp.exp(masked_again - logsums[batch_index]), 0.0)
        probs_again = probs.astype(jnp.bfloat16)
        grad_probs = product("shd,thd->hst", grad_attended[batch_index], values_three)
        delta = jnp.sum(probs * grad_probs, axis=-1, keepdims=True)
        grad_scores = (probs * (grad_probs - delta) * scale).astype(jnp.bfloat16)
        query_parts.append(product("hst,thd->shd", grad_scores, keys_three))
        key_parts.append(
            product("hst,shd->thd", grad_scores, query_rows[batch_index]).reshape(
                seq_total, width_local
            )
        )
        value_parts.append(
            product("hst,shd->thd", probs_again, grad_attended[batch_index]).reshape(
                seq_total, width_local
            )
        )
    grad_query_rot = jnp.concatenate(query_parts, axis=0)
    grad_keys, grad_values = (
        lax.psum_scatter(jnp.stack(key_parts, axis=0), "ctx", scatter_dimension=1, tiled=True),
        lax.psum_scatter(jnp.stack(value_parts, axis=0), "ctx", scatter_dimension=1, tiled=True),
    )
    unused_query, query_pull = jax.vjp(rope_here, query_pre)
    unused_key, key_pull = jax.vjp(rope_here, key_pre)
    grad_query_b = query_pull(grad_query_rot)[0].reshape(tokens, width_local).astype(jnp.bfloat16)
    grad_key_b = (
        key_pull(grad_keys.reshape(tokens, heads_local, HD))[0]
        .reshape(tokens, width_local)
        .astype(jnp.bfloat16)
    )
    grad_value_b = grad_values.reshape(tokens, width_local).astype(jnp.bfloat16)
    grad_query_w = product("tc,te->ce", query_in, grad_query_b)
    grad_key_w = product("tc,te->ce", key_in, grad_key_b)
    grad_value_w = product("tc,te->ce", value_in, grad_value_b)
    grad_query_in, grad_key_in, grad_value_in = lax.psum(
        (
            product("te,ce->tc", grad_query_b, full_query),
            product("te,ce->tc", grad_key_b, full_key),
            product("te,ce->tc", grad_value_b, full_value),
        ),
        "tp",
    )
    stream_grads = []
    grad_gain_first = jnp.zeros_like(gain_first)
    grad_shift_first = jnp.zeros_like(shift_first)
    for stream_index, grad_in in ((0, grad_query_in), (1, grad_key_in), (2, grad_value_in)):
        unused_first, first_pull = jax.vjp(
            layer_norm, streams[stream_index], gain_first, shift_first
        )
        grad_stream, grad_gain_part, grad_shift_part = first_pull(grad_in)
        stream_grads.append(grad_stream)
        grad_gain_first = grad_gain_first + grad_gain_part
        grad_shift_first = grad_shift_first + grad_shift_part
    stream_grads.append(grad_residual)
    grad_streams = jnp.stack(stream_grads, axis=0)
    grad_earlier = (
        jnp.einsum("sjt,std->jtd", coeff, grad_streams, precision=HIGHEST)
        .astype(jnp.bfloat16)
        .reshape(count_prev, micro_count, seq_local, width)
    )
    grad_mix_in = jnp.einsum(
        "jtd,std->sjt", inputs.astype(jnp.float32), grad_streams, precision=HIGHEST
    ).reshape(STREAMS * count_prev, micro_count, seq_local)
    front = (
        lax.psum_scatter(grad_query_w, ("fsdp", "ctx"), scatter_dimension=0, tiled=True),
        lax.psum_scatter(grad_key_w, ("fsdp", "ctx"), scatter_dimension=0, tiled=True),
        lax.psum_scatter(grad_value_w, ("fsdp", "ctx"), scatter_dimension=0, tiled=True),
        lax.psum_scatter(grad_up_w, ("fsdp", "ctx"), scatter_dimension=0, tiled=True),
        lax.psum_scatter(grad_mixer_first, ("fsdp", "ctx"), scatter_dimension=0, tiled=True),
        lax.psum_scatter(grad_gain_first, ("fsdp", "ctx"), scatter_dimension=0, tiled=True),
        lax.psum_scatter(grad_shift_first, ("fsdp", "ctx"), scatter_dimension=0, tiled=True),
        lax.psum_scatter(grad_gain_second, ("fsdp", "ctx"), scatter_dimension=0, tiled=True),
        lax.psum_scatter(grad_shift_second, ("fsdp", "ctx"), scatter_dimension=0, tiled=True),
    )
    behind = (
        lax.psum_scatter(grad_proj_w, ("fsdp", "ctx"), scatter_dimension=1, tiled=True),
        lax.psum_scatter(grad_down_w, ("fsdp", "ctx"), scatter_dimension=1, tiled=True),
    )
    small_parts = lax.psum((grad_mixer_second, grad_mixer_shift), ("fsdp", "ctx"))
    return (
        output,
        mix_out,
        grad_earlier,
        grad_mix_in,
        front[0],
        front[1],
        front[2],
        behind[0],
        front[3],
        behind[1],
        front[5],
        front[6],
        front[7],
        front[8],
        front[4],
        small_parts[0],
        small_parts[1],
    )


def solution(mesh):
    placed = (
        P(None, "fsdp", "ctx", None),
        P(None, "fsdp", "ctx"),
        P("fsdp"),
        P(("fsdp", "ctx"), "tp"),
        P(("fsdp", "ctx"), "tp"),
        P(("fsdp", "ctx"), "tp"),
        P("tp", ("fsdp", "ctx")),
        P(("fsdp", "ctx"), "tp"),
        P("tp", ("fsdp", "ctx")),
        P(("fsdp", "ctx")),
        P(("fsdp", "ctx")),
        P(("fsdp", "ctx")),
        P(("fsdp", "ctx")),
        P(("fsdp", "ctx"), None),
        P(),
        P(),
        P("fsdp", "ctx", None),
        P(None, "fsdp", "ctx"),
    )
    return jax.shard_map(
        body,
        mesh=mesh,
        in_specs=placed,
        out_specs=(
            P("fsdp", "ctx", None),
            P(None, "fsdp", "ctx"),
            P(None, "fsdp", "ctx", None),
            P(None, "fsdp", "ctx"),
            P(("fsdp", "ctx"), "tp"),
            P(("fsdp", "ctx"), "tp"),
            P(("fsdp", "ctx"), "tp"),
            P("tp", ("fsdp", "ctx")),
            P(("fsdp", "ctx"), "tp"),
            P("tp", ("fsdp", "ctx")),
            P(("fsdp", "ctx")),
            P(("fsdp", "ctx")),
            P(("fsdp", "ctx")),
            P(("fsdp", "ctx")),
            P(("fsdp", "ctx"), None),
            P(),
            P(),
        ),
        check_vma=False,
    )
```

profile of v0, /device:TPU:0, one launch (start us, length us, event | category | flops | bytes accessed | tf_op | source)
XLA Modules:
  0.0 3636.9 jit_solution(12877278955106275811)
XLA Ops:
  9.5 33.8 all-gather
  43.3 28.6 all-gather.1
  73.6 8.1 fusion.175
  96.1 13.9 multiply_add_fusion
  116.2 6.9 fusion.73
  123.7 6.5 copy.108
  130.2 36.1 all-gather.17.cloned.1.call-done
  166.3 6.5 copy.107
  172.9 6.8 fusion.54
  192.9 54.8 %all-gather.15.cloned.1.call-done = bf16[2,1024,1024]{2,1,0:T(8,128)(2,1)} async-done(((bf16[2,256,1024]{2,1,0:T(8,128)(2,1)}), bf16[2,1024,1024]{2,1,0:T(8,128)(2,1)}) %all-gather.15.cloned.1.call-update) | async-done | bytes 4194320 | tf_op jit(solution)/shard_map/all_gather | solution.py:182
  257.2 71.6 %all-gather.21.cloned.1.call-done = bf16[2,1024,1024]{1,2,0:T(8,128)(2,1)} async-done(((bf16[2,256,1024]{1,2,0:T(8,128)(2,1)}), bf16[2,1024,1024]{1,2,0:T(8,128)(2,1)}) %all-gather.21.cloned.1.call-update) | async-done | bytes 4194320 | tf_op jit(solution)/shard_map/all_gather | solution.py:179
  346.2 35.4 all-gather.23.cloned.1.call-done
  381.6 6.6 fusion.99
  389.8 29.6 all-gather.2
  419.5 29.1 all-gather.3
  448.6 45.9 %all-reduce.17.cloned.1.call-done = f32[512,2048]{1,0:T(8,128)} async-done(((f32[512,2048]{1,0:T(8,128)}), f32[512,2048]{1,0:T(8,128)}) %all-reduce.17.cloned.1.call-update) | async-done | bytes 4194320 | tf_op jit(solution)/shard_map/psum | solution.py:203
  501.0 122.9 %all-gather.25.cloned.1.call-done = bf16[2048,4096]{1,0:T(8,128)(2,1)} async-done(((bf16[128,4096]{1,0:T(8,128)(2,1)}), bf16[2048,4096]{1,0:T(8,128)(2,1)}) %all-gather.25.cloned.1.call-update) | async-done | bytes 16777232 | tf_op jit(solution)/shard_map/all_gather | solution.py:73
  623.8 32.3 multiply_convert_fusion.2
  656.1 98.6 %all-gather.27.cloned.1.call-done = bf16[4096,2048]{1,0:T(8,128)(2,1)} async-done(((bf16[4096,128]{1,0:T(8,128)(2,1)}), bf16[4096,2048]{1,0:T(8,128)(2,1)}) %all-gather.27.cloned.1.call-update) | async-done | bytes 16777232 | tf_op jit(solution)/shard_map/all_gather | solution.py:82
  754.7 15.0 fusion.181
  770.6 31.9 all_gather.51
  802.5 73.4 %all-reduce.19.cloned.1.call-done = f32[512,2048]{1,0:T(8,128)} async-done(((f32[512,2048]{1,0:T(8,128)}), f32[512,2048]{1,0:T(8,128)}) %all-reduce.19.cloned.1.call-update) | async-done | bytes 4194320 | tf_op jit(solution)/shard_map/psum | solution.py:208
  888.1 21.4 add_convert_fusion
  909.6 15.1 fusion.182
  925.5 107.3 %all-reduce.21.cloned.1.call-done = f32[512,2048]{1,0:T(8,128)} async-done(((f32[512,2048]{1,0:T(8,128)}), f32[512,2048]{1,0:T(8,128)}) %all-reduce.21.cloned.1.call-update) | async-done | bytes 4194320 | tf_op jit(solution)/shard_map/psum | solution.py:225
  1032.7 5.5 multiply_reduce_fusion.2
  1047.5 5.7 fusion.183
  1053.3 24.5 fusion.33
  1077.8 8.7 copy.119
  1091.1 24.2 fusion.39
  1115.3 8.6 copy.120
  1123.9 9.7 pad_maximum_fusion.1
  1133.7 235.5 %copy.137 = f32[2,1024,1024]{0,2,1:T(8,128)} copy(f32[2,1024,1024]{1,0,2:T(2,128)} %pad_maximum_fusion.1) | data formatting | bytes 16777216
  1369.1 422.1 %reshape.683 = f32[1024,2048]{1,0:T(8,128)} reshape(f32[1024,1024,2]{2,1,0:T(8,128)} %bitcast.73) | data formatting | bytes 16777216
  1792.4 8.0 fusion.28
  1800.3 5.8 copy.124
  1806.1 8.1 fusion.30
  1819.6 8.4 pad_maximum_fusion.2
  1829.6 22.2 fusion.77
  1851.8 22.6 fusion.74
  1875.8 60.1 %reduce-scatter.28.cloned.1.call-done = f32[256,2048]{1,0:T(8,128)} async-done(((f32[1024,2048]{1,0:T(8,128)}), f32[256,2048]{1,0:T(8,128)}) %reduce-scatter.28.cloned.1.call-update) | async-done | bytes 2097168
  1935.9 139.2 %reshape.684 = f32[256,1024,2]{2,1,0:T(8,128)} reshape(f32[256,2048]{1,0:T(8,128)} %reduce-scatter.28.cloned.1.call-done) | data formatting | bytes 4194304
  2075.1 71.0 %copy.138 = f32[2,256,1024]{1,0,2:T(2,128)} copy(f32[2,256,1024]{0,2,1:T(8,128)} %bitcast.74) | data formatting | bytes 4194304
  2154.1 6.7 fusion.187
  2170.4 5.8 fusion.46
  2176.3 8.4 fusion.88
  2185.5 8.2 fusion.52
  2194.3 8.2 fusion.60
  2203.2 8.4 fusion.56
  2212.3 19.3 fusion.166
  2232.1 18.7 fusion.91
  2254.8 205.1 %all-reduce.23.cloned.1.call-done = (f32[512,2048]{1,0:T(8,128)}, f32[512,2048]{1,0:T(8,128)}, f32[512,2048]{1,0:T(8,128)}) async-done(((f32[512,2048]{1,0:T(8,128)}, f32[512,2048]{1,0:T(8,128)}, f32[512,2048]{1,0:T(8,128)}), (f32[512,2048]{1,0:T(8,128)}, f32[512,2048]{1,0:T(8,128)}, f32[512,2048]{1,0:T(8,128)})) %all-reduce.23.cloned.1.call-update) | async-done | bytes 12582928 | tf_op jit(solution)/shard_map/psum | solution.py:276
  2459.9 10.3 multiply_reduce_fusion.3
  2470.3 61.8 %all-reduce.10 = (f32[2048]{0:T(1024)S(1)}, f32[2048]{0:T(1024)S(1)}, f32[2048]{0:T(1024)S(1)}, f32[2048]{0:T(1024)S(1)}, f32[36,36]{1,0:T(8,128)}, /*index=5*/f32[36]{0:T(128)}) all-reduce(f32[2048]{0:T(1024)S(1)} %add_add_fusion.7, f32[2048]{0:T(1024)S(1)} %add_add_fusion.6, ...), channel_id=10, replica_groups=mesh['fsdp'=4,'ctx'=4,'tp'=2] {'fsdp','ctx'}, use_global_device_ids=true, to_apply=%region_41.42.clone | all-reduce | flops 9524 | bytes 76192
  2534.5 12.2 fusion.168
  2550.8 6.3 copy-done.5
  2557.1 47.1 %fusion.80 = f32[4,8,512]{1,0,2:T(4,128)S(1)} fusion(bf16[8,512,2048]{2,1,0:T(8,128)(2,1)} %bitcast.223, f32[4,512,2048]{2,1,0:T(8,128)S(1)} %pad_maximum_fusion), kind=kOutput, calls=%fused_computation.141 | convolution fusion | flops 402653184 | bytes 33619968 | tf_op jit(solution)/shard_map/jtd,std->sjt/dot_general | solution.py:302
  2605.3 45.1 %fusion.7 = bf16[512,2048,8]{1,2,0:T(8,128)(2,1)S(1)} fusion(f32[4,8,512]{1,0,2:T(4,128)S(1)} %copy.126, f32[4,512,2048]{2,1,0:T(8,128)} %copy-done.5), kind=kOutput, calls=%fused_computation.9 | convolution fusion | flops 411041792 | bytes 33619968 | tf_op jit(solution)/shard_map/sjt,std->jtd/dot_general | solution.py:298
  2650.3 21.2 copy.130
  2671.5 64.3 %reduce-scatter.18.cloned.1.call-done = f32[128,1024]{1,0:T(8,128)} async-done(((f32[2048,1024]{1,0:T(8,128)}), f32[128,1024]{1,0:T(8,128)}) %reduce-scatter.18.cloned.1.call-update) | async-done | bytes 524304 | tf_op jit(solution)/shard_map/reduce_scatter | solution.py:308
  2735.8 109.5 %reduce-scatter.14.cloned.1.call-done = f32[128,1024]{1,0:T(8,128)} async-done(((f32[2048,1024]{1,0:T(8,128)}), f32[128,1024]{1,0:T(8,128)}) %reduce-scatter.14.cloned.1.call-update) | async-done | bytes 524304 | tf_op jit(solution)/shard_map/reduce_scatter | solution.py:306
  2845.3 109.6 %reduce-scatter.16.cloned.1.call-done = f32[128,1024]{1,0:T(8,128)} async-done(((f32[2048,1024]{1,0:T(8,128)}), f32[128,1024]{1,0:T(8,128)}) %reduce-scatter.16.cloned.1.call-update) | async-done | bytes 524304 | tf_op jit(solution)/shard_map/reduce_scatter | solution.py:307
  2954.9 337.6 %reduce-scatter.22.cloned.1.call-done = f32[128,4096]{1,0:T(8,128)} async-done(((f32[2048,4096]{1,0:T(8,128)}), f32[128,4096]{1,0:T(8,128)}) %reduce-scatter.22.cloned.1.call-update) | async-done | bytes 2097168 | tf_op jit(solution)/shard_map/reduce_scatter | solution.py:309
  3292.6 337.2 %reduce-scatter.24.cloned.1.call-done = f32[4096,128]{1,0:T(8,128)} async-done(((f32[4096,2048]{1,0:T(8,128)}), f32[4096,128]{1,0:T(8,128)}) %reduce-scatter.24.cloned.1.call-update) | async-done | bytes 2097168 | tf_op jit(solution)/shard_map/reduce_scatter | solution.py:318
  (382 shorter events, 141.1 us)
Async XLA Ops:
  7.2 875.4 %copy-start = (f32[36,36]{1,0:T(8,128)S(1)}, f32[36,36]{1,0:T(8,128)}, u32[]{:S(2)}) copy-start(f32[36,36]{1,0:T(8,128)} %param.32) | copy-start | bytes 15556
  7.2 109.0 %all-gather.13.cloned.1.call-start = ((), (), s32[]{:S(2)}) async-start(), calls=%async_computation.9 | async-start | bytes 4456448 | tf_op jit(solution)/shard_map/all_gather | solution.py:72
  7.9 115.8 %all-gather.19.cloned.1.call-start = ((), (), s32[]{:S(2)}) async-start(), calls=%async_computation.12 | async-start | bytes 4456448 | tf_op jit(solution)/shard_map/all_gather | solution.py:71
  8.7 157.7 %all-gather.17.cloned.1.call-start = ((), (), s32[]{:S(2)}) async-start(), calls=%async_computation.11 | async-start | bytes 4456448 | tf_op jit(solution)/shard_map/all_gather | solution.py:70
  9.4 238.2 %all-gather.15.cloned.1.call-start = ((), (), s32[]{:S(2)}) async-start(), calls=%async_computation.10 | async-start | bytes 5242880 | tf_op jit(solution)/shard_map/all_gather | solution.py:182
  43.3 136.5 %copy-start.63 = (f32[16,1,128]{2,1,0:T(1,128)}, f32[16,1,128]{2,1,0:T(1,128)S(1)}, u32[]{:S(2)}) copy-start(f32[16,1,128]{2,1,0:T(1,128)S(1)} %convert_element_type.296) | copy-start | bytes 24580
  72.0 107.8 %copy-start.102 = (f32[16,1,128]{2,1,0:T(1,128)}, f32[16,1,128]{2,1,0:T(1,128)S(1)}, u32[]{:S(2)}) copy-start(f32[16,1,128]{2,1,0:T(1,128)S(1)} %convert_element_type.297) | copy-start | bytes 24580
  110.6 69.2 %copy-start.67 = (f32[512]{0:T(512)}, f32[512]{0:T(512)S(1)}, u32[]{:S(2)}) copy-start(f32[512]{0:T(512)S(1)} %broadcast_multiply_fusion.2) | copy-start | bytes 6148
  110.7 62.2 %copy-start.71 = (f32[512]{0:T(512)}, f32[512]{0:T(512)S(1)}, u32[]{:S(2)}) copy-start(f32[512]{0:T(512)S(1)} %broadcast_multiply_fusion.1) | copy-start | bytes 6148
  116.2 6.9 copy-start.91
  116.2 7.2 copy-start.95
  116.2 7.3 copy-start.93
  116.2 6.9 copy-start.81
  123.1 205.7 %all-gather.21.cloned.1.call-start = ((), (), s32[]{:S(2)}) async-start(), calls=%async_computation.13 | async-start | bytes 5242880 | tf_op jit(solution)/shard_map/all_gather | solution.py:179
  123.4 56.4 %copy-start.83 = (f32[512]{0:T(512)}, f32[512]{0:T(512)S(1)}, u32[]{:S(2)}) copy-start(f32[512]{0:T(512)S(1)} %fusion.122) | copy-start | bytes 6148
  123.4 49.4 %copy-start.85 = (f32[512]{0:T(512)}, f32[512]{0:T(512)S(1)}, u32[]{:S(2)}) copy-start(f32[512]{0:T(512)S(1)} %fusion.123) | copy-start | bytes 6148
  123.6 61.0 %copy-start.43 = (f32[512,16]{0,1:T(8,128)}, f32[512,16]{0,1:T(8,128)S(1)}, u32[]{:S(2)}) copy-start(f32[512,16]{0,1:T(8,128)S(1)} %get-tuple-element.152) | copy-start | bytes 98308
  123.7 61.0 %copy-start.45 = (f32[512,16]{0,1:T(8,128)}, f32[512,16]{0,1:T(8,128)S(1)}, u32[]{:S(2)}) copy-start(f32[512,16]{0,1:T(8,128)S(1)} %get-tuple-element.153) | copy-start | bytes 98308
  172.9 7.0 copy-start.27
  187.6 194.0 %all-gather.23.cloned.1.call-start = ((), (), s32[]{:S(2)}) async-start(), calls=%async_computation.14 | async-start | bytes 4456448 | tf_op jit(solution)/shard_map/all_gather | solution.py:81
  188.1 306.3 %all-reduce.17.cloned.1.call-start = ((), (), s32[]{:S(2)}) async-start(), calls=%async_computation.15 | async-start | bytes 8388608 | tf_op jit(solution)/shard_map/psum | solution.py:203
  191.1 148.5 %copy-start.28 = (pred[256,1024]{1,0:T(8,128)(4,1)}, pred[256,1024]{1,0:T(8,128)(4,1)S(1)}, u32[]{:S(2)}) copy-start(pred[256,1024]{1,0:T(8,128)(4,1)S(1)} %get-tuple-element.157) | copy-start | bytes 786436
  192.8 140.5 %copy-start.23 = (bf16[512,8,128]{0,2,1:T(8,128)(2,1)}, bf16[512,8,128]{0,2,1:T(8,128)(2,1)S(1)}, u32[]{:S(2)}) copy-start(bf16[512,8,128]{0,2,1:T(8,128)(2,1)S(1)} %pad_maximum_fusion.3) | copy-start | bytes 3145732
  257.2 82.5 %copy-start.18 = (bf16[1,1024,1024]{1,2,0:T(8,128)(2,1)}, bf16[1,1024,1024]{1,2,0:T(8,128)(2,1)S(1)}, u32[]{:S(2)}) copy-start(bf16[1,1024,1024]{1,2,0:T(8,128)(2,1)S(1)} %copy.112) | copy-start | bytes 6291460
  333.3 6.4 copy-start.8
  335.2 7.6 copy-start.9
  335.2 7.6 copy-start.61
  342.8 38.8 %copy-start.49 = (bf16[8,128,256]{2,1,0:T(8,128)(2,1)}, bf16[8,128,256]{2,1,0:T(8,128)(2,1)S(1)}, u32[]{:S(2)}) copy-start(bf16[8,128,256]{2,1,0:T(8,128)(2,1)S(1)} %fusion.85) | copy-start | bytes 1572868
  346.1 42.1 %copy-start.50 = (bf16[8,128,256]{2,1,0:T(8,128)(2,1)}, bf16[8,128,256]{2,1,0:T(8,128)(2,1)S(1)}, u32[]{:S(2)}) copy-start(bf16[8,128,256]{2,1,0:T(8,128)(2,1)S(1)} %fusion.86) | copy-start | bytes 1572868
  388.2 31.2 copy-start.110
  388.2 235.6 %all-gather.25.cloned.1.call-start = ((), (), s32[]{:S(2)}) async-start(), calls=%async_computation.16 | async-start | bytes 17825792 | tf_op jit(solution)/shard_map/all_gather | solution.py:73
  389.0 365.7 %all-gather.27.cloned.1.call-start = ((), (), s32[]{:S(2)}) async-start(), calls=%async_computation.17 | async-start | bytes 17825792 | tf_op jit(solution)/shard_map/all_gather | solution.py:82
  389.7 486.2 %all-reduce.19.cloned.1.call-start = ((), (), s32[]{:S(2)}) async-start(), calls=%async_computation.18 | async-start | bytes 8388608 | tf_op jit(solution)/shard_map/psum | solution.py:208
  419.4 618.8 %copy-start.57 = (f32[16,1,128]{2,1,0:T(1,128)}, f32[16,1,128]{2,1,0:T(1,128)S(1)}, u32[]{:S(2)}) copy-start(f32[16,1,128]{2,1,0:T(1,128)S(1)} %convert_element_type.298) | copy-start | bytes 24580
  448.5 175.3 %copy-start.104 = (f32[16,1,128]{2,1,0:T(1,128)}, f32[16,1,128]{2,1,0:T(1,128)S(1)}, u32[]{:S(2)}) copy-start(f32[16,1,128]{2,1,0:T(1,128)S(1)} %convert_element_type.299) | copy-start | bytes 24580
  498.4 539.8 %copy-start.65 = (f32[512]{0:T(512)}, f32[512]{0:T(512)S(1)}, u32[]{:S(2)}) copy-start(f32[512]{0:T(512)S(1)} %broadcast_multiply_fusion) | copy-start | bytes 6148
  501.0 537.3 %copy-start.89 = (f32[512]{0:T(512)}, f32[512]{0:T(512)S(1)}, u32[]{:S(2)}) copy-start(f32[512]{0:T(512)S(1)} %fusion.124) | copy-start | bytes 6148
  769.7 263.0 %all-reduce.21.cloned.1.call-start = ((), (), s32[]{:S(2)}) async-start(), calls=%async_computation.19 | async-start | bytes 8388608 | tf_op jit(solution)/shard_map/psum | solution.py:225
  770.6 114.7 %copy-start.87 = (f32[1,2,2,128]{3,1,2,0:T(2,128)}, f32[1,2,2,128]{3,1,2,0:T(2,128)S(1)}, u32[]{:S(2)}) copy-start(f32[1,2,2,128]{3,1,2,0:T(2,128)S(1)} %copy.150) | copy-start | bytes 6148
  770.6 111.9 %copy-start.53 = (f32[5,8,2,256]{3,1,2,0:T(8,128)}, f32[5,8,2,256]{3,1,2,0:T(8,128)S(1)}, u32[]{:S(2)}) copy-start(f32[5,8,2,256]{3,1,2,0:T(8,128)S(1)} %copy.151) | copy-start | bytes 245764
  888.1 21.4 copy-start.10
  924.7 1011.1 %reduce-scatter.28.cloned.1.call-start = ((), (), s32[]{:S(2)}) async-start(), calls=%async_computation.28 | async-start | bytes 10485760
  925.4 165.6 %copy-start.98 = (f32[8,256]{1,0:T(8,128)}, f32[8,256]{1,0:T(8,128)S(1)}, u32[]{:S(2)}) copy-start(f32[8,256]{1,0:T(8,128)S(1)} %log_add_fusion) | copy-start | bytes 24580
  925.4 127.8 %copy-start.100 = (f32[8,256]{1,0:T(8,128)}, f32[8,256]{1,0:T(8,128)S(1)}, u32[]{:S(2)}) copy-start(f32[8,256]{1,0:T(8,128)S(1)} %log_add_fusion.1) | copy-start | bytes 24580
  1077.8 8.7 copy-start.19
  1077.8 8.7 copy-start.34
  1115.3 8.7 copy-start.13
  1791.3 361.1 %reduce-scatter.12.cloned.1.call-start = ((), (), s32[]{:S(2)}) async-start(), calls=%async_computation.20 | async-start | bytes 10485760 | tf_op jit(solution)/shard_map/reduce_scatter | solution.py:262
  1828.0 631.9 %all-reduce.23.cloned.1.call-start = ((), (), s32[]{:S(2)}) async-start(), calls=%async_computation.29 | async-start | bytes 25165824 | tf_op jit(solution)/shard_map/psum | solution.py:276
  1851.8 24.0 copy-start.44
  1851.8 24.0 copy-start.46
  2154.1 6.7 copy-start.26
  2169.6 502.0 %reduce-scatter.26.cloned.1.call-start = ((), (), s32[]{:S(2)}) async-start(), calls=%async_computation.27 | async-start | bytes 348160 | tf_op jit(solution)/shard_map/reduce_scatter | solution.py:310
  2176.3 495.3 %reduce-scatter.20.cloned.1.call-start = ((), (), s32[]{:S(2)}) async-start(), calls=%async_computation.24 | async-start | bytes 8912896 | tf_op jit(solution)/shard_map/reduce_scatter | solution.py:317
  2184.8 551.0 %reduce-scatter.18.cloned.1.call-start = ((), (), s32[]{:S(2)}) async-start(), calls=%async_computation.23 | async-start | bytes 8912896 | tf_op jit(solution)/shard_map/reduce_scatter | solution.py:308
  2193.7 651.6 %reduce-scatter.14.cloned.1.call-start = ((), (), s32[]{:S(2)}) async-start(), calls=%async_computation.21 | async-start | bytes 8912896 | tf_op jit(solution)/shard_map/reduce_scatter | solution.py:306
  2202.5 752.4 %reduce-scatter.16.cloned.1.call-start = ((), (), s32[]{:S(2)}) async-start(), calls=%async_computation.22 | async-start | bytes 8912896 | tf_op jit(solution)/shard_map/reduce_scatter | solution.py:307
  2211.6 1081.0 %reduce-scatter.22.cloned.1.call-start = ((), (), s32[]{:S(2)}) async-start(), calls=%async_computation.25 | async-start | bytes 35651584 | tf_op jit(solution)/shard_map/reduce_scatter | solution.py:309
  2231.6 1398.2 %reduce-scatter.24.cloned.1.call-start = ((), (), s32[]{:S(2)}) async-start(), calls=%async_computation.26 | async-start | bytes 35651584 | tf_op jit(solution)/shard_map/reduce_scatter | solution.py:318
  2459.9 10.4 copy-start.75
  2459.9 10.4 copy-start.76
  2459.9 74.6 %copy-start.96 = (f32[512]{0:T(512)S(1)}, f32[512]{0:T(512)}, u32[]{:S(2)}) copy-start(f32[512]{0:T(512)} %copy-done.95) | copy-start | bytes 6148
  2459.9 74.6 %copy-start.94 = (f32[512]{0:T(512)S(1)}, f32[512]{0:T(512)}, u32[]{:S(2)}) copy-start(f32[512]{0:T(512)} %copy-done.93) | copy-start | bytes 6148
  2459.9 74.6 %copy-start.92 = (f32[512]{0:T(512)S(1)}, f32[512]{0:T(512)}, u32[]{:S(2)}) copy-start(f32[512]{0:T(512)} %copy-done.91) | copy-start | bytes 6148
  (71 other events, 178.0 us)
Sparse Core Ops, SparseCore 0:
  10.2 53.2 all-gather.12
  65.8 49.2 all-gather.18
  117.3 49.0 all-gather.16
  168.3 79.2 all-gather.14
  249.6 79.0 all-gather.20
  330.7 50.8 all-gather.22
  388.4 106.0 all-reduce.16
  496.9 126.8 all-gather.24
  626.1 128.5 all-gather.26
  769.8 106.0 all-reduce.18
  924.9 107.8 all-reduce.20
  1791.4 144.4 reduce-scatter.27
  1938.3 145.2 reduce-scatter.11
  2169.7 290.1 all-reduce.22
  2464.2 53.1 reduce-scatter.25
  2522.4 103.8 reduce-scatter.19
  2631.3 104.4 reduce-scatter.17
  2740.8 104.4 reduce-scatter.13
  2850.5 104.3 reduce-scatter.15
  2960.2 332.3 reduce-scatter.21
  3298.0 331.7 reduce-scatter.23
where the time goes:
time: 3650 us; the launch traced here: 3640 us
  waiting for transfers between devices  1870 us (51%)
  local copies, waits for them, and re-layouts  993 us (27%)
  matrix products  431 us (12%)
  blocking collectives  215 us (6%)
  other arithmetic  105 us (3%)
    unnamed x241, local copies, waits for them, and re-layouts  918 us
    reduce_scatter x1, waiting for transfers between devices, body(): lax.psum_scatter(grad_up_w, ('fsdp', 'ctx'), scatter_dimension=0, tiled=T...  338 us
    reduce_scatter x1, waiting for transfers between devices, body(): lax.psum_scatter(grad_down_w, ('fsdp', 'ctx'), scatter_dimension=1, tiled...  337 us
    dot_general x24, matrix products, product(): return jnp.einsum(form, left, right, preferred_element_type=jnp.float32)  255 us
    psum x1, waiting for transfers between devices, body(): lax.psum((product('te,ce->tc', grad_query_b, full_query), product('te,ce-...  205 us
    all_gather x1, waiting for transfers between devices, gather_weights(): lax.all_gather(w_up, ('fsdp', 'ctx'), axis=0, tiled=True)  123 us
    reduce_scatter x1, waiting for transfers between devices, body(): lax.psum_scatter(grad_key_w, ('fsdp', 'ctx'), scatter_dimension=0, tiled=...  110 us
    reduce_scatter x1, waiting for transfers between devices, body(): lax.psum_scatter(grad_query_w, ('fsdp', 'ctx'), scatter_dimension=0, tile...  110 us
  transfers between devices with their start and end apart: 21, of which 16 were waited for; matrix products, arithmetic and copies ran while one was open for 18% of the time, Pallas kernels for 0%

commit v1 on v0

v1 whole, which is shorter than its diff:
```python
from functools import partial
import math

import jax
import jax.numpy as jnp
from jax import lax
from jax.experimental import pallas as pl
from jax.experimental.pallas import tpu as pltpu
from jax.sharding import PartitionSpec as P

HD = 128
ROT = 32
STREAMS = 4
MIXW = 36
EPSILON = 1e-05
RMS_EPSILON = 1e-06
HIGHEST = lax.Precision.HIGHEST
NEGATIVE = -1e30
F32 = jnp.float32
BF16 = jnp.bfloat16
GROUP = 16


def params(grid_rank):
    return pltpu.CompilerParams(
        dimension_semantics=("arbitrary",) * grid_rank, vmem_limit_bytes=56 * 1024 * 1024
    )


def xor_pairs(size, mask):
    return [(i, i ^ mask) for i in range(size)]


def over_fsdp(values, mask):
    return lax.ppermute(values, "fsdp", xor_pairs(lax.axis_size("fsdp"), mask))


def over_tp(values):
    return lax.ppermute(values, "tp", xor_pairs(lax.axis_size("tp"), 1))


def shift_ctx(values, step):
    size = lax.axis_size("ctx")
    return lax.ppermute(values, "ctx", [(i, (i + step) % size) for i in range(size)])


def bits_of(size):
    return [1 << b for b in reversed(range(size.bit_length() - 1))]


def block_masks(size):
    masks = [0]
    for bit in bits_of(size):
        masks = masks + [m ^ bit for m in masks]
    return masks


def gather_blocks(shard):
    parts = [lax.all_gather(shard, "ctx", axis=0, tiled=True)]
    for bit in bits_of(lax.axis_size("fsdp")):
        parts = parts + [over_fsdp(p, bit) for p in parts]
    return parts


def scatter_blocks(blocks):
    for bit in reversed(bits_of(lax.axis_size("fsdp"))):
        half = len(blocks) // 2
        masks = block_masks(len(blocks))
        keep, send = blocks[:half], blocks[half:]
        blocks = [k + over_fsdp(s.astype(BF16), bit).astype(F32) for k, s in zip(keep, send)]
    return lax.psum_scatter(
        blocks[0].astype(BF16), "ctx", scatter_dimension=0, tiled=True
    ).astype(F32)


def tp_sum(part):
    mine = lax.optimization_barrier(part.astype(BF16))
    return mine.astype(F32) + over_tp(mine).astype(F32)


def mix_kernel(perm_ref, earlier_ref, coeff_ref, gain_ref, shift_ref, a_ref, z_ref):
    prev = earlier_ref.shape[0]
    width = earlier_ref.shape[2]
    parts = perm_ref.shape[0]
    block = width // parts
    step = min(block, 256)

    def group(i, carry):
        rows = pl.ds(pl.multiple_of(i * GROUP, GROUP), GROUP)
        coeff = coeff_ref[rows, :]
        for p in range(parts):
            for c in range(0, block, step):
                source = pl.ds(pl.multiple_of(perm_ref[p] * block + c, 128), step)
                sums = [None] * STREAMS
                for j in range(prev):
                    x = earlier_ref[j, rows, source].astype(F32)
                    for s in range(STREAMS):
                        k = s * prev + j
                        term = coeff[:, k : k + 1] * x
                        sums[s] = term if sums[s] is None else sums[s] + term
                for s in range(STREAMS):
                    z_ref[s, rows, p * block + c : p * block + c + step] = sums[s]
        for s in range(STREAMS - 1):
            z = z_ref[s, rows, :]
            center = z - jnp.mean(z, axis=-1, keepdims=True)
            spread = jnp.mean(center * center, axis=-1, keepdims=True)
            a_ref[s, rows, :] = (
                center * lax.rsqrt(spread + EPSILON) * gain_ref[...] + shift_ref[...]
            ).astype(BF16)
        return carry

    lax.fori_loop(0, earlier_ref.shape[1] // GROUP, group, 0)


def mix_streams(perm, inputs, coeff, gain, shift, tile=64):
    prev, tokens, width = inputs.shape
    return pl.pallas_call(
        mix_kernel,
        name="mix",
        grid_spec=pltpu.PrefetchScalarGridSpec(
            num_scalar_prefetch=1,
            grid=(tokens // tile,),
            in_specs=[
                pl.BlockSpec((prev, tile, width), lambda t, *_: (0, t, 0)),
                pl.BlockSpec((tile, coeff.shape[1]), lambda t, *_: (t, 0)),
                pl.BlockSpec((1, width), lambda t, *_: (0, 0)),
                pl.BlockSpec((1, width), lambda t, *_: (0, 0)),
            ],
            out_specs=[
                pl.BlockSpec((STREAMS - 1, tile, width), lambda t, *_: (0, t, 0)),
                pl.BlockSpec((STREAMS, tile, width), lambda t, *_: (0, t, 0)),
            ],
        ),
        out_shape=[
            jax.ShapeDtypeStruct((STREAMS - 1, tokens, width), BF16),
            jax.ShapeDtypeStruct((STREAMS, tokens, width), F32),
        ],
        compiler_params=params(1),
    )(perm, inputs, coeff, gain, shift)


def turn(values, tables, sign):
    base, up, down = tables
    return (
        values * base
        + sign * (pltpu.roll(values, ROT // 2, 1) * up)
        + sign * (pltpu.roll(values, HD - ROT // 2, 1) * down)
    )


def blocks_kernel(place_ref, a_ref, *refs, parts, turned):
    weights = refs[:parts]
    tables = refs[parts : parts + 3]
    out_ref = refs[-1]
    block = a_ref.shape[1] // parts
    total = None
    for p in range(parts):
        term = jnp.dot(
            a_ref[:, p * block : (p + 1) * block], weights[p][...], preferred_element_type=F32
        )
        total = term if total is None else total + term
    if turned:
        tabs = [t[...] for t in tables]
        for h in range(total.shape[1] // HD):
            cols = slice(h * HD, (h + 1) * HD)
            out_ref[0, :, cols] = turn(total[:, cols], tabs, 1.0).astype(BF16)
    else:
        out_ref[0] = total.astype(BF16)


def blocks_product(place, a, weights, tables, turned):
    tokens, width = a.shape
    parts = len(weights)
    chunks = place.shape[0]
    columns = weights[0].shape[1] // chunks
    block = width // parts
    return pl.pallas_call(
        partial(blocks_kernel, parts=parts, turned=turned),
        name="heads",
        grid_spec=pltpu.PrefetchScalarGridSpec(
            num_scalar_prefetch=1,
            grid=(chunks,),
            in_specs=[pl.BlockSpec((tokens, width), lambda n, *_: (0, 0))]
            + [pl.BlockSpec((block, columns), lambda n, *_: (0, n))] * parts
            + [pl.BlockSpec((tokens, HD), lambda n, *_: (0, 0))] * 3,
            out_specs=pl.BlockSpec((1, tokens, columns), lambda n, place: (place[n], 0, 0)),
        ),
        out_shape=jax.ShapeDtypeStruct((chunks, tokens, columns), BF16),
        compiler_params=params(1),
    )(place, a, *weights, *tables)


def weights_of(query, keys, tile_index, tile, length, scale):
    count = keys.shape[0]
    scores = (
        lax.dot_general(query, keys, (((1,), (1,)), ((), ())), preferred_element_type=F32) * scale
    )
    row = tile_index * tile + lax.broadcasted_iota(jnp.int32, (tile, count), 0)
    col = lax.broadcasted_iota(jnp.int32, (tile, count), 1)
    masked = jnp.where((col <= row) & (col < length), scores, NEGATIVE)
    expo = jnp.exp(masked - jnp.max(masked, axis=-1, keepdims=True))
    return expo / jnp.sum(expo, axis=-1, keepdims=True)


def collect(source_ref, pieces, scratch, span):
    for s, piece in enumerate(pieces):
        at = pl.ds(pl.multiple_of(source_ref[s] * span, span), span)
        scratch[at, :] = piece[...]


def spread_out(source_ref, scratch, pieces, span):
    for s, piece in enumerate(pieces):
        at = pl.ds(pl.multiple_of(source_ref[s] * span, span), span)
        piece[...] = scratch[at, :]


def attend_kernel(source_ref, length_ref, *refs, chunks):
    q_in, k_in, v_in = refs[:chunks], refs[chunks : 2 * chunks], refs[2 * chunks : 3 * chunks]
    outs = refs[3 * chunks : 4 * chunks]
    q_all, k_all, v_all, o_all = refs[4 * chunks :]
    span = q_in[0].shape[0]
    length = length_ref[pl.program_id(0)]
    scale = 1.0 / math.sqrt(HD)
    collect(source_ref, q_in, q_all, span)
    collect(source_ref, k_in, k_all, span)
    collect(source_ref, v_in, v_all, span)
    for h in range(q_all.shape[1] // HD):
        cols = slice(h * HD, (h + 1) * HD)
        for i in range(chunks):
            rows = slice(i * span, (i + 1) * span)
            seen = slice(0, (i + 1) * span)
            probs = weights_of(q_all[rows, cols], k_all[seen, cols], i, span, length, scale)
            o_all[rows, cols] = jnp.dot(
                probs.astype(BF16), v_all[seen, cols], preferred_element_type=F32
            ).astype(BF16)
    spread_out(source_ref, o_all, outs, span)


def attend(source, lengths, queries, keys, values):
    chunks = len(queries)
    rows = lengths.shape[0]
    tokens, columns = queries[0].shape
    span = tokens // rows
    spec = pl.BlockSpec((span, columns), lambda r, *_: (r, 0))
    return pl.pallas_call(
        partial(attend_kernel, chunks=chunks),
        name="attend",
        grid_spec=pltpu.PrefetchScalarGridSpec(
            num_scalar_prefetch=2,
            grid=(rows,),
            in_specs=[spec] * (3 * chunks),
            out_specs=[spec] * chunks,
            scratch_shapes=[pltpu.VMEM((span * chunks, columns), BF16)] * 4,
        ),
        out_shape=[jax.ShapeDtypeStruct((tokens, columns), BF16)] * chunks,
        compiler_params=params(1),
    )(source, lengths, *queries, *keys, *values)


def attend_back_kernel(source_ref, length_ref, *refs, chunks):
    q_in, k_in, v_in, g_in = [refs[n * chunks : (n + 1) * chunks] for n in range(4)]
    tabs = refs[4 * chunks : 4 * chunks + 3]
    outs = refs[4 * chunks + 3 : 7 * chunks + 3]
    q_all, k_all, v_all, g_all, dk_sum, dv_sum, dq_all, dk_all, dv_all = refs[7 * chunks + 3 :]
    span = q_in[0].shape[0]
    length = length_ref[pl.program_id(0)]
    scale = 1.0 / math.sqrt(HD)
    collect(source_ref, q_in, q_all, span)
    collect(source_ref, k_in, k_all, span)
    collect(source_ref, v_in, v_all, span)
    collect(source_ref, g_in, g_all, span)
    by_rows = (((0,), (0,)), ((), ()))
    for h in range(q_all.shape[1] // HD):
        cols = slice(h * HD, (h + 1) * HD)
        for i in reversed(range(chunks)):
            rows = slice(i * span, (i + 1) * span)
            seen = slice(0, (i + 1) * span)
            query, grad = q_all[rows, cols], g_all[rows, cols]
            keys, values = k_all[seen, cols], v_all[seen, cols]
            probs = weights_of(query, keys, i, span, length, scale)
            grad_probs = lax.dot_general(
                grad, values, (((1,), (1,)), ((), ())), preferred_element_type=F32
            )
            delta = jnp.sum(probs * grad_probs, axis=-1, keepdims=True)
            scores = (probs * (grad_probs - delta) * scale).astype(BF16)
            turned = [t[rows, :] for t in tabs]
            dq_all[rows, cols] = turn(
                jnp.dot(scores, keys, preferred_element_type=F32), turned, -1.0
            ).astype(BF16)
            dk = lax.dot_general(scores, query, by_rows, preferred_element_type=F32)
            dv = lax.dot_general(probs.astype(BF16), grad, by_rows, preferred_element_type=F32)
            if i == chunks - 1:
                dk_sum[...] = dk
                dv_sum[...] = dv
            else:
                dk_sum[seen, :] += dk
                dv_sum[seen, :] += dv
        dk_all[:, cols] = turn(dk_sum[...], [t[...] for t in tabs], -1.0).astype(BF16)
        dv_all[:, cols] = dv_sum[...].astype(BF16)
    spread_out(source_ref, dq_all, outs[:chunks], span)
    spread_out(source_ref, dk_all, outs[chunks : 2 * chunks], span)
    spread_out(source_ref, dv_all, outs[2 * chunks :], span)


def attend_back(source, lengths, queries, keys, values, grads, tables):
    chunks = len(queries)
    rows = lengths.shape[0]
    tokens, columns = queries[0].shape
    span = tokens // rows
    seq = span * chunks
    spec = pl.BlockSpec((span, columns), lambda r, *_: (r, 0))
    whole = pl.BlockSpec((seq, HD), lambda r, *_: (0, 0))
    wide = pltpu.VMEM((seq, columns), BF16)
    outs = pl.pallas_call(
        partial(attend_back_kernel, chunks=chunks),
        name="attend_back",
        grid_spec=pltpu.PrefetchScalarGridSpec(
            num_scalar_prefetch=2,
            grid=(rows,),
            in_specs=[spec] * (4 * chunks) + [whole] * 3,
            out_specs=[spec] * (3 * chunks),
            scratch_shapes=[wide] * 4 + [pltpu.VMEM((seq, HD), F32)] * 2 + [wide] * 3,
        ),
        out_shape=[jax.ShapeDtypeStruct((tokens, columns), BF16)] * (3 * chunks),
        compiler_params=params(1),
    )(source, lengths, *queries, *keys, *values, *grads, *tables)
    return outs[:chunks], outs[chunks : 2 * chunks], outs[2 * chunks :]


def last_kernel(
    perm_ref,
    earlier_ref,
    coeff_ref,
    z_ref,
    mine_ref,
    theirs_ref,
    grad_ref,
    gain_ref,
    out_ref,
    mix_ref,
    dz_ref,
    acc_ref,
):
    prev = earlier_ref.shape[0]
    width = earlier_ref.shape[2]
    parts = perm_ref.shape[0]
    block = width // parts
    step = min(block, 256)

    def group(i, carry):
        rows = pl.ds(pl.multiple_of(i * GROUP, GROUP), GROUP)
        coeff = coeff_ref[rows, :]
        for s in range(STREAMS - 1):
            z = z_ref[s, rows, :]
            center = z - jnp.mean(z, axis=-1, keepdims=True)
            spread = jnp.mean(center * center, axis=-1, keepdims=True)
            inverse = lax.rsqrt(spread + EPSILON)
            hat = center * inverse
            e = (mine_ref[s, rows, :].astype(F32) + theirs_ref[s, rows, :].astype(F32)) * gain_ref[
                ...
            ]
            first = jnp.mean(e, axis=-1, keepdims=True)
            second = jnp.mean(e * hat, axis=-1, keepdims=True)
            dz_ref[s] = (e - first - hat * second) * inverse
        dz_ref[STREAMS - 1] = grad_ref[rows, :]
        acc_ref[...] = jnp.zeros_like(acc_ref)
        for p in range(parts):
            for c in range(0, block, step):
                here = slice(p * block + c, p * block + c + step)
                there = pl.ds(pl.multiple_of(perm_ref[p] * block + c, 128), step)
                grads = [dz_ref[s, :, here] for s in range(STREAMS)]
                for j in range(prev):
                    x = earlier_ref[j, rows, there].astype(F32)
                    total = None
                    for s in range(STREAMS):
                        k = s * prev + j
                        term = coeff[:, k : k + 1] * grads[s]
                        total = term if total is None else total + term
                        both = x * grads[s]
                        folded = both[:, :128]
                        for f in range(128, step, 128):
                            folded = folded + both[:, f : f + 128]
                        acc_ref[k] += folded
                    out_ref[j, rows, there] = total.astype(BF16)
        lane = lax.broadcasted_iota(jnp.int32, (GROUP, 128), 1)
        mixed = jnp.zeros((GROUP, 128), F32)
        for k in range(STREAMS * prev):
            mixed = jnp.where(lane == k, jnp.sum(acc_ref[k], axis=-1, keepdims=True), mixed)
        mix_ref[rows, :] = mixed
        return carry

    lax.fori_loop(0, earlier_ref.shape[1] // GROUP, group, 0)


def last_stage(perm, inputs, coeff, streams, mine, theirs, grad, gain, tile=64):
    prev, tokens, width = inputs.shape
    three = pl.BlockSpec((STREAMS - 1, tile, width), lambda t, *_: (0, t, 0))
    return pl.pallas_call(
        last_kernel,
        name="last",
        grid_spec=pltpu.PrefetchScalarGridSpec(
            num_scalar_prefetch=1,
            grid=(tokens // tile,),
            in_specs=[
                pl.BlockSpec((prev, tile, width), lambda t, *_: (0, t, 0)),
                pl.BlockSpec((tile, coeff.shape[1]), lambda t, *_: (t, 0)),
                three,
                three,
                three,
                pl.BlockSpec((tile, width), lambda t, *_: (t, 0)),
                pl.BlockSpec((1, width), lambda t, *_: (0, 0)),
            ],
            out_specs=[
                pl.BlockSpec((prev, tile, width), lambda t, *_: (0, t, 0)),
                pl.BlockSpec((tile, 128), lambda t, *_: (t, 0)),
            ],
            scratch_shapes=[
                pltpu.VMEM((STREAMS, GROUP, width), F32),
                pltpu.VMEM((STREAMS * prev, GROUP, 128), F32),
            ],
        ),
        out_shape=[
            jax.ShapeDtypeStruct((prev, tokens, width), BF16),
            jax.ShapeDtypeStruct((tokens, 128), F32),
        ],
        compiler_params=params(1),
    )(perm, inputs, coeff, streams, mine, theirs, grad, gain)


def layer_norm(values, gain, shift):
    center = values - jnp.mean(values, axis=-1, keepdims=True)
    spread = jnp.mean(center * center, axis=-1, keepdims=True)
    return center * lax.rsqrt(spread + EPSILON) * gain + shift


def activate(values):
    return jax.nn.gelu(values, approximate=False)


def mixer(final, weight_in, weight_out, bias):
    normed = final * lax.rsqrt(jnp.mean(final * final, axis=-1, keepdims=True) + RMS_EPSILON)
    hidden = activate(
        lax.dot_general(
            normed,
            weight_in,
            (((1,), (1,)), ((), ())),
            precision=HIGHEST,
            preferred_element_type=F32,
        )
    )
    return jnp.dot(hidden, weight_out, precision=HIGHEST, preferred_element_type=F32) + bias


def times_transposed(left, right):
    return lax.dot_general(left, right, (((1,), (1,)), ((), ())), preferred_element_type=F32)


def over_tokens(left, right):
    return lax.dot_general(left, right, (((0,), (0,)), ((), ())), preferred_element_type=F32)


def turn_tables(positions):
    half = ROT // 2
    frequency = 10000.0 ** (-2.0 * jnp.arange(half, dtype=F32) / ROT)
    angles = positions.astype(F32)[:, None] * frequency[None, :]
    cosine, sine = jnp.cos(angles), jnp.sin(angles)
    count = positions.shape[0]
    rest = HD - ROT
    base = jnp.concatenate([cosine, cosine, jnp.ones((count, rest), F32)], axis=1)
    up = jnp.concatenate([jnp.zeros((count, half), F32), sine, jnp.zeros((count, rest), F32)], 1)
    down = jnp.concatenate([-sine, jnp.zeros((count, half + rest), F32)], axis=1)
    return base, up, down


def body(
    earlier,
    mix_in,
    lengths,
    w_query,
    w_key,
    w_value,
    w_proj,
    w_up,
    w_down,
    first_gain,
    first_shift,
    second_gain,
    second_shift,
    mixer_in,
    mixer_out,
    mixer_bias,
    grad_out,
    grad_mix,
):
    count_prev, rows, span, width = earlier.shape
    tokens = rows * span
    fsdp, ctx = lax.axis_size("fsdp"), lax.axis_size("ctx")
    me, z = lax.axis_index("fsdp"), lax.axis_index("ctx")
    masks = block_masks(fsdp)
    place_of = [masks.index(m) for m in range(fsdp)]
    block = width // fsdp
    piece = block // ctx
    perm = jnp.stack([me ^ m for m in masks]).astype(jnp.int32)
    table = jnp.array(place_of, jnp.int32)
    ring = jnp.arange(ctx, dtype=jnp.int32)
    source = (z - ring + ctx) % ctx
    chunk_place = (ring - z + ctx) % ctx
    slots = z * span + jnp.arange(span, dtype=jnp.int32)
    valid = (slots[None, :] < lengths[:, None]).astype(F32).reshape(tokens)

    def relative(values):
        return jnp.concatenate(
            [
                lax.dynamic_slice_in_dim(values, perm[p] * block, block, values.ndim - 1)
                for p in range(fsdp)
            ],
            axis=-1,
        )

    def absolute(values):
        return jnp.concatenate(
            [
                lax.dynamic_slice_in_dim(values, table[a ^ me] * block, block, values.ndim - 1)
                for a in range(fsdp)
            ],
            axis=-1,
        )

    def part(values, p):
        return values[:, p * block : (p + 1) * block]

    small = jnp.concatenate(
        [mixer_in.T, first_gain[None], first_shift[None], second_gain[None], second_shift[None]], 0
    )
    small_all = lax.all_gather(small, ("fsdp", "ctx"), axis=0, tiled=False)
    small_all = small_all.transpose(1, 0, 2).reshape(small.shape[0], width)
    small_all = relative(small_all).astype(F32)
    mixer_full = small_all[:MIXW]
    gain_first, shift_first, gain_second, shift_second = [
        small_all[MIXW + n : MIXW + n + 1] for n in range(4)
    ]
    blocks_query = gather_blocks(w_query)
    blocks_key = gather_blocks(w_key)
    blocks_value = gather_blocks(w_value)
    blocks_proj = gather_blocks(w_proj.T)
    blocks_up = gather_blocks(w_up)
    blocks_down = gather_blocks(w_down.T)

    inputs = earlier.reshape(count_prev, tokens, width)
    coeff = mix_in.reshape(STREAMS * count_prev, tokens).T
    normed_in, streams = mix_streams(perm, inputs, coeff, gain_first, shift_first)

    tables_here = turn_tables(jnp.tile(slots, rows))
    tables_all = turn_tables(jnp.arange(span * ctx, dtype=jnp.int32))

    def to_heads(chunks):
        return [chunks[0]] + [shift_ctx(chunks[s], s) for s in range(1, ctx)]

    def to_slots(pieces):
        back = [pieces[0]] + [shift_ctx(pieces[s], -s) for s in range(1, ctx)]
        columns = back[0].shape[1]
        whole = jnp.zeros((tokens, columns * ctx), back[0].dtype)
        for s in range(ctx):
            whole = lax.dynamic_update_slice(whole, back[s], (0, ((z + s) % ctx) * columns))
        return whole

    queries = to_heads(
        blocks_product(chunk_place, normed_in[0], blocks_query, tables_here, True)
    )
    keys = to_heads(blocks_product(chunk_place, normed_in[1], blocks_key, tables_here, True))
    values = to_heads(blocks_product(chunk_place, normed_in[2], blocks_value, tables_here, False))
    attended = to_slots(attend(source, lengths, queries, keys, values))
    branch = tp_sum(
        jnp.concatenate([times_transposed(attended, w) for w in blocks_proj], axis=1)
    )
    residual = streams[STREAMS - 1] + branch

    normed = layer_norm(residual, gain_second, shift_second).astype(BF16)
    upward = sum(
        jnp.dot(part(normed, p), w, preferred_element_type=F32) for p, w in enumerate(blocks_up)
    )
    active = activate(upward).astype(BF16)
    downward = tp_sum(
        jnp.concatenate([times_transposed(active, w) for w in blocks_down], axis=1)
    )
    final = residual + downward
    output = absolute(final.astype(BF16)).reshape(rows, span, width)

    mix_value, mix_pull = jax.vjp(mixer, final, mixer_full, mixer_out, mixer_bias)
    mix_out = mix_value.T.reshape(MIXW, rows, span)
    mix_cotangent = (grad_mix.reshape(MIXW, tokens) * valid[None]).T
    grad_final_mix, grad_mixer_first, grad_mixer_second, grad_mixer_shift = mix_pull(mix_cotangent)
    grad_final = (
        relative(grad_out.reshape(tokens, width)).astype(F32) * valid[:, None] + grad_final_mix
    )

    grad_down_b = grad_final.astype(BF16)
    grad_active = sum(
        jnp.dot(part(grad_down_b, p), w, preferred_element_type=F32)
        for p, w in enumerate(blocks_down)
    )
    unused_up, gelu_pull = jax.vjp(activate, upward)
    grad_upward_b = gelu_pull(grad_active)[0].astype(BF16)
    grad_normed = tp_sum(
        jnp.concatenate([times_transposed(grad_upward_b, w) for w in blocks_up], axis=1)
    )
    grad_down = scatter_blocks([over_tokens(part(grad_down_b, p), active) for p in range(fsdp)]).T
    grad_up = scatter_blocks([over_tokens(part(normed, p), grad_upward_b) for p in range(fsdp)])
    unused_norm, norm_pull = jax.vjp(layer_norm, residual, gain_second, shift_second)
    grad_residual_norm, grad_gain_second, grad_shift_second = norm_pull(grad_normed)
    grad_residual = grad_final + grad_residual_norm
    grad_branch_b = grad_residual.astype(BF16)

    grad_proj = scatter_blocks(
        [over_tokens(part(grad_branch_b, p), attended) for p in range(fsdp)]
    ).T
    grad_heads = to_heads(
        blocks_product(chunk_place, grad_branch_b, blocks_proj, tables_here, False)
    )
    grad_q, grad_k, grad_v = attend_back(
        source, lengths, queries, keys, values, grad_heads, tables_all
    )
    grad_query_b, grad_key_b, grad_value_b = to_slots(grad_q), to_slots(grad_k), to_slots(grad_v)

    weight_blocks = (blocks_query, blocks_key, blocks_value)
    grads_b = (grad_query_b, grad_key_b, grad_value_b)
    mine = lax.optimization_barrier(
        jnp.stack(
            [
                jnp.concatenate([times_transposed(g, w) for w in ws], axis=1).astype(BF16)
                for g, ws in zip(grads_b, weight_blocks)
            ]
        )
    )
    theirs = over_tp(mine)
    weight_grads = [
        scatter_blocks([over_tokens(part(normed_in[s], p), grads_b[s]) for p in range(fsdp)])
        for s in range(3)
    ]

    center = streams[:3] - jnp.mean(streams[:3], axis=-1, keepdims=True)
    hats = center * lax.rsqrt(jnp.mean(center * center, axis=-1, keepdims=True) + EPSILON)
    mine_wide = mine.astype(F32)
    first_own = jnp.stack([jnp.sum(mine_wide * hats, (0, 1)), jnp.sum(mine_wide, (0, 1))])
    first_pair = first_own + over_tp(first_own)
    packed = jnp.concatenate(
        [grad_mixer_first, first_pair, grad_gain_second, grad_shift_second], axis=0
    )
    packed = packed.reshape(packed.shape[0], fsdp, ctx, piece).transpose(1, 2, 0, 3)
    for bit in reversed(bits_of(fsdp)):
        half = packed.shape[0] // 2
        packed = packed[:half] + over_fsdp(packed[half:], bit)
    packed = packed[0]
    own = lax.dynamic_index_in_dim(packed, z, 0, keepdims=False)
    for s in range(1, ctx):
        own = own + shift_ctx(
            lax.dynamic_index_in_dim(packed, (z + s) % ctx, 0, keepdims=False), s
        )
    tail = jnp.concatenate([grad_mixer_second, grad_mixer_shift[None]], axis=0)
    for bit in reversed(bits_of(fsdp)):
        tail = tail + over_fsdp(tail, bit)
    for bit in reversed(bits_of(ctx)):
        tail = tail + lax.ppermute(tail, "ctx", xor_pairs(ctx, bit))

    grad_inputs, grad_coeff = last_stage(
        perm, inputs, coeff, streams, mine, theirs, grad_residual, gain_first
    )
    grad_earlier = grad_inputs.reshape(earlier.shape)
    grad_mix_in = grad_coeff[:, : STREAMS * count_prev].T.reshape(mix_in.shape)
    return (
        output,
        mix_out,
        grad_earlier,
        grad_mix_in,
        weight_grads[0],
        weight_grads[1],
        weight_grads[2],
        grad_proj,
        grad_up,
        grad_down,
        own[MIXW],
        own[MIXW + 1],
        own[MIXW + 2],
        own[MIXW + 3],
        own[:MIXW].T,
        tail[:MIXW],
        tail[MIXW],
    )


def solution(mesh):
    placed = (
        P(None, "fsdp", "ctx", None),
        P(None, "fsdp", "ctx"),
        P("fsdp"),
        P(("fsdp", "ctx"), "tp"),
        P(("fsdp", "ctx"), "tp"),
        P(("fsdp", "ctx"), "tp"),
        P("tp", ("fsdp", "ctx")),
        P(("fsdp", "ctx"), "tp"),
        P("tp", ("fsdp", "ctx")),
        P(("fsdp", "ctx")),
        P(("fsdp", "ctx")),
        P(("fsdp", "ctx")),
        P(("fsdp", "ctx")),
        P(("fsdp", "ctx"), None),
        P(),
        P(),
        P("fsdp", "ctx", None),
        P(None, "fsdp", "ctx"),
    )
    return jax.shard_map(
        body,
        mesh=mesh,
        in_specs=placed,
        out_specs=(
            P("fsdp", "ctx", None),
            P(None, "fsdp", "ctx"),
            P(None, "fsdp", "ctx", None),
            P(None, "fsdp", "ctx"),
            P(("fsdp", "ctx"), "tp"),
            P(("fsdp", "ctx"), "tp"),
            P(("fsdp", "ctx"), "tp"),
            P("tp", ("fsdp", "ctx")),
            P(("fsdp", "ctx"), "tp"),
            P("tp", ("fsdp", "ctx")),
            P(("fsdp", "ctx")),
            P(("fsdp", "ctx")),
            P(("fsdp", "ctx")),
            P(("fsdp", "ctx")),
            P(("fsdp", "ctx"), None),
            P(),
            P(),
        ),
        check_vma=False,
    )
```

time: 3650 us -> 1370 us (0.38)
  waiting for transfers between devices: 1870 us -> 709 us
  local copies, waits for them, and re-layouts: 993 us -> 40.4 us
  matrix products: 431 us -> 238 us
  blocking collectives: 215 us -> 32.7 us
  Pallas kernels: 0 us -> 125 us
  starting transfers between devices: 1.65 us -> 103 us
    reduce_scatter x8 -> x6, waiting for transfers between devices: 958 us -> 0.01 us  [scatter_blocks(): lax.psum_scatter(blocks[0].astype(BF16), 'ctx', scatter_dimension=0, tile...]
    unnamed x241 -> x215, local copies, waits for them, and re-layouts: 918 us -> 14.2 us
    ppermute x0 -> x74, waiting for transfers between devices: none -> 600 us  [the longest x5 247 us: over_tp(): return lax.ppermute(values, 'tp', xor_pairs(lax.axis_size('tp'), 1))]
    psum x4 -> x0, waiting for transfers between devices: 432 us -> none  [the longest x1 205 us: body(): lax.psum((product('te,ce->tc', grad_query_b, full_query), product('te,ce-...]
    all_gather x8 -> x6, waiting for transfers between devices: 419 us -> 106 us  [gather_blocks(): parts = [lax.all_gather(shard, 'ctx', axis=0, tiled=True)]]
    dot_general x38 -> x62, matrix products: 431 us -> 238 us  [the longest x24 79.6 us: over_tokens(): lax.dot_general(left, right, (((0,), (0,)), ((), ())), preferred_element_...]
    pallas_call x0 -> x8, Pallas kernels: none -> 125 us  [the longest x1 40.9 us: last_stage(): pl.pallas_call(last_kernel, name='last', grid_spec=pltpu.PrefetchScalarGr...]
    all_gather x5 -> x1, blocking collectives: 153 us -> 32.7 us  [body(): small_all = lax.all_gather(small, ('fsdp', 'ctx'), axis=0, tiled=False)]
  transfers between devices with their start and end apart: 21 -> 86, of which waited for: 16 -> 28; matrix products, arithmetic and copies ran while one was open for 18% -> 21% of each run, Pallas kernels for 0% -> 9%
where the time goes in v1:
time: 1370 us; the launch traced here: 1360 us
  waiting for transfers between devices  709 us (52%)
  matrix products  238 us (17%)
  Pallas kernels  125 us (9%)
  starting transfers between devices  103 us (8%)
  other arithmetic  91.4 us (7%)
  local copies, waits for them, and re-layouts  40.4 us (3%)
  blocking collectives  32.7 us (2%)
  between operations  19.3 us (1%)
    ppermute x5, waiting for transfers between devices, over_tp(): return lax.ppermute(values, 'tp', xor_pairs(lax.axis_size('tp'), 1))  247 us
    ppermute x40, waiting for transfers between devices, over_fsdp(): return lax.ppermute(values, 'fsdp', xor_pairs(lax.axis_size('fsdp'), mask))  224 us
    ppermute x27, waiting for transfers between devices, shift_ctx(): lax.ppermute(values, 'ctx', [(i, (i + step) % size) for i in range(size)])  125 us
    all_gather x6, waiting for transfers between devices, gather_blocks(): parts = [lax.all_gather(shard, 'ctx', axis=0, tiled=True)]  106 us
    ppermute x27, starting transfers between devices, shift_ctx(): lax.ppermute(values, 'ctx', [(i, (i + step) % size) for i in range(size)])  83.2 us
    dot_general x24, matrix products, over_tokens(): lax.dot_general(left, right, (((0,), (0,)), ((), ())), preferred_element_...  79.6 us
    dot_general x24, matrix products, times_transposed(): lax.dot_general(left, right, (((1,), (1,)), ((), ())), preferred_element_...  63.9 us
    dot_general x4, matrix products, body(): jnp.dot(part(grad_down_b, p), w, preferred_element_type=F32)  47.2 us
  transfers between devices with their start and end apart: 86, of which 28 were waited for; matrix products, arithmetic and copies ran while one was open for 21% of the time, Pallas kernels for 9%

profile of v1, /device:TPU:0, one launch (start us, length us, event | category | flops | bytes accessed | tf_op | source)
XLA Modules:
  0.0 1359.1 jit_solution(13737962787484025062)
XLA Ops:
  11.9 28.3 %all-gather.10.cloned.1.call-done.refs_0_ = bf16[512,1024]{1,0:T(8,128)(2,1)} async-done(((bf16[128,1024]{1,0:T(8,128)(2,1)}), bf16[512,1024]{1,0:T(8,128)(2,1)}) %all-gather.10.cloned.1.call-update) | async-done | bytes 1048592 | tf_op jit(solution)/shard_map/all_gather | solution.py:59
  43.3 32.7 %all-gather = bf16[640,128]{1,0:T(8,128)(2,1)S(1)} all-gather(bf16[40,128]{1,0:T(8,128)(2,1)S(1)} %concatenate.114), channel_id=2, replica_groups=mesh['fsdp'=4,'ctx'=4,'tp'=2] {'fsdp','ctx'}, dimensions={0}, use_global_device_ids=true | all-gather | bytes 174080 | tf_op jit(solution)/shard_map/all_gather | solution.py:535
  79.6 23.5 %mix.1 = (bf16[3,512,2048]{2,1,0:T(8,128)(2,1)}, f32[4,512,2048]{2,1,0:T(8,128)}) custom-call(s32[4]{0:T(128)} %pad_add_fusion.perm_ref, bf16[8,512,2048]{2,1,0:T(8,128)(2,1)} %bitcast.224, f32[512,32]{1,0:T(8,128)} %bitcast.226, f32[1,2048]{1,0:T(1,128)} %get-tuple-element.137.gain_ref, f32[1,2048]{1,0:T(1,128)} %get-tuple-element.136.shift_ref), custom_call_target="tpu_custom_call" | custom-call | tf_op jit(solution)/shard_map/mix/pallas_call | solution.py:117
  104.2 5.9 slice_bitcast_fusion
  111.2 17.9 %collective-permute-done.refs_1_ = bf16[512,1024]{1,0:T(8,128)(2,1)} collective-permute-done((bf16[512,1024]{1,0:T(8,128)(2,1)}, bf16[512,1024]{1,0:T(8,128)(2,1)}, u32[]{:S(2)}, u32[]{:S(2)}) %collective-permute-start) | collective-permute-done | bytes 1048608 | tf_op jit(solution)/shard_map/ppermute | solution.py:35
  133.3 8.0 heads.5
  146.8 7.2 heads.6
  156.1 77.7 %all-gather.16.cloned.1.call-done = bf16[512,4096]{1,0:T(8,128)(2,1)} async-done(((bf16[128,4096]{1,0:T(8,128)(2,1)}), bf16[512,4096]{1,0:T(8,128)(2,1)}) %all-gather.16.cloned.1.call-update) | async-done | bytes 4194320 | tf_op jit(solution)/shard_map/all_gather | solution.py:59
  237.4 7.9 heads.4
  247.3 19.9 %collective-permute-done.16.refs_10_ = bf16[512,256]{1,0:T(8,128)(2,1)S(1)} collective-permute-done((bf16[512,256]{1,0:T(8,128)(2,1)}, bf16[512,256]{1,0:T(8,128)(2,1)S(1)}, u32[]{:S(2)}, u32[]{:S(2)}) %collective-permute-start.16) | collective-permute-done | bytes 262176 | tf_op jit(solution)/shard_map/ppermute | solution.py:44
  270.8 24.0 %collective-permute-start.4 = (bf16[512,256]{1,0:T(8,128)(2,1)S(1)}, bf16[512,256]{1,0:T(8,128)(2,1)S(1)}, u32[]{:S(2)}, u32[]{:S(2)}) collective-permute-start(bf16[512,256]{1,0:T(8,128)(2,1)S(1)} %get-tuple-element.131), channel_id=1, source_target_pairs={{0,4},{2,6},{4,0},{6,2},{1,5},{3,7},{5,1},{7,3},{8,12},{10,14},{12... | collective-permute-start | bytes 786440 | tf_op jit(solution)/shard_map/ppermute | solution.py:44
  298.7 14.4 %collective-permute-done.4.refs_2_ = bf16[512,256]{1,0:T(8,128)(2,1)S(1)} collective-permute-done((bf16[512,256]{1,0:T(8,128)(2,1)S(1)}, bf16[512,256]{1,0:T(8,128)(2,1)S(1)}, u32[]{:S(2)}, u32[]{:S(2)}) %collective-permute-start.4) | collective-permute-done | bytes 262176 | tf_op jit(solution)/shard_map/ppermute | solution.py:44
  313.1 8.6 collective-permute-done.5.refs_3_
  322.4 11.6 attend.1
  334.0 19.2 %collective-permute-start.18 = (bf16[512,256]{1,0:T(8,128)(2,1)}, bf16[512,256]{1,0:T(8,128)(2,1)S(1)}, u32[]{:S(2)}, u32[]{:S(2)}) collective-permute-start(bf16[512,256]{1,0:T(8,128)(2,1)} %get-tuple-element.40), channel_id=1, source_target_pairs={{0,6},{2,0},{4,2},{6,4},{1,7},{3,1},{5,3},{7,5},{8,14},{10,8},{12,... | collective-permute-start | bytes 786440 | tf_op jit(solution)/shard_map/ppermute | solution.py:44
  355.4 5.0 collective-permute-done.18
  360.4 14.4 %collective-permute-done.19 = bf16[512,256]{1,0:T(8,128)(2,1)S(1)} collective-permute-done((bf16[512,256]{1,0:T(8,128)(2,1)}, bf16[512,256]{1,0:T(8,128)(2,1)S(1)}, u32[]{:S(2)}, u32[]{:S(2)}) %collective-permute-start.19) | collective-permute-done | bytes 262176 | tf_op jit(solution)/shard_map/ppermute | solution.py:44
  383.7 43.8 %collective-permute-done.24 = bf16[512,2048]{1,0:T(8,128)(2,1)} collective-permute-done((bf16[512,2048]{1,0:T(8,128)(2,1)S(1)}, bf16[512,2048]{1,0:T(8,128)(2,1)}, u32[]{:S(2)}, u32[]{:S(2)}) %collective-permute-start.24) | collective-permute-done | bytes 2097184 | tf_op jit(solution)/shard_map/ppermute | solution.py:39
  427.5 3.6 fusion.111
  436.3 37.8 %collective-permute-done.28 = bf16[512,4096]{0,1:T(8,128)(2,1)} collective-permute-done((bf16[512,4096]{0,1:T(8,128)(2,1)}, bf16[512,4096]{0,1:T(8,128)(2,1)}, u32[]{:S(2)}, u32[]{:S(2)}) %collective-permute-start.28) | collective-permute-done | bytes 4194336 | tf_op jit(solution)/shard_map/ppermute | solution.py:35
  474.1 4.5 fusion.70
  478.6 7.9 fusion.66
  486.6 24.0 %multiply_convert_fusion = (bf16[512,4096]{1,0:T(8,128)(2,1)S(1)}, f32[512,4096]{1,0:T(8,128)}) fusion(bf16[512,4096]{1,0:T(8,128)(2,1)} %collective-permute-done.27, bf16[512,2048]{1,0:T(8,128)(2,1)S(1)} %add_convert_fusion.5, f32[512,4096]{1,0:T(8,128)} %fusion.66, f32[512,4096]{1,0:T(8,128)S(1)} %fusion.76, f32[512,4096]{1,0:T(8,128)S(1)} %fusion.70), kind=kOutput, calls=%fused_computation.12 | convolution fusion | flops 2290089984 | bytes 42467328 | tf_op jit(solution)/shard_map/dot_general | solution.py:580
  510.6 6.1 convolution_convert_fusion.18
  521.4 4.5 convolution_convert_fusion.17
  527.8 46.5 %collective-permute-done.31 = bf16[512,2048]{1,0:T(8,128)(2,1)S(1)} collective-permute-done((bf16[512,2048]{1,0:T(8,128)(2,1)S(1)}, bf16[512,2048]{1,0:T(8,128)(2,1)S(1)}, u32[]{:S(2)}, u32[]{:S(2)}) %collective-permute-start.31) | collective-permute-done | bytes 2097184 | tf_op jit(solution)/shard_map/ppermute | solution.py:39
  584.1 8.7 fusion.51
  592.8 7.9 fusion.55
  600.7 5.7 fusion.61
  606.4 24.9 %add_convert_fusion.4 = bf16[512,4096]{1,0:T(8,128)(2,1)S(1)} fusion(f32[512,4096]{1,0:T(8,128)} %fusion.51, f32[512,4096]{1,0:T(8,128)} %fusion.61, f32[512,4096]{1,0:T(8,128)} %fusion.55, f32[512,4096]{1,0:T(8,128)} %get-tuple-element.165, bf16[512,4096]{0,1:T(8,128)(2,1)S(1)} %copy-done.93, bf16[512,2048]{1,0:T(8,128)(2,1)S(1)} %get-tuple-element.100), kind=kOutput, calls=%fused_computation.11 | convolution fusion | flops 2304770048 | bytes 42467328 | tf_op jit(solution)/shard_map/dot_general | solution.py:599
  631.3 6.3 convolution_convert_fusion.14
  637.6 4.9 convolution_convert_fusion.13
  644.9 4.7 convolution_convert_fusion.12
  654.5 4.7 convolution_convert_fusion
  659.2 38.1 %collective-permute-done.32 = bf16[512,2048]{1,0:T(8,128)(2,1)S(1)} collective-permute-done((bf16[512,2048]{1,0:T(8,128)(2,1)S(1)}, bf16[512,2048]{1,0:T(8,128)(2,1)S(1)}, u32[]{:S(2)}, u32[]{:S(2)}) %collective-permute-start.32) | collective-permute-done | bytes 2097184 | tf_op jit(solution)/shard_map/ppermute | solution.py:39
  705.8 7.2 heads.7
  726.1 9.0 collective-permute-done.34.refs_14_
  735.9 19.0 %attend_back.1 = (bf16[512,256]{1,0:T(8,128)(2,1)}, bf16[512,256]{1,0:T(8,128)(2,1)}, bf16[512,256]{1,0:T(8,128)(2,1)}, bf16[512,256]{1,0:T(8,128)(2,1)}, bf16[5...) custom-call(s32[4]{0:T(128)} %and_select_fusion.1.source_ref, ...), custom_call_target="tpu_custom_call" | custom-call | tf_op jit(solution)/shard_map/attend_back/pallas_call | solution.py:314
  755.0 8.7 collective-permute-start.39
  765.0 5.9 collective-permute-done.39
  770.9 5.6 collective-permute-done.42
  776.6 23.6 %collective-permute-done.43 = bf16[512,256]{1,0:T(8,128)(2,1)S(1)} collective-permute-done((bf16[512,256]{1,0:T(8,128)(2,1)}, bf16[512,256]{1,0:T(8,128)(2,1)S(1)}, u32[]{:S(2)}, u32[]{:S(2)}) %collective-permute-start.43) | collective-permute-done | bytes 262176 | tf_op jit(solution)/shard_map/ppermute | solution.py:44
  805.0 5.3 collective-permute-done.40
  823.5 7.0 convolution_convert_fusion.1
  841.0 5.4 collective-permute-done.54
  849.4 8.0 add_convert_fusion.1
  858.0 9.5 collective-permute-done.37
  876.7 6.8 collective-permute-done.51
  890.0 4.5 convolution_convert_fusion.2
  896.5 98.9 %collective-permute-done.48 = bf16[512,1024]{1,0:T(8,128)(2,1)S(1)} collective-permute-done((bf16[512,1024]{1,0:T(8,128)(2,1)S(1)}, bf16[512,1024]{1,0:T(8,128)(2,1)S(1)}, u32[]{:S(2)}, u32[]{:S(2)}) %collective-permute-start.48) | collective-permute-done | bytes 1048608 | tf_op jit(solution)/shard_map/ppermute | solution.py:35
  997.0 8.1 fusion.59
  1005.1 10.0 add_convert_fusion
  1019.0 4.8 convolution_convert_fusion.3
  1023.9 4.7 add_convert_fusion.3
  1029.2 6.0 slice_reduce_fusion
  1035.2 5.8 fusion.74
  1066.9 54.8 %collective-permute-done.60 = bf16[512,4096]{1,0:T(8,128)(2,1)} collective-permute-done((bf16[512,4096]{1,0:T(8,128)(2,1)S(1)}, bf16[512,4096]{1,0:T(8,128)(2,1)}, u32[]{:S(2)}, u32[]{:S(2)}) %collective-permute-start.60) | collective-permute-done | bytes 4194336 | tf_op jit(solution)/shard_map/ppermute | solution.py:35
  1121.7 10.0 add_convert_fusion.2
  1132.8 8.5 maximum_maximum_fusion.mine_ref
  1141.7 6.7 multiply_reduce_fusion
  1151.7 5.4 fusion
  1159.7 119.0 %collective-permute-done.64 = f32[2,2048]{1,0:T(2,128)S(1)} collective-permute-done((f32[2,2048]{1,0:T(2,128)S(1)}, f32[2,2048]{1,0:T(2,128)S(1)}, u32[]{:S(2)}, u32[]{:S(2)}) %collective-permute-start.64) | collective-permute-done | bytes 16416 | tf_op jit(solution)/shard_map/ppermute | solution.py:39
  1285.7 4.3 collective-permute-start.67
  1303.2 40.9 %last.1 = (bf16[8,512,2048]{2,1,0:T(8,128)(2,1)}, f32[512,128]{1,0:T(8,128)}) custom-call(s32[4]{0:T(128)} %pad_add_fusion.perm_ref, bf16[8,512,2048]{2,1,0:T(8,128)(2,1)} %bitcast.225, f32[512,32]{1,0:T(8,128)} %bitcast.227, f32[4,512,2048]{2,1,0:T(8,128)} %get-tuple-element.37.z_ref, bf16[3,512,2048]{2,1,0:T(8,128)(2,1)} %maximum_maximum_fusion.mine_ref, ...), custom_call_target="tpu_custom_call" | custom-call | tf_op jit(solution)/shard_map/last/pallas_call | solution.py:398
  (517 shorter events, 215.5 us)
Async XLA Ops:
  7.2 33.1 %all-gather.10.cloned.1.call-start = ((), (), s32[]{:S(2)}) async-start(), calls=%async_computation.7 | async-start | bytes 1310720 | tf_op jit(solution)/shard_map/all_gather | solution.py:59
  7.9 68.2 %all-gather.12.cloned.1.call-start = ((), (), s32[]{:S(2)}) async-start(), calls=%async_computation.8 | async-start | bytes 1310720 | tf_op jit(solution)/shard_map/all_gather | solution.py:59
  8.7 94.5 %all-gather.8.cloned.1.call-start = ((), (), s32[]{:S(2)}) async-start(), calls=%async_computation.6 | async-start | bytes 1310720 | tf_op jit(solution)/shard_map/all_gather | solution.py:59
  9.4 123.0 %all-gather.14.cloned.1.call-start = ((), (), s32[]{:S(2)}) async-start(), calls=%async_computation.9 | async-start | bytes 1310720 | tf_op jit(solution)/shard_map/all_gather | solution.py:59
  11.3 222.5 %all-gather.16.cloned.1.call-start = ((), (), s32[]{:S(2)}) async-start(), calls=%async_computation.10 | async-start | bytes 5242880 | tf_op jit(solution)/shard_map/all_gather | solution.py:59
  11.9 370.9 %all-gather.18.cloned.1.call-start = ((), (), s32[]{:S(2)}) async-start(), calls=%async_computation.11 | async-start | bytes 5242880 | tf_op jit(solution)/shard_map/all_gather | solution.py:59
  40.3 63.8 %collective-permute-start.6 = (bf16[512,1024]{1,0:T(8,128)(2,1)}, bf16[512,1024]{1,0:T(8,128)(2,1)}, u32[]{:S(2)}, u32[]{:S(2)}) collective-permute-start(bf16[512,1024]{1,0:T(8,128)(2,1)} %all-gather.10.cloned.1.call-done.refs_0_), channel_id=1, source_target_pairs={{0,16},{8,24},{16,0},{24,8},{1,17},{9,25},{17,1},{25,9},{2,18},{10... | collective-permute-start | bytes 3145736 | tf_op jit(solution)/shard_map/ppermute | solution.py:35
  41.8 1254.1 %reduce-scatter.13.cloned.1.call-start = ((), (), s32[]{:S(2)}) async-start(), calls=%async_computation.15 | async-start | bytes 1310720 | tf_op jit(solution)/shard_map/reduce_scatter | solution.py:71
  76.2 34.3 %collective-permute-start.12 = (bf16[512,1024]{1,0:T(8,128)(2,1)}, bf16[512,1024]{1,0:T(8,128)(2,1)}, u32[]{:S(2)}, u32[]{:S(2)}) collective-permute-start(bf16[512,1024]{1,0:T(8,128)(2,1)} %all-gather.12.cloned.1.call-done.refs_0_), channel_id=1, source_target_pairs={{0,16},{8,24},{16,0},{24,8},{1,17},{9,25},{17,1},{25,9},{2,18},{10... | collective-permute-start | bytes 3145736 | tf_op jit(solution)/shard_map/ppermute | solution.py:35
  103.2 25.9 %collective-permute-start = (bf16[512,1024]{1,0:T(8,128)(2,1)}, bf16[512,1024]{1,0:T(8,128)(2,1)}, u32[]{:S(2)}, u32[]{:S(2)}) collective-permute-start(bf16[512,1024]{1,0:T(8,128)(2,1)} %all-gather.8.cloned.1.call-done.refs_0_), channel_id=1, source_target_pairs={{0,16},{8,24},{16,0},{24,8},{1,17},{9,25},{17,1},{25,9},{2,18},{10... | collective-permute-start | bytes 3145736 | tf_op jit(solution)/shard_map/ppermute | solution.py:35
  104.1 28.4 %collective-permute-start.8 = (bf16[512,1024]{1,0:T(8,128)(2,1)}, bf16[512,1024]{1,0:T(8,128)(2,1)}, u32[]{:S(2)}, u32[]{:S(2)}) collective-permute-start(bf16[512,1024]{1,0:T(8,128)(2,1)} %collective-permute-done.6.refs_1_), channel_id=1, source_target_pairs={{0,8},{8,0},{16,24},{24,16},{1,9},{9,1},{17,25},{25,17},{2,10},{10... | collective-permute-start | bytes 3145736 | tf_op jit(solution)/shard_map/ppermute | solution.py:35
  110.1 33.3 %collective-permute-start.13 = (bf16[512,1024]{1,0:T(8,128)(2,1)S(1)}, bf16[512,1024]{1,0:T(8,128)(2,1)}, u32[]{:S(2)}, u32[]{:S(2)}) collective-permute-start(bf16[512,1024]{1,0:T(8,128)(2,1)S(1)} %copy-done.37), channel_id=1, source_target_pairs={{0,8},{8,0},{16,24},{24,16},{1,9},{9,1},{17,25},{25,17},{2,10},{10... | collective-permute-start | bytes 3145736 | tf_op jit(solution)/shard_map/ppermute | solution.py:35
  110.5 32.9 %collective-permute-start.14 = (bf16[512,1024]{1,0:T(8,128)(2,1)}, bf16[512,1024]{1,0:T(8,128)(2,1)}, u32[]{:S(2)}, u32[]{:S(2)}) collective-permute-start(bf16[512,1024]{1,0:T(8,128)(2,1)} %collective-permute-done.12.refs_1_), channel_id=1, source_target_pairs={{0,8},{8,0},{16,24},{24,16},{1,9},{9,1},{17,25},{25,17},{2,10},{10... | collective-permute-start | bytes 3145736 | tf_op jit(solution)/shard_map/ppermute | solution.py:35
  110.7 45.3 %collective-permute-start.1 = (bf16[512,1024]{1,0:T(8,128)(2,1)}, bf16[512,1024]{1,0:T(8,128)(2,1)S(1)}, u32[]{:S(2)}, u32[]{:S(2)}) collective-permute-start(bf16[512,1024]{1,0:T(8,128)(2,1)} %all-gather.8.cloned.1.call-done.refs_0_), channel_id=1, source_target_pairs={{0,8},{8,0},{16,24},{24,16},{1,9},{9,1},{17,25},{25,17},{2,10},{10... | collective-permute-start | bytes 3145736 | tf_op jit(solution)/shard_map/ppermute | solution.py:35
  129.0 27.1 %collective-permute-start.2 = (bf16[512,1024]{1,0:T(8,128)(2,1)}, bf16[512,1024]{1,0:T(8,128)(2,1)}, u32[]{:S(2)}, u32[]{:S(2)}) collective-permute-start(bf16[512,1024]{1,0:T(8,128)(2,1)} %collective-permute-done.refs_1_), channel_id=1, source_target_pairs={{0,8},{8,0},{16,24},{24,16},{1,9},{9,1},{17,25},{25,17},{2,10},{10... | collective-permute-start | bytes 3145736 | tf_op jit(solution)/shard_map/ppermute | solution.py:35
  132.5 220.8 %collective-permute-start.21 = (bf16[512,1024]{1,0:T(8,128)(2,1)}, bf16[512,1024]{1,0:T(8,128)(2,1)}, u32[]{:S(2)}, u32[]{:S(2)}) collective-permute-start(bf16[512,1024]{1,0:T(8,128)(2,1)} %all-gather.14.cloned.1.call-done.refs_0_), channel_id=1, source_target_pairs={{0,16},{8,24},{16,0},{24,8},{1,17},{9,25},{17,1},{25,9},{2,18},{10... | collective-permute-start | bytes 3145736 | tf_op jit(solution)/shard_map/ppermute | solution.py:35
  143.4 91.9 %collective-permute-start.10 = (bf16[512,256]{1,0:T(8,128)(2,1)}, bf16[512,256]{1,0:T(8,128)(2,1)S(1)}, u32[]{:S(2)}, u32[]{:S(2)}) collective-permute-start(bf16[512,256]{1,0:T(8,128)(2,1)} %get-tuple-element.127), channel_id=1, source_target_pairs={{0,4},{2,6},{4,0},{6,2},{1,5},{3,7},{5,1},{7,3},{8,12},{10,14},{12... | collective-permute-start | bytes 786440 | tf_op jit(solution)/shard_map/ppermute | solution.py:44
  143.4 91.9 %collective-permute-start.11 = (bf16[512,256]{1,0:T(8,128)(2,1)}, bf16[512,256]{1,0:T(8,128)(2,1)S(1)}, u32[]{:S(2)}, u32[]{:S(2)}) collective-permute-start(bf16[512,256]{1,0:T(8,128)(2,1)} %get-tuple-element.126), channel_id=1, source_target_pairs={{0,6},{2,0},{4,2},{6,4},{1,7},{3,1},{5,3},{7,5},{8,14},{10,8},{12,... | collective-permute-start | bytes 786440 | tf_op jit(solution)/shard_map/ppermute | solution.py:44
  156.1 80.2 %collective-permute-start.15 = (bf16[512,256]{1,0:T(8,128)(2,1)S(1)}, bf16[512,256]{1,0:T(8,128)(2,1)S(1)}, u32[]{:S(2)}, u32[]{:S(2)}) collective-permute-start(bf16[512,256]{1,0:T(8,128)(2,1)S(1)} %get-tuple-element.124), channel_id=1, source_target_pairs={{0,2},{2,4},{4,6},{6,0},{1,3},{3,5},{5,7},{7,1},{8,10},{10,12},{12... | collective-permute-start | bytes 786440 | tf_op jit(solution)/shard_map/ppermute | solution.py:44
  233.8 149.4 %collective-permute-start.25 = (bf16[512,4096]{1,0:T(8,128)(2,1)}, bf16[512,4096]{1,0:T(8,128)(2,1)}, u32[]{:S(2)}, u32[]{:S(2)}) collective-permute-start(bf16[512,4096]{1,0:T(8,128)(2,1)} %all-gather.16.cloned.1.call-done), channel_id=1, source_target_pairs={{0,16},{8,24},{16,0},{24,8},{1,17},{9,25},{17,1},{25,9},{2,18},{10... | collective-permute-start | bytes 12582920 | tf_op jit(solution)/shard_map/ppermute | solution.py:35
  235.3 31.9 %collective-permute-start.16 = (bf16[512,256]{1,0:T(8,128)(2,1)}, bf16[512,256]{1,0:T(8,128)(2,1)S(1)}, u32[]{:S(2)}, u32[]{:S(2)}) collective-permute-start(bf16[512,256]{1,0:T(8,128)(2,1)} %get-tuple-element.123), channel_id=1, source_target_pairs={{0,4},{2,6},{4,0},{6,2},{1,5},{3,7},{5,1},{7,3},{8,12},{10,14},{12... | collective-permute-start | bytes 786440 | tf_op jit(solution)/shard_map/ppermute | solution.py:44
  235.3 35.5 %collective-permute-start.17 = (bf16[512,256]{1,0:T(8,128)(2,1)S(1)}, bf16[512,256]{1,0:T(8,128)(2,1)S(1)}, u32[]{:S(2)}, u32[]{:S(2)}) collective-permute-start(bf16[512,256]{1,0:T(8,128)(2,1)S(1)} %get-tuple-element.122), channel_id=1, source_target_pairs={{0,6},{2,0},{4,2},{6,4},{1,7},{3,1},{5,3},{7,5},{8,14},{10,8},{12,... | collective-permute-start | bytes 786440 | tf_op jit(solution)/shard_map/ppermute | solution.py:44
  236.2 58.5 %collective-permute-start.9 = (bf16[512,256]{1,0:T(8,128)(2,1)S(1)}, bf16[512,256]{1,0:T(8,128)(2,1)S(1)}, u32[]{:S(2)}, u32[]{:S(2)}) collective-permute-start(bf16[512,256]{1,0:T(8,128)(2,1)S(1)} %get-tuple-element.128), channel_id=1, source_target_pairs={{0,2},{2,4},{4,6},{6,0},{1,3},{3,5},{5,7},{7,1},{8,10},{10,12},{12... | collective-permute-start | bytes 786440 | tf_op jit(solution)/shard_map/ppermute | solution.py:44
  267.2 31.4 %collective-permute-start.3 = (bf16[512,256]{1,0:T(8,128)(2,1)S(1)}, bf16[512,256]{1,0:T(8,128)(2,1)S(1)}, u32[]{:S(2)}, u32[]{:S(2)}) collective-permute-start(bf16[512,256]{1,0:T(8,128)(2,1)S(1)} %get-tuple-element.132), channel_id=1, source_target_pairs={{0,2},{2,4},{4,6},{6,0},{1,3},{3,5},{5,7},{7,1},{8,10},{10,12},{12... | collective-permute-start | bytes 786440 | tf_op jit(solution)/shard_map/ppermute | solution.py:44
  270.8 42.3 %collective-permute-start.4 = (bf16[512,256]{1,0:T(8,128)(2,1)S(1)}, bf16[512,256]{1,0:T(8,128)(2,1)S(1)}, u32[]{:S(2)}, u32[]{:S(2)}) collective-permute-start(bf16[512,256]{1,0:T(8,128)(2,1)S(1)} %get-tuple-element.131), channel_id=1, source_target_pairs={{0,4},{2,6},{4,0},{6,2},{1,5},{3,7},{5,1},{7,3},{8,12},{10,14},{12... | collective-permute-start | bytes 786440 | tf_op jit(solution)/shard_map/ppermute | solution.py:44
  294.8 26.9 %collective-permute-start.5 = (bf16[512,256]{1,0:T(8,128)(2,1)S(1)}, bf16[512,256]{1,0:T(8,128)(2,1)S(1)}, u32[]{:S(2)}, u32[]{:S(2)}) collective-permute-start(bf16[512,256]{1,0:T(8,128)(2,1)S(1)} %get-tuple-element.130), channel_id=1, source_target_pairs={{0,6},{2,0},{4,2},{6,4},{1,7},{3,1},{5,3},{7,5},{8,14},{10,8},{12,... | collective-permute-start | bytes 786440 | tf_op jit(solution)/shard_map/ppermute | solution.py:44
  334.0 26.3 %collective-permute-start.18 = (bf16[512,256]{1,0:T(8,128)(2,1)}, bf16[512,256]{1,0:T(8,128)(2,1)S(1)}, u32[]{:S(2)}, u32[]{:S(2)}) collective-permute-start(bf16[512,256]{1,0:T(8,128)(2,1)} %get-tuple-element.40), channel_id=1, source_target_pairs={{0,6},{2,0},{4,2},{6,4},{1,7},{3,1},{5,3},{7,5},{8,14},{10,8},{12,... | collective-permute-start | bytes 786440 | tf_op jit(solution)/shard_map/ppermute | solution.py:44
  353.3 21.5 %collective-permute-start.19 = (bf16[512,256]{1,0:T(8,128)(2,1)}, bf16[512,256]{1,0:T(8,128)(2,1)S(1)}, u32[]{:S(2)}, u32[]{:S(2)}) collective-permute-start(bf16[512,256]{1,0:T(8,128)(2,1)} %get-tuple-element.41), channel_id=1, source_target_pairs={{0,4},{2,6},{4,0},{6,2},{1,5},{3,7},{5,1},{7,3},{8,12},{10,14},{12... | collective-permute-start | bytes 786440 | tf_op jit(solution)/shard_map/ppermute | solution.py:44
  353.3 24.7 %collective-permute-start.23 = (bf16[512,1024]{1,0:T(8,128)(2,1)}, bf16[512,1024]{1,0:T(8,128)(2,1)S(1)}, u32[]{:S(2)}, u32[]{:S(2)}) collective-permute-start(bf16[512,1024]{1,0:T(8,128)(2,1)} %collective-permute-done.21.refs_1_), channel_id=1, source_target_pairs={{0,8},{8,0},{16,24},{24,16},{1,9},{9,1},{17,25},{25,17},{2,10},{10... | collective-permute-start | bytes 3145736 | tf_op jit(solution)/shard_map/ppermute | solution.py:35
  353.3 21.5 %collective-permute-start.20 = (bf16[512,256]{1,0:T(8,128)(2,1)}, bf16[512,256]{1,0:T(8,128)(2,1)S(1)}, u32[]{:S(2)}, u32[]{:S(2)}) collective-permute-start(bf16[512,256]{1,0:T(8,128)(2,1)} %get-tuple-element.42), channel_id=1, source_target_pairs={{0,2},{2,4},{4,6},{6,0},{1,3},{3,5},{5,7},{7,1},{8,10},{10,12},{12... | collective-permute-start | bytes 786440 | tf_op jit(solution)/shard_map/ppermute | solution.py:44
  381.1 46.4 %collective-permute-start.24 = (bf16[512,2048]{1,0:T(8,128)(2,1)S(1)}, bf16[512,2048]{1,0:T(8,128)(2,1)}, u32[]{:S(2)}, u32[]{:S(2)}) collective-permute-start(bf16[512,2048]{1,0:T(8,128)(2,1)S(1)} %pad_maximum_fusion), channel_id=1, source_target_pairs={{0,1},{1,0},{2,3},{3,2},{4,5},{5,4},{6,7},{7,6},{8,9},{9,8},{10,11... | collective-permute-start | bytes 6291464 | tf_op jit(solution)/shard_map/ppermute | solution.py:39
  382.8 91.3 %collective-permute-start.28 = (bf16[512,4096]{0,1:T(8,128)(2,1)}, bf16[512,4096]{0,1:T(8,128)(2,1)}, u32[]{:S(2)}, u32[]{:S(2)}) collective-permute-start(bf16[512,4096]{0,1:T(8,128)(2,1)} %all-gather.18.cloned.1.call-done), channel_id=1, source_target_pairs={{0,16},{8,24},{16,0},{24,8},{1,17},{9,25},{17,1},{25,9},{2,18},{10... | collective-permute-start | bytes 12582920 | tf_op jit(solution)/shard_map/ppermute | solution.py:35
  383.2 95.5 %collective-permute-start.26 = (bf16[512,4096]{1,0:T(8,128)(2,1)}, bf16[512,4096]{1,0:T(8,128)(2,1)}, u32[]{:S(2)}, u32[]{:S(2)}) collective-permute-start(bf16[512,4096]{1,0:T(8,128)(2,1)} %all-gather.16.cloned.1.call-done), channel_id=1, source_target_pairs={{0,8},{8,0},{16,24},{24,16},{1,9},{9,1},{17,25},{25,17},{2,10},{10... | collective-permute-start | bytes 12582920 | tf_op jit(solution)/shard_map/ppermute | solution.py:35
  383.2 103.4 %collective-permute-start.27 = (bf16[512,4096]{1,0:T(8,128)(2,1)}, bf16[512,4096]{1,0:T(8,128)(2,1)}, u32[]{:S(2)}, u32[]{:S(2)}) collective-permute-start(bf16[512,4096]{1,0:T(8,128)(2,1)} %collective-permute-done.25), channel_id=1, source_target_pairs={{0,8},{8,0},{16,24},{24,16},{1,9},{9,1},{17,25},{25,17},{2,10},{10... | collective-permute-start | bytes 12582920 | tf_op jit(solution)/shard_map/ppermute | solution.py:35
  383.7 137.7 %collective-permute-start.29 = (bf16[512,4096]{0,1:T(8,128)(2,1)}, bf16[512,4096]{0,1:T(8,128)(2,1)}, u32[]{:S(2)}, u32[]{:S(2)}) collective-permute-start(bf16[512,4096]{0,1:T(8,128)(2,1)} %all-gather.18.cloned.1.call-done), channel_id=1, source_target_pairs={{0,8},{8,0},{16,24},{24,16},{1,9},{9,1},{17,25},{25,17},{2,10},{10... | collective-permute-start | bytes 12582920 | tf_op jit(solution)/shard_map/ppermute | solution.py:35
  474.1 44.9 %collective-permute-start.30 = (bf16[512,4096]{0,1:T(8,128)(2,1)}, bf16[512,4096]{0,1:T(8,128)(2,1)S(1)}, u32[]{:S(2)}, u32[]{:S(2)}) collective-permute-start(bf16[512,4096]{0,1:T(8,128)(2,1)} %collective-permute-done.28), channel_id=1, source_target_pairs={{0,8},{8,0},{16,24},{24,16},{1,9},{9,1},{17,25},{25,17},{2,10},{10... | collective-permute-start | bytes 12582920 | tf_op jit(solution)/shard_map/ppermute | solution.py:35
  526.2 48.1 %collective-permute-start.31 = (bf16[512,2048]{1,0:T(8,128)(2,1)S(1)}, bf16[512,2048]{1,0:T(8,128)(2,1)S(1)}, u32[]{:S(2)}, u32[]{:S(2)}) collective-permute-start(bf16[512,2048]{1,0:T(8,128)(2,1)S(1)} %pad_maximum_fusion.1), channel_id=1, source_target_pairs={{0,1},{1,0},{2,3},{3,2},{4,5},{5,4},{6,7},{7,6},{8,9},{9,8},{10,11... | collective-permute-start | bytes 6291464 | tf_op jit(solution)/shard_map/ppermute | solution.py:39
  649.9 47.3 %collective-permute-start.32 = (bf16[512,2048]{1,0:T(8,128)(2,1)S(1)}, bf16[512,2048]{1,0:T(8,128)(2,1)S(1)}, u32[]{:S(2)}, u32[]{:S(2)}) collective-permute-start(bf16[512,2048]{1,0:T(8,128)(2,1)S(1)} %pad_maximum_fusion.3), channel_id=1, source_target_pairs={{0,1},{1,0},{2,3},{3,2},{4,5},{5,4},{6,7},{7,6},{8,9},{9,8},{10,11... | collective-permute-start | bytes 6291464 | tf_op jit(solution)/shard_map/ppermute | solution.py:39
  659.2 190.1 %collective-permute-start.62 = (bf16[512,4096]{1,0:T(8,128)(2,1)}, bf16[512,4096]{1,0:T(8,128)(2,1)}, u32[]{:S(2)}, u32[]{:S(2)}) collective-permute-start(bf16[512,4096]{1,0:T(8,128)(2,1)} %convolution_convert_fusion), channel_id=1, source_target_pairs={{0,8},{8,0},{16,24},{24,16},{1,9},{9,1},{17,25},{25,17},{2,10},{10... | collective-permute-start | bytes 12582920 | tf_op jit(solution)/shard_map/ppermute | solution.py:35
  721.9 78.5 %collective-permute-start.56 = (bf16[512,1024]{1,0:T(8,128)(2,1)}, bf16[512,1024]{1,0:T(8,128)(2,1)}, u32[]{:S(2)}, u32[]{:S(2)}) collective-permute-start(bf16[512,1024]{1,0:T(8,128)(2,1)} %convolution_convert_fusion.4), channel_id=1, source_target_pairs={{0,8},{8,0},{16,24},{24,16},{1,9},{9,1},{17,25},{25,17},{2,10},{10... | collective-permute-start | bytes 3145736 | tf_op jit(solution)/shard_map/ppermute | solution.py:35
  764.6 35.6 %collective-permute-start.43 = (bf16[512,256]{1,0:T(8,128)(2,1)}, bf16[512,256]{1,0:T(8,128)(2,1)S(1)}, u32[]{:S(2)}, u32[]{:S(2)}) collective-permute-start(bf16[512,256]{1,0:T(8,128)(2,1)} %get-tuple-element.53), channel_id=1, source_target_pairs={{0,4},{2,6},{4,0},{6,2},{1,5},{3,7},{5,1},{7,3},{8,12},{10,14},{12... | collective-permute-start | bytes 786440 | tf_op jit(solution)/shard_map/ppermute | solution.py:44
  770.9 29.3 %collective-permute-start.44 = (bf16[512,256]{1,0:T(8,128)(2,1)S(1)}, bf16[512,256]{1,0:T(8,128)(2,1)S(1)}, u32[]{:S(2)}, u32[]{:S(2)}) collective-permute-start(bf16[512,256]{1,0:T(8,128)(2,1)S(1)} %copy-done.97), channel_id=1, source_target_pairs={{0,2},{2,4},{4,6},{6,0},{1,3},{3,5},{5,7},{7,1},{8,10},{10,12},{12... | collective-permute-start | bytes 786440 | tf_op jit(solution)/shard_map/ppermute | solution.py:44
  776.5 40.0 %collective-permute-start.55 = (bf16[512,1024]{1,0:T(8,128)(2,1)S(1)}, bf16[512,1024]{1,0:T(8,128)(2,1)S(1)}, u32[]{:S(2)}, u32[]{:S(2)}) collective-permute-start(bf16[512,1024]{1,0:T(8,128)(2,1)S(1)} %convolution_convert_fusion.5), channel_id=1, source_target_pairs={{0,8},{8,0},{16,24},{24,16},{1,9},{9,1},{17,25},{25,17},{2,10},{10... | collective-permute-start | bytes 3145736 | tf_op jit(solution)/shard_map/ppermute | solution.py:35
  812.0 28.1 %collective-permute-start.52 = (bf16[512,1024]{1,0:T(8,128)(2,1)}, bf16[512,1024]{1,0:T(8,128)(2,1)}, u32[]{:S(2)}, u32[]{:S(2)}) collective-permute-start(bf16[512,1024]{1,0:T(8,128)(2,1)} %convolution_convert_fusion.7), channel_id=1, source_target_pairs={{0,8},{8,0},{16,24},{24,16},{1,9},{9,1},{17,25},{25,17},{2,10},{10... | collective-permute-start | bytes 3145736 | tf_op jit(solution)/shard_map/ppermute | solution.py:35
  820.5 477.3 %reduce-scatter.11.cloned.1.call-start = ((), (), s32[]{:S(2)}) async-start(), calls=%async_computation.14 | async-start | bytes 1310720 | tf_op jit(solution)/shard_map/reduce_scatter | solution.py:71
  823.1 23.3 %collective-permute-start.54 = (bf16[512,1024]{1,0:T(8,128)(2,1)S(1)}, bf16[512,1024]{1,0:T(8,128)(2,1)S(1)}, u32[]{:S(2)}, u32[]{:S(2)}) collective-permute-start(bf16[512,1024]{1,0:T(8,128)(2,1)S(1)} %add_convert_fusion.9), channel_id=1, source_target_pairs={{0,16},{8,24},{16,0},{24,8},{1,17},{9,25},{17,1},{25,9},{2,18},{10... | collective-permute-start | bytes 3145736 | tf_op jit(solution)/shard_map/ppermute | solution.py:35
  830.5 174.6 %collective-permute-start.61 = (bf16[512,4096]{1,0:T(8,128)(2,1)}, bf16[512,4096]{1,0:T(8,128)(2,1)}, u32[]{:S(2)}, u32[]{:S(2)}) collective-permute-start(bf16[512,4096]{1,0:T(8,128)(2,1)} %convolution_convert_fusion.1), channel_id=1, source_target_pairs={{0,8},{8,0},{16,24},{24,16},{1,9},{9,1},{17,25},{25,17},{2,10},{10... | collective-permute-start | bytes 12582920 | tf_op jit(solution)/shard_map/ppermute | solution.py:35
  834.0 23.3 %collective-permute-start.36 = (bf16[512,256]{1,0:T(8,128)(2,1)}, bf16[512,256]{1,0:T(8,128)(2,1)S(1)}, u32[]{:S(2)}, u32[]{:S(2)}) collective-permute-start(bf16[512,256]{1,0:T(8,128)(2,1)} %get-tuple-element.44), channel_id=1, source_target_pairs={{0,6},{2,0},{4,2},{6,4},{1,7},{3,1},{5,3},{7,5},{8,14},{10,8},{12,... | collective-permute-start | bytes 786440 | tf_op jit(solution)/shard_map/ppermute | solution.py:44
  840.1 27.4 %collective-permute-start.37 = (bf16[512,256]{1,0:T(8,128)(2,1)}, bf16[512,256]{1,0:T(8,128)(2,1)S(1)}, u32[]{:S(2)}, u32[]{:S(2)}) collective-permute-start(bf16[512,256]{1,0:T(8,128)(2,1)} %get-tuple-element.45), channel_id=1, source_target_pairs={{0,4},{2,6},{4,0},{6,2},{1,5},{3,7},{5,1},{7,3},{8,12},{10,14},{12... | collective-permute-start | bytes 786440 | tf_op jit(solution)/shard_map/ppermute | solution.py:44
  846.4 24.7 %collective-permute-start.38 = (bf16[512,256]{1,0:T(8,128)(2,1)}, bf16[512,256]{1,0:T(8,128)(2,1)}, u32[]{:S(2)}, u32[]{:S(2)}) collective-permute-start(bf16[512,256]{1,0:T(8,128)(2,1)} %get-tuple-element.46), channel_id=1, source_target_pairs={{0,2},{2,4},{4,6},{6,0},{1,3},{3,5},{5,7},{7,1},{8,10},{10,12},{12... | collective-permute-start | bytes 786440 | tf_op jit(solution)/shard_map/ppermute | solution.py:44
  849.2 450.4 %reduce-scatter.9.cloned.1.call-start = ((), (), s32[]{:S(2)}) async-start(), calls=%async_computation.13 | async-start | bytes 1310720 | tf_op jit(solution)/shard_map/reduce_scatter | solution.py:71
  849.3 27.4 %collective-permute-start.49 = (bf16[512,1024]{1,0:T(8,128)(2,1)}, bf16[512,1024]{1,0:T(8,128)(2,1)S(1)}, u32[]{:S(2)}, u32[]{:S(2)}) collective-permute-start(bf16[512,1024]{1,0:T(8,128)(2,1)} %convolution_convert_fusion.9), channel_id=1, source_target_pairs={{0,8},{8,0},{16,24},{24,16},{1,9},{9,1},{17,25},{25,17},{2,10},{10... | collective-permute-start | bytes 3145736 | tf_op jit(solution)/shard_map/ppermute | solution.py:35
  857.4 26.0 %collective-permute-start.51 = (bf16[512,1024]{1,0:T(8,128)(2,1)S(1)}, bf16[512,1024]{1,0:T(8,128)(2,1)S(1)}, u32[]{:S(2)}, u32[]{:S(2)}) collective-permute-start(bf16[512,1024]{1,0:T(8,128)(2,1)S(1)} %copy-done.94), channel_id=1, source_target_pairs={{0,16},{8,24},{16,0},{24,8},{1,17},{9,25},{17,1},{25,9},{2,18},{10... | collective-permute-start | bytes 3145736 | tf_op jit(solution)/shard_map/ppermute | solution.py:35
  867.5 137.7 %collective-permute-start.63 = (bf16[512,4096]{1,0:T(8,128)(2,1)}, bf16[512,4096]{1,0:T(8,128)(2,1)}, u32[]{:S(2)}, u32[]{:S(2)}) collective-permute-start(bf16[512,4096]{1,0:T(8,128)(2,1)} %add_convert_fusion.1), channel_id=1, source_target_pairs={{0,16},{8,24},{16,0},{24,8},{1,17},{9,25},{17,1},{25,9},{2,18},{10... | collective-permute-start | bytes 12582920 | tf_op jit(solution)/shard_map/ppermute | solution.py:35
  885.0 416.4 %reduce-scatter.7.cloned.1.call-start = ((), (), s32[]{:S(2)}) async-start(), calls=%async_computation.12 | async-start | bytes 1310720 | tf_op jit(solution)/shard_map/reduce_scatter | solution.py:71
  889.4 105.9 %collective-permute-start.48 = (bf16[512,1024]{1,0:T(8,128)(2,1)S(1)}, bf16[512,1024]{1,0:T(8,128)(2,1)S(1)}, u32[]{:S(2)}, u32[]{:S(2)}) collective-permute-start(bf16[512,1024]{1,0:T(8,128)(2,1)S(1)} %add_convert_fusion.13), channel_id=1, source_target_pairs={{0,16},{8,24},{16,0},{24,8},{1,17},{9,25},{17,1},{25,9},{2,18},{10... | collective-permute-start | bytes 3145736 | tf_op jit(solution)/shard_map/ppermute | solution.py:35
  894.5 129.4 %collective-permute-start.59 = (bf16[512,4096]{1,0:T(8,128)(2,1)}, bf16[512,4096]{1,0:T(8,128)(2,1)}, u32[]{:S(2)}, u32[]{:S(2)}) collective-permute-start(bf16[512,4096]{1,0:T(8,128)(2,1)} %convolution_convert_fusion.2), channel_id=1, source_target_pairs={{0,8},{8,0},{16,24},{24,16},{1,9},{9,1},{17,25},{25,17},{2,10},{10... | collective-permute-start | bytes 12582920 | tf_op jit(solution)/shard_map/ppermute | solution.py:35
  996.9 348.9 %reduce-scatter.17.cloned.1.call-start = ((), (), s32[]{:S(2)}) async-start(), calls=%async_computation.17 | async-start | bytes 5242880 | tf_op jit(solution)/shard_map/reduce_scatter | solution.py:71
  1015.1 333.9 %reduce-scatter.15.cloned.1.call-start = ((), (), s32[]{:S(2)}) async-start(), calls=%async_computation.16 | async-start | bytes 5242880 | tf_op jit(solution)/shard_map/reduce_scatter | solution.py:71
  1023.8 43.2 %collective-permute-start.58 = (bf16[512,4096]{1,0:T(8,128)(2,1)S(1)}, bf16[512,4096]{1,0:T(8,128)(2,1)}, u32[]{:S(2)}, u32[]{:S(2)}) collective-permute-start(bf16[512,4096]{1,0:T(8,128)(2,1)S(1)} %convolution_convert_fusion.3), channel_id=1, source_target_pairs={{0,8},{8,0},{16,24},{24,16},{1,9},{9,1},{17,25},{25,17},{2,10},{10... | collective-permute-start | bytes 12582920 | tf_op jit(solution)/shard_map/ppermute | solution.py:35
  1028.6 93.1 %collective-permute-start.60 = (bf16[512,4096]{1,0:T(8,128)(2,1)S(1)}, bf16[512,4096]{1,0:T(8,128)(2,1)}, u32[]{:S(2)}, u32[]{:S(2)}) collective-permute-start(bf16[512,4096]{1,0:T(8,128)(2,1)S(1)} %add_convert_fusion.3), channel_id=1, source_target_pairs={{0,16},{8,24},{16,0},{24,8},{1,17},{9,25},{17,1},{25,9},{2,18},{10... | collective-permute-start | bytes 12582920 | tf_op jit(solution)/shard_map/ppermute | solution.py:35
  1141.3 162.0 %collective-permute-start.45 = (bf16[3,512,2048]{2,1,0:T(8,128)(2,1)}, bf16[3,512,2048]{2,1,0:T(8,128)(2,1)}, u32[]{:S(2)}, u32[]{:S(2)}) collective-permute-start(bf16[3,512,2048]{2,1,0:T(8,128)(2,1)} %maximum_maximum_fusion.mine_ref), channel_id=1, source_target_pairs={{0,1},{1,0},{2,3},{3,2},{4,5},{5,4},{6,7},{7,6},{8,9},{9,8},{10,11... | collective-permute-start | bytes 18874376 | tf_op jit(solution)/shard_map/ppermute | solution.py:39
  1157.1 121.6 %collective-permute-start.64 = (f32[2,2048]{1,0:T(2,128)S(1)}, f32[2,2048]{1,0:T(2,128)S(1)}, u32[]{:S(2)}, u32[]{:S(2)}) collective-permute-start(f32[2,2048]{1,0:T(2,128)S(1)} %pad_maximum_fusion.6), channel_id=1, source_target_pairs={{0,1},{1,0},{2,3},{3,2},{4,5},{5,4},{6,7},{7,6},{8,9},{9,8},{10,11... | collective-permute-start | bytes 49160 | tf_op jit(solution)/shard_map/ppermute | solution.py:39
  1159.6 120.9 %collective-permute-start.72 = (f32[37,36]{1,0:T(8,128)S(1)}, f32[37,36]{1,0:T(8,128)S(1)}, u32[]{:S(2)}, u32[]{:S(2)}) collective-permute-start(f32[37,36]{1,0:T(8,128)S(1)} %add.430), channel_id=1, source_target_pairs={{0,2},{2,0},{4,6},{6,4},{1,3},{3,1},{5,7},{7,5},{8,10},{10,8},{12,... | collective-permute-start | bytes 15992 | tf_op jit(solution)/shard_map/ppermute | solution.py:663
  (124 other events, 3134.0 us)
Sparse Core Ops, SparseCore 0:
  9.6 30.6 all-gather.9
  41.8 29.9 all-gather.11
  73.4 27.0 all-gather.7
  102.5 27.4 all-gather.13
  131.4 102.3 all-gather.15
  235.2 115.1 all-gather.17
  820.6 32.0 reduce-scatter.12
  855.1 31.7 reduce-scatter.10
  889.7 25.8 reduce-scatter.8
  997.1 26.6 reduce-scatter.6
  1026.1 75.4 reduce-scatter.16
  1131.8 76.7 reduce-scatter.14

commit v2 on v1

v2 whole, which is shorter than its diff:
```python
from functools import partial
import math

import jax
import jax.numpy as jnp
from jax import lax
from jax.experimental import pallas as pl
from jax.experimental.pallas import tpu as pltpu
from jax.sharding import PartitionSpec as P

HD = 128
ROT = 32
STREAMS = 4
MIXW = 36
EPSILON = 1e-05
RMS_EPSILON = 1e-06
HIGHEST = lax.Precision.HIGHEST
NEGATIVE = -1e30
F32 = jnp.float32
BF16 = jnp.bfloat16
GROUP = 32
FORWARD_PACE = 3.0e7
BACKWARD_PACE = 1.5e9


def params(grid_rank):
    return pltpu.CompilerParams(
        dimension_semantics=("arbitrary",) * grid_rank, vmem_limit_bytes=56 * 1024 * 1024
    )


class Pace:
    value = FORWARD_PACE


def cost(time):
    return pl.CostEstimate(flops=int(time * Pace.value), transcendentals=0, bytes_accessed=1024)


def xor_pairs(size, mask):
    return [(i, i ^ mask) for i in range(size)]


def over_fsdp(values, mask):
    return lax.ppermute(values, "fsdp", xor_pairs(lax.axis_size("fsdp"), mask))


def over_tp(values):
    return lax.ppermute(values, "tp", xor_pairs(lax.axis_size("tp"), 1))


def shift_ctx(values, step):
    size = lax.axis_size("ctx")
    return lax.ppermute(values, "ctx", [(i, (i + step) % size) for i in range(size)])


def bits_of(size):
    return [1 << b for b in reversed(range(size.bit_length() - 1))]


def block_masks(size):
    masks = [0]
    for bit in bits_of(size):
        masks = masks + [m ^ bit for m in masks]
    return masks


def after(values, *earlier):
    return lax.optimization_barrier((values, earlier))[0]


class Order:
    def __init__(self):
        self.last = ()

    def __call__(self, values):
        return after(values, self.last)

    def keep(self, values):
        self.last = values
        return values

    def wait(self, values):
        return self.keep(self(values))


def gather_ctx(shard):
    return lax.all_gather(shard, "ctx", axis=0, tiled=True)


def cross(own):
    parts = [own]
    for bit in bits_of(lax.axis_size("fsdp"))[:-1]:
        parts = parts + [over_fsdp(p, bit) for p in parts]
    return parts


class Scatter:
    def __init__(self, order, left, rights, left_far, rights_far):
        self.order, self.left, self.far, self.rights = order, left, left_far, (rights, rights_far)
        self.count = lax.axis_size("fsdp")
        self.received = [[] for _ in range(self.count)]

    def blocks(self, chosen, first, kinds):
        near, far = self.order(self.rights)
        added = [[r for r in self.received[p] if r[2] == first] for p in chosen]
        made = grad_blocks(self.left, self.far, near, far, self.count, chosen, added, first, kinds)
        return self.order.keep(made)

    def make(self, level, first=0, kinds=None):
        half = self.count >> (level + 1)
        chosen = list(range(half, 2 * half))
        return self.blocks(chosen, first, kinds or self.left.shape[0])

    def send(self, level, made, first=0):
        half = self.count >> (level + 1)
        bit = bits_of(self.count)[::-1][level]
        got = over_fsdp(made, bit)
        for n in range(half):
            self.received[n].append((got, n, first))
        return got

    def launch(self, first=0, kinds=None, made=None):
        for level in range(1, len(bits_of(self.count))):
            if made is None:
                made = self.make(level, first, kinds)
            self.send(level, made, first)
            made = None

    def finish(self, first=0, kinds=None):
        return self.blocks([0], first, kinds or self.left.shape[0])[0]


def scatter_ctx(total):
    return lax.psum_scatter(total, "ctx", scatter_dimension=0, tiled=True).astype(F32)


def tp_sum(mine, theirs):
    return mine.astype(F32) + theirs.astype(F32)


NT = (((1,), (1,)), ((), ()))
TN = (((0,), (0,)), ((), ()))


def spread(coeff):
    count = coeff.shape[0]
    token = lax.broadcasted_iota(jnp.int32, (count, STREAMS * GROUP), 0) % GROUP
    lane = lax.broadcasted_iota(jnp.int32, (count, STREAMS * GROUP), 1)
    out = jnp.zeros((count, STREAMS * GROUP), F32)
    for s in range(STREAMS):
        out = jnp.where(lane == token + s * GROUP, coeff[:, s : s + 1], out)
    high = out.astype(BF16)
    return high, (out - high.astype(F32)).astype(BF16)


def mix_kernel(perm_ref, earlier_ref, coeff_ref, gain_ref, shift_ref, a_ref, z_ref):
    prev, tile, width = earlier_ref.shape
    parts = perm_ref.shape[0]
    block = width // parts
    for g in range(tile // GROUP):
        rows = slice(g * GROUP, (g + 1) * GROUP)
        high, low = spread(coeff_ref[g])
        for p in range(parts):
            source = pl.ds(pl.multiple_of(perm_ref[p] * block, 128), block)
            x = earlier_ref[:, rows, source].reshape(prev * GROUP, block)
            z_ref[:, rows, p * block : (p + 1) * block] = (
                lax.dot_general(high, x, TN, preferred_element_type=F32)
                + lax.dot_general(low, x, TN, preferred_element_type=F32)
            ).reshape(STREAMS, GROUP, block)
        for s in range(STREAMS - 1):
            z = z_ref[s, rows, :]
            center = z - jnp.mean(z, axis=-1, keepdims=True)
            spread_of = jnp.mean(center * center, axis=-1, keepdims=True)
            a_ref[s, rows, :] = (
                center * lax.rsqrt(spread_of + EPSILON) * gain_ref[...] + shift_ref[...]
            ).astype(BF16)


def mix_streams(perm, inputs, coeff, gain, shift, tile=64):
    prev, tokens, width = inputs.shape
    return pl.pallas_call(
        mix_kernel,
        name="mix",
        grid_spec=pltpu.PrefetchScalarGridSpec(
            num_scalar_prefetch=1,
            grid=(tokens // tile,),
            in_specs=[
                pl.BlockSpec((prev, tile, width), lambda t, *_: (0, t, 0)),
                pl.BlockSpec((tile // GROUP,) + coeff.shape[1:], lambda t, *_: (t, 0, 0)),
                pl.BlockSpec((1, width), lambda t, *_: (0, 0)),
                pl.BlockSpec((1, width), lambda t, *_: (0, 0)),
            ],
            out_specs=[
                pl.BlockSpec((STREAMS - 1, tile, width), lambda t, *_: (0, t, 0)),
                pl.BlockSpec((STREAMS, tile, width), lambda t, *_: (0, t, 0)),
            ],
        ),
        out_shape=[
            jax.ShapeDtypeStruct((STREAMS - 1, tokens, width), BF16),
            jax.ShapeDtypeStruct((STREAMS, tokens, width), F32),
        ],
        cost_estimate=cost(14),
        compiler_params=params(1),
    )(perm, inputs, coeff, gain, shift)


def turn(values, tables, sign):
    base, up, down = tables
    return (
        values * base
        + sign * (pltpu.roll(values, ROT // 2, 1) * up)
        + sign * (pltpu.roll(values, HD - ROT // 2, 1) * down)
    )


def blocks_dot(a_ref, weights):
    parts = len(weights)
    block = a_ref.shape[-1] // parts
    total = None
    for p in range(parts):
        term = jnp.dot(
            a_ref[:, p * block : (p + 1) * block], weights[p][...], preferred_element_type=F32
        )
        total = term if total is None else total + term
    return total


def block_specs(weights, rows, columns, at):
    return [pl.BlockSpec((rows, columns), lambda *ids: (0, at(*ids)))] * len(weights)


def heads_kernel(target_ref, perm_ref, a_ref, *refs, parts, turned):
    weights = refs[:parts]
    tables = refs[parts : parts + 3]
    outs = refs[parts + 3 :]
    total = blocks_dot(a_ref.at[0], weights)
    kind, step = pl.program_id(0), pl.program_id(1)
    for s, out_ref in enumerate(outs):

        @pl.when((step == s) & (kind < turned))
        def _():
            tabs = [t[...] for t in tables]
            for h in range(total.shape[1] // HD):
                cols = slice(h * HD, (h + 1) * HD)
                out_ref[0, :, cols] = turn(total[:, cols], tabs, 1.0).astype(BF16)

        @pl.when((step == s) & (kind >= turned))
        def _():
            out_ref[0] = total.astype(BF16)


def to_chunks(target, perm, a, weights, tables, turned):
    kinds, tokens, width = a.shape
    parts = perm.shape[0]
    chunks = target.shape[0]
    columns = weights[0].shape[1] // chunks // kinds
    specs = block_specs(
        weights, width // parts, columns, lambda s, n, target, _: s * chunks + target[n]
    )
    return pl.pallas_call(
        partial(heads_kernel, parts=parts, turned=turned),
        name="heads",
        grid_spec=pltpu.PrefetchScalarGridSpec(
            num_scalar_prefetch=2,
            grid=(kinds, chunks),
            in_specs=[pl.BlockSpec((1, tokens, width), lambda s, n, *_: (s, 0, 0))]
            + specs
            + [pl.BlockSpec((tokens, HD), lambda s, n, *_: (0, 0))] * 3,
            out_specs=[pl.BlockSpec((1, tokens, columns), lambda s, n, *_: (s, 0, 0))] * chunks,
        ),
        out_shape=[jax.ShapeDtypeStruct((kinds, tokens, columns), BF16)] * chunks,
        cost_estimate=cost(2 * kinds * chunks),
        compiler_params=params(2),
    )(target, perm, a, *weights, *tables)


def join_kernel(target_ref, *refs):
    for s in range(len(refs) - 1):

        @pl.when(pl.program_id(0) == s)
        def _():
            refs[-1][...] = refs[s][...]


def join(target, pieces):
    kinds, count, columns = pieces[0].shape
    chunks = len(pieces)
    return pl.pallas_call(
        join_kernel,
        name="join",
        grid_spec=pltpu.PrefetchScalarGridSpec(
            num_scalar_prefetch=1,
            grid=(chunks,),
            in_specs=[pl.BlockSpec((kinds, count, columns), lambda n, _: (0, 0, 0))] * chunks,
            out_specs=pl.BlockSpec((kinds, count, columns), lambda n, target: (0, 0, target[n])),
        ),
        out_shape=jax.ShapeDtypeStruct((kinds, count, columns * chunks), BF16),
        cost_estimate=cost(2),
        compiler_params=params(1),
    )(target, *pieces)


def weights_of(query, keys, tile_index, tile, length, scale):
    count = keys.shape[0]
    scores = (
        lax.dot_general(query, keys, (((1,), (1,)), ((), ())), preferred_element_type=F32) * scale
    )
    row = tile_index * tile + lax.broadcasted_iota(jnp.int32, (tile, count), 0)
    col = lax.broadcasted_iota(jnp.int32, (tile, count), 1)
    masked = jnp.where((col <= row) & (col < length), scores, NEGATIVE)
    expo = jnp.exp(masked - jnp.max(masked, axis=-1, keepdims=True))
    return expo / jnp.sum(expo, axis=-1, keepdims=True)


def collect(source_ref, pieces, scratch, span):
    for s, piece in enumerate(pieces):
        at = pl.ds(pl.multiple_of(source_ref[s] * span, span), span)
        scratch[at, :] = piece[...]


def spread_out(source_ref, scratch, pieces, span):
    for s, piece in enumerate(pieces):
        at = pl.ds(pl.multiple_of(source_ref[s] * span, span), span)
        piece[...] = scratch[at, :]


def collect(source_ref, pieces, kind, scratch):
    span = pieces[0].shape[1]
    for s, piece in enumerate(pieces):
        at = pl.ds(pl.multiple_of(source_ref[s] * span, span), span)
        scratch[at, :] = piece[kind]


def spread_out(source_ref, scratch, pieces, kind):
    span = pieces[0].shape[1]
    for s, piece in enumerate(pieces):
        at = pl.ds(pl.multiple_of(source_ref[s] * span, span), span)
        piece[kind] = scratch[at, :]


def attend_kernel(source_ref, length_ref, *refs, chunks):
    ins, outs = refs[:chunks], refs[chunks : 2 * chunks]
    q_all, k_all, v_all, o_all = refs[2 * chunks :]
    span = ins[0].shape[1]
    length = length_ref[pl.program_id(0)]
    scale = 1.0 / math.sqrt(HD)
    for kind, scratch in enumerate((q_all, k_all, v_all)):
        collect(source_ref, ins, kind, scratch)
    for h in range(q_all.shape[1] // HD):
        cols = slice(h * HD, (h + 1) * HD)
        for i in range(chunks):
            rows = slice(i * span, (i + 1) * span)
            seen = slice(0, (i + 1) * span)
            probs = weights_of(q_all[rows, cols], k_all[seen, cols], i, span, length, scale)
            o_all[rows, cols] = jnp.dot(
                probs.astype(BF16), v_all[seen, cols], preferred_element_type=F32
            ).astype(BF16)
    spread_out(source_ref, o_all, outs, 0)


def attend(source, lengths, pieces):
    chunks = len(pieces)
    rows = lengths.shape[0]
    kinds, tokens, columns = pieces[0].shape
    span = tokens // rows
    return pl.pallas_call(
        partial(attend_kernel, chunks=chunks),
        name="attend",
        grid_spec=pltpu.PrefetchScalarGridSpec(
            num_scalar_prefetch=2,
            grid=(rows,),
            in_specs=[pl.BlockSpec((kinds, span, columns), lambda r, *_: (0, r, 0))] * chunks,
            out_specs=[pl.BlockSpec((1, span, columns), lambda r, *_: (0, r, 0))] * chunks,
            scratch_shapes=[pltpu.VMEM((span * chunks, columns), BF16)] * 4,
        ),
        out_shape=[jax.ShapeDtypeStruct((1, tokens, columns), BF16)] * chunks,
        cost_estimate=cost(6 * rows),
        compiler_params=params(1),
    )(source, lengths, *pieces)


def attend_back_kernel(source_ref, length_ref, *refs, chunks, row):
    ins, grads = refs[:chunks], refs[chunks : 2 * chunks]
    tabs = refs[2 * chunks : 2 * chunks + 3]
    outs = refs[2 * chunks + 3 : 3 * chunks + 3]
    q_all, k_all, v_all, g_all, dk_sum, dv_sum, dq_all, dk_all, dv_all = refs[3 * chunks + 3 :]
    span = ins[0].shape[1]
    length = length_ref[row]
    scale = 1.0 / math.sqrt(HD)
    for kind, scratch in enumerate((q_all, k_all, v_all)):
        collect(source_ref, ins, kind, scratch)
    collect(source_ref, grads, 0, g_all)
    for h in range(q_all.shape[1] // HD):
        cols = slice(h * HD, (h + 1) * HD)
        for i in reversed(range(chunks)):
            rows = slice(i * span, (i + 1) * span)
            seen = slice(0, (i + 1) * span)
            query, grad = q_all[rows, cols], g_all[rows, cols]
            keys, values = k_all[seen, cols], v_all[seen, cols]
            probs = weights_of(query, keys, i, span, length, scale)
            grad_probs = lax.dot_general(grad, values, NT, preferred_element_type=F32)
            delta = jnp.sum(probs * grad_probs, axis=-1, keepdims=True)
            scores = (probs * (grad_probs - delta) * scale).astype(BF16)
            turned = [t[rows, :] for t in tabs]
            dq_all[rows, cols] = turn(
                jnp.dot(scores, keys, preferred_element_type=F32), turned, -1.0
            ).astype(BF16)
            dk = lax.dot_general(scores, query, TN, preferred_element_type=F32)
            dv = lax.dot_general(probs.astype(BF16), grad, TN, preferred_element_type=F32)
            if i == chunks - 1:
                dk_sum[...] = dk
                dv_sum[...] = dv
            else:
                dk_sum[seen, :] += dk
                dv_sum[seen, :] += dv
        dk_all[:, cols] = turn(dk_sum[...], [t[...] for t in tabs], -1.0).astype(BF16)
        dv_all[:, cols] = dv_sum[...].astype(BF16)
    for kind, scratch in enumerate((dq_all, dk_all, dv_all)):
        spread_out(source_ref, scratch, outs, kind)


def attend_back(source, lengths, pieces, grads, tables, row):
    chunks = len(pieces)
    rows = lengths.shape[0]
    kinds, tokens, columns = pieces[0].shape
    span = tokens // rows
    seq = span * chunks
    wide = pltpu.VMEM((seq, columns), BF16)
    return pl.pallas_call(
        partial(attend_back_kernel, chunks=chunks, row=row),
        name="attend_back",
        grid_spec=pltpu.PrefetchScalarGridSpec(
            num_scalar_prefetch=2,
            grid=(1,),
            in_specs=[pl.BlockSpec((kinds, span, columns), lambda r, *_: (0, row, 0))] * chunks
            + [pl.BlockSpec((1, span, columns), lambda r, *_: (0, row, 0))] * chunks
            + [pl.BlockSpec((seq, HD), lambda r, *_: (0, 0))] * 3,
            out_specs=[pl.BlockSpec((kinds, span, columns), lambda r, *_: (0, 0, 0))] * chunks,
            scratch_shapes=[wide] * 4 + [pltpu.VMEM((seq, HD), F32)] * 2 + [wide] * 3,
        ),
        out_shape=[jax.ShapeDtypeStruct((kinds, span, columns), BF16)] * chunks,
        cost_estimate=cost(12),
        compiler_params=params(1),
    )(source, lengths, *pieces, *grads, *tables)


def up_kernel(perm_ref, a_ref, *refs, parts):
    weights = refs[:parts]
    active_ref, slope_ref = refs[parts:]
    u = blocks_dot(a_ref, weights)
    half = 0.5 * (1.0 + lax.erf(u * math.sqrt(0.5)))
    active_ref[...] = (u * half).astype(BF16)
    slope_ref[...] = half + u * jnp.exp(-0.5 * u * u) * (1.0 / math.sqrt(2.0 * math.pi))


def up_stage(perm, a, weights, tile=512):
    tokens, width = a.shape
    parts = perm.shape[0]
    columns = weights[0].shape[1]
    tile = min(tile, columns)
    specs = block_specs(weights, width // parts, tile, lambda n, *_: n)
    out = pl.BlockSpec((tokens, tile), lambda n, *_: (0, n))
    return pl.pallas_call(
        partial(up_kernel, parts=parts),
        name="up",
        grid_spec=pltpu.PrefetchScalarGridSpec(
            num_scalar_prefetch=1,
            grid=(columns // tile,),
            in_specs=[pl.BlockSpec((tokens, width), lambda n, *_: (0, 0))] + specs,
            out_specs=[out, out],
        ),
        out_shape=[
            jax.ShapeDtypeStruct((tokens, columns), BF16),
            jax.ShapeDtypeStruct((tokens, columns), F32),
        ],
        cost_estimate=cost(columns / 200),
        compiler_params=params(1),
    )(perm, a, *weights)


def up_back_kernel(perm_ref, a_ref, slope_ref, *refs, parts):
    weights = refs[:parts]
    refs[parts][...] = (blocks_dot(a_ref, weights) * slope_ref[...]).astype(BF16)


def up_back(perm, a, slope, weights, offset, tile=512):
    tokens, width = a.shape
    parts = perm.shape[0]
    columns = slope.shape[1]
    tile = min(tile, columns)
    specs = block_specs(
        weights, width // parts, tile, lambda n, *_: offset // tile + n
    )
    out = pl.BlockSpec((tokens, tile), lambda n, *_: (0, n))
    return pl.pallas_call(
        partial(up_back_kernel, parts=parts),
        name="up_back",
        grid_spec=pltpu.PrefetchScalarGridSpec(
            num_scalar_prefetch=1,
            grid=(columns // tile,),
            in_specs=[pl.BlockSpec((tokens, width), lambda n, *_: (0, 0)), out] + specs,
            out_specs=out,
        ),
        out_shape=jax.ShapeDtypeStruct((tokens, columns), BF16),
        cost_estimate=cost(columns / 200),
        compiler_params=params(1),
    )(perm, a, slope, *weights)


def back_kernel(*refs, lefts, parts, adds):
    out_ref = refs[-1]
    block = out_ref.shape[1] // parts
    tile = refs[lefts].shape[0]
    n = pl.program_id(0)
    for p in range(parts):
        at = pl.ds(pl.multiple_of(p * block + n * tile, 128), tile)
        total = refs[-2][:, at] if adds else None
        for h in range(lefts):
            term = lax.dot_general(
                refs[h][...], refs[lefts + h * parts + p][...], NT, preferred_element_type=F32
            )
            total = term if total is None else total + term
        out_ref[:, at] = total.astype(out_ref.dtype)


def to_width(lefts, weights, width, added=(), dtype=BF16):
    parts = len(weights[0])
    block = width // parts
    tile = min(block, 256)
    tokens = lefts[0].shape[0]
    left_specs, specs, arrays = [], [], []
    for left, weight in zip(lefts, weights):
        columns = left.shape[1]
        left_specs.append(pl.BlockSpec((tokens, columns), lambda n: (0, 0)))
        specs += [pl.BlockSpec((tile, columns), lambda n: (n, 0))] * parts
        arrays += weight
    whole = pl.BlockSpec((tokens, width), lambda n: (0, 0))
    return pl.pallas_call(
        partial(back_kernel, lefts=len(lefts), parts=parts, adds=len(added)),
        name="to_width",
        grid=(block // tile,),
        in_specs=left_specs + specs + [whole] * len(added),
        out_specs=whole,
        out_shape=jax.ShapeDtypeStruct((tokens, width), dtype),
        cost_estimate=cost(sum(a.shape[1] for a in lefts) / 256),
        compiler_params=params(1),
    )(*lefts, *arrays, *added)


def grad_kernel(*refs, count, rights, adds):
    lefts, fars = refs[:count], refs[count : 2 * count]
    sides = refs[2 * count : 2 * count + rights], refs[2 * count + rights : 2 * count + 2 * rights]
    add_refs, out_ref = refs[2 * count + 2 * rights : -1], refs[-1]
    at = 0
    for b in range(count):
        total = None
        for left, right_refs in zip((lefts[b], fars[b]), sides):
            start = 0
            for right in right_refs:
                size = right.shape[1]
                term = lax.dot_general(
                    left[0, start : start + size, :], right[0], TN, preferred_element_type=F32
                )
                total = term if total is None else total + term
                start += size
        for n in range(adds[b]):
            total = total + add_refs[at + n][0].astype(F32)
        at += adds[b]
        out_ref[b] = total.astype(BF16)


def grad_blocks(left, left_far, near, far, parts, chosen, added, first, kinds, tile=512):
    _, tokens, width = left.shape
    columns = near[0].shape[2]
    tile = min(tile, columns)
    steps = columns // tile
    block = width // parts

    def place(start, row):
        return lambda s, n: (row, 0, (first - start + s) * steps + n)

    flat = [a for arrays in added for a in arrays]
    left_specs = [
        pl.BlockSpec((1, tokens, block), lambda s, n, p=p: (first + s, 0, p)) for p in chosen
    ]
    return pl.pallas_call(
        partial(
            grad_kernel,
            count=len(chosen),
            rights=len(near),
            adds=tuple(len(a) for a in added),
        ),
        name="grad",
        grid=(kinds, steps),
        in_specs=left_specs * 2
        + [
            pl.BlockSpec((1, r.shape[1], tile), lambda s, n: (first + s, 0, n))
            for r in (*near, *far)
        ]
        + [pl.BlockSpec((1, block, tile), place(start, row)) for _, row, start in flat],
        out_specs=pl.BlockSpec((len(chosen), block, tile), lambda s, n: (0, 0, s * steps + n)),
        out_shape=jax.ShapeDtypeStruct((len(chosen), block, kinds * columns), BF16),
        cost_estimate=cost(len(chosen) * kinds * columns / 512),
        compiler_params=params(2),
    )(*[left] * len(chosen), *[left_far] * len(chosen), *near, *far, *[a for a, _, _ in flat])


def part_kernel(in_ref, out_ref, *, turned):
    values = in_ref[...]
    out_ref[...] = values.astype(F32).T.astype(BF16) if turned else values


def shard_part(shard, n, size, turned):
    short = shard.shape[1] if turned else shard.shape[0]
    spec = pl.BlockSpec((size, short), lambda i: (n, 0))
    if not turned:
        spec = pl.BlockSpec((short, size), lambda i: (0, n))
    return pl.pallas_call(
        partial(part_kernel, turned=turned),
        name="part",
        grid=(1,),
        in_specs=[spec],
        out_specs=pl.BlockSpec((short, size), lambda i: (0, 0)),
        out_shape=jax.ShapeDtypeStruct((short, size), BF16),
        cost_estimate=cost(1),
        compiler_params=params(1),
    )(shard)


def hat_of(z):
    center = z - jnp.mean(z, axis=-1, keepdims=True)
    inverse = lax.rsqrt(jnp.mean(center * center, axis=-1, keepdims=True) + EPSILON)
    return center * inverse, inverse


def own_kernel(perm_ref, grad_ref, z_ref, *refs, parts):
    weights = refs[:parts]
    out_ref, sum_ref = refs[parts:]
    block = weights[0].shape[0]
    for p in range(parts):
        out_ref[0, :, p * block : (p + 1) * block] = lax.dot_general(
            grad_ref[0], weights[p][...], NT, preferred_element_type=F32
        )
    tile = 32
    tokens, width = out_ref.shape[1:]
    gain = jnp.zeros((8, width), F32)
    shift = jnp.zeros((8, width), F32)
    for t in range(0, tokens, tile):
        d = out_ref[0, t : t + tile, :]
        hat, _ = hat_of(z_ref[0, t : t + tile, :])
        gain = gain + jnp.sum((d * hat).reshape(tile // 8, 8, width), axis=0)
        shift = shift + jnp.sum(d.reshape(tile // 8, 8, width), axis=0)
    sum_ref[0, :8] = gain
    sum_ref[0, 8:] = shift


def own_part(perm, grads, streams, weights, row):
    kinds, span, columns = grads.shape
    width = streams.shape[2]
    parts = perm.shape[0]
    specs = block_specs(weights, width // parts, columns, lambda s, *_: s)
    return pl.pallas_call(
        partial(own_kernel, parts=parts),
        name="own",
        grid_spec=pltpu.PrefetchScalarGridSpec(
            num_scalar_prefetch=1,
            grid=(kinds,),
            in_specs=[
                pl.BlockSpec((1, span, columns), lambda s, *_: (s, 0, 0)),
                pl.BlockSpec((1, span, width), lambda s, *_: (s, row, 0)),
            ]
            + specs,
            out_specs=[
                pl.BlockSpec((1, span, width), lambda s, *_: (s, 0, 0)),
                pl.BlockSpec((1, 16, width), lambda s, *_: (s, 0, 0)),
            ],
        ),
        out_shape=[
            jax.ShapeDtypeStruct((kinds, span, width), F32),
            jax.ShapeDtypeStruct((kinds, 16, width), F32),
        ],
        cost_estimate=cost(12),
        compiler_params=params(1),
    )(perm, grads, streams, *weights)


def other_kernel(grad_ref, part_ref, z_ref, gain_ref, *refs, parts):
    weights = refs[:parts]
    out_ref, total_ref = refs[parts:]
    block = weights[0].shape[0]
    for p in range(parts):
        cols = slice(p * block, (p + 1) * block)
        total_ref[:, cols] = part_ref[0, :, cols] + lax.dot_general(
            grad_ref[0], weights[p][...], NT, preferred_element_type=F32
        )
    tile = 32
    for t in range(0, total_ref.shape[0], tile):
        rows = slice(t, t + tile)
        hat, inverse = hat_of(z_ref[0, rows, :])
        e = total_ref[rows, :] * gain_ref[...]
        first = jnp.mean(e, axis=-1, keepdims=True)
        second = jnp.mean(e * hat, axis=-1, keepdims=True)
        out_ref[0, rows, :] = ((e - first - hat * second) * inverse).astype(BF16)


def other_part(grads, own, streams, gain, weights, row):
    kinds, span, columns = grads.shape
    width = streams.shape[2]
    parts = len(weights)
    block = width // parts
    return pl.pallas_call(
        partial(other_kernel, parts=parts),
        name="other",
        grid=(kinds,),
        in_specs=[
            pl.BlockSpec((1, span, columns), lambda s: (s, 0, 0)),
            pl.BlockSpec((1, span, width), lambda s: (s, 0, 0)),
            pl.BlockSpec((1, span, width), lambda s: (s, row, 0)),
            pl.BlockSpec((1, width), lambda s: (0, 0)),
        ]
        + [pl.BlockSpec((block, columns), lambda s: (0, s))] * parts,
        out_specs=pl.BlockSpec((1, span, width), lambda s: (s, 0, 0)),
        out_shape=jax.ShapeDtypeStruct((kinds, span, width), BF16),
        scratch_shapes=[pltpu.VMEM((span, width), F32)],
        cost_estimate=cost(14),
        compiler_params=params(1),
    )(grads, own, streams, gain, *weights)


def last_kernel(perm_ref, earlier_ref, coeff_ref, dz_ref, dr_ref, *refs):
    out_ref, mix_ref = refs[-2:]
    prev, tile, width = earlier_ref.shape
    parts = perm_ref.shape[0]
    block = width // parts
    count, half = prev * GROUP, STREAMS * GROUP
    for g in range(tile // GROUP):
        rows = slice(g * GROUP, (g + 1) * GROUP)
        high, low = spread(coeff_ref[g])
        pairs = jnp.zeros((count, half), F32)
        for p in range(parts):
            here = slice(p * block, (p + 1) * block)
            there = pl.ds(pl.multiple_of(perm_ref[p] * block, 128), block)
            grads = jnp.concatenate(
                [dz_ref[s, rows, here] for s in range(STREAMS - 1)] + [dr_ref[rows, here]], axis=0
            )
            x = earlier_ref[:, rows, there].reshape(count, block)
            pairs = pairs + lax.dot_general(x, grads, NT, preferred_element_type=F32)
            total = jnp.dot(high, grads, preferred_element_type=F32) + jnp.dot(
                low, grads, preferred_element_type=F32
            )
            out_ref[:, rows, there] = total.astype(BF16).reshape(prev, GROUP, block)
        token = lax.broadcasted_iota(jnp.int32, (count, half), 0) % GROUP
        lane = lax.broadcasted_iota(jnp.int32, (count, half), 1)
        wide = lax.broadcasted_iota(jnp.int32, (count, 128), 1)
        mixed = jnp.zeros((count, 128), F32)
        for s in range(STREAMS):
            own = jnp.where(lane == token + s * GROUP, pairs, 0.0)
            mixed = jnp.where(wide == s, jnp.sum(own, axis=-1, keepdims=True), mixed)
        mix_ref[g] = mixed


def last_stage(perm, inputs, coeff, dz, dr, row, rows, before, tile=64):
    prev, tokens, width = inputs.shape
    steps = tokens // rows // tile
    count = prev * GROUP
    here = lambda t, *_: (0, row * steps + t, 0)
    return pl.pallas_call(
        last_kernel,
        name="last",
        grid_spec=pltpu.PrefetchScalarGridSpec(
            num_scalar_prefetch=1,
            grid=(steps,),
            in_specs=[
                pl.BlockSpec((prev, tile, width), here),
                pl.BlockSpec(
                    (tile // GROUP,) + coeff.shape[1:], lambda t, *_: (row * steps + t, 0, 0)
                ),
                pl.BlockSpec((STREAMS - 1, tile, width), lambda t, *_: (0, t, 0)),
                pl.BlockSpec((tile, width), lambda t, *_: (row * steps + t, 0)),
            ]
            + [pl.BlockSpec(memory_space=pl.ANY)] * len(before),
            out_specs=[
                pl.BlockSpec((prev, tile, width), here),
                pl.BlockSpec(
                    (tile // GROUP, count, 128), lambda t, *_: (row * steps + t, 0, 0)
                ),
            ],
        ),
        out_shape=[
            jax.ShapeDtypeStruct((prev, tokens, width), BF16),
            jax.ShapeDtypeStruct((tokens // GROUP, count, 128), F32),
        ],
        input_output_aliases={5 + n: n for n in range(len(before))},
        cost_estimate=cost(12),
        compiler_params=params(1),
    )(perm, inputs, coeff, dz, dr, *before)


def layer_norm(values, gain, shift):
    center = values - jnp.mean(values, axis=-1, keepdims=True)
    spread = jnp.mean(center * center, axis=-1, keepdims=True)
    return center * lax.rsqrt(spread + EPSILON) * gain + shift


def activate(values):
    return jax.nn.gelu(values, approximate=False)


def mixer(final, weight_in, weight_out, bias):
    normed = final * lax.rsqrt(jnp.mean(final * final, axis=-1, keepdims=True) + RMS_EPSILON)
    hidden = activate(
        lax.dot_general(
            normed, weight_in, NT, precision=HIGHEST, preferred_element_type=F32
        )
    )
    return jnp.dot(hidden, weight_out, precision=HIGHEST, preferred_element_type=F32) + bias


def turn_tables(positions):
    half = ROT // 2
    frequency = 10000.0 ** (-2.0 * jnp.arange(half, dtype=F32) / ROT)
    angles = positions.astype(F32)[:, None] * frequency[None, :]
    cosine, sine = jnp.cos(angles), jnp.sin(angles)
    count = positions.shape[0]
    rest = HD - ROT
    base = jnp.concatenate([cosine, cosine, jnp.ones((count, rest), F32)], axis=1)
    up = jnp.concatenate([jnp.zeros((count, half), F32), sine, jnp.zeros((count, rest), F32)], 1)
    down = jnp.concatenate([-sine, jnp.zeros((count, half + rest), F32)], axis=1)
    return base, up, down


def group_coeff(mix_in, count_prev, tokens):
    groups = tokens // GROUP
    c = mix_in.reshape(STREAMS, count_prev, groups, GROUP).transpose(2, 1, 3, 0)
    return c.reshape(groups, count_prev * GROUP, STREAMS)


def body(
    earlier,
    mix_in,
    lengths,
    w_query,
    w_key,
    w_value,
    w_proj,
    w_up,
    w_down,
    first_gain,
    first_shift,
    second_gain,
    second_shift,
    mixer_in,
    mixer_out,
    mixer_bias,
    grad_out,
    grad_mix,
):
    count_prev, rows, span, width = earlier.shape
    tokens = rows * span
    fsdp, ctx = lax.axis_size("fsdp"), lax.axis_size("ctx")
    me, z = lax.axis_index("fsdp"), lax.axis_index("ctx")
    masks = block_masks(fsdp)
    place_of = [masks.index(m) for m in range(fsdp)]
    block = width // fsdp
    piece = block // ctx
    heads_width = w_query.shape[1]
    hidden = w_up.shape[1]
    perm = jnp.stack([me ^ m for m in masks]).astype(jnp.int32)
    table = jnp.array(place_of, jnp.int32)
    ring = jnp.arange(ctx, dtype=jnp.int32)
    source = (z - ring + ctx) % ctx
    slots = z * span + jnp.arange(span, dtype=jnp.int32)
    valid = (slots[None, :] < lengths[:, None]).astype(F32).reshape(tokens)

    def relative(values):
        return jnp.concatenate(
            [
                lax.dynamic_slice_in_dim(values, perm[p] * block, block, values.ndim - 1)
                for p in range(fsdp)
            ],
            axis=-1,
        )

    def absolute(values):
        return jnp.concatenate(
            [
                lax.dynamic_slice_in_dim(values, table[a ^ me] * block, block, values.ndim - 1)
                for a in range(fsdp)
            ],
            axis=-1,
        )

    def part(values, p):
        return values[:, p * block : (p + 1) * block]

    small = jnp.concatenate(
        [mixer_in.T, first_gain[None], first_shift[None], second_gain[None], second_shift[None]], 0
    )
    around = jnp.zeros((ctx,) + small.shape, BF16)
    for s in range(ctx):
        got = small if s == 0 else shift_ctx(small, s)
        around = lax.dynamic_update_slice(around, got[None], (source[s], 0, 0))
    around = cross(around)
    around = jnp.stack(around + [over_fsdp(a, 1) for a in around])
    small_all = around.transpose(2, 0, 1, 3).reshape(small.shape[0], width).astype(F32)
    mixer_full = small_all[:MIXW]
    gain_first, shift_first, gain_second, shift_second = [
        small_all[MIXW + n : MIXW + n + 1] for n in range(4)
    ]

    half = hidden // 2
    ctx_qkv = gather_ctx(jnp.concatenate([w_query, w_key, w_value], axis=1))
    ctx_up = [gather_ctx(shard_part(w_up, 0, half, False))]

    order = Order()
    Pace.value = FORWARD_PACE
    inputs = earlier.reshape(count_prev, tokens, width)
    coeff = group_coeff(mix_in, count_prev, tokens)
    normed_in, streams = order.keep(
        mix_streams(perm, inputs, coeff, gain_first, shift_first)
    )
    tables_here = turn_tables(jnp.tile(slots, rows))
    tables_all = turn_tables(jnp.arange(span * ctx, dtype=jnp.int32))
    target = (z + ring) % ctx
    tables_here, tables_all = order.wait((tables_here, tables_all))

    def to_heads(chunks):
        return [chunks[0]] + [shift_ctx(chunks[s], s) for s in range(1, ctx)]

    def to_slots(pieces):
        return [pieces[0]] + [shift_ctx(pieces[s], -s) for s in range(1, ctx)]

    def to_core(parts):
        return [over_fsdp(p, 1) for p in parts]

    near_qkv = cross(order.wait(ctx_qkv))
    ctx_up.append(gather_ctx(order.keep(shard_part(order(w_up), 1, half, False))))
    far_qkv = to_core(near_qkv[:1])
    other = [over_tp(near_qkv[0])]
    near_up = [cross(order.wait(ctx_up[0]))]
    ctx_proj = gather_ctx(order.keep(shard_part(order(w_proj), 0, heads_width, True)))
    far_qkv = order.wait(far_qkv)
    other = order.wait(other)
    near_qkv = order.wait(near_qkv)
    far_qkv = order.wait(far_qkv + to_core(near_qkv[1:]))
    blocks_qkv = near_qkv + far_qkv
    pieces = to_heads(
        order.keep(to_chunks(target, perm, order(normed_in), blocks_qkv, tables_here, 2))
    )
    near_up.append(cross(order.wait(ctx_up[1])))
    ctx_down = [gather_ctx(order.keep(shard_part(order(w_down), 0, half, True)))]
    pieces = order.wait(pieces)
    near_up = order.wait(near_up)
    far_up = [to_core(order(near)) for near in near_up]
    near_proj = cross(order.wait(ctx_proj))
    outs = order.keep(attend(source, lengths, order(pieces)))
    far_up = order.wait(far_up)
    outs = to_slots(order(outs))
    ctx_down.append(gather_ctx(order.keep(shard_part(order(w_down), 1, half, True))))
    outs = order.wait(outs)
    attended = order.keep(join(target, order(outs)))[0]
    near_proj = order.wait(near_proj)
    blocks_proj = near_proj + order.wait(to_core(near_proj))
    branch_mine = order.keep(to_width([order(attended)], [blocks_proj], width))
    branch_theirs = over_tp(branch_mine)
    near_down = [cross(order.wait(ctx_down[0]))]
    branch_theirs = order.wait(branch_theirs)
    blocks_up = [near + far for near, far in zip(near_up, far_up)]
    residual = streams[STREAMS - 1] + tp_sum(branch_mine, branch_theirs)

    def far_half(values):
        return over_fsdp(values[..., width // 2 :], 1)

    normed = layer_norm(residual, gain_second, shift_second).astype(BF16)
    normed = order.wait(normed)
    near_down.append(cross(order.wait(ctx_down[1])))
    near_down[0] = order.wait(near_down[0])
    far_down = [to_core(near_down[0])]
    active, slope = [], []
    for w in blocks_up:
        a, b = order.keep(up_stage(perm, order(normed), w))
        active.append(a)
        slope.append(b)
    other = other + [over_tp(p) for p in order(near_qkv[1:])]
    far_down[0] = order.wait(far_down[0])
    down_first = order.keep(
        to_width([order(active[0])], [near_down[0] + far_down[0]], width, (), F32)
    )
    near_down[1] = order.wait(near_down[1])
    far_down.append(order.wait(to_core(near_down[1])))
    blocks_down = [near + far for near, far in zip(near_down, far_down)]
    other = order.wait(other)
    down_mine = order.keep(
        to_width([order(active[1])], blocks_down[1:], width, (down_first,))
    )
    other_far = to_core(other)
    down_theirs = over_tp(down_mine)
    active_far = [over_fsdp(a, 1) for a in order(active)]
    grad_out_here = order.wait(relative(grad_out.reshape(tokens, width)))
    active_far = order.wait(active_far)
    normed_far = order.wait(far_half(normed))
    attended_far = order.wait(over_fsdp(attended, 1))
    normed_in_far = order.wait(far_half(normed_in))
    other = other + order.wait(other_far)
    final = residual + tp_sum(down_mine, order.wait(down_theirs))
    output = absolute(final.astype(BF16)).reshape(rows, span, width)

    mix_value, mix_pull = jax.vjp(mixer, final, mixer_full, mixer_out, mixer_bias)
    mix_out = mix_value.T.reshape(MIXW, rows, span)
    mix_cotangent = (grad_mix.reshape(MIXW, tokens) * valid[None]).T
    grad_final_mix, grad_mixer_first, grad_mixer_second, grad_mixer_shift = mix_pull(mix_cotangent)
    grad_final = grad_out_here.astype(F32) * valid[:, None] + grad_final_mix

    Pace.value = BACKWARD_PACE
    grad_down_b = order.wait(grad_final.astype(BF16))
    grad_down_far = order.wait(far_half(grad_down_b))
    down = [
        Scatter(order, grad_down_b[None], [a[None]], grad_down_far[None], [f[None]])
        for a, f in zip(active, active_far)
    ]
    for d in down:
        d.launch()
    grad_upward, upward_far = [], []
    for n in range(2):
        grad_upward.append(
            order.keep(up_back(perm, order(grad_down_b), slope[n], blocks_down[n], 0))
        )
        upward_far.append(over_fsdp(grad_upward[n], 1))
    normed_mine = order.keep(to_width(order(grad_upward), blocks_up, width))
    normed_theirs = over_tp(normed_mine)
    grad_down = [scatter_ctx(down[0].finish())]
    upward_far = order.wait(upward_far)
    up = [
        Scatter(order, normed[None], [u[None]], normed_far[None], [f[None]])
        for u, f in zip(grad_upward, upward_far)
    ]
    up[0].launch()
    tail = jnp.concatenate([grad_mixer_second, grad_mixer_shift[None]], axis=0)
    tail, grad_mixer_first, output, mix_out = order.wait(
        (tail, grad_mixer_first, output, mix_out)
    )
    normed_theirs = order.wait(normed_theirs)
    grad_normed = tp_sum(normed_mine, normed_theirs)
    unused_norm, norm_pull = jax.vjp(layer_norm, residual, gain_second, shift_second)
    grad_residual_norm, grad_gain_second, grad_shift_second = norm_pull(grad_normed)
    grad_branch_b = order.wait((grad_final + grad_residual_norm).astype(BF16))

    grad_branch_far = far_half(grad_branch_b)
    grad_chunks = order.keep(
        to_chunks(target, perm, order(grad_branch_b)[None], blocks_proj, tables_here, 0)
    )
    grad_branch_far = order.wait(grad_branch_far)
    grad_pieces = to_heads(grad_chunks)
    grad_down.append(scatter_ctx(down[1].finish()))
    up[1].launch()
    proj = Scatter(
        order, grad_branch_b[None], [attended[None]], grad_branch_far[None], [attended_far[None]]
    )
    made_proj = proj.make(1)
    grad_up = [scatter_ctx(up[0].finish())]
    proj.launch(0, None, order(made_proj))
    grad_pieces = order.wait(grad_pieces)
    back = [
        order.keep(attend_back(source, lengths, pieces, order(grad_pieces), tables_all, 0))
    ]
    sent = [to_slots(back[0])]
    back.append(
        order.keep(attend_back(source, lengths, pieces, order(grad_pieces), tables_all, 1))
    )
    grad_down[0] = order.wait(grad_down[0])
    mine, theirs, own = [], [], []
    grad_up.append(scatter_ctx(up[1].finish()))
    sent[0] = order.wait(sent[0])
    mine.append(order.keep(join(target, sent[0])))
    theirs.append(over_tp(mine[0]))
    sent.append(to_slots(order(back[1])))
    own.append(order.keep(own_part(perm, order(mine[0]), streams, blocks_qkv, 0)))
    grad_down[1] = order.wait(grad_down[1])
    grad_proj = scatter_ctx(proj.finish())
    sent[1] = order.wait(sent[1])
    mine.append(order.keep(join(target, sent[1])))
    theirs.append(over_tp(mine[1]))
    mine_far = order.wait([over_fsdp(m, 1) for m in order(mine)])
    qkv = Scatter(order, normed_in, mine, normed_in_far, mine_far)
    qkv.launch(0, 1)
    qkv.launch(1, 2)
    own.append(order.keep(own_part(perm, order(mine[1]), streams, blocks_qkv, 1)))
    grad_up[0] = order.wait(grad_up[0])
    theirs[0] = order.wait(theirs[0])
    grad_query = scatter_ctx(qkv.finish(0, 1))
    sums = (own[0][1] + own[1][1]).sum(0).reshape(2, 8, width).sum(1)
    sums = order.wait(sums)

    dz = order.keep(other_part(order(theirs[0]), own[0][0], streams, gain_first, other, 0))
    done = order.keep(
        last_stage(perm, inputs, coeff, order(dz), grad_branch_b, 0, rows, ())
    )
    theirs[1] = order.wait(theirs[1])
    sums_far = over_tp(order(sums))
    dz = order.keep(other_part(order(theirs[1]), own[1][0], streams, gain_first, other, 1))
    sums_far = order.wait(sums_far)
    packed = jnp.concatenate(
        [grad_mixer_first, sums + sums_far, grad_gain_second, grad_shift_second], axis=0
    )
    packed = packed.reshape(packed.shape[0], fsdp, ctx, piece)
    packed = jnp.stack(
        [lax.dynamic_index_in_dim(packed, z ^ m, 2, keepdims=False) for m in block_masks(ctx)]
    ).transpose(0, 2, 1, 3)
    tail = jnp.pad(tail, ((0, 0), (0, HD - MIXW)))
    packed, tail = order.wait((packed, tail))

    def fold(packed, tail, move):
        split = packed.shape[0] // 2
        return packed[:split], tail, move(packed[split:]), move(tail)

    def landed(packed, tail, got_packed, got_tail):
        got_packed, got_tail = order.wait((got_packed, got_tail))
        return packed + got_packed, tail + got_tail

    ctx_steps = [
        (lambda v, bit=bit: lax.ppermute(v, "ctx", xor_pairs(ctx, bit)))
        for bit in reversed(bits_of(ctx))
    ]
    fsdp_steps = [(lambda v, bit=bit: over_fsdp(v, bit)) for bit in reversed(bits_of(fsdp))]
    moving = fold(packed, tail, ctx_steps[0])
    grad_rest = scatter_ctx(qkv.finish(1, 2))
    grad_up[1] = order.wait(grad_up[1])
    for step in ctx_steps[1:]:
        moving = fold(*landed(*moving), step)
    grad_inputs, grad_coeff = order.keep(
        last_stage(perm, inputs, coeff, order(dz), grad_branch_b, 1, rows, done)
    )
    packed, tail = landed(*moving)
    moving = fold(packed[0], tail, fsdp_steps[0])
    grad_proj = order.wait(grad_proj)
    for step in fsdp_steps[1:]:
        moving = fold(*landed(*moving), step)
    packed, tail = landed(*moving)
    norms = packed[0]
    grad_key, grad_value = jnp.split(grad_rest, 2, axis=1)
    grad_proj = grad_proj.T
    grad_earlier = grad_inputs.reshape(earlier.shape)
    grad_mix_in = (
        grad_coeff[:, :, :STREAMS]
        .reshape(tokens // GROUP, count_prev, GROUP, STREAMS)
        .transpose(3, 1, 0, 2)
        .reshape(mix_in.shape)
    )
    return (
        output,
        mix_out,
        grad_earlier,
        grad_mix_in,
        grad_query,
        grad_key,
        grad_value,
        grad_proj,
        jnp.concatenate(grad_up, axis=1),
        jnp.concatenate(grad_down, axis=1).T,
        norms[MIXW],
        norms[MIXW + 1],
        norms[MIXW + 2],
        norms[MIXW + 3],
        norms[:MIXW].T,
        tail[:MIXW, :MIXW],
        tail[MIXW, :MIXW],
    )


def solution(mesh):
    placed = (
        P(None, "fsdp", "ctx", None),
        P(None, "fsdp", "ctx"),
        P("fsdp"),
        P(("fsdp", "ctx"), "tp"),
        P(("fsdp", "ctx"), "tp"),
        P(("fsdp", "ctx"), "tp"),
        P("tp", ("fsdp", "ctx")),
        P(("fsdp", "ctx"), "tp"),
        P("tp", ("fsdp", "ctx")),
        P(("fsdp", "ctx")),
        P(("fsdp", "ctx")),
        P(("fsdp", "ctx")),
        P(("fsdp", "ctx")),
        P(("fsdp", "ctx"), None),
        P(),
        P(),
        P("fsdp", "ctx", None),
        P(None, "fsdp", "ctx"),
    )
    return jax.shard_map(
        body,
        mesh=mesh,
        in_specs=placed,
        out_specs=(
            P("fsdp", "ctx", None),
            P(None, "fsdp", "ctx"),
            P(None, "fsdp", "ctx", None),
            P(None, "fsdp", "ctx"),
            P(("fsdp", "ctx"), "tp"),
            P(("fsdp", "ctx"), "tp"),
            P(("fsdp", "ctx"), "tp"),
            P("tp", ("fsdp", "ctx")),
            P(("fsdp", "ctx"), "tp"),
            P("tp", ("fsdp", "ctx")),
            P(("fsdp", "ctx")),
            P(("fsdp", "ctx")),
            P(("fsdp", "ctx")),
            P(("fsdp", "ctx")),
            P(("fsdp", "ctx"), None),
            P(),
            P(),
        ),
        check_vma=False,
    )
```

time: 1370 us -> 1100 us (0.80)
  matrix products: 238 us -> 8.3 us
  Pallas kernels: 125 us -> 353 us
  waiting for transfers between devices: 709 us -> 519 us
  other arithmetic: 91.4 us -> 52.1 us
  blocking collectives: 32.7 us -> 0 us
    pallas_call x5 -> x38, Pallas kernels: 49.4 us -> 294 us  [the longest x14 82 us: grad_blocks(): pl.pallas_call(partial(grad_kernel, count=len(chosen), rights=len(near),...]
    dot_general x59 -> x3, matrix products: 237 us -> 7.58 us  [mixer(): lax.dot_general(normed, weight_in, NT, precision=HIGHEST, preferred_eleme...]
    ppermute x40 -> x45, waiting for transfers between devices: 224 us -> 90.7 us  [over_fsdp(): return lax.ppermute(values, 'fsdp', xor_pairs(lax.axis_size('fsdp'), mask))]
    ppermute x5 -> x8, waiting for transfers between devices: 247 us -> 160 us  [over_tp(): return lax.ppermute(values, 'tp', xor_pairs(lax.axis_size('tp'), 1))]
    ppermute x27 -> x18, waiting for transfers between devices: 125 us -> 178 us  [shift_ctx(): lax.ppermute(values, 'ctx', [(i, (i + step) % size) for i in range(size)])]
    ppermute x27 -> x18, starting transfers between devices: 83.2 us -> 39.1 us  [shift_ctx(): lax.ppermute(values, 'ctx', [(i, (i + step) % size) for i in range(size)])]
    all_gather x1 -> x0, blocking collectives: 32.7 us -> none  [body(): small_all = lax.all_gather(small, ('fsdp', 'ctx'), axis=0, tiled=False)]
    all_gather x6, waiting for transfers between devices: 106 us -> 74.3 us  [gather_ctx(): return lax.all_gather(shard, 'ctx', axis=0, tiled=True)]
  transfers between devices with their start and end apart: 86 -> 88, of which waited for: 28 -> 31; matrix products, arithmetic and copies ran while one was open for 21% -> 6% of each run, Pallas kernels for 9% -> 32%
where the time goes in v2:
time: 1100 us; the launch traced here: 1090 us
  waiting for transfers between devices  519 us (47%)
  Pallas kernels  353 us (32%)
  starting transfers between devices  91.1 us (8%)
  other arithmetic  52.1 us (5%)
  local copies, waits for them, and re-layouts  39.1 us (4%)
  between operations  25.7 us (2%)
    ppermute x18, waiting for transfers between devices, shift_ctx(): lax.ppermute(values, 'ctx', [(i, (i + step) % size) for i in range(size)])  178 us
    ppermute x8, waiting for transfers between devices, over_tp(): return lax.ppermute(values, 'tp', xor_pairs(lax.axis_size('tp'), 1))  160 us
    ppermute x45, waiting for transfers between devices, over_fsdp(): return lax.ppermute(values, 'fsdp', xor_pairs(lax.axis_size('fsdp'), mask))  90.7 us
    pallas_call x14, Pallas kernels, grad_blocks(): pl.pallas_call(partial(grad_kernel, count=len(chosen), rights=len(near),...  82 us
    all_gather x6, waiting for transfers between devices, gather_ctx(): return lax.all_gather(shard, 'ctx', axis=0, tiled=True)  74.3 us
    pallas_call x4, Pallas kernels, to_width(): pl.pallas_call(partial(back_kernel, lefts=len(lefts), parts=parts, adds=l...  43.8 us
    ppermute x18, starting transfers between devices, shift_ctx(): lax.ppermute(values, 'ctx', [(i, (i + step) % size) for i in range(size)])  39.1 us
    ppermute x45, starting transfers between devices, over_fsdp(): return lax.ppermute(values, 'fsdp', xor_pairs(lax.axis_size('fsdp'), mask))  35.1 us
  transfers between devices with their start and end apart: 88, of which 31 were waited for; matrix products, arithmetic and copies ran while one was open for 6% of the time, Pallas kernels for 32%

profile of v2, /device:TPU:0, one launch (start us, length us, event | category | flops | bytes accessed | tf_op | source)
XLA Modules:
  0.0 1088.1 jit_solution(13691711161060657581)
XLA Ops:
  42.5 21.1 %mix.1 = (bf16[3,512,2048]{2,1,0:T(8,128)(2,1)}, f32[4,512,2048]{2,1,0:T(8,128)}) custom-call(s32[4]{0:T(128)} %get-tuple-element.578.perm_ref, bf16[8,512,2048]{2,1,0:T(8,128)(2,1)} %bitcast.143, f32[16,256,4]{2,1,0:T(8,128)} %bitcast.146, f32[1,2048]{1,0:T(1,128)} %bitcast.188, f32[1,2048]{1,0:T(1,128)} %bitcast.192), custom_call_target="tpu_custom_call" | custom-call | flops 420000000 | bytes 1024 | tf_op jit(solution)/shard_map/mix/pallas_call | solution.py:182
  63.6 12.8 %all-gather.7.cloned.1.call-done.refs_0_ = bf16[512,3072]{1,0:T(8,128)(2,1)} async-done(((bf16[128,3072]{1,0:T(8,128)(2,1)}), bf16[512,3072]{1,0:T(8,128)(2,1)}) %all-gather.7.cloned.1.call-update) | async-done | bytes 3145744 | tf_op jit(solution)/shard_map/all_gather | solution.py:88
  81.2 42.0 %all-gather.9.cloned.1.call-done.refs_0_.refs_2_ = bf16[512,2048]{1,0:T(8,128)(2,1)} async-done(((bf16[128,2048]{1,0:T(8,128)(2,1)}), bf16[512,2048]{1,0:T(8,128)(2,1)}) %all-gather.9.cloned.1.call-update) | async-done | bytes 2097168 | tf_op jit(solution)/shard_map/all_gather | solution.py:88
  125.0 22.2 %collective-permute-done.8.refs_0_ = bf16[512,3072]{1,0:T(8,128)(2,1)} collective-permute-done((bf16[512,3072]{1,0:T(8,128)(2,1)}, bf16[512,3072]{1,0:T(8,128)(2,1)}, u32[]{:S(2)}, u32[]{:S(2)}) %collective-permute-start.8) | collective-permute-done | bytes 3145760 | tf_op jit(solution)/shard_map/ppermute | solution.py:49
  150.5 3.9 collective-permute-done.9.refs_3_
  154.5 18.6 %heads.2 = (bf16[3,512,256]{2,1,0:T(8,128)(2,1)}, bf16[3,512,256]{2,1,0:T(8,128)(2,1)}, bf16[3,512,256]{2,1,0:T(8,128)(2,1)}, bf16[3,512,256]{2,1,0:T(8,128)(2,1)}) custom-call(s32[4]{0:T(128)} %and_select_fusion.target_ref, s32[4]{0:T(128)} %get-tuple-element.578.perm_ref, bf16[3,512,2048]{2,1,0:T(8,128)(2,1)} %get-tuple-element.263.a_ref.refs_0_, ...), custom_call_target="tpu_custom_call" | custom-call | flops 720000000 | bytes 1024 | tf_op jit(solution)/shard_map/heads/pallas_call | solution.py:261
  173.1 19.4 %all-gather.11.cloned.1.call-done.refs_0_.refs_6_ = bf16[512,2048]{1,0:T(8,128)(2,1)} async-done(((bf16[128,2048]{1,0:T(8,128)(2,1)}), bf16[512,2048]{1,0:T(8,128)(2,1)}) %all-gather.11.cloned.1.call-update) | async-done | bytes 2097168 | tf_op jit(solution)/shard_map/all_gather | solution.py:88
  200.0 24.1 %collective-permute-done.10.refs_1_ = bf16[3,512,256]{2,1,0:T(8,128)(2,1)S(1)} collective-permute-done((bf16[3,512,256]{2,1,0:T(8,128)(2,1)}, bf16[3,512,256]{2,1,0:T(8,128)(2,1)S(1)}, u32[]{:S(2)}, u32[]{:S(2)}) %collective-permute-start.10) | collective-permute-done | bytes 786464 | tf_op jit(solution)/shard_map/ppermute | solution.py:54
  224.1 41.7 %collective-permute-done.11.refs_2_ = bf16[3,512,256]{2,1,0:T(8,128)(2,1)} collective-permute-done((bf16[3,512,256]{2,1,0:T(8,128)(2,1)}, bf16[3,512,256]{2,1,0:T(8,128)(2,1)}, u32[]{:S(2)}, u32[]{:S(2)}) %collective-permute-start.11) | collective-permute-done | bytes 786464 | tf_op jit(solution)/shard_map/ppermute | solution.py:54
  267.9 11.5 %attend.1 = (bf16[1,512,256]{2,1,0:T(8,128)(2,1)}, bf16[1,512,256]{2,1,0:T(8,128)(2,1)}, bf16[1,512,256]{2,1,0:T(8,128)(2,1)}, bf16[1,512,256]{2,1,0:T(8,128)(2,1)}) custom-call(s32[4]{0:T(128)} %copy-done.41, s32[2]{0:T(128)} %length_ref.5, bf16[3,512,256]{2,1,0:T(8,128)(2,1)} %get-tuple-element.279.refs_0_, bf16[3,512,256]{2,1,0:T(8,128)(2,1)} %copy-done.29, ...), custom_call_target="tpu_custom_call" | custom-call | flops 360000000 | bytes 1024 | tf_op jit(solution)/shard_map/attend/pallas_call | solution.py:367
  279.4 16.8 %collective-permute-start.19 = (bf16[1,512,256]{2,1,0:T(8,128)(2,1)}, bf16[1,512,256]{2,1,0:T(8,128)(2,1)}, u32[]{:S(2)}, u32[]{:S(2)}) collective-permute-start(bf16[1,512,256]{2,1,0:T(8,128)(2,1)} %get-tuple-element.296), channel_id=1, source_target_pairs={{0,6},{2,0},{4,2},{6,4},{1,7},{3,1},{5,3},{7,5},{8,14},{10,8},{12,... | collective-permute-start | bytes 786440 | tf_op jit(solution)/shard_map/ppermute | solution.py:54
  299.3 14.8 %collective-permute-done.19.refs_1_ = bf16[1,512,256]{2,1,0:T(8,128)(2,1)} collective-permute-done((bf16[1,512,256]{2,1,0:T(8,128)(2,1)}, bf16[1,512,256]{2,1,0:T(8,128)(2,1)}, u32[]{:S(2)}, u32[]{:S(2)}) %collective-permute-start.19) | collective-permute-done | bytes 262176 | tf_op jit(solution)/shard_map/ppermute | solution.py:54
  314.1 32.4 %collective-permute-done.20.refs_2_ = bf16[1,512,256]{2,1,0:T(8,128)(2,1)} collective-permute-done((bf16[1,512,256]{2,1,0:T(8,128)(2,1)}, bf16[1,512,256]{2,1,0:T(8,128)(2,1)}, u32[]{:S(2)}, u32[]{:S(2)}) %collective-permute-start.20) | collective-permute-done | bytes 262176 | tf_op jit(solution)/shard_map/ppermute | solution.py:54
  346.6 3.5 join.3.refs_2_
  355.5 6.1 to_width.4
  364.6 44.9 %collective-permute-done.25 = bf16[512,2048]{1,0:T(8,128)(2,1)S(1)} collective-permute-done((bf16[512,2048]{1,0:T(8,128)(2,1)}, bf16[512,2048]{1,0:T(8,128)(2,1)S(1)}, u32[]{:S(2)}, u32[]{:S(2)}) %collective-permute-start.25) | collective-permute-done | bytes 2097184 | tf_op jit(solution)/shard_map/ppermute | solution.py:49
  409.5 3.7 fusion.38
  419.2 11.5 %up.2 = (bf16[512,2048]{1,0:T(8,128)(2,1)}, f32[512,2048]{1,0:T(8,128)}) custom-call(s32[4]{0:T(128)} %get-tuple-element.578.perm_ref, bf16[512,2048]{1,0:T(8,128)(2,1)} %add_convert_fusion.1.a_ref, bf16[512,2048]{1,0:T(8,128)(2,1)} %all-gather.9.cloned.1.call-done.refs_0_.refs_2_, bf16[512,2048]{1,0:T(8,128)(2,1)} %collective-permute-done.13.refs_1_.refs_3_, ...), custom_call_target="tpu_custom_call" | custom-call | flops 307200000 | bytes 1024 | tf_op jit(solution)/shard_map/up/pallas_call | solution.py:464
  430.7 11.4 %up.3 = (bf16[512,2048]{1,0:T(8,128)(2,1)}, f32[512,2048]{1,0:T(8,128)}) custom-call(s32[4]{0:T(128)} %get-tuple-element.578.perm_ref, bf16[512,2048]{1,0:T(8,128)(2,1)} %add_convert_fusion.1.a_ref, bf16[512,2048]{1,0:T(8,128)(2,1)} %all-gather.11.cloned.1.call-done.refs_0_.refs_6_, bf16[512,2048]{1,0:T(8,128)(2,1)} %copy-done.23, ...), custom_call_target="tpu_custom_call" | custom-call | flops 307200000 | bytes 1024 | tf_op jit(solution)/shard_map/up/pallas_call | solution.py:464
  446.1 10.1 to_width.5.refs_5_
  456.2 9.5 collective-permute-done.28.refs_2_.refs_1_
  473.2 39.0 %collective-permute-done.27.refs_1_ = bf16[512,3072]{1,0:T(8,128)(2,1)} collective-permute-done((bf16[512,3072]{1,0:T(8,128)(2,1)}, bf16[512,3072]{1,0:T(8,128)(2,1)}, u32[]{:S(2)}, u32[]{:S(2)}) %collective-permute-start.27) | collective-permute-done | bytes 3145760 | tf_op jit(solution)/shard_map/ppermute | solution.py:49
  512.2 11.0 %to_width.6 = bf16[512,2048]{1,0:T(8,128)(2,1)} custom-call(bf16[512,2048]{1,0:T(8,128)(2,1)} %get-tuple-element.337.refs_0_, bf16[512,2048]{1,0:T(8,128)(2,1)} %all-gather.17.cloned.1.call-done.refs_1_.refs_0_, bf16[512,2048]{1,0:T(8,128)(2,1)} %collective-permute-done.28.refs_2_.refs_1_, bf16[512,2048]{1,0:T(8,128)(2,1)} %collective-permute-done.31.refs_3_.refs_2_, ...), custom_call_target="tpu_custom_call" | custom-call | flops 240000000 | bytes 1024 | tf_op jit(solution)/shard_map/to_width/pallas_call | solution.py:539
  529.3 4.6 collective-permute-done.40
  538.2 7.7 collective-permute-done.37
  545.9 30.0 %collective-permute-done.33 = bf16[512,2048]{1,0:T(8,128)(2,1)} collective-permute-done((bf16[512,2048]{1,0:T(8,128)(2,1)}, bf16[512,2048]{1,0:T(8,128)(2,1)}, u32[]{:S(2)}, u32[]{:S(2)}) %collective-permute-start.33) | collective-permute-done | bytes 2097184 | tf_op jit(solution)/shard_map/ppermute | solution.py:49
  575.9 6.1 fusion.37
  594.7 6.1 grad.14
  601.5 6.1 grad.15
  607.5 10.4 up_back.2.refs_0_
  618.0 10.5 up_back.3.refs_1_
  629.0 16.6 %to_width.7 = bf16[512,2048]{1,0:T(8,128)(2,1)} custom-call(bf16[512,2048]{1,0:T(8,128)(2,1)} %up_back.2.refs_0_, bf16[512,2048]{1,0:T(8,128)(2,1)} %up_back.3.refs_1_, bf16[512,2048]{1,0:T(8,128)(2,1)} %all-gather.9.cloned.1.call-done.refs_0_.refs_2_, bf16[512,2048]{1,0:T(8,128)(2,1)} %collective-permute-done.13.refs_1_.refs_3_, ...), custom_call_target="tpu_custom_call" | custom-call | flops 24000000000 | bytes 1024 | tf_op jit(solution)/shard_map/to_width/pallas_call | solution.py:539
  655.4 6.6 grad.16
  662.1 7.1 grad.17
  669.3 24.3 %collective-permute-done.45 = bf16[512,2048]{1,0:T(8,128)(2,1)} collective-permute-done((bf16[512,2048]{1,0:T(8,128)(2,1)}, bf16[512,2048]{1,0:T(8,128)(2,1)}, u32[]{:S(2)}, u32[]{:S(2)}) %collective-permute-start.45) | collective-permute-done | bytes 2097184 | tf_op jit(solution)/shard_map/ppermute | solution.py:49
  693.6 4.1 multiply_reduce_fusion
  702.6 7.5 heads.3
  710.1 7.0 grad.18
  718.7 3.8 collective-permute-start.48
  722.5 6.3 grad.19
  728.8 3.8 grad.20
  732.6 31.6 %collective-permute-done.51.refs_4_ = bf16[1,512,2048]{2,1,0:T(8,128)(2,1)S(1)} collective-permute-done((bf16[1,512,2048]{2,1,0:T(8,128)(2,1)S(1)}, bf16[1,512,2048]{2,1,0:T(8,128)(2,1)S(1)}, u32[]{:S(2)}, u32[]{:S(2)}) %collective-permute-start.51) | collective-permute-done | bytes 2097184 | tf_op jit(solution)/shard_map/ppermute | solution.py:45
  765.6 6.8 grad.21
  775.4 11.4 %attend_back.2 = (bf16[3,256,256]{2,1,0:T(8,128)(2,1)}, bf16[3,256,256]{2,1,0:T(8,128)(2,1)}, bf16[3,256,256]{2,1,0:T(8,128)(2,1)}, bf16[3,256,256]{2,1,0:T(8,128)(2,1)}) custom-call(s32[4]{0:T(128)} %copy-done.41, s32[2]{0:T(128)} %length_ref.5, bf16[3,512,256]{2,1,0:T(8,128)(2,1)} %get-tuple-element.279.refs_0_, bf16[3,512,256]{2,1,0:T(8,128)(2,1)} %copy-done.29, ...), custom_call_target="tpu_custom_call" | custom-call | flops 17999998976 | bytes 1024 | tf_op jit(solution)/shard_map/attend_back/pallas_call | solution.py:430
  789.2 11.3 %attend_back.3 = (bf16[3,256,256]{2,1,0:T(8,128)(2,1)}, bf16[3,256,256]{2,1,0:T(8,128)(2,1)}, bf16[3,256,256]{2,1,0:T(8,128)(2,1)}, bf16[3,256,256]{2,1,0:T(8,128)(2,1)}) custom-call(s32[4]{0:T(128)} %copy-done.41, s32[2]{0:T(128)} %length_ref.5, bf16[3,512,256]{2,1,0:T(8,128)(2,1)} %get-tuple-element.279.refs_0_, bf16[3,512,256]{2,1,0:T(8,128)(2,1)} %copy-done.29, ...), custom_call_target="tpu_custom_call" | custom-call | flops 17999998976 | bytes 1024 | tf_op jit(solution)/shard_map/attend_back/pallas_call | solution.py:430
  802.7 16.0 %collective-permute-done.55.refs_4_ = bf16[1,512,2048]{2,1,0:T(8,128)(2,1)} collective-permute-done((bf16[1,512,2048]{2,1,0:T(8,128)(2,1)S(1)}, bf16[1,512,2048]{2,1,0:T(8,128)(2,1)}, u32[]{:S(2)}, u32[]{:S(2)}) %collective-permute-start.55) | collective-permute-done | bytes 2097184 | tf_op jit(solution)/shard_map/ppermute | solution.py:45
  818.7 6.6 grad.22
  826.9 26.5 %collective-permute-done.53.refs_2_ = bf16[3,256,256]{2,1,0:T(8,128)(2,1)} collective-permute-done((bf16[3,256,256]{2,1,0:T(8,128)(2,1)}, bf16[3,256,256]{2,1,0:T(8,128)(2,1)}, u32[]{:S(2)}, u32[]{:S(2)}) %collective-permute-start.53) | collective-permute-done | bytes 393248 | tf_op jit(solution)/shard_map/ppermute | solution.py:54
  853.4 3.9 join.4.grad_ref.refs_2_
  861.3 13.2 %own.2 = (f32[3,256,2048]{2,1,0:T(8,128)}, f32[3,16,2048]{2,1,0:T(8,128)}) custom-call(s32[4]{0:T(128)} %get-tuple-element.578.perm_ref, bf16[3,256,1024]{2,1,0:T(8,128)(2,1)} %join.4.grad_ref.refs_2_, f32[4,512,2048]{2,1,0:T(8,128)} %get-tuple-element.245.z_ref, bf16[512,3072]{1,0:T(8,128)(2,1)} %all-gather.7.cloned.1.call-done.refs_0_, ...), custom_call_target="tpu_custom_call" | custom-call | flops 17999998976 | bytes 1024 | tf_op jit(solution)/shard_map/own/pallas_call | solution.py:663
  877.5 4.2 grad.23
  881.7 38.0 %collective-permute-done.57.refs_2_ = bf16[3,256,256]{2,1,0:T(8,128)(2,1)} collective-permute-done((bf16[3,256,256]{2,1,0:T(8,128)(2,1)}, bf16[3,256,256]{2,1,0:T(8,128)(2,1)}, u32[]{:S(2)}, u32[]{:S(2)}) %collective-permute-start.57) | collective-permute-done | bytes 393248 | tf_op jit(solution)/shard_map/ppermute | solution.py:54
  919.7 3.9 join.5.refs_3_.grad_ref
  930.6 3.9 grad.24
  934.5 9.8 collective-permute-start.64
  944.4 6.4 grad.25
  950.8 13.2 %own.3 = (f32[3,256,2048]{2,1,0:T(8,128)}, f32[3,16,2048]{2,1,0:T(8,128)}) custom-call(s32[4]{0:T(128)} %get-tuple-element.578.perm_ref, bf16[3,256,1024]{2,1,0:T(8,128)(2,1)} %join.5.refs_3_.grad_ref, f32[4,512,2048]{2,1,0:T(8,128)} %get-tuple-element.245.z_ref, bf16[512,3072]{1,0:T(8,128)(2,1)} %all-gather.7.cloned.1.call-done.refs_0_, ...), custom_call_target="tpu_custom_call" | custom-call | flops 17999998976 | bytes 1024 | tf_op jit(solution)/shard_map/own/pallas_call | solution.py:663
  969.6 4.2 grad.26
  973.8 14.1 %other.2.dz_ref = bf16[3,256,2048]{2,1,0:T(8,128)(2,1)} custom-call(bf16[3,256,1024]{2,1,0:T(8,128)(2,1)} %collective-permute-done.61.grad_ref, f32[3,256,2048]{2,1,0:T(8,128)} %get-tuple-element.415.part_ref, f32[4,512,2048]{2,1,0:T(8,128)} %get-tuple-element.245.z_ref, f32[1,2048]{1,0:T(1,128)} %bitcast.189, ...), custom_call_target="tpu_custom_call" | custom-call | flops 20999999488 | bytes 1024 | tf_op jit(solution)/shard_map/other/pallas_call | solution.py:712
  987.9 13.0 %last.2 = (bf16[8,512,2048]{2,1,0:T(8,128)(2,1)}, f32[16,256,128]{2,1,0:T(8,128)}) custom-call(s32[4]{0:T(128)} %get-tuple-element.578.perm_ref, bf16[8,512,2048]{2,1,0:T(8,128)(2,1)} %bitcast.144, f32[16,256,4]{2,1,0:T(8,128)} %bitcast.147, bf16[3,256,2048]{2,1,0:T(8,128)(2,1)} %other.2.dz_ref, bf16[512,2048]{1,0:T(8,128)(2,1)} %copy-done.15), custom_call_target="tpu_custom_call" | custom-call | flops 17999998976 | bytes 1024 | tf_op jit(solution)/shard_map/last/pallas_call | solution.py:768
  1002.7 14.2 %other.3.dz_ref = bf16[3,256,2048]{2,1,0:T(8,128)(2,1)} custom-call(bf16[3,256,1024]{2,1,0:T(8,128)(2,1)} %collective-permute-done.60.grad_ref, f32[3,256,2048]{2,1,0:T(8,128)} %get-tuple-element.438.part_ref, f32[4,512,2048]{2,1,0:T(8,128)} %get-tuple-element.245.z_ref, f32[1,2048]{1,0:T(1,128)} %bitcast.190, ...), custom_call_target="tpu_custom_call" | custom-call | flops 20999999488 | bytes 1024 | tf_op jit(solution)/shard_map/other/pallas_call | solution.py:712
  1021.8 6.9 grad.27
  1033.3 13.3 %last.3 = (bf16[8,512,2048]{2,1,0:T(8,128)(2,1)}, f32[16,256,128]{2,1,0:T(8,128)}) custom-call(s32[4]{0:T(128)} %get-tuple-element.578.perm_ref, bf16[8,512,2048]{2,1,0:T(8,128)(2,1)} %bitcast.145, f32[16,256,4]{2,1,0:T(8,128)} %bitcast.148, bf16[3,256,2048]{2,1,0:T(8,128)(2,1)} %other.3.dz_ref, ...), custom_call_target="tpu_custom_call", output_to_operand_aliasing={{0}: (5, {}), {1}: (6, {})} | custom-call | flops 17999998976 | bytes 1024 | tf_op jit(solution)/shard_map/last/pallas_call | solution.py:768
  1064.8 14.4 %reduce-scatter.18.cloned.1.call-done = bf16[128,2048]{1,0:T(8,128)(2,1)} async-done(((bf16[512,2048]{1,0:T(8,128)(2,1)}), bf16[128,2048]{1,0:T(8,128)(2,1)}) %reduce-scatter.18.cloned.1.call-update) | async-done | bytes 524304 | tf_op jit(solution)/shard_map/reduce_scatter | solution.py:135
  (398 shorter events, 175.1 us)
Async XLA Ops:
  7.2 69.2 %all-gather.7.cloned.1.call-start = ((), (), s32[]{:S(2)}) async-start(), calls=%async_computation.7 | async-start | bytes 3932160 | tf_op jit(solution)/shard_map/all_gather | solution.py:88
  9.3 113.9 %all-gather.9.cloned.1.call-start = ((), (), s32[]{:S(2)}) async-start(), calls=%async_computation.8 | async-start | bytes 2621440 | tf_op jit(solution)/shard_map/all_gather | solution.py:88
  10.8 21.6 %collective-permute-start = (bf16[40,128]{1,0:T(8,128)(2,1)S(1)}, bf16[40,128]{1,0:T(8,128)(2,1)S(1)}, u32[]{:S(2)}, u32[]{:S(2)}) collective-permute-start(bf16[40,128]{1,0:T(8,128)(2,1)S(1)} %concatenate.51), channel_id=1, source_target_pairs={{0,2},{2,4},{4,6},{6,0},{1,3},{3,5},{5,7},{7,1},{8,10},{10,12},{12... | collective-permute-start | bytes 30728 | tf_op jit(solution)/shard_map/ppermute | solution.py:54
  13.9 18.6 %collective-permute-start.1 = (bf16[40,128]{1,0:T(8,128)(2,1)S(1)}, bf16[40,128]{1,0:T(8,128)(2,1)S(1)}, u32[]{:S(2)}, u32[]{:S(2)}) collective-permute-start(bf16[40,128]{1,0:T(8,128)(2,1)S(1)} %concatenate.51), channel_id=1, source_target_pairs={{0,4},{2,6},{4,0},{6,2},{1,5},{3,7},{5,1},{7,3},{8,12},{10,14},{12... | collective-permute-start | bytes 30728 | tf_op jit(solution)/shard_map/ppermute | solution.py:54
  16.5 16.0 %collective-permute-start.2 = (bf16[40,128]{1,0:T(8,128)(2,1)S(1)}, bf16[40,128]{1,0:T(8,128)(2,1)S(1)}, u32[]{:S(2)}, u32[]{:S(2)}) collective-permute-start(bf16[40,128]{1,0:T(8,128)(2,1)S(1)} %concatenate.51), channel_id=1, source_target_pairs={{0,6},{2,0},{4,2},{6,4},{1,7},{3,1},{5,3},{7,5},{8,14},{10,8},{12,... | collective-permute-start | bytes 30728 | tf_op jit(solution)/shard_map/ppermute | solution.py:54
  19.7 172.8 %all-gather.11.cloned.1.call-start = ((), (), s32[]{:S(2)}) async-start(), calls=%async_computation.9 | async-start | bytes 2621440 | tf_op jit(solution)/shard_map/all_gather | solution.py:88
  76.4 48.6 %collective-permute-start.6 = (bf16[512,3072]{1,0:T(8,128)(2,1)}, bf16[512,3072]{1,0:T(8,128)(2,1)S(1)}, u32[]{:S(2)}, u32[]{:S(2)}) collective-permute-start(bf16[512,3072]{1,0:T(8,128)(2,1)} %all-gather.7.cloned.1.call-done.refs_0_), channel_id=1, source_target_pairs={{0,8},{8,0},{16,24},{24,16},{1,9},{9,1},{17,25},{25,17},{2,10},{10... | collective-permute-start | bytes 9437192 | tf_op jit(solution)/shard_map/ppermute | solution.py:45
  76.4 70.8 %collective-permute-start.8 = (bf16[512,3072]{1,0:T(8,128)(2,1)}, bf16[512,3072]{1,0:T(8,128)(2,1)}, u32[]{:S(2)}, u32[]{:S(2)}) collective-permute-start(bf16[512,3072]{1,0:T(8,128)(2,1)} %all-gather.7.cloned.1.call-done.refs_0_), channel_id=1, source_target_pairs={{0,1},{1,0},{2,3},{3,2},{4,5},{5,4},{6,7},{7,6},{8,9},{9,8},{10,11... | collective-permute-start | bytes 9437192 | tf_op jit(solution)/shard_map/ppermute | solution.py:49
  77.9 70.5 %collective-permute-start.7 = (bf16[512,3072]{1,0:T(8,128)(2,1)}, bf16[512,3072]{1,0:T(8,128)(2,1)}, u32[]{:S(2)}, u32[]{:S(2)}) collective-permute-start(bf16[512,3072]{1,0:T(8,128)(2,1)} %all-gather.7.cloned.1.call-done.refs_0_), channel_id=1, source_target_pairs={{0,16},{8,24},{16,0},{24,8},{1,17},{9,25},{17,1},{25,9},{2,18},{10... | collective-permute-start | bytes 9437192 | tf_op jit(solution)/shard_map/ppermute | solution.py:45
  148.5 118.8 %all-gather.13.cloned.1.call-start = ((), (), s32[]{:S(2)}) async-start(), calls=%async_computation.10 | async-start | bytes 1310720 | tf_op jit(solution)/shard_map/all_gather | solution.py:88
  149.1 116.8 %collective-permute-start.13 = (bf16[512,2048]{1,0:T(8,128)(2,1)}, bf16[512,2048]{1,0:T(8,128)(2,1)}, u32[]{:S(2)}, u32[]{:S(2)}) collective-permute-start(bf16[512,2048]{1,0:T(8,128)(2,1)} %all-gather.9.cloned.1.call-done.refs_0_.refs_2_), channel_id=1, source_target_pairs={{0,16},{8,24},{16,0},{24,8},{1,17},{9,25},{17,1},{25,9},{2,18},{10... | collective-permute-start | bytes 6291464 | tf_op jit(solution)/shard_map/ppermute | solution.py:45
  192.5 73.3 %collective-permute-start.14 = (bf16[512,2048]{1,0:T(8,128)(2,1)}, bf16[512,2048]{1,0:T(8,128)(2,1)S(1)}, u32[]{:S(2)}, u32[]{:S(2)}) collective-permute-start(bf16[512,2048]{1,0:T(8,128)(2,1)} %all-gather.11.cloned.1.call-done.refs_0_.refs_6_), channel_id=1, source_target_pairs={{0,16},{8,24},{16,0},{24,8},{1,17},{9,25},{17,1},{25,9},{2,18},{10... | collective-permute-start | bytes 6291464 | tf_op jit(solution)/shard_map/ppermute | solution.py:45
  194.0 30.2 %collective-permute-start.10 = (bf16[3,512,256]{2,1,0:T(8,128)(2,1)}, bf16[3,512,256]{2,1,0:T(8,128)(2,1)S(1)}, u32[]{:S(2)}, u32[]{:S(2)}) collective-permute-start(bf16[3,512,256]{2,1,0:T(8,128)(2,1)} %get-tuple-element.265), channel_id=1, source_target_pairs={{0,2},{2,4},{4,6},{6,0},{1,3},{3,5},{5,7},{7,1},{8,10},{10,12},{12... | collective-permute-start | bytes 2359304 | tf_op jit(solution)/shard_map/ppermute | solution.py:54
  194.0 71.9 %collective-permute-start.11 = (bf16[3,512,256]{2,1,0:T(8,128)(2,1)}, bf16[3,512,256]{2,1,0:T(8,128)(2,1)}, u32[]{:S(2)}, u32[]{:S(2)}) collective-permute-start(bf16[3,512,256]{2,1,0:T(8,128)(2,1)} %get-tuple-element.266), channel_id=1, source_target_pairs={{0,4},{2,6},{4,0},{6,2},{1,5},{3,7},{5,1},{7,3},{8,12},{10,14},{12... | collective-permute-start | bytes 2359304 | tf_op jit(solution)/shard_map/ppermute | solution.py:54
  195.7 70.2 %collective-permute-start.12 = (bf16[3,512,256]{2,1,0:T(8,128)(2,1)}, bf16[3,512,256]{2,1,0:T(8,128)(2,1)}, u32[]{:S(2)}, u32[]{:S(2)}) collective-permute-start(bf16[3,512,256]{2,1,0:T(8,128)(2,1)} %get-tuple-element.267), channel_id=1, source_target_pairs={{0,6},{2,0},{4,2},{6,4},{1,7},{3,1},{5,3},{7,5},{8,14},{10,8},{12,... | collective-permute-start | bytes 2359304 | tf_op jit(solution)/shard_map/ppermute | solution.py:54
  198.0 165.2 %all-gather.15.cloned.1.call-start = ((), (), s32[]{:S(2)}) async-start(), calls=%async_computation.11 | async-start | bytes 2621440 | tf_op jit(solution)/shard_map/all_gather | solution.py:88
  265.9 13.5 %collective-permute-start.17 = (bf16[512,2048]{1,0:T(8,128)(2,1)}, bf16[512,2048]{1,0:T(8,128)(2,1)}, u32[]{:S(2)}, u32[]{:S(2)}) collective-permute-start(bf16[512,2048]{1,0:T(8,128)(2,1)} %all-gather.11.cloned.1.call-done.refs_0_.refs_6_), channel_id=1, source_target_pairs={{0,8},{8,0},{16,24},{24,16},{1,9},{9,1},{17,25},{25,17},{2,10},{10... | collective-permute-start | bytes 6291464 | tf_op jit(solution)/shard_map/ppermute | solution.py:45
  267.0 150.3 %all-gather.17.cloned.1.call-start = ((), (), s32[]{:S(2)}) async-start(), calls=%async_computation.12 | async-start | bytes 2621440 | tf_op jit(solution)/shard_map/all_gather | solution.py:88
  267.3 82.8 %collective-permute-start.22 = (bf16[512,1024]{1,0:T(8,128)(2,1)}, bf16[512,1024]{1,0:T(8,128)(2,1)}, u32[]{:S(2)}, u32[]{:S(2)}) collective-permute-start(bf16[512,1024]{1,0:T(8,128)(2,1)} %all-gather.13.cloned.1.call-done.refs_1_.refs_0_), channel_id=1, source_target_pairs={{0,16},{8,24},{16,0},{24,8},{1,17},{9,25},{17,1},{25,9},{2,18},{10... | collective-permute-start | bytes 3145736 | tf_op jit(solution)/shard_map/ppermute | solution.py:45
  279.4 34.7 %collective-permute-start.19 = (bf16[1,512,256]{2,1,0:T(8,128)(2,1)}, bf16[1,512,256]{2,1,0:T(8,128)(2,1)}, u32[]{:S(2)}, u32[]{:S(2)}) collective-permute-start(bf16[1,512,256]{2,1,0:T(8,128)(2,1)} %get-tuple-element.296), channel_id=1, source_target_pairs={{0,6},{2,0},{4,2},{6,4},{1,7},{3,1},{5,3},{7,5},{8,14},{10,8},{12,... | collective-permute-start | bytes 786440 | tf_op jit(solution)/shard_map/ppermute | solution.py:54
  296.3 50.3 %collective-permute-start.20 = (bf16[1,512,256]{2,1,0:T(8,128)(2,1)}, bf16[1,512,256]{2,1,0:T(8,128)(2,1)}, u32[]{:S(2)}, u32[]{:S(2)}) collective-permute-start(bf16[1,512,256]{2,1,0:T(8,128)(2,1)} %get-tuple-element.297), channel_id=1, source_target_pairs={{0,4},{2,6},{4,0},{6,2},{1,5},{3,7},{5,1},{7,3},{8,12},{10,14},{12... | collective-permute-start | bytes 786440 | tf_op jit(solution)/shard_map/ppermute | solution.py:54
  297.3 49.3 %collective-permute-start.21 = (bf16[1,512,256]{2,1,0:T(8,128)(2,1)}, bf16[1,512,256]{2,1,0:T(8,128)(2,1)}, u32[]{:S(2)}, u32[]{:S(2)}) collective-permute-start(bf16[1,512,256]{2,1,0:T(8,128)(2,1)} %get-tuple-element.298), channel_id=1, source_target_pairs={{0,2},{2,4},{4,6},{6,0},{1,3},{3,5},{5,7},{7,1},{8,10},{10,12},{12... | collective-permute-start | bytes 786440 | tf_op jit(solution)/shard_map/ppermute | solution.py:54
  361.6 47.9 %collective-permute-start.25 = (bf16[512,2048]{1,0:T(8,128)(2,1)}, bf16[512,2048]{1,0:T(8,128)(2,1)S(1)}, u32[]{:S(2)}, u32[]{:S(2)}) collective-permute-start(bf16[512,2048]{1,0:T(8,128)(2,1)} %to_width.4), channel_id=1, source_target_pairs={{0,1},{1,0},{2,3},{3,2},{4,5},{5,4},{6,7},{7,6},{8,9},{9,8},{10,11... | collective-permute-start | bytes 6291464 | tf_op jit(solution)/shard_map/ppermute | solution.py:49
  363.1 437.4 %reduce-scatter.8.cloned.1.call-start = ((), (), s32[]{:S(2)}) async-start(), calls=%async_computation.13 | async-start | bytes 2621440 | tf_op jit(solution)/shard_map/reduce_scatter | solution.py:135
  363.2 54.1 %collective-permute-start.26 = (bf16[512,2048]{1,0:T(8,128)(2,1)}, bf16[512,2048]{1,0:T(8,128)(2,1)}, u32[]{:S(2)}, u32[]{:S(2)}) collective-permute-start(bf16[512,2048]{1,0:T(8,128)(2,1)} %all-gather.15.cloned.1.call-done.refs_1_.refs_0_), channel_id=1, source_target_pairs={{0,16},{8,24},{16,0},{24,8},{1,17},{9,25},{17,1},{25,9},{2,18},{10... | collective-permute-start | bytes 6291464 | tf_op jit(solution)/shard_map/ppermute | solution.py:45
  417.3 26.2 %collective-permute-start.29 = (bf16[512,2048]{1,0:T(8,128)(2,1)}, bf16[512,2048]{1,0:T(8,128)(2,1)S(1)}, u32[]{:S(2)}, u32[]{:S(2)}) collective-permute-start(bf16[512,2048]{1,0:T(8,128)(2,1)} %all-gather.15.cloned.1.call-done.refs_1_.refs_0_), channel_id=1, source_target_pairs={{0,8},{8,0},{16,24},{24,16},{1,9},{9,1},{17,25},{25,17},{2,10},{10... | collective-permute-start | bytes 6291464 | tf_op jit(solution)/shard_map/ppermute | solution.py:45
  417.3 26.2 %collective-permute-start.30 = (bf16[512,2048]{1,0:T(8,128)(2,1)}, bf16[512,2048]{1,0:T(8,128)(2,1)S(1)}, u32[]{:S(2)}, u32[]{:S(2)}) collective-permute-start(bf16[512,2048]{1,0:T(8,128)(2,1)} %collective-permute-done.26.refs_2_.refs_1_), channel_id=1, source_target_pairs={{0,8},{8,0},{16,24},{24,16},{1,9},{9,1},{17,25},{25,17},{2,10},{10... | collective-permute-start | bytes 6291464 | tf_op jit(solution)/shard_map/ppermute | solution.py:45
  417.8 47.9 %collective-permute-start.28 = (bf16[512,2048]{1,0:T(8,128)(2,1)}, bf16[512,2048]{1,0:T(8,128)(2,1)}, u32[]{:S(2)}, u32[]{:S(2)}) collective-permute-start(bf16[512,2048]{1,0:T(8,128)(2,1)} %all-gather.17.cloned.1.call-done.refs_1_.refs_0_), channel_id=1, source_target_pairs={{0,16},{8,24},{16,0},{24,8},{1,17},{9,25},{17,1},{25,9},{2,18},{10... | collective-permute-start | bytes 6291464 | tf_op jit(solution)/shard_map/ppermute | solution.py:45
  442.1 70.1 %collective-permute-start.27 = (bf16[512,3072]{1,0:T(8,128)(2,1)}, bf16[512,3072]{1,0:T(8,128)(2,1)}, u32[]{:S(2)}, u32[]{:S(2)}) collective-permute-start(bf16[512,3072]{1,0:T(8,128)(2,1)} %collective-permute-done.7.refs_1_), channel_id=1, source_target_pairs={{0,1},{1,0},{2,3},{3,2},{4,5},{5,4},{6,7},{7,6},{8,9},{9,8},{10,11... | collective-permute-start | bytes 9437192 | tf_op jit(solution)/shard_map/ppermute | solution.py:49
  467.3 59.3 %collective-permute-start.38 = (bf16[512,1024]{1,0:T(8,128)(2,1)}, bf16[512,1024]{1,0:T(8,128)(2,1)}, u32[]{:S(2)}, u32[]{:S(2)}) collective-permute-start(bf16[512,1024]{1,0:T(8,128)(2,1)} %slice.126), channel_id=1, source_target_pairs={{0,8},{8,0},{16,24},{24,16},{1,9},{9,1},{17,25},{25,17},{2,10},{10... | collective-permute-start | bytes 3145736 | tf_op jit(solution)/shard_map/ppermute | solution.py:45
  526.1 19.8 %collective-permute-start.36 = (bf16[3,512,1024]{2,1,0:T(8,128)(2,1)}, bf16[3,512,1024]{2,1,0:T(8,128)(2,1)S(1)}, u32[]{:S(2)}, u32[]{:S(2)}) collective-permute-start(bf16[3,512,1024]{2,1,0:T(8,128)(2,1)} %slice.125), channel_id=1, source_target_pairs={{0,8},{8,0},{16,24},{24,16},{1,9},{9,1},{17,25},{25,17},{2,10},{10... | collective-permute-start | bytes 9437192 | tf_op jit(solution)/shard_map/ppermute | solution.py:45
  526.2 19.7 %collective-permute-start.34 = (bf16[512,3072]{1,0:T(8,128)(2,1)}, bf16[512,3072]{1,0:T(8,128)(2,1)}, u32[]{:S(2)}, u32[]{:S(2)}) collective-permute-start(bf16[512,3072]{1,0:T(8,128)(2,1)} %collective-permute-done.8.refs_0_), channel_id=1, source_target_pairs={{0,8},{8,0},{16,24},{24,16},{1,9},{9,1},{17,25},{25,17},{2,10},{10... | collective-permute-start | bytes 9437192 | tf_op jit(solution)/shard_map/ppermute | solution.py:45
  526.6 19.3 %collective-permute-start.35 = (bf16[512,3072]{1,0:T(8,128)(2,1)}, bf16[512,3072]{1,0:T(8,128)(2,1)}, u32[]{:S(2)}, u32[]{:S(2)}) collective-permute-start(bf16[512,3072]{1,0:T(8,128)(2,1)} %collective-permute-done.27.refs_1_), channel_id=1, source_target_pairs={{0,8},{8,0},{16,24},{24,16},{1,9},{9,1},{17,25},{25,17},{2,10},{10... | collective-permute-start | bytes 9437192 | tf_op jit(solution)/shard_map/ppermute | solution.py:45
  527.9 48.0 %collective-permute-start.33 = (bf16[512,2048]{1,0:T(8,128)(2,1)}, bf16[512,2048]{1,0:T(8,128)(2,1)}, u32[]{:S(2)}, u32[]{:S(2)}) collective-permute-start(bf16[512,2048]{1,0:T(8,128)(2,1)} %to_width.6), channel_id=1, source_target_pairs={{0,1},{1,0},{2,3},{3,2},{4,5},{5,4},{6,7},{7,6},{8,9},{9,8},{10,11... | collective-permute-start | bytes 6291464 | tf_op jit(solution)/shard_map/ppermute | solution.py:49
  600.8 54.6 %collective-permute-start.44 = (bf16[1,512,2048]{2,1,0:T(8,128)(2,1)}, bf16[1,512,2048]{2,1,0:T(8,128)(2,1)}, u32[]{:S(2)}, u32[]{:S(2)}) collective-permute-start(bf16[1,512,2048]{2,1,0:T(8,128)(2,1)} %grad.14), channel_id=1, source_target_pairs={{0,16},{8,24},{16,0},{24,8},{1,17},{9,25},{17,1},{25,9},{2,18},{10... | collective-permute-start | bytes 6291464 | tf_op jit(solution)/shard_map/ppermute | solution.py:45
  628.5 33.6 %collective-permute-start.43 = (bf16[512,2048]{1,0:T(8,128)(2,1)}, bf16[512,2048]{1,0:T(8,128)(2,1)}, u32[]{:S(2)}, u32[]{:S(2)}) collective-permute-start(bf16[512,2048]{1,0:T(8,128)(2,1)} %up_back.3.refs_1_), channel_id=1, source_target_pairs={{0,8},{8,0},{16,24},{24,16},{1,9},{9,1},{17,25},{25,17},{2,10},{10... | collective-permute-start | bytes 6291464 | tf_op jit(solution)/shard_map/ppermute | solution.py:45
  628.5 33.5 %collective-permute-start.42 = (bf16[512,2048]{1,0:T(8,128)(2,1)}, bf16[512,2048]{1,0:T(8,128)(2,1)}, u32[]{:S(2)}, u32[]{:S(2)}) collective-permute-start(bf16[512,2048]{1,0:T(8,128)(2,1)} %up_back.2.refs_0_), channel_id=1, source_target_pairs={{0,8},{8,0},{16,24},{24,16},{1,9},{9,1},{17,25},{25,17},{2,10},{10... | collective-permute-start | bytes 6291464 | tf_op jit(solution)/shard_map/ppermute | solution.py:45
  645.6 47.9 %collective-permute-start.45 = (bf16[512,2048]{1,0:T(8,128)(2,1)}, bf16[512,2048]{1,0:T(8,128)(2,1)}, u32[]{:S(2)}, u32[]{:S(2)}) collective-permute-start(bf16[512,2048]{1,0:T(8,128)(2,1)} %to_width.7), channel_id=1, source_target_pairs={{0,1},{1,0},{2,3},{3,2},{4,5},{5,4},{6,7},{7,6},{8,9},{9,8},{10,11... | collective-permute-start | bytes 6291464 | tf_op jit(solution)/shard_map/ppermute | solution.py:49
  654.0 56.1 %collective-permute-start.50 = (bf16[1,512,2048]{2,1,0:T(8,128)(2,1)}, bf16[1,512,2048]{2,1,0:T(8,128)(2,1)}, u32[]{:S(2)}, u32[]{:S(2)}) collective-permute-start(bf16[1,512,2048]{2,1,0:T(8,128)(2,1)} %grad.15), channel_id=1, source_target_pairs={{0,16},{8,24},{16,0},{24,8},{1,17},{9,25},{17,1},{25,9},{2,18},{10... | collective-permute-start | bytes 6291464 | tf_op jit(solution)/shard_map/ppermute | solution.py:45
  662.1 212.3 %reduce-scatter.10.cloned.1.call-start = ((), (), s32[]{:S(2)}) async-start(), calls=%async_computation.14 | async-start | bytes 2621440 | tf_op jit(solution)/shard_map/reduce_scatter | solution.py:135
  717.2 210.1 %reduce-scatter.12.cloned.1.call-start = ((), (), s32[]{:S(2)}) async-start(), calls=%async_computation.15 | async-start | bytes 2621440 | tf_op jit(solution)/shard_map/reduce_scatter | solution.py:135
  717.2 47.0 %collective-permute-start.51 = (bf16[1,512,2048]{2,1,0:T(8,128)(2,1)S(1)}, bf16[1,512,2048]{2,1,0:T(8,128)(2,1)S(1)}, u32[]{:S(2)}, u32[]{:S(2)}) collective-permute-start(bf16[1,512,2048]{2,1,0:T(8,128)(2,1)S(1)} %copy-done.45), channel_id=1, source_target_pairs={{0,16},{8,24},{16,0},{24,8},{1,17},{9,25},{17,1},{25,9},{2,18},{10... | collective-permute-start | bytes 6291464 | tf_op jit(solution)/shard_map/ppermute | solution.py:45
  718.7 55.2 %collective-permute-start.46 = (bf16[1,512,256]{2,1,0:T(8,128)(2,1)}, bf16[1,512,256]{2,1,0:T(8,128)(2,1)S(1)}, u32[]{:S(2)}, u32[]{:S(2)}) collective-permute-start(bf16[1,512,256]{2,1,0:T(8,128)(2,1)} %get-tuple-element.371), channel_id=1, source_target_pairs={{0,2},{2,4},{4,6},{6,0},{1,3},{3,5},{5,7},{7,1},{8,10},{10,12},{12... | collective-permute-start | bytes 786440 | tf_op jit(solution)/shard_map/ppermute | solution.py:54
  718.7 55.2 %collective-permute-start.47 = (bf16[1,512,256]{2,1,0:T(8,128)(2,1)}, bf16[1,512,256]{2,1,0:T(8,128)(2,1)S(1)}, u32[]{:S(2)}, u32[]{:S(2)}) collective-permute-start(bf16[1,512,256]{2,1,0:T(8,128)(2,1)} %get-tuple-element.372), channel_id=1, source_target_pairs={{0,4},{2,6},{4,0},{6,2},{1,5},{3,7},{5,1},{7,3},{8,12},{10,14},{12... | collective-permute-start | bytes 786440 | tf_op jit(solution)/shard_map/ppermute | solution.py:54
  718.7 55.2 %collective-permute-start.48 = (bf16[1,512,256]{2,1,0:T(8,128)(2,1)}, bf16[1,512,256]{2,1,0:T(8,128)(2,1)S(1)}, u32[]{:S(2)}, u32[]{:S(2)}) collective-permute-start(bf16[1,512,256]{2,1,0:T(8,128)(2,1)} %get-tuple-element.373), channel_id=1, source_target_pairs={{0,6},{2,0},{4,2},{6,4},{1,7},{3,1},{5,3},{7,5},{8,14},{10,8},{12,... | collective-permute-start | bytes 786440 | tf_op jit(solution)/shard_map/ppermute | solution.py:54
  772.4 247.3 %reduce-scatter.14.cloned.1.call-start = ((), (), s32[]{:S(2)}) async-start(), calls=%async_computation.16 | async-start | bytes 2621440 | tf_op jit(solution)/shard_map/reduce_scatter | solution.py:135
  772.4 46.3 %collective-permute-start.55 = (bf16[1,512,2048]{2,1,0:T(8,128)(2,1)S(1)}, bf16[1,512,2048]{2,1,0:T(8,128)(2,1)}, u32[]{:S(2)}, u32[]{:S(2)}) collective-permute-start(bf16[1,512,2048]{2,1,0:T(8,128)(2,1)S(1)} %copy-done.46), channel_id=1, source_target_pairs={{0,16},{8,24},{16,0},{24,8},{1,17},{9,25},{17,1},{25,9},{2,18},{10... | collective-permute-start | bytes 6291464 | tf_op jit(solution)/shard_map/ppermute | solution.py:45
  786.8 40.1 %collective-permute-start.52 = (bf16[3,256,256]{2,1,0:T(8,128)(2,1)}, bf16[3,256,256]{2,1,0:T(8,128)(2,1)}, u32[]{:S(2)}, u32[]{:S(2)}) collective-permute-start(bf16[3,256,256]{2,1,0:T(8,128)(2,1)} %get-tuple-element.392), channel_id=1, source_target_pairs={{0,6},{2,0},{4,2},{6,4},{1,7},{3,1},{5,3},{7,5},{8,14},{10,8},{12,... | collective-permute-start | bytes 1179656 | tf_op jit(solution)/shard_map/ppermute | solution.py:54
  786.8 66.6 %collective-permute-start.53 = (bf16[3,256,256]{2,1,0:T(8,128)(2,1)}, bf16[3,256,256]{2,1,0:T(8,128)(2,1)}, u32[]{:S(2)}, u32[]{:S(2)}) collective-permute-start(bf16[3,256,256]{2,1,0:T(8,128)(2,1)} %get-tuple-element.393), channel_id=1, source_target_pairs={{0,4},{2,6},{4,0},{6,2},{1,5},{3,7},{5,1},{7,3},{8,12},{10,14},{12... | collective-permute-start | bytes 1179656 | tf_op jit(solution)/shard_map/ppermute | solution.py:54
  786.8 66.6 %collective-permute-start.54 = (bf16[3,256,256]{2,1,0:T(8,128)(2,1)}, bf16[3,256,256]{2,1,0:T(8,128)(2,1)}, u32[]{:S(2)}, u32[]{:S(2)}) collective-permute-start(bf16[3,256,256]{2,1,0:T(8,128)(2,1)} %get-tuple-element.394), channel_id=1, source_target_pairs={{0,2},{2,4},{4,6},{6,0},{1,3},{3,5},{5,7},{7,1},{8,10},{10,12},{12... | collective-permute-start | bytes 1179656 | tf_op jit(solution)/shard_map/ppermute | solution.py:54
  825.4 223.8 %reduce-scatter.20.cloned.1.call-start = ((), (), s32[]{:S(2)}) async-start(), calls=%async_computation.19 | async-start | bytes 1310720 | tf_op jit(solution)/shard_map/reduce_scatter | solution.py:135
  825.5 51.1 %collective-permute-start.59 = (bf16[1,512,1024]{2,1,0:T(8,128)(2,1)S(1)}, bf16[1,512,1024]{2,1,0:T(8,128)(2,1)S(1)}, u32[]{:S(2)}, u32[]{:S(2)}) collective-permute-start(bf16[1,512,1024]{2,1,0:T(8,128)(2,1)S(1)} %copy-done.49), channel_id=1, source_target_pairs={{0,16},{8,24},{16,0},{24,8},{1,17},{9,25},{17,1},{25,9},{2,18},{10... | collective-permute-start | bytes 3145736 | tf_op jit(solution)/shard_map/ppermute | solution.py:45
  857.3 24.4 %collective-permute-start.56 = (bf16[3,256,256]{2,1,0:T(8,128)(2,1)}, bf16[3,256,256]{2,1,0:T(8,128)(2,1)}, u32[]{:S(2)}, u32[]{:S(2)}) collective-permute-start(bf16[3,256,256]{2,1,0:T(8,128)(2,1)} %get-tuple-element.411), channel_id=1, source_target_pairs={{0,6},{2,0},{4,2},{6,4},{1,7},{3,1},{5,3},{7,5},{8,14},{10,8},{12,... | collective-permute-start | bytes 1179656 | tf_op jit(solution)/shard_map/ppermute | solution.py:54
  857.3 62.4 %collective-permute-start.57 = (bf16[3,256,256]{2,1,0:T(8,128)(2,1)}, bf16[3,256,256]{2,1,0:T(8,128)(2,1)}, u32[]{:S(2)}, u32[]{:S(2)}) collective-permute-start(bf16[3,256,256]{2,1,0:T(8,128)(2,1)} %get-tuple-element.412), channel_id=1, source_target_pairs={{0,4},{2,6},{4,0},{6,2},{1,5},{3,7},{5,1},{7,3},{8,12},{10,14},{12... | collective-permute-start | bytes 1179656 | tf_op jit(solution)/shard_map/ppermute | solution.py:54
  859.2 60.5 %collective-permute-start.58 = (bf16[3,256,256]{2,1,0:T(8,128)(2,1)S(1)}, bf16[3,256,256]{2,1,0:T(8,128)(2,1)}, u32[]{:S(2)}, u32[]{:S(2)}) collective-permute-start(bf16[3,256,256]{2,1,0:T(8,128)(2,1)S(1)} %copy-done.51), channel_id=1, source_target_pairs={{0,2},{2,4},{4,6},{6,0},{1,3},{3,5},{5,7},{7,1},{8,10},{10,12},{12... | collective-permute-start | bytes 1179656 | tf_op jit(solution)/shard_map/ppermute | solution.py:54
  925.0 39.0 %collective-permute-start.61 = (bf16[3,256,1024]{2,1,0:T(8,128)(2,1)S(1)}, bf16[3,256,1024]{2,1,0:T(8,128)(2,1)}, u32[]{:S(2)}, u32[]{:S(2)}) collective-permute-start(bf16[3,256,1024]{2,1,0:T(8,128)(2,1)S(1)} %copy-done.12), channel_id=1, source_target_pairs={{0,1},{1,0},{2,3},{3,2},{4,5},{5,4},{6,7},{7,6},{8,9},{9,8},{10,11... | collective-permute-start | bytes 4718600 | tf_op jit(solution)/shard_map/ppermute | solution.py:49
  926.5 74.4 %collective-permute-start.60 = (bf16[3,256,1024]{2,1,0:T(8,128)(2,1)}, bf16[3,256,1024]{2,1,0:T(8,128)(2,1)}, u32[]{:S(2)}, u32[]{:S(2)}) collective-permute-start(bf16[3,256,1024]{2,1,0:T(8,128)(2,1)} %join.5.refs_3_.grad_ref), channel_id=1, source_target_pairs={{0,1},{1,0},{2,3},{3,2},{4,5},{5,4},{6,7},{7,6},{8,9},{9,8},{10,11... | collective-permute-start | bytes 4718600 | tf_op jit(solution)/shard_map/ppermute | solution.py:49
  927.1 136.0 %reduce-scatter.16.cloned.1.call-start = ((), (), s32[]{:S(2)}) async-start(), calls=%async_computation.17 | async-start | bytes 1310720 | tf_op jit(solution)/shard_map/reduce_scatter | solution.py:135
  934.5 34.1 %collective-permute-start.64 = (bf16[1,512,1024]{2,1,0:T(8,128)(2,1)}, bf16[1,512,1024]{2,1,0:T(8,128)(2,1)S(1)}, u32[]{:S(2)}, u32[]{:S(2)}) collective-permute-start(bf16[1,512,1024]{2,1,0:T(8,128)(2,1)} %grad.24), channel_id=1, source_target_pairs={{0,16},{8,24},{16,0},{24,8},{1,17},{9,25},{17,1},{25,9},{2,18},{10... | collective-permute-start | bytes 3145736 | tf_op jit(solution)/shard_map/ppermute | solution.py:45
  950.8 71.0 %collective-permute-start.68 = (bf16[1,512,2048]{2,1,0:T(8,128)(2,1)}, bf16[1,512,2048]{2,1,0:T(8,128)(2,1)}, u32[]{:S(2)}, u32[]{:S(2)}) collective-permute-start(bf16[1,512,2048]{2,1,0:T(8,128)(2,1)} %grad.25), channel_id=1, source_target_pairs={{0,16},{8,24},{16,0},{24,8},{1,17},{9,25},{17,1},{25,9},{2,18},{10... | collective-permute-start | bytes 6291464 | tf_op jit(solution)/shard_map/ppermute | solution.py:45
  1000.9 16.1 %collective-permute-start.65 = (f32[2,2048]{1,0:T(2,128)S(1)}, f32[2,2048]{1,0:T(2,128)S(1)}, u32[]{:S(2)}, u32[]{:S(2)}) collective-permute-start(f32[2,2048]{1,0:T(2,128)S(1)} %bitcast_reduce_fusion), channel_id=1, source_target_pairs={{0,1},{1,0},{2,3},{3,2},{4,5},{5,4},{6,7},{7,6},{8,9},{9,8},{10,11... | collective-permute-start | bytes 49160 | tf_op jit(solution)/shard_map/ppermute | solution.py:49
  1002.5 76.7 %reduce-scatter.18.cloned.1.call-start = ((), (), s32[]{:S(2)}) async-start(), calls=%async_computation.18 | async-start | bytes 2621440 | tf_op jit(solution)/shard_map/reduce_scatter | solution.py:135
  1030.2 16.3 %collective-permute-start.70 = (f32[37,128]{1,0:T(8,128)S(1)}, f32[37,128]{1,0:T(8,128)S(1)}, u32[]{:S(2)}, u32[]{:S(2)}) collective-permute-start(f32[37,128]{1,0:T(8,128)S(1)} %add.250), channel_id=1, source_target_pairs={{0,4},{2,6},{4,0},{6,2},{1,5},{3,7},{5,1},{7,3},{8,12},{10,14},{12... | collective-permute-start | bytes 56840 | tf_op jit(solution)/shard_map/ppermute | solution.py:1122
  1030.3 16.3 %collective-permute-start.69 = (f32[1,4,40,128]{3,2,1,0:T(8,128)S(1)}, f32[1,4,40,128]{3,2,1,0:T(8,128)S(1)}, u32[]{:S(2)}, u32[]{:S(2)}) collective-permute-start(f32[1,4,40,128]{3,2,1,0:T(8,128)S(1)} %slice.155), channel_id=1, source_target_pairs={{0,4},{2,6},{4,0},{6,2},{1,5},{3,7},{5,1},{7,3},{8,12},{10,14},{12... | collective-permute-start | bytes 245768 | tf_op jit(solution)/shard_map/ppermute | solution.py:1122
  (81 other events, 1652.3 us)
Sparse Core Ops, SparseCore 0:
  10.2 66.1 all-gather.6
  78.6 44.6 all-gather.8
  148.6 43.8 all-gather.10
  198.1 59.5 all-gather.12
  267.1 81.6 all-gather.14
  363.2 43.1 all-gather.16
  662.2 40.3 reduce-scatter.7
  717.3 59.0 reduce-scatter.9
  778.7 71.8 reduce-scatter.11
  852.9 73.3 reduce-scatter.13
  928.6 32.0 reduce-scatter.19
  1002.6 32.1 reduce-scatter.15
  1037.1 42.0 reduce-scatter.17

commit v3 on v2

--- a/solution.py
+++ b/solution.py
@@ -454,12 +454,11 @@
     slope_ref[...] = half + u * jnp.exp(-0.5 * u * u) * (1.0 / math.sqrt(2.0 * math.pi))
 
 
-def up_stage(perm, a, weights, tile=512):
+def up_stage(perm, a, weights, part, columns, tile=512):
     tokens, width = a.shape
     parts = perm.shape[0]
-    columns = weights[0].shape[1]
     tile = min(tile, columns)
-    specs = block_specs(weights, width // parts, tile, lambda n, *_: n)
+    specs = block_specs(weights, width // parts, tile, lambda n, *_: part * (columns // tile) + n)
     out = pl.BlockSpec((tokens, tile), lambda n, *_: (0, n))
     return pl.pallas_call(
         partial(up_kernel, parts=parts),
@@ -524,16 +523,16 @@
         out_ref[:, at] = total.astype(out_ref.dtype)
 
 
-def to_width(lefts, weights, width, added=(), dtype=BF16):
+def to_width(lefts, weights, width, added=(), dtype=BF16, across=(0,)):
     parts = len(weights[0])
     block = width // parts
     tile = min(block, 256)
     tokens = lefts[0].shape[0]
     left_specs, specs, arrays = [], [], []
-    for left, weight in zip(lefts, weights):
+    for left, weight, at in zip(lefts, weights, across):
         columns = left.shape[1]
         left_specs.append(pl.BlockSpec((tokens, columns), lambda n: (0, 0)))
-        specs += [pl.BlockSpec((tile, columns), lambda n: (n, 0))] * parts
+        specs += [pl.BlockSpec((tile, columns), lambda n, at=at: (n, at))] * parts
         arrays += weight
     whole = pl.BlockSpec((tokens, width), lambda n: (0, 0))
     return pl.pallas_call(
@@ -911,7 +910,7 @@
 
     half = hidden // 2
     ctx_qkv = gather_ctx(jnp.concatenate([w_query, w_key, w_value], axis=1))
-    ctx_up = [gather_ctx(shard_part(w_up, 0, half, False))]
+    ctx_both = gather_ctx(jnp.concatenate([w_up, w_proj.T], axis=1))
 
     order = Order()
     Pace.value = FORWARD_PACE
@@ -935,11 +934,8 @@
         return [over_fsdp(p, 1) for p in parts]
 
     near_qkv = cross(order.wait(ctx_qkv))
-    ctx_up.append(gather_ctx(order.keep(shard_part(order(w_up), 1, half, False))))
     far_qkv = to_core(near_qkv[:1])
     other = [over_tp(near_qkv[0])]
-    near_up = [cross(order.wait(ctx_up[0]))]
-    ctx_proj = gather_ctx(order.keep(shard_part(order(w_proj), 0, heads_width, True)))
     far_qkv = order.wait(far_qkv)
     other = order.wait(other)
     near_qkv = order.wait(near_qkv)
@@ -948,25 +944,25 @@
     pieces = to_heads(
         order.keep(to_chunks(target, perm, order(normed_in), blocks_qkv, tables_here, 2))
     )
-    near_up.append(cross(order.wait(ctx_up[1])))
-    ctx_down = [gather_ctx(order.keep(shard_part(order(w_down), 0, half, True)))]
+    other = other + [over_tp(p) for p in near_qkv[1:]]
+    near_both = cross(order.wait(ctx_both))
     pieces = order.wait(pieces)
-    near_up = order.wait(near_up)
-    far_up = [to_core(order(near)) for near in near_up]
-    near_proj = cross(order.wait(ctx_proj))
-    outs = order.keep(attend(source, lengths, order(pieces)))
-    far_up = order.wait(far_up)
-    outs = to_slots(order(outs))
-    ctx_down.append(gather_ctx(order.keep(shard_part(order(w_down), 1, half, True))))
+    other = order.wait(other)
+    outs = to_slots(order.keep(attend(source, lengths, order(pieces))))
+    ctx_down = [
+        gather_ctx(order.keep(shard_part(order(w_down), n, half, True))) for n in range(2)
+    ]
     outs = order.wait(outs)
     attended = order.keep(join(target, order(outs)))[0]
-    near_proj = order.wait(near_proj)
+    near_both = order.wait(near_both)
+    near_proj = order.wait([b[:, hidden:] for b in near_both])
     blocks_proj = near_proj + order.wait(to_core(near_proj))
     branch_mine = order.keep(to_width([order(attended)], [blocks_proj], width))
     branch_theirs = over_tp(branch_mine)
     near_down = [cross(order.wait(ctx_down[0]))]
+    blocks_up = near_both + order.wait(to_core(order(near_both)))
+    near_down.append(cross(order.wait(ctx_down[1])))
     branch_theirs = order.wait(branch_theirs)
-    blocks_up = [near + far for near, far in zip(near_up, far_up)]
     residual = streams[STREAMS - 1] + tp_sum(branch_mine, branch_theirs)
 
     def far_half(values):
@@ -974,15 +970,13 @@
 
     normed = layer_norm(residual, gain_second, shift_second).astype(BF16)
     normed = order.wait(normed)
-    near_down.append(cross(order.wait(ctx_down[1])))
     near_down[0] = order.wait(near_down[0])
     far_down = [to_core(near_down[0])]
     active, slope = [], []
-    for w in blocks_up:
-        a, b = order.keep(up_stage(perm, order(normed), w))
+    for n in range(2):
+        a, b = order.keep(up_stage(perm, order(normed), blocks_up, n, half))
         active.append(a)
         slope.append(b)
-    other = other + [over_tp(p) for p in order(near_qkv[1:])]
     far_down[0] = order.wait(far_down[0])
     down_first = order.keep(
         to_width([order(active[0])], [near_down[0] + far_down[0]], width, (), F32)
@@ -990,7 +984,6 @@
     near_down[1] = order.wait(near_down[1])
     far_down.append(order.wait(to_core(near_down[1])))
     blocks_down = [near + far for near, far in zip(near_down, far_down)]
-    other = order.wait(other)
     down_mine = order.keep(
         to_width([order(active[1])], blocks_down[1:], width, (down_first,))
     )
@@ -1027,7 +1020,7 @@
             order.keep(up_back(perm, order(grad_down_b), slope[n], blocks_down[n], 0))
         )
         upward_far.append(over_fsdp(grad_upward[n], 1))
-    normed_mine = order.keep(to_width(order(grad_upward), blocks_up, width))
+    normed_mine = order.keep(to_width(order(grad_upward), [blocks_up] * 2, width, (), BF16, (0, 1)))
     normed_theirs = over_tp(normed_mine)
     grad_down = [scatter_ctx(down[0].finish())]
     upward_far = order.wait(upward_far)
@@ -1070,18 +1063,19 @@
     )
     grad_down[0] = order.wait(grad_down[0])
     mine, theirs, own = [], [], []
-    grad_up.append(scatter_ctx(up[1].finish()))
     sent[0] = order.wait(sent[0])
     mine.append(order.keep(join(target, sent[0])))
     theirs.append(over_tp(mine[0]))
     sent.append(to_slots(order(back[1])))
     own.append(order.keep(own_part(perm, order(mine[0]), streams, blocks_qkv, 0)))
     grad_down[1] = order.wait(grad_down[1])
-    grad_proj = scatter_ctx(proj.finish())
     sent[1] = order.wait(sent[1])
     mine.append(order.keep(join(target, sent[1])))
     theirs.append(over_tp(mine[1]))
-    mine_far = order.wait([over_fsdp(m, 1) for m in order(mine)])
+    mine_far = [over_fsdp(m, 1) for m in order(mine)]
+    grad_proj = scatter_ctx(proj.finish())
+    grad_up.append(scatter_ctx(up[1].finish()))
+    mine_far = order.wait(mine_far)
     qkv = Scatter(order, normed_in, mine, normed_in_far, mine_far)
     qkv.launch(0, 1)
     qkv.launch(1, 2)
@@ -1096,7 +1090,10 @@
     done = order.keep(
         last_stage(perm, inputs, coeff, order(dz), grad_branch_b, 0, rows, ())
     )
+    grad_proj = order.wait(grad_proj)
     theirs[1] = order.wait(theirs[1])
+    grad_rest = scatter_ctx(qkv.finish(1, 2))
+    Pace.value = FORWARD_PACE
     sums_far = over_tp(order(sums))
     dz = order.keep(other_part(order(theirs[1]), own[1][0], streams, gain_first, other, 1))
     sums_far = order.wait(sums_far)
@@ -1124,7 +1121,6 @@
     ]
     fsdp_steps = [(lambda v, bit=bit: over_fsdp(v, bit)) for bit in reversed(bits_of(fsdp))]
     moving = fold(packed, tail, ctx_steps[0])
-    grad_rest = scatter_ctx(qkv.finish(1, 2))
     grad_up[1] = order.wait(grad_up[1])
     for step in ctx_steps[1:]:
         moving = fold(*landed(*moving), step)
@@ -1133,7 +1129,6 @@
     )
     packed, tail = landed(*moving)
     moving = fold(packed[0], tail, fsdp_steps[0])
-    grad_proj = order.wait(grad_proj)
     for step in fsdp_steps[1:]:
         moving = fold(*landed(*moving), step)
     packed, tail = landed(*moving)

time: 1100 us -> 1000 us (0.909)
  waiting for transfers between devices: 519 us -> 425 us
    ppermute x8, waiting for transfers between devices: 160 us -> 124 us  [over_tp(): return lax.ppermute(values, 'tp', xor_pairs(lax.axis_size('tp'), 1))]
    all_gather x6 -> x4, waiting for transfers between devices: 74.3 us -> 41.2 us  [gather_ctx(): return lax.all_gather(shard, 'ctx', axis=0, tiled=True)]
    ppermute x18, waiting for transfers between devices: 178 us -> 158 us  [shift_ctx(): lax.ppermute(values, 'ctx', [(i, (i + step) % size) for i in range(size)])]
    reduce_scatter x7, waiting for transfers between devices: 14.4 us -> 0.05 us  [scatter_ctx(): lax.psum_scatter(total, 'ctx', scatter_dimension=0, tiled=True).astype(F32)]
    ppermute x45 -> x41, starting transfers between devices: 35.1 us -> 20.8 us  [over_fsdp(): return lax.ppermute(values, 'fsdp', xor_pairs(lax.axis_size('fsdp'), mask))]
    ppermute x45 -> x41, waiting for transfers between devices: 90.7 us -> 91.1 us  [over_fsdp(): return lax.ppermute(values, 'fsdp', xor_pairs(lax.axis_size('fsdp'), mask))]
  transfers between devices with their start and end apart: 88 -> 82, of which waited for: 31 -> 32; matrix products, arithmetic and copies ran while one was open for 6% -> 8% of each run, Pallas kernels for 32% -> 34%
where the time goes in v3:
time: 1000 us; the launch traced here: 993 us
  waiting for transfers between devices  425 us (42%)
  Pallas kernels  347 us (35%)
  starting transfers between devices  85.1 us (9%)
  other arithmetic  57.2 us (6%)
  local copies, waits for them, and re-layouts  43 us (4%)
  between operations  25.7 us (3%)
    ppermute x18, waiting for transfers between devices, shift_ctx(): lax.ppermute(values, 'ctx', [(i, (i + step) % size) for i in range(size)])  158 us
    ppermute x8, waiting for transfers between devices, over_tp(): return lax.ppermute(values, 'tp', xor_pairs(lax.axis_size('tp'), 1))  124 us
    ppermute x41, waiting for transfers between devices, over_fsdp(): return lax.ppermute(values, 'fsdp', xor_pairs(lax.axis_size('fsdp'), mask))  91.1 us
    pallas_call x14, Pallas kernels, grad_blocks(): pl.pallas_call(partial(grad_kernel, count=len(chosen), rights=len(near),...  82.3 us
    ppermute x18, starting transfers between devices, shift_ctx(): lax.ppermute(values, 'ctx', [(i, (i + step) % size) for i in range(size)])  48.1 us
    pallas_call x4, Pallas kernels, to_width(): pl.pallas_call(partial(back_kernel, lefts=len(lefts), parts=parts, adds=l...  44.2 us
    all_gather x4, waiting for transfers between devices, gather_ctx(): return lax.all_gather(shard, 'ctx', axis=0, tiled=True)  41.2 us
    pallas_call x2, Pallas kernels, other_part(): pl.pallas_call(partial(other_kernel, parts=parts), name='other', grid=(ki...  28.8 us
  transfers between devices with their start and end apart: 82, of which 32 were waited for; matrix products, arithmetic and copies ran while one was open for 8% of the time, Pallas kernels for 34%

profile of v3, /device:TPU:0, one launch (start us, length us, event | category | flops | bytes accessed | tf_op | source)
XLA Modules:
  0.0 992.5 jit_solution(8585674429261931299)
XLA Ops:
  44.2 20.9 %mix.1 = (bf16[3,512,2048]{2,1,0:T(8,128)(2,1)}, f32[4,512,2048]{2,1,0:T(8,128)}) custom-call(s32[4]{0:T(128)} %get-tuple-element.548.perm_ref, bf16[8,512,2048]{2,1,0:T(8,128)(2,1)} %bitcast.140, f32[16,256,4]{2,1,0:T(8,128)} %bitcast.147, f32[1,2048]{1,0:T(1,128)} %bitcast.185, f32[1,2048]{1,0:T(1,128)} %bitcast.195), custom_call_target="tpu_custom_call" | custom-call | flops 420000000 | bytes 1024 | tf_op jit(solution)/shard_map/mix/pallas_call | solution.py:182
  65.1 11.3 %all-gather.5.cloned.1.call-done.refs_0_ = bf16[512,3072]{1,0:T(8,128)(2,1)} async-done(((bf16[128,3072]{1,0:T(8,128)(2,1)}), bf16[512,3072]{1,0:T(8,128)(2,1)}) %all-gather.5.cloned.1.call-update) | async-done | bytes 3145744 | tf_op jit(solution)/shard_map/all_gather | solution.py:88
  82.3 65.0 %collective-permute-done.8.refs_0_ = bf16[512,3072]{1,0:T(8,128)(2,1)} collective-permute-done((bf16[512,3072]{1,0:T(8,128)(2,1)}, bf16[512,3072]{1,0:T(8,128)(2,1)}, u32[]{:S(2)}, u32[]{:S(2)}) %collective-permute-start.8) | collective-permute-done | bytes 3145760 | tf_op jit(solution)/shard_map/ppermute | solution.py:49
  149.5 4.7 collective-permute-done.9.refs_3_
  154.1 18.6 %heads.2 = (bf16[3,512,256]{2,1,0:T(8,128)(2,1)}, bf16[3,512,256]{2,1,0:T(8,128)(2,1)}, bf16[3,512,256]{2,1,0:T(8,128)(2,1)}, bf16[3,512,256]{2,1,0:T(8,128)(2,1)}) custom-call(s32[4]{0:T(128)} %and_select_fusion.target_ref, s32[4]{0:T(128)} %get-tuple-element.548.perm_ref, bf16[3,512,2048]{2,1,0:T(8,128)(2,1)} %get-tuple-element.245.a_ref.refs_0_, ...), custom_call_target="tpu_custom_call" | custom-call | flops 720000000 | bytes 1024 | tf_op jit(solution)/shard_map/heads/pallas_call | solution.py:261
  180.8 18.5 %collective-permute-done.10.refs_1_ = bf16[3,512,256]{2,1,0:T(8,128)(2,1)S(1)} collective-permute-done((bf16[3,512,256]{2,1,0:T(8,128)(2,1)}, bf16[3,512,256]{2,1,0:T(8,128)(2,1)S(1)}, u32[]{:S(2)}, u32[]{:S(2)}) %collective-permute-start.10) | collective-permute-done | bytes 786464 | tf_op jit(solution)/shard_map/ppermute | solution.py:54
  199.3 32.5 %collective-permute-done.11.refs_2_ = bf16[3,512,256]{2,1,0:T(8,128)(2,1)S(1)} collective-permute-done((bf16[3,512,256]{2,1,0:T(8,128)(2,1)}, bf16[3,512,256]{2,1,0:T(8,128)(2,1)S(1)}, u32[]{:S(2)}, u32[]{:S(2)}) %collective-permute-start.11) | collective-permute-done | bytes 786464 | tf_op jit(solution)/shard_map/ppermute | solution.py:54
  233.0 11.5 %attend.1 = (bf16[1,512,256]{2,1,0:T(8,128)(2,1)}, bf16[1,512,256]{2,1,0:T(8,128)(2,1)}, bf16[1,512,256]{2,1,0:T(8,128)(2,1)}, bf16[1,512,256]{2,1,0:T(8,128)(2,1)}) custom-call(s32[4]{0:T(128)} %copy-done.48, s32[2]{0:T(128)} %length_ref.5, bf16[3,512,256]{2,1,0:T(8,128)(2,1)} %get-tuple-element.257.refs_0_, bf16[3,512,256]{2,1,0:T(8,128)(2,1)} %copy-done.30, ...), custom_call_target="tpu_custom_call" | custom-call | flops 360000000 | bytes 1024 | tf_op jit(solution)/shard_map/attend/pallas_call | solution.py:367
  246.6 16.4 %collective-permute-start.14 = (bf16[1,512,256]{2,1,0:T(8,128)(2,1)}, bf16[1,512,256]{2,1,0:T(8,128)(2,1)S(1)}, u32[]{:S(2)}, u32[]{:S(2)}) collective-permute-start(bf16[1,512,256]{2,1,0:T(8,128)(2,1)} %get-tuple-element.262), channel_id=1, source_target_pairs={{0,6},{2,0},{4,2},{6,4},{1,7},{3,1},{5,3},{7,5},{8,14},{10,8},{12,... | collective-permute-start | bytes 786440 | tf_op jit(solution)/shard_map/ppermute | solution.py:54
  266.3 5.8 collective-permute-done.14.refs_1_
  272.1 38.5 %collective-permute-done.15.refs_2_ = bf16[1,512,256]{2,1,0:T(8,128)(2,1)S(1)} collective-permute-done((bf16[1,512,256]{2,1,0:T(8,128)(2,1)}, bf16[1,512,256]{2,1,0:T(8,128)(2,1)S(1)}, u32[]{:S(2)}, u32[]{:S(2)}) %collective-permute-start.15) | collective-permute-done | bytes 262176 | tf_op jit(solution)/shard_map/ppermute | solution.py:54
  323.8 6.1 to_width.4
  332.8 6.1 collective-permute-done.21.refs_2_.refs_4_.refs_8_
  338.9 7.5 collective-permute-done.22.refs_3_.refs_5_.refs_9_
  346.4 27.3 %all-gather.9.cloned.1.call-done.refs_1_.refs_0_ = bf16[512,2048]{1,0:T(8,128)(2,1)} async-done(((bf16[128,2048]{1,0:T(8,128)(2,1)}), bf16[512,2048]{1,0:T(8,128)(2,1)}) %all-gather.9.cloned.1.call-update) | async-done | bytes 2097168 | tf_op jit(solution)/shard_map/all_gather | solution.py:88
  373.7 5.1 collective-permute-done.20
  378.8 4.2 fusion.38
  387.7 11.2 %up.2 = (bf16[512,2048]{1,0:T(8,128)(2,1)}, f32[512,2048]{1,0:T(8,128)}) custom-call(s32[4]{0:T(128)} %get-tuple-element.548.perm_ref, bf16[512,2048]{1,0:T(8,128)(2,1)} %add_convert_fusion.1.a_ref, bf16[512,5120]{1,0:T(8,128)(2,1)} %all-gather.7.cloned.1.call-done.refs_0_.refs_2_.refs_6_, bf16[512,5120]{1,0:T(8,128)(2,1)} %collective-permute-done.17.refs_1_.refs_3_.refs_7_, ...), custom_call_target="tpu_custom_call" | custom-call | flops 307200000 | bytes 1024 | tf_op jit(solution)/shard_map/up/pallas_call | solution.py:463
  398.9 11.2 %up.3 = (bf16[512,2048]{1,0:T(8,128)(2,1)}, f32[512,2048]{1,0:T(8,128)}) custom-call(s32[4]{0:T(128)} %get-tuple-element.548.perm_ref, bf16[512,2048]{1,0:T(8,128)(2,1)} %add_convert_fusion.1.a_ref, bf16[512,5120]{1,0:T(8,128)(2,1)} %all-gather.7.cloned.1.call-done.refs_0_.refs_2_.refs_6_, bf16[512,5120]{1,0:T(8,128)(2,1)} %collective-permute-done.17.refs_1_.refs_3_.refs_7_, ...), custom_call_target="tpu_custom_call" | custom-call | flops 307200000 | bytes 1024 | tf_op jit(solution)/shard_map/up/pallas_call | solution.py:463
  411.4 10.3 %to_width.5.refs_5_ = f32[512,2048]{1,0:T(8,128)} custom-call(bf16[512,2048]{1,0:T(8,128)(2,1)} %get-tuple-element.306.refs_0_, bf16[512,2048]{1,0:T(8,128)(2,1)} %all-gather.11.cloned.1.call-done.refs_1_.refs_0_, bf16[512,2048]{1,0:T(8,128)(2,1)} %copy-done.25, bf16[512,2048]{1,0:T(8,128)(2,1)} %copy-done.26, ...), custom_call_target="tpu_custom_call" | custom-call | flops 240000000 | bytes 1024 | tf_op jit(solution)/shard_map/to_width/pallas_call | solution.py:538
  421.7 13.3 %collective-permute-done.24.refs_2_.refs_1_ = bf16[512,2048]{1,0:T(8,128)(2,1)} collective-permute-done((bf16[512,2048]{1,0:T(8,128)(2,1)}, bf16[512,2048]{1,0:T(8,128)(2,1)}, u32[]{:S(2)}, u32[]{:S(2)}) %collective-permute-start.24) | collective-permute-done | bytes 2097184 | tf_op jit(solution)/shard_map/ppermute | solution.py:45
  442.6 11.1 %to_width.6 = bf16[512,2048]{1,0:T(8,128)(2,1)} custom-call(bf16[512,2048]{1,0:T(8,128)(2,1)} %get-tuple-element.307.refs_0_, bf16[512,2048]{1,0:T(8,128)(2,1)} %all-gather.9.cloned.1.call-done.refs_1_.refs_0_, bf16[512,2048]{1,0:T(8,128)(2,1)} %collective-permute-done.24.refs_2_.refs_1_, bf16[512,2048]{1,0:T(8,128)(2,1)} %collective-permute-done.27.refs_3_.refs_2_, ...), custom_call_target="tpu_custom_call" | custom-call | flops 240000000 | bytes 1024 | tf_op jit(solution)/shard_map/to_width/pallas_call | solution.py:538
  459.7 4.6 collective-permute-done.36
  468.6 7.7 collective-permute-done.33
  476.3 30.0 %collective-permute-done.29 = bf16[512,2048]{1,0:T(8,128)(2,1)} collective-permute-done((bf16[512,2048]{1,0:T(8,128)(2,1)}, bf16[512,2048]{1,0:T(8,128)(2,1)}, u32[]{:S(2)}, u32[]{:S(2)}) %collective-permute-start.29) | collective-permute-done | bytes 2097184 | tf_op jit(solution)/shard_map/ppermute | solution.py:49
  506.3 6.1 fusion.37
  525.2 6.1 grad.14
  531.8 6.1 grad.15
  537.9 10.4 %up_back.2.refs_0_ = bf16[512,2048]{1,0:T(8,128)(2,1)} custom-call(s32[4]{0:T(128)} %get-tuple-element.548.perm_ref, bf16[512,2048]{1,0:T(8,128)(2,1)} %copy-done.16, f32[512,2048]{1,0:T(8,128)} %get-tuple-element.294.slope_ref, bf16[512,2048]{1,0:T(8,128)(2,1)} %all-gather.11.cloned.1.call-done.refs_1_.refs_0_, bf16[512,2048]{1,0:T(8,128)(2,1)} %copy-done.25, ...), custom_call_target="tpu_custom_call" | custom-call | flops 15360000000 | bytes 1024 | tf_op jit(solution)/shard_map/up_back/pallas_call | solution.py:495
  548.3 10.4 %up_back.3.refs_1_ = bf16[512,2048]{1,0:T(8,128)(2,1)} custom-call(s32[4]{0:T(128)} %get-tuple-element.548.perm_ref, bf16[512,2048]{1,0:T(8,128)(2,1)} %copy-done.16, f32[512,2048]{1,0:T(8,128)} %get-tuple-element.297.slope_ref, bf16[512,2048]{1,0:T(8,128)(2,1)} %all-gather.9.cloned.1.call-done.refs_1_.refs_0_, ...), custom_call_target="tpu_custom_call" | custom-call | flops 15360000000 | bytes 1024 | tf_op jit(solution)/shard_map/up_back/pallas_call | solution.py:495
  559.3 16.7 %to_width.7 = bf16[512,2048]{1,0:T(8,128)(2,1)} custom-call(bf16[512,2048]{1,0:T(8,128)(2,1)} %up_back.2.refs_0_, bf16[512,2048]{1,0:T(8,128)(2,1)} %up_back.3.refs_1_, bf16[512,5120]{1,0:T(8,128)(2,1)} %all-gather.7.cloned.1.call-done.refs_0_.refs_2_.refs_6_, bf16[512,5120]{1,0:T(8,128)(2,1)} %collective-permute-done.17.refs_1_.refs_3_.refs_7_, ...), custom_call_target="tpu_custom_call" | custom-call | flops 24000000000 | bytes 1024 | tf_op jit(solution)/shard_map/to_width/pallas_call | solution.py:538
  586.9 6.6 grad.16
  593.7 7.1 grad.17
  600.8 23.1 %collective-permute-done.41 = bf16[512,2048]{1,0:T(8,128)(2,1)} collective-permute-done((bf16[512,2048]{1,0:T(8,128)(2,1)}, bf16[512,2048]{1,0:T(8,128)(2,1)}, u32[]{:S(2)}, u32[]{:S(2)}) %collective-permute-start.41) | collective-permute-done | bytes 2097184 | tf_op jit(solution)/shard_map/ppermute | solution.py:49
  623.9 4.1 multiply_reduce_fusion
  634.8 7.5 heads.3
  642.3 7.0 grad.18
  649.6 3.7 collective-permute-start.44
  653.3 6.3 grad.19
  660.3 3.9 grad.20
  664.2 17.7 %collective-permute-done.47.refs_4_ = bf16[1,512,2048]{2,1,0:T(8,128)(2,1)} collective-permute-done((bf16[1,512,2048]{2,1,0:T(8,128)(2,1)S(1)}, bf16[1,512,2048]{2,1,0:T(8,128)(2,1)}, u32[]{:S(2)}, u32[]{:S(2)}) %collective-permute-start.47) | collective-permute-done | bytes 2097184 | tf_op jit(solution)/shard_map/ppermute | solution.py:45
  681.9 6.7 grad.21
  691.7 11.3 %attend_back.2 = (bf16[3,256,256]{2,1,0:T(8,128)(2,1)}, bf16[3,256,256]{2,1,0:T(8,128)(2,1)}, bf16[3,256,256]{2,1,0:T(8,128)(2,1)}, bf16[3,256,256]{2,1,0:T(8,128)(2,1)}) custom-call(s32[4]{0:T(128)} %copy-done.48, s32[2]{0:T(128)} %length_ref.5, bf16[3,512,256]{2,1,0:T(8,128)(2,1)} %get-tuple-element.257.refs_0_, bf16[3,512,256]{2,1,0:T(8,128)(2,1)} %copy-done.30, ...), custom_call_target="tpu_custom_call" | custom-call | flops 17999998976 | bytes 1024 | tf_op jit(solution)/shard_map/attend_back/pallas_call | solution.py:430
  703.0 5.1 collective-permute-start.48
  708.1 8.4 collective-permute-start.49
  717.0 11.3 %attend_back.3 = (bf16[3,256,256]{2,1,0:T(8,128)(2,1)}, bf16[3,256,256]{2,1,0:T(8,128)(2,1)}, bf16[3,256,256]{2,1,0:T(8,128)(2,1)}, bf16[3,256,256]{2,1,0:T(8,128)(2,1)}) custom-call(s32[4]{0:T(128)} %copy-done.48, s32[2]{0:T(128)} %length_ref.5, bf16[3,512,256]{2,1,0:T(8,128)(2,1)} %get-tuple-element.257.refs_0_, bf16[3,512,256]{2,1,0:T(8,128)(2,1)} %copy-done.30, ...), custom_call_target="tpu_custom_call" | custom-call | flops 17999998976 | bytes 1024 | tf_op jit(solution)/shard_map/attend_back/pallas_call | solution.py:430
  730.5 57.4 %collective-permute-done.49.refs_2_ = bf16[3,256,256]{2,1,0:T(8,128)(2,1)S(1)} collective-permute-done((bf16[3,256,256]{2,1,0:T(8,128)(2,1)}, bf16[3,256,256]{2,1,0:T(8,128)(2,1)S(1)}, u32[]{:S(2)}, u32[]{:S(2)}) %collective-permute-start.49) | collective-permute-done | bytes 393248 | tf_op jit(solution)/shard_map/ppermute | solution.py:54
  789.5 3.8 join.4.grad_ref.refs_2_
  795.4 12.9 %own.2 = (f32[3,256,2048]{2,1,0:T(8,128)}, f32[3,16,2048]{2,1,0:T(8,128)}) custom-call(s32[4]{0:T(128)} %get-tuple-element.548.perm_ref, bf16[3,256,1024]{2,1,0:T(8,128)(2,1)} %join.4.grad_ref.refs_2_, f32[4,512,2048]{2,1,0:T(8,128)} %get-tuple-element.230.z_ref, bf16[512,3072]{1,0:T(8,128)(2,1)} %all-gather.5.cloned.1.call-done.refs_0_, ...), custom_call_target="tpu_custom_call" | custom-call | flops 17999998976 | bytes 1024 | tf_op jit(solution)/shard_map/own/pallas_call | solution.py:662
  810.4 5.6 collective-permute-done.52.refs_2_
  817.5 3.9 join.5.refs_3_.grad_ref
  821.4 4.3 grad.22
  828.4 6.7 grad.23
  837.6 4.0 grad.24
  842.0 6.3 grad.25
  849.9 13.2 %own.3 = (f32[3,256,2048]{2,1,0:T(8,128)}, f32[3,16,2048]{2,1,0:T(8,128)}) custom-call(s32[4]{0:T(128)} %get-tuple-element.548.perm_ref, bf16[3,256,1024]{2,1,0:T(8,128)(2,1)} %join.5.refs_3_.grad_ref, f32[4,512,2048]{2,1,0:T(8,128)} %get-tuple-element.230.z_ref, bf16[512,3072]{1,0:T(8,128)(2,1)} %all-gather.5.cloned.1.call-done.refs_0_, ...), custom_call_target="tpu_custom_call" | custom-call | flops 17999998976 | bytes 1024 | tf_op jit(solution)/shard_map/own/pallas_call | solution.py:662
  867.9 4.2 grad.26
  872.2 14.3 %other.2.dz_ref = bf16[3,256,2048]{2,1,0:T(8,128)(2,1)} custom-call(bf16[3,256,1024]{2,1,0:T(8,128)(2,1)} %collective-permute-done.56.grad_ref, f32[3,256,2048]{2,1,0:T(8,128)} %get-tuple-element.383.part_ref, f32[4,512,2048]{2,1,0:T(8,128)} %get-tuple-element.230.z_ref, f32[1,2048]{1,0:T(1,128)} %bitcast.186, ...), custom_call_target="tpu_custom_call" | custom-call | flops 20999999488 | bytes 1024 | tf_op jit(solution)/shard_map/other/pallas_call | solution.py:711
  886.5 13.0 %last.2 = (bf16[8,512,2048]{2,1,0:T(8,128)(2,1)}, f32[16,256,128]{2,1,0:T(8,128)}) custom-call(s32[4]{0:T(128)} %get-tuple-element.548.perm_ref, bf16[8,512,2048]{2,1,0:T(8,128)(2,1)} %bitcast.141, f32[16,256,4]{2,1,0:T(8,128)} %bitcast.148, bf16[3,256,2048]{2,1,0:T(8,128)(2,1)} %other.2.dz_ref, bf16[512,2048]{1,0:T(8,128)(2,1)} %copy-done.8), custom_call_target="tpu_custom_call" | custom-call | flops 17999998976 | bytes 1024 | tf_op jit(solution)/shard_map/last/pallas_call | solution.py:767
  899.5 11.9 %collective-permute-done.61.refs_6_ = bf16[1,512,2048]{2,1,0:T(8,128)(2,1)} collective-permute-done((bf16[1,512,2048]{2,1,0:T(8,128)(2,1)}, bf16[1,512,2048]{2,1,0:T(8,128)(2,1)}, u32[]{:S(2)}, u32[]{:S(2)}) %collective-permute-start.61) | collective-permute-done | bytes 2097184 | tf_op jit(solution)/shard_map/ppermute | solution.py:45
  911.5 6.9 grad.27
  920.1 14.5 %other.3.dz_ref = bf16[3,256,2048]{2,1,0:T(8,128)(2,1)} custom-call(bf16[3,256,1024]{2,1,0:T(8,128)(2,1)} %collective-permute-done.54.grad_ref, f32[3,256,2048]{2,1,0:T(8,128)} %get-tuple-element.408.part_ref, f32[4,512,2048]{2,1,0:T(8,128)} %get-tuple-element.230.z_ref, f32[1,2048]{1,0:T(1,128)} %bitcast.187, ...), custom_call_target="tpu_custom_call" | custom-call | flops 420000000 | bytes 1024 | tf_op jit(solution)/shard_map/other/pallas_call | solution.py:711
  939.4 10.7 %collective-permute-done.64 = f32[37,128]{1,0:T(8,128)S(1)} collective-permute-done((f32[37,128]{1,0:T(8,128)S(1)}, f32[37,128]{1,0:T(8,128)S(1)}, u32[]{:S(2)}, u32[]{:S(2)}) %collective-permute-start.64) | collective-permute-done | bytes 18976 | tf_op jit(solution)/shard_map/ppermute | solution.py:1119
  953.2 13.0 %last.3 = (bf16[8,512,2048]{2,1,0:T(8,128)(2,1)}, f32[16,256,128]{2,1,0:T(8,128)}) custom-call(s32[4]{0:T(128)} %get-tuple-element.548.perm_ref, bf16[8,512,2048]{2,1,0:T(8,128)(2,1)} %bitcast.142, f32[16,256,4]{2,1,0:T(8,128)} %bitcast.149, bf16[3,256,2048]{2,1,0:T(8,128)(2,1)} %other.3.dz_ref, ...), custom_call_target="tpu_custom_call", output_to_operand_aliasing={{0}: (5, {}), {1}: (6, {})} | custom-call | flops 360000000 | bytes 1024 | tf_op jit(solution)/shard_map/last/pallas_call | solution.py:767
  (409 shorter events, 175.0 us)
Async XLA Ops:
  7.2 69.2 %all-gather.5.cloned.1.call-start = ((), (), s32[]{:S(2)}) async-start(), calls=%async_computation.7 | async-start | bytes 3932160 | tf_op jit(solution)/shard_map/all_gather | solution.py:88
  9.3 166.0 %all-gather.7.cloned.1.call-start = ((), (), s32[]{:S(2)}) async-start(), calls=%async_computation.8 | async-start | bytes 6553600 | tf_op jit(solution)/shard_map/all_gather | solution.py:88
  10.8 23.3 %collective-permute-start = (bf16[40,128]{1,0:T(8,128)(2,1)S(1)}, bf16[40,128]{1,0:T(8,128)(2,1)S(1)}, u32[]{:S(2)}, u32[]{:S(2)}) collective-permute-start(bf16[40,128]{1,0:T(8,128)(2,1)S(1)} %concatenate.54), channel_id=1, source_target_pairs={{0,2},{2,4},{4,6},{6,0},{1,3},{3,5},{5,7},{7,1},{8,10},{10,12},{12... | collective-permute-start | bytes 30728 | tf_op jit(solution)/shard_map/ppermute | solution.py:54
  13.9 20.2 %collective-permute-start.1 = (bf16[40,128]{1,0:T(8,128)(2,1)S(1)}, bf16[40,128]{1,0:T(8,128)(2,1)S(1)}, u32[]{:S(2)}, u32[]{:S(2)}) collective-permute-start(bf16[40,128]{1,0:T(8,128)(2,1)S(1)} %concatenate.54), channel_id=1, source_target_pairs={{0,4},{2,6},{4,0},{6,2},{1,5},{3,7},{5,1},{7,3},{8,12},{10,14},{12... | collective-permute-start | bytes 30728 | tf_op jit(solution)/shard_map/ppermute | solution.py:54
  16.5 17.7 %collective-permute-start.2 = (bf16[40,128]{1,0:T(8,128)(2,1)S(1)}, bf16[40,128]{1,0:T(8,128)(2,1)S(1)}, u32[]{:S(2)}, u32[]{:S(2)}) collective-permute-start(bf16[40,128]{1,0:T(8,128)(2,1)S(1)} %concatenate.54), channel_id=1, source_target_pairs={{0,6},{2,0},{4,2},{6,4},{1,7},{3,1},{5,3},{7,5},{8,14},{10,8},{12,... | collective-permute-start | bytes 30728 | tf_op jit(solution)/shard_map/ppermute | solution.py:54
  21.4 308.5 %all-gather.11.cloned.1.call-start = ((), (), s32[]{:S(2)}) async-start(), calls=%async_computation.10 | async-start | bytes 2621440 | tf_op jit(solution)/shard_map/all_gather | solution.py:88
  76.4 70.8 %collective-permute-start.8 = (bf16[512,3072]{1,0:T(8,128)(2,1)}, bf16[512,3072]{1,0:T(8,128)(2,1)}, u32[]{:S(2)}, u32[]{:S(2)}) collective-permute-start(bf16[512,3072]{1,0:T(8,128)(2,1)} %all-gather.5.cloned.1.call-done.refs_0_), channel_id=1, source_target_pairs={{0,1},{1,0},{2,3},{3,2},{4,5},{5,4},{6,7},{7,6},{8,9},{9,8},{10,11... | collective-permute-start | bytes 9437192 | tf_op jit(solution)/shard_map/ppermute | solution.py:49
  77.9 70.4 %collective-permute-start.7 = (bf16[512,3072]{1,0:T(8,128)(2,1)}, bf16[512,3072]{1,0:T(8,128)(2,1)S(1)}, u32[]{:S(2)}, u32[]{:S(2)}) collective-permute-start(bf16[512,3072]{1,0:T(8,128)(2,1)} %all-gather.5.cloned.1.call-done.refs_0_), channel_id=1, source_target_pairs={{0,16},{8,24},{16,0},{24,8},{1,17},{9,25},{17,1},{25,9},{2,18},{10... | collective-permute-start | bytes 9437192 | tf_op jit(solution)/shard_map/ppermute | solution.py:45
  148.9 82.9 %collective-permute-start.13 = (bf16[512,3072]{1,0:T(8,128)(2,1)S(1)}, bf16[512,3072]{1,0:T(8,128)(2,1)}, u32[]{:S(2)}, u32[]{:S(2)}) collective-permute-start(bf16[512,3072]{1,0:T(8,128)(2,1)S(1)} %collective-permute-done.7.refs_1_), channel_id=1, source_target_pairs={{0,1},{1,0},{2,3},{3,2},{4,5},{5,4},{6,7},{7,6},{8,9},{9,8},{10,11... | collective-permute-start | bytes 9437192 | tf_op jit(solution)/shard_map/ppermute | solution.py:49
  175.3 140.3 %collective-permute-start.17 = (bf16[512,5120]{1,0:T(8,128)(2,1)}, bf16[512,5120]{1,0:T(8,128)(2,1)}, u32[]{:S(2)}, u32[]{:S(2)}) collective-permute-start(bf16[512,5120]{1,0:T(8,128)(2,1)} %all-gather.7.cloned.1.call-done.refs_0_.refs_2_.refs_6_), channel_id=1, source_target_pairs={{0,16},{8,24},{16,0},{24,8},{1,17},{9,25},{17,1},{25,9},{2,18},{10... | collective-permute-start | bytes 15728648 | tf_op jit(solution)/shard_map/ppermute | solution.py:45
  176.8 22.6 %collective-permute-start.10 = (bf16[3,512,256]{2,1,0:T(8,128)(2,1)}, bf16[3,512,256]{2,1,0:T(8,128)(2,1)S(1)}, u32[]{:S(2)}, u32[]{:S(2)}) collective-permute-start(bf16[3,512,256]{2,1,0:T(8,128)(2,1)} %get-tuple-element.247), channel_id=1, source_target_pairs={{0,2},{2,4},{4,6},{6,0},{1,3},{3,5},{5,7},{7,1},{8,10},{10,12},{12... | collective-permute-start | bytes 2359304 | tf_op jit(solution)/shard_map/ppermute | solution.py:54
  176.8 55.0 %collective-permute-start.11 = (bf16[3,512,256]{2,1,0:T(8,128)(2,1)}, bf16[3,512,256]{2,1,0:T(8,128)(2,1)S(1)}, u32[]{:S(2)}, u32[]{:S(2)}) collective-permute-start(bf16[3,512,256]{2,1,0:T(8,128)(2,1)} %get-tuple-element.248), channel_id=1, source_target_pairs={{0,4},{2,6},{4,0},{6,2},{1,5},{3,7},{5,1},{7,3},{8,12},{10,14},{12... | collective-permute-start | bytes 2359304 | tf_op jit(solution)/shard_map/ppermute | solution.py:54
  178.0 53.8 %collective-permute-start.12 = (bf16[3,512,256]{2,1,0:T(8,128)(2,1)}, bf16[3,512,256]{2,1,0:T(8,128)(2,1)S(1)}, u32[]{:S(2)}, u32[]{:S(2)}) collective-permute-start(bf16[3,512,256]{2,1,0:T(8,128)(2,1)} %get-tuple-element.249), channel_id=1, source_target_pairs={{0,6},{2,0},{4,2},{6,4},{1,7},{3,1},{5,3},{7,5},{8,14},{10,8},{12,... | collective-permute-start | bytes 2359304 | tf_op jit(solution)/shard_map/ppermute | solution.py:54
  246.6 127.2 %all-gather.9.cloned.1.call-start = ((), (), s32[]{:S(2)}) async-start(), calls=%async_computation.9 | async-start | bytes 2621440 | tf_op jit(solution)/shard_map/all_gather | solution.py:88
  246.6 25.5 %collective-permute-start.14 = (bf16[1,512,256]{2,1,0:T(8,128)(2,1)}, bf16[1,512,256]{2,1,0:T(8,128)(2,1)S(1)}, u32[]{:S(2)}, u32[]{:S(2)}) collective-permute-start(bf16[1,512,256]{2,1,0:T(8,128)(2,1)} %get-tuple-element.262), channel_id=1, source_target_pairs={{0,6},{2,0},{4,2},{6,4},{1,7},{3,1},{5,3},{7,5},{8,14},{10,8},{12,... | collective-permute-start | bytes 786440 | tf_op jit(solution)/shard_map/ppermute | solution.py:54
  263.1 47.6 %collective-permute-start.15 = (bf16[1,512,256]{2,1,0:T(8,128)(2,1)}, bf16[1,512,256]{2,1,0:T(8,128)(2,1)S(1)}, u32[]{:S(2)}, u32[]{:S(2)}) collective-permute-start(bf16[1,512,256]{2,1,0:T(8,128)(2,1)} %get-tuple-element.263), channel_id=1, source_target_pairs={{0,4},{2,6},{4,0},{6,2},{1,5},{3,7},{5,1},{7,3},{8,12},{10,14},{12... | collective-permute-start | bytes 786440 | tf_op jit(solution)/shard_map/ppermute | solution.py:54
  264.3 46.4 %collective-permute-start.16 = (bf16[1,512,256]{2,1,0:T(8,128)(2,1)}, bf16[1,512,256]{2,1,0:T(8,128)(2,1)S(1)}, u32[]{:S(2)}, u32[]{:S(2)}) collective-permute-start(bf16[1,512,256]{2,1,0:T(8,128)(2,1)} %get-tuple-element.264), channel_id=1, source_target_pairs={{0,2},{2,4},{4,6},{6,0},{1,3},{3,5},{5,7},{7,1},{8,10},{10,12},{12... | collective-permute-start | bytes 786440 | tf_op jit(solution)/shard_map/ppermute | solution.py:54
  330.0 16.4 %collective-permute-start.22 = (bf16[512,5120]{1,0:T(8,128)(2,1)}, bf16[512,5120]{1,0:T(8,128)(2,1)}, u32[]{:S(2)}, u32[]{:S(2)}) collective-permute-start(bf16[512,5120]{1,0:T(8,128)(2,1)} %collective-permute-done.17.refs_1_.refs_3_.refs_7_), channel_id=1, source_target_pairs={{0,8},{8,0},{16,24},{24,16},{1,9},{9,1},{17,25},{25,17},{2,10},{10... | collective-permute-start | bytes 15728648 | tf_op jit(solution)/shard_map/ppermute | solution.py:45
  330.4 397.9 %reduce-scatter.8.cloned.1.call-start = ((), (), s32[]{:S(2)}) async-start(), calls=%async_computation.11 | async-start | bytes 2621440 | tf_op jit(solution)/shard_map/reduce_scatter | solution.py:135
  330.7 48.1 %collective-permute-start.20 = (bf16[512,2048]{1,0:T(8,128)(2,1)}, bf16[512,2048]{1,0:T(8,128)(2,1)}, u32[]{:S(2)}, u32[]{:S(2)}) collective-permute-start(bf16[512,2048]{1,0:T(8,128)(2,1)} %to_width.4), channel_id=1, source_target_pairs={{0,1},{1,0},{2,3},{3,2},{4,5},{5,4},{6,7},{7,6},{8,9},{9,8},{10,11... | collective-permute-start | bytes 6291464 | tf_op jit(solution)/shard_map/ppermute | solution.py:49
  332.2 53.6 %collective-permute-start.23 = (bf16[512,2048]{1,0:T(8,128)(2,1)}, bf16[512,2048]{1,0:T(8,128)(2,1)S(1)}, u32[]{:S(2)}, u32[]{:S(2)}) collective-permute-start(bf16[512,2048]{1,0:T(8,128)(2,1)} %all-gather.11.cloned.1.call-done.refs_1_.refs_0_), channel_id=1, source_target_pairs={{0,16},{8,24},{16,0},{24,8},{1,17},{9,25},{17,1},{25,9},{2,18},{10... | collective-permute-start | bytes 6291464 | tf_op jit(solution)/shard_map/ppermute | solution.py:45
  386.7 23.4 %collective-permute-start.25 = (bf16[512,2048]{1,0:T(8,128)(2,1)S(1)}, bf16[512,2048]{1,0:T(8,128)(2,1)S(1)}, u32[]{:S(2)}, u32[]{:S(2)}) collective-permute-start(bf16[512,2048]{1,0:T(8,128)(2,1)S(1)} %copy-done.24), channel_id=1, source_target_pairs={{0,8},{8,0},{16,24},{24,16},{1,9},{9,1},{17,25},{25,17},{2,10},{10... | collective-permute-start | bytes 6291464 | tf_op jit(solution)/shard_map/ppermute | solution.py:45
  386.7 23.4 %collective-permute-start.26 = (bf16[512,2048]{1,0:T(8,128)(2,1)S(1)}, bf16[512,2048]{1,0:T(8,128)(2,1)}, u32[]{:S(2)}, u32[]{:S(2)}) collective-permute-start(bf16[512,2048]{1,0:T(8,128)(2,1)S(1)} %collective-permute-done.23.refs_2_.refs_1_), channel_id=1, source_target_pairs={{0,8},{8,0},{16,24},{24,16},{1,9},{9,1},{17,25},{25,17},{2,10},{10... | collective-permute-start | bytes 6291464 | tf_op jit(solution)/shard_map/ppermute | solution.py:45
  387.2 47.9 %collective-permute-start.24 = (bf16[512,2048]{1,0:T(8,128)(2,1)}, bf16[512,2048]{1,0:T(8,128)(2,1)}, u32[]{:S(2)}, u32[]{:S(2)}) collective-permute-start(bf16[512,2048]{1,0:T(8,128)(2,1)} %all-gather.9.cloned.1.call-done.refs_1_.refs_0_), channel_id=1, source_target_pairs={{0,16},{8,24},{16,0},{24,8},{1,17},{9,25},{17,1},{25,9},{2,18},{10... | collective-permute-start | bytes 6291464 | tf_op jit(solution)/shard_map/ppermute | solution.py:45
  436.7 20.2 %collective-permute-start.34 = (bf16[512,1024]{1,0:T(8,128)(2,1)}, bf16[512,1024]{1,0:T(8,128)(2,1)}, u32[]{:S(2)}, u32[]{:S(2)}) collective-permute-start(bf16[512,1024]{1,0:T(8,128)(2,1)} %slice.134), channel_id=1, source_target_pairs={{0,8},{8,0},{16,24},{24,16},{1,9},{9,1},{17,25},{25,17},{2,10},{10... | collective-permute-start | bytes 3145736 | tf_op jit(solution)/shard_map/ppermute | solution.py:45
  456.4 19.9 %collective-permute-start.32 = (bf16[3,512,1024]{2,1,0:T(8,128)(2,1)}, bf16[3,512,1024]{2,1,0:T(8,128)(2,1)S(1)}, u32[]{:S(2)}, u32[]{:S(2)}) collective-permute-start(bf16[3,512,1024]{2,1,0:T(8,128)(2,1)} %slice.133), channel_id=1, source_target_pairs={{0,8},{8,0},{16,24},{24,16},{1,9},{9,1},{17,25},{25,17},{2,10},{10... | collective-permute-start | bytes 9437192 | tf_op jit(solution)/shard_map/ppermute | solution.py:45
  456.5 19.8 %collective-permute-start.30 = (bf16[512,3072]{1,0:T(8,128)(2,1)}, bf16[512,3072]{1,0:T(8,128)(2,1)}, u32[]{:S(2)}, u32[]{:S(2)}) collective-permute-start(bf16[512,3072]{1,0:T(8,128)(2,1)} %collective-permute-done.8.refs_0_), channel_id=1, source_target_pairs={{0,8},{8,0},{16,24},{24,16},{1,9},{9,1},{17,25},{25,17},{2,10},{10... | collective-permute-start | bytes 9437192 | tf_op jit(solution)/shard_map/ppermute | solution.py:45
  456.9 19.4 %collective-permute-start.31 = (bf16[512,3072]{1,0:T(8,128)(2,1)}, bf16[512,3072]{1,0:T(8,128)(2,1)}, u32[]{:S(2)}, u32[]{:S(2)}) collective-permute-start(bf16[512,3072]{1,0:T(8,128)(2,1)} %collective-permute-done.13.refs_1_), channel_id=1, source_target_pairs={{0,8},{8,0},{16,24},{24,16},{1,9},{9,1},{17,25},{25,17},{2,10},{10... | collective-permute-start | bytes 9437192 | tf_op jit(solution)/shard_map/ppermute | solution.py:45
  458.3 48.0 %collective-permute-start.29 = (bf16[512,2048]{1,0:T(8,128)(2,1)}, bf16[512,2048]{1,0:T(8,128)(2,1)}, u32[]{:S(2)}, u32[]{:S(2)}) collective-permute-start(bf16[512,2048]{1,0:T(8,128)(2,1)} %to_width.6), channel_id=1, source_target_pairs={{0,1},{1,0},{2,3},{3,2},{4,5},{5,4},{6,7},{7,6},{8,9},{9,8},{10,11... | collective-permute-start | bytes 6291464 | tf_op jit(solution)/shard_map/ppermute | solution.py:49
  464.3 12.0 %collective-permute-start.33 = (bf16[512,1024]{1,0:T(8,128)(2,1)}, bf16[512,1024]{1,0:T(8,128)(2,1)}, u32[]{:S(2)}, u32[]{:S(2)}) collective-permute-start(bf16[512,1024]{1,0:T(8,128)(2,1)} %bitcast.32.refs_0_), channel_id=1, source_target_pairs={{0,8},{8,0},{16,24},{24,16},{1,9},{9,1},{17,25},{25,17},{2,10},{10... | collective-permute-start | bytes 3145736 | tf_op jit(solution)/shard_map/ppermute | solution.py:45
  531.3 55.6 %collective-permute-start.40 = (bf16[1,512,2048]{2,1,0:T(8,128)(2,1)}, bf16[1,512,2048]{2,1,0:T(8,128)(2,1)}, u32[]{:S(2)}, u32[]{:S(2)}) collective-permute-start(bf16[1,512,2048]{2,1,0:T(8,128)(2,1)} %grad.14), channel_id=1, source_target_pairs={{0,16},{8,24},{16,0},{24,8},{1,17},{9,25},{17,1},{25,9},{2,18},{10... | collective-permute-start | bytes 6291464 | tf_op jit(solution)/shard_map/ppermute | solution.py:45
  558.8 34.8 %collective-permute-start.39 = (bf16[512,2048]{1,0:T(8,128)(2,1)}, bf16[512,2048]{1,0:T(8,128)(2,1)}, u32[]{:S(2)}, u32[]{:S(2)}) collective-permute-start(bf16[512,2048]{1,0:T(8,128)(2,1)} %up_back.3.refs_1_), channel_id=1, source_target_pairs={{0,8},{8,0},{16,24},{24,16},{1,9},{9,1},{17,25},{25,17},{2,10},{10... | collective-permute-start | bytes 6291464 | tf_op jit(solution)/shard_map/ppermute | solution.py:45
  558.8 34.7 %collective-permute-start.38 = (bf16[512,2048]{1,0:T(8,128)(2,1)}, bf16[512,2048]{1,0:T(8,128)(2,1)}, u32[]{:S(2)}, u32[]{:S(2)}) collective-permute-start(bf16[512,2048]{1,0:T(8,128)(2,1)} %up_back.2.refs_0_), channel_id=1, source_target_pairs={{0,8},{8,0},{16,24},{24,16},{1,9},{9,1},{17,25},{25,17},{2,10},{10... | collective-permute-start | bytes 6291464 | tf_op jit(solution)/shard_map/ppermute | solution.py:45
  576.0 47.9 %collective-permute-start.41 = (bf16[512,2048]{1,0:T(8,128)(2,1)}, bf16[512,2048]{1,0:T(8,128)(2,1)}, u32[]{:S(2)}, u32[]{:S(2)}) collective-permute-start(bf16[512,2048]{1,0:T(8,128)(2,1)} %to_width.7), channel_id=1, source_target_pairs={{0,1},{1,0},{2,3},{3,2},{4,5},{5,4},{6,7},{7,6},{8,9},{9,8},{10,11... | collective-permute-start | bytes 6291464 | tf_op jit(solution)/shard_map/ppermute | solution.py:49
  585.5 56.8 %collective-permute-start.46 = (bf16[1,512,2048]{2,1,0:T(8,128)(2,1)}, bf16[1,512,2048]{2,1,0:T(8,128)(2,1)}, u32[]{:S(2)}, u32[]{:S(2)}) collective-permute-start(bf16[1,512,2048]{2,1,0:T(8,128)(2,1)} %grad.15), channel_id=1, source_target_pairs={{0,16},{8,24},{16,0},{24,8},{1,17},{9,25},{17,1},{25,9},{2,18},{10... | collective-permute-start | bytes 6291464 | tf_op jit(solution)/shard_map/ppermute | solution.py:45
  593.6 214.7 %reduce-scatter.10.cloned.1.call-start = ((), (), s32[]{:S(2)}) async-start(), calls=%async_computation.12 | async-start | bytes 2621440 | tf_op jit(solution)/shard_map/reduce_scatter | solution.py:135
  633.3 48.7 %collective-permute-start.47 = (bf16[1,512,2048]{2,1,0:T(8,128)(2,1)S(1)}, bf16[1,512,2048]{2,1,0:T(8,128)(2,1)}, u32[]{:S(2)}, u32[]{:S(2)}) collective-permute-start(bf16[1,512,2048]{2,1,0:T(8,128)(2,1)S(1)} %copy-done.52), channel_id=1, source_target_pairs={{0,16},{8,24},{16,0},{24,8},{1,17},{9,25},{17,1},{25,9},{2,18},{10... | collective-permute-start | bytes 6291464 | tf_op jit(solution)/shard_map/ppermute | solution.py:45
  649.4 186.1 %reduce-scatter.14.cloned.1.call-start = ((), (), s32[]{:S(2)}) async-start(), calls=%async_computation.14 | async-start | bytes 2621440 | tf_op jit(solution)/shard_map/reduce_scatter | solution.py:135
  649.4 40.7 %collective-permute-start.42 = (bf16[1,512,256]{2,1,0:T(8,128)(2,1)}, bf16[1,512,256]{2,1,0:T(8,128)(2,1)S(1)}, u32[]{:S(2)}, u32[]{:S(2)}) collective-permute-start(bf16[1,512,256]{2,1,0:T(8,128)(2,1)} %get-tuple-element.341), channel_id=1, source_target_pairs={{0,2},{2,4},{4,6},{6,0},{1,3},{3,5},{5,7},{7,1},{8,10},{10,12},{12... | collective-permute-start | bytes 786440 | tf_op jit(solution)/shard_map/ppermute | solution.py:54
  649.5 40.7 %collective-permute-start.43 = (bf16[1,512,256]{2,1,0:T(8,128)(2,1)}, bf16[1,512,256]{2,1,0:T(8,128)(2,1)S(1)}, u32[]{:S(2)}, u32[]{:S(2)}) collective-permute-start(bf16[1,512,256]{2,1,0:T(8,128)(2,1)} %get-tuple-element.342), channel_id=1, source_target_pairs={{0,4},{2,6},{4,0},{6,2},{1,5},{3,7},{5,1},{7,3},{8,12},{10,14},{12... | collective-permute-start | bytes 786440 | tf_op jit(solution)/shard_map/ppermute | solution.py:54
  649.6 40.6 %collective-permute-start.44 = (bf16[1,512,256]{2,1,0:T(8,128)(2,1)S(1)}, bf16[1,512,256]{2,1,0:T(8,128)(2,1)S(1)}, u32[]{:S(2)}, u32[]{:S(2)}) collective-permute-start(bf16[1,512,256]{2,1,0:T(8,128)(2,1)S(1)} %copy-done.66), channel_id=1, source_target_pairs={{0,6},{2,0},{4,2},{6,4},{1,7},{3,1},{5,3},{7,5},{8,14},{10,8},{12,... | collective-permute-start | bytes 786440 | tf_op jit(solution)/shard_map/ppermute | solution.py:54
  659.6 168.9 %collective-permute-start.59 = (bf16[1,512,2048]{2,1,0:T(8,128)(2,1)}, bf16[1,512,2048]{2,1,0:T(8,128)(2,1)}, u32[]{:S(2)}, u32[]{:S(2)}) collective-permute-start(bf16[1,512,2048]{2,1,0:T(8,128)(2,1)} %grad.19), channel_id=1, source_target_pairs={{0,16},{8,24},{16,0},{24,8},{1,17},{9,25},{17,1},{25,9},{2,18},{10... | collective-permute-start | bytes 6291464 | tf_op jit(solution)/shard_map/ppermute | solution.py:45
  688.6 132.8 %collective-permute-start.55 = (bf16[1,512,1024]{2,1,0:T(8,128)(2,1)}, bf16[1,512,1024]{2,1,0:T(8,128)(2,1)}, u32[]{:S(2)}, u32[]{:S(2)}) collective-permute-start(bf16[1,512,1024]{2,1,0:T(8,128)(2,1)} %grad.20), channel_id=1, source_target_pairs={{0,16},{8,24},{16,0},{24,8},{1,17},{9,25},{17,1},{25,9},{2,18},{10... | collective-permute-start | bytes 3145736 | tf_op jit(solution)/shard_map/ppermute | solution.py:45
  703.0 27.5 %collective-permute-start.48 = (bf16[3,256,256]{2,1,0:T(8,128)(2,1)}, bf16[3,256,256]{2,1,0:T(8,128)(2,1)S(1)}, u32[]{:S(2)}, u32[]{:S(2)}) collective-permute-start(bf16[3,256,256]{2,1,0:T(8,128)(2,1)} %get-tuple-element.362), channel_id=1, source_target_pairs={{0,6},{2,0},{4,2},{6,4},{1,7},{3,1},{5,3},{7,5},{8,14},{10,8},{12,... | collective-permute-start | bytes 1179656 | tf_op jit(solution)/shard_map/ppermute | solution.py:54
  708.1 79.9 %collective-permute-start.49 = (bf16[3,256,256]{2,1,0:T(8,128)(2,1)}, bf16[3,256,256]{2,1,0:T(8,128)(2,1)S(1)}, u32[]{:S(2)}, u32[]{:S(2)}) collective-permute-start(bf16[3,256,256]{2,1,0:T(8,128)(2,1)} %get-tuple-element.363), channel_id=1, source_target_pairs={{0,4},{2,6},{4,0},{6,2},{1,5},{3,7},{5,1},{7,3},{8,12},{10,14},{12... | collective-permute-start | bytes 1179656 | tf_op jit(solution)/shard_map/ppermute | solution.py:54
  716.5 71.5 %collective-permute-start.50 = (bf16[3,256,256]{2,1,0:T(8,128)(2,1)}, bf16[3,256,256]{2,1,0:T(8,128)(2,1)S(1)}, u32[]{:S(2)}, u32[]{:S(2)}) collective-permute-start(bf16[3,256,256]{2,1,0:T(8,128)(2,1)} %get-tuple-element.364), channel_id=1, source_target_pairs={{0,2},{2,4},{4,6},{6,0},{1,3},{3,5},{5,7},{7,1},{8,10},{10,12},{12... | collective-permute-start | bytes 1179656 | tf_op jit(solution)/shard_map/ppermute | solution.py:54
  716.5 148.4 %reduce-scatter.12.cloned.1.call-start = ((), (), s32[]{:S(2)}) async-start(), calls=%async_computation.13 | async-start | bytes 1310720 | tf_op jit(solution)/shard_map/reduce_scatter | solution.py:135
  793.3 17.1 %collective-permute-start.51 = (bf16[3,256,256]{2,1,0:T(8,128)(2,1)S(1)}, bf16[3,256,256]{2,1,0:T(8,128)(2,1)S(1)}, u32[]{:S(2)}, u32[]{:S(2)}) collective-permute-start(bf16[3,256,256]{2,1,0:T(8,128)(2,1)S(1)} %copy-done.56), channel_id=1, source_target_pairs={{0,6},{2,0},{4,2},{6,4},{1,7},{3,1},{5,3},{7,5},{8,14},{10,8},{12,... | collective-permute-start | bytes 1179656 | tf_op jit(solution)/shard_map/ppermute | solution.py:54
  793.3 22.7 %collective-permute-start.52 = (bf16[3,256,256]{2,1,0:T(8,128)(2,1)S(1)}, bf16[3,256,256]{2,1,0:T(8,128)(2,1)S(1)}, u32[]{:S(2)}, u32[]{:S(2)}) collective-permute-start(bf16[3,256,256]{2,1,0:T(8,128)(2,1)S(1)} %copy-done.55), channel_id=1, source_target_pairs={{0,4},{2,6},{4,0},{6,2},{1,5},{3,7},{5,1},{7,3},{8,12},{10,14},{12... | collective-permute-start | bytes 1179656 | tf_op jit(solution)/shard_map/ppermute | solution.py:54
  793.4 22.6 %collective-permute-start.53 = (bf16[3,256,256]{2,1,0:T(8,128)(2,1)S(1)}, bf16[3,256,256]{2,1,0:T(8,128)(2,1)S(1)}, u32[]{:S(2)}, u32[]{:S(2)}) collective-permute-start(bf16[3,256,256]{2,1,0:T(8,128)(2,1)S(1)} %copy-done.54), channel_id=1, source_target_pairs={{0,2},{2,4},{4,6},{6,0},{1,3},{3,5},{5,7},{7,1},{8,10},{10,12},{12... | collective-permute-start | bytes 1179656 | tf_op jit(solution)/shard_map/ppermute | solution.py:54
  825.8 111.5 %reduce-scatter.16.cloned.1.call-start = ((), (), s32[]{:S(2)}) async-start(), calls=%async_computation.15 | async-start | bytes 2621440 | tf_op jit(solution)/shard_map/reduce_scatter | solution.py:135
  825.8 11.8 %collective-permute-start.57 = (bf16[3,256,1024]{2,1,0:T(8,128)(2,1)S(1)}, bf16[3,256,1024]{2,1,0:T(8,128)(2,1)}, u32[]{:S(2)}, u32[]{:S(2)}) collective-permute-start(bf16[3,256,1024]{2,1,0:T(8,128)(2,1)S(1)} %copy-done.14), channel_id=1, source_target_pairs={{0,8},{8,0},{16,24},{24,16},{1,9},{9,1},{17,25},{25,17},{2,10},{10... | collective-permute-start | bytes 4718600 | tf_op jit(solution)/shard_map/ppermute | solution.py:45
  825.9 11.7 %collective-permute-start.58 = (bf16[3,256,1024]{2,1,0:T(8,128)(2,1)S(1)}, bf16[3,256,1024]{2,1,0:T(8,128)(2,1)}, u32[]{:S(2)}, u32[]{:S(2)}) collective-permute-start(bf16[3,256,1024]{2,1,0:T(8,128)(2,1)S(1)} %copy-done.15), channel_id=1, source_target_pairs={{0,8},{8,0},{16,24},{24,16},{1,9},{9,1},{17,25},{25,17},{2,10},{10... | collective-permute-start | bytes 4718600 | tf_op jit(solution)/shard_map/ppermute | solution.py:45
  826.4 37.4 %collective-permute-start.56 = (bf16[3,256,1024]{2,1,0:T(8,128)(2,1)S(1)}, bf16[3,256,1024]{2,1,0:T(8,128)(2,1)}, u32[]{:S(2)}, u32[]{:S(2)}) collective-permute-start(bf16[3,256,1024]{2,1,0:T(8,128)(2,1)S(1)} %copy-done.14), channel_id=1, source_target_pairs={{0,1},{1,0},{2,3},{3,2},{4,5},{5,4},{6,7},{7,6},{8,9},{9,8},{10,11... | collective-permute-start | bytes 4718600 | tf_op jit(solution)/shard_map/ppermute | solution.py:49
  827.8 71.7 %collective-permute-start.54 = (bf16[3,256,1024]{2,1,0:T(8,128)(2,1)S(1)}, bf16[3,256,1024]{2,1,0:T(8,128)(2,1)}, u32[]{:S(2)}, u32[]{:S(2)}) collective-permute-start(bf16[3,256,1024]{2,1,0:T(8,128)(2,1)S(1)} %copy-done.15), channel_id=1, source_target_pairs={{0,1},{1,0},{2,3},{3,2},{4,5},{5,4},{6,7},{7,6},{8,9},{9,8},{10,11... | collective-permute-start | bytes 4718600 | tf_op jit(solution)/shard_map/ppermute | solution.py:49
  835.2 146.7 %reduce-scatter.18.cloned.1.call-start = ((), (), s32[]{:S(2)}) async-start(), calls=%async_computation.16 | async-start | bytes 1310720 | tf_op jit(solution)/shard_map/reduce_scatter | solution.py:135
  841.5 26.4 %collective-permute-start.60 = (bf16[1,512,1024]{2,1,0:T(8,128)(2,1)}, bf16[1,512,1024]{2,1,0:T(8,128)(2,1)}, u32[]{:S(2)}, u32[]{:S(2)}) collective-permute-start(bf16[1,512,1024]{2,1,0:T(8,128)(2,1)} %grad.24), channel_id=1, source_target_pairs={{0,16},{8,24},{16,0},{24,8},{1,17},{9,25},{17,1},{25,9},{2,18},{10... | collective-permute-start | bytes 3145736 | tf_op jit(solution)/shard_map/ppermute | solution.py:45
  848.3 63.2 %collective-permute-start.61 = (bf16[1,512,2048]{2,1,0:T(8,128)(2,1)}, bf16[1,512,2048]{2,1,0:T(8,128)(2,1)}, u32[]{:S(2)}, u32[]{:S(2)}) collective-permute-start(bf16[1,512,2048]{2,1,0:T(8,128)(2,1)} %grad.25), channel_id=1, source_target_pairs={{0,16},{8,24},{16,0},{24,8},{1,17},{9,25},{17,1},{25,9},{2,18},{10... | collective-permute-start | bytes 6291464 | tf_op jit(solution)/shard_map/ppermute | solution.py:45
  886.5 97.2 %reduce-scatter.20.cloned.1.call-start = ((), (), s32[]{:S(2)}) async-start(), calls=%async_computation.17 | async-start | bytes 2621440 | tf_op jit(solution)/shard_map/reduce_scatter | solution.py:135
  918.7 15.9 %collective-permute-start.62 = (f32[2,2048]{1,0:T(2,128)S(1)}, f32[2,2048]{1,0:T(2,128)S(1)}, u32[]{:S(2)}, u32[]{:S(2)}) collective-permute-start(f32[2,2048]{1,0:T(2,128)S(1)} %bitcast_reduce_fusion), channel_id=1, source_target_pairs={{0,1},{1,0},{2,3},{3,2},{4,5},{5,4},{6,7},{7,6},{8,9},{9,8},{10,11... | collective-permute-start | bytes 49160 | tf_op jit(solution)/shard_map/ppermute | solution.py:49
  935.2 14.9 %collective-permute-start.63 = (f32[2,4,40,128]{3,2,1,0:T(8,128)S(1)}, f32[2,4,40,128]{3,2,1,0:T(8,128)S(1)}, u32[]{:S(2)}, u32[]{:S(2)}) collective-permute-start(f32[2,4,40,128]{3,2,1,0:T(8,128)S(1)} %slice.139), channel_id=1, source_target_pairs={{0,2},{2,0},{4,6},{6,4},{1,3},{3,1},{5,7},{7,5},{8,10},{10,8},{12,... | collective-permute-start | bytes 491528 | tf_op jit(solution)/shard_map/ppermute | solution.py:1119
  935.2 14.8 %collective-permute-start.64 = (f32[37,128]{1,0:T(8,128)S(1)}, f32[37,128]{1,0:T(8,128)S(1)}, u32[]{:S(2)}, u32[]{:S(2)}) collective-permute-start(f32[37,128]{1,0:T(8,128)S(1)} %pad.6), channel_id=1, source_target_pairs={{0,2},{2,0},{4,6},{6,4},{1,3},{3,1},{5,7},{7,5},{8,10},{10,8},{12,... | collective-permute-start | bytes 56840 | tf_op jit(solution)/shard_map/ppermute | solution.py:1119
  950.1 16.1 %collective-permute-start.65 = (f32[1,4,40,128]{3,2,1,0:T(8,128)S(1)}, f32[1,4,40,128]{3,2,1,0:T(8,128)S(1)}, u32[]{:S(2)}, u32[]{:S(2)}) collective-permute-start(f32[1,4,40,128]{3,2,1,0:T(8,128)S(1)} %slice.164), channel_id=1, source_target_pairs={{0,4},{2,6},{4,0},{6,2},{1,5},{3,7},{5,1},{7,3},{8,12},{10,14},{12... | collective-permute-start | bytes 245768 | tf_op jit(solution)/shard_map/ppermute | solution.py:1119
  950.2 16.0 %collective-permute-start.66 = (f32[37,128]{1,0:T(8,128)S(1)}, f32[37,128]{1,0:T(8,128)S(1)}, u32[]{:S(2)}, u32[]{:S(2)}) collective-permute-start(f32[37,128]{1,0:T(8,128)S(1)} %add.250), channel_id=1, source_target_pairs={{0,4},{2,6},{4,0},{6,2},{1,5},{3,7},{5,1},{7,3},{8,12},{10,14},{12... | collective-permute-start | bytes 56840 | tf_op jit(solution)/shard_map/ppermute | solution.py:1119
  (87 other events, 1540.8 us)
Sparse Core Ops, SparseCore 0:
  10.2 66.1 all-gather.4
  78.6 96.7 all-gather.6
  246.7 74.2 all-gather.10
  330.5 43.1 all-gather.8
  593.7 40.2 reduce-scatter.7
  649.5 59.0 reduce-scatter.9
  716.6 65.4 reduce-scatter.13
  825.9 24.3 reduce-scatter.11
  852.6 42.4 reduce-scatter.15
  897.4 26.4 reduce-scatter.17
  926.2 48.4 reduce-scatter.19

commit v4 on v3

--- a/solution.py
+++ b/solution.py
@@ -796,6 +796,125 @@
     )(perm, inputs, coeff, dz, dr, *before)
 
 
+def two_terms(values):
+    high = values.astype(BF16)
+    return high, (values - high.astype(F32)).astype(BF16)
+
+
+def final_kernel(res_ref, mine_ref, theirs_ref, out_ref, cot_ref, valid_ref, in_ref, mix_ref, *refs):
+    final_ref, grad_ref, low_ref, far_ref, high_ref, rest_ref, back_ref, inverse_ref = refs
+    tile, width = res_ref.shape
+    step = 16
+    for t in range(0, tile, step):
+        rows = slice(t, t + step)
+        final = res_ref[rows, :] + (
+            mine_ref[rows, :].astype(F32) + theirs_ref[rows, :].astype(F32)
+        )
+        inverse = lax.rsqrt(jnp.mean(final * final, axis=-1, keepdims=True) + RMS_EPSILON)
+        final_ref[rows, :] = final
+        inverse_ref[rows, :] = jnp.broadcast_to(inverse, (step, HD))
+        high_ref[rows, :], rest_ref[rows, :] = two_terms(final * inverse)
+    pre = sum(
+        lax.dot_general(n[...], in_ref[...], NT, preferred_element_type=F32)
+        for n in (high_ref, rest_ref)
+    )
+    grad_pre = lax.dot_general(
+        cot_ref[...], mix_ref[...], NT, precision=HIGHEST, preferred_element_type=F32
+    ) * (
+        0.5 * (1.0 + lax.erf(pre * math.sqrt(0.5)))
+        + pre * jnp.exp(-0.5 * pre * pre) * (1.0 / math.sqrt(2.0 * math.pi))
+    )
+    back_ref[...] = sum(
+        jnp.dot(g, in_ref[...], preferred_element_type=F32) for g in two_terms(grad_pre)
+    )
+    for t in range(0, tile, step):
+        rows = slice(t, t + step)
+        inverse = inverse_ref[rows, :1]
+        normed = final_ref[rows, :] * inverse
+        grad = back_ref[rows, :]
+        grad = inverse * (grad - normed * jnp.mean(grad * normed, axis=-1, keepdims=True))
+        grad = out_ref[rows, :].astype(F32) * valid_ref[rows, :] + grad
+        grad_ref[rows, :] = grad
+        low = grad.astype(BF16)
+        low_ref[rows, :] = low
+        far_ref[rows, :] = low[:, width // 2 :]
+
+
+def final_stage(residual, mine, theirs, grad_out, cotangent, valid, weight_in, weight_out, tile=128):
+    tokens, width = residual.shape
+    rows = pl.BlockSpec((tile, width), lambda t: (t, 0))
+    cotangent = jnp.pad(cotangent, ((0, 0), (0, HD - MIXW)))
+    weight_in = jnp.pad(weight_in, ((0, HD - MIXW), (0, 0))).astype(BF16)
+    weight_out = jnp.pad(weight_out, ((0, HD - MIXW), (0, HD - MIXW)))
+    return pl.pallas_call(
+        final_kernel,
+        name="final",
+        grid=(tokens // tile,),
+        in_specs=[
+            rows,
+            rows,
+            rows,
+            rows,
+            pl.BlockSpec((tile, HD), lambda t: (t, 0)),
+            pl.BlockSpec((tile, 1), lambda t: (t, 0)),
+            pl.BlockSpec((HD, width), lambda t: (0, 0)),
+            pl.BlockSpec((HD, HD), lambda t: (0, 0)),
+        ],
+        out_specs=[rows, rows, rows, pl.BlockSpec((tile, width // 2), lambda t: (t, 0))],
+        out_shape=[
+            jax.ShapeDtypeStruct((tokens, width), F32),
+            jax.ShapeDtypeStruct((tokens, width), F32),
+            jax.ShapeDtypeStruct((tokens, width), BF16),
+            jax.ShapeDtypeStruct((tokens, width // 2), BF16),
+        ],
+        scratch_shapes=[
+            pltpu.VMEM((tile, width), BF16),
+            pltpu.VMEM((tile, width), BF16),
+            pltpu.VMEM((tile, width), F32),
+            pltpu.VMEM((tile, HD), F32),
+        ],
+        cost_estimate=cost(8),
+        compiler_params=params(1),
+    )(residual, mine, theirs, grad_out, cotangent, valid, weight_in, weight_out)
+
+
+def second_kernel(res_ref, mine_ref, theirs_ref, grad_ref, gain_ref, out_ref, sum_ref):
+    @pl.when(pl.program_id(0) == 0)
+    def _():
+        sum_ref[...] = jnp.zeros_like(sum_ref)
+
+    step = 32
+    width = res_ref.shape[1]
+    for t in range(0, res_ref.shape[0], step):
+        rows = slice(t, t + step)
+        hat, inverse = hat_of(res_ref[rows, :])
+        d = mine_ref[rows, :].astype(F32) + theirs_ref[rows, :].astype(F32)
+        sum_ref[:8] += jnp.sum((d * hat).reshape(step // 8, 8, width), axis=0)
+        sum_ref[8:] += jnp.sum(d.reshape(step // 8, 8, width), axis=0)
+        e = d * gain_ref[...]
+        first = jnp.mean(e, axis=-1, keepdims=True)
+        second = jnp.mean(e * hat, axis=-1, keepdims=True)
+        out_ref[rows, :] = (grad_ref[rows, :] + (e - first - hat * second) * inverse).astype(BF16)
+
+
+def second_norm_back(residual, mine, theirs, grad, gain, tile=128):
+    tokens, width = residual.shape
+    rows = pl.BlockSpec((tile, width), lambda t: (t, 0))
+    return pl.pallas_call(
+        second_kernel,
+        name="second",
+        grid=(tokens // tile,),
+        in_specs=[rows, rows, rows, rows, pl.BlockSpec((1, width), lambda t: (0, 0))],
+        out_specs=[rows, pl.BlockSpec((16, width), lambda t: (0, 0))],
+        out_shape=[
+            jax.ShapeDtypeStruct((tokens, width), BF16),
+            jax.ShapeDtypeStruct((16, width), F32),
+        ],
+        cost_estimate=cost(6),
+        compiler_params=params(1),
+    )(residual, mine, theirs, grad, gain)
+
+
 def layer_norm(values, gain, shift):
     center = values - jnp.mean(values, axis=-1, keepdims=True)
     spread = jnp.mean(center * center, axis=-1, keepdims=True)
@@ -916,6 +1035,9 @@
     Pace.value = FORWARD_PACE
     inputs = earlier.reshape(count_prev, tokens, width)
     coeff = group_coeff(mix_in, count_prev, tokens)
+    def far_half(values):
+        return over_fsdp(values[..., width // 2 :], 1)
+
     normed_in, streams = order.keep(
         mix_streams(perm, inputs, coeff, gain_first, shift_first)
     )
@@ -923,6 +1045,7 @@
     tables_all = turn_tables(jnp.arange(span * ctx, dtype=jnp.int32))
     target = (z + ring) % ctx
     tables_here, tables_all = order.wait((tables_here, tables_all))
+    normed_in_far = order.wait(far_half(order(normed_in)))
 
     def to_heads(chunks):
         return [chunks[0]] + [shift_ctx(chunks[s], s) for s in range(1, ctx)]
@@ -957,27 +1080,27 @@
     near_both = order.wait(near_both)
     near_proj = order.wait([b[:, hidden:] for b in near_both])
     blocks_proj = near_proj + order.wait(to_core(near_proj))
+    near_down = [cross(order.wait(ctx_down[0]))]
+    far_both = to_core(order(near_both))
     branch_mine = order.keep(to_width([order(attended)], [blocks_proj], width))
     branch_theirs = over_tp(branch_mine)
-    near_down = [cross(order.wait(ctx_down[0]))]
-    blocks_up = near_both + order.wait(to_core(order(near_both)))
+    blocks_up = near_both + order.wait(far_both)
+    near_down[0] = order.wait(near_down[0])
     near_down.append(cross(order.wait(ctx_down[1])))
     branch_theirs = order.wait(branch_theirs)
     residual = streams[STREAMS - 1] + tp_sum(branch_mine, branch_theirs)
 
-    def far_half(values):
-        return over_fsdp(values[..., width // 2 :], 1)
-
     normed = layer_norm(residual, gain_second, shift_second).astype(BF16)
     normed = order.wait(normed)
-    near_down[0] = order.wait(near_down[0])
     far_down = [to_core(near_down[0])]
+    other_far = to_core(other)
     active, slope = [], []
     for n in range(2):
         a, b = order.keep(up_stage(perm, order(normed), blocks_up, n, half))
         active.append(a)
         slope.append(b)
     far_down[0] = order.wait(far_down[0])
+    other = other + order.wait(other_far)
     down_first = order.keep(
         to_width([order(active[0])], [near_down[0] + far_down[0]], width, (), F32)
     )
@@ -987,27 +1110,32 @@
     down_mine = order.keep(
         to_width([order(active[1])], blocks_down[1:], width, (down_first,))
     )
-    other_far = to_core(other)
     down_theirs = over_tp(down_mine)
-    active_far = [over_fsdp(a, 1) for a in order(active)]
     grad_out_here = order.wait(relative(grad_out.reshape(tokens, width)))
-    active_far = order.wait(active_far)
-    normed_far = order.wait(far_half(normed))
-    attended_far = order.wait(over_fsdp(attended, 1))
-    normed_in_far = order.wait(far_half(normed_in))
-    other = other + order.wait(other_far)
-    final = residual + tp_sum(down_mine, order.wait(down_theirs))
-    output = absolute(final.astype(BF16)).reshape(rows, span, width)
-
-    mix_value, mix_pull = jax.vjp(mixer, final, mixer_full, mixer_out, mixer_bias)
-    mix_out = mix_value.T.reshape(MIXW, rows, span)
-    mix_cotangent = (grad_mix.reshape(MIXW, tokens) * valid[None]).T
-    grad_final_mix, grad_mixer_first, grad_mixer_second, grad_mixer_shift = mix_pull(mix_cotangent)
-    grad_final = grad_out_here.astype(F32) * valid[:, None] + grad_final_mix
+    mix_cotangent = order.wait((grad_mix.reshape(MIXW, tokens) * valid[None]).T)
+    down_theirs = order.wait(down_theirs)
+
+    final, grad_final, grad_down_b, grad_down_near = order.keep(
+        final_stage(
+            residual,
+            down_mine,
+            order(down_theirs),
+            grad_out_here,
+            mix_cotangent,
+            valid[:, None],
+            mixer_full,
+            mixer_out,
+        )
+    )
 
     Pace.value = BACKWARD_PACE
-    grad_down_b = order.wait(grad_final.astype(BF16))
-    grad_down_far = order.wait(far_half(grad_down_b))
+    active_far = [over_fsdp(a, 1) for a in active]
+    normed_far = far_half(normed)
+    attended_far = over_fsdp(attended, 1)
+    grad_down_far = over_fsdp(grad_down_near, 1)
+    active_far, normed_far, attended_far, grad_down_far = order.wait(
+        (active_far, normed_far, attended_far, grad_down_far)
+    )
     down = [
         Scatter(order, grad_down_b[None], [a[None]], grad_down_far[None], [f[None]])
         for a, f in zip(active, active_far)
@@ -1022,22 +1150,30 @@
         upward_far.append(over_fsdp(grad_upward[n], 1))
     normed_mine = order.keep(to_width(order(grad_upward), [blocks_up] * 2, width, (), BF16, (0, 1)))
     normed_theirs = over_tp(normed_mine)
+    Pace.value = 3 * BACKWARD_PACE
     grad_down = [scatter_ctx(down[0].finish())]
+    Pace.value = BACKWARD_PACE
     upward_far = order.wait(upward_far)
     up = [
         Scatter(order, normed[None], [u[None]], normed_far[None], [f[None]])
         for u, f in zip(grad_upward, upward_far)
     ]
     up[0].launch()
+    mix_value, mix_pull = jax.vjp(
+        lambda *weights: mixer(order(final), *weights), mixer_full, mixer_out, mixer_bias
+    )
+    mix_out = mix_value.T.reshape(MIXW, rows, span)
+    grad_mixer_first, grad_mixer_second, grad_mixer_shift = mix_pull(mix_cotangent)
+    output = absolute(order(final).astype(BF16)).reshape(rows, span, width)
     tail = jnp.concatenate([grad_mixer_second, grad_mixer_shift[None]], axis=0)
     tail, grad_mixer_first, output, mix_out = order.wait(
         (tail, grad_mixer_first, output, mix_out)
     )
     normed_theirs = order.wait(normed_theirs)
-    grad_normed = tp_sum(normed_mine, normed_theirs)
-    unused_norm, norm_pull = jax.vjp(layer_norm, residual, gain_second, shift_second)
-    grad_residual_norm, grad_gain_second, grad_shift_second = norm_pull(grad_normed)
-    grad_branch_b = order.wait((grad_final + grad_residual_norm).astype(BF16))
+    grad_branch_b, second_sums = order.keep(
+        second_norm_back(residual, normed_mine, order(normed_theirs), grad_final, gain_second)
+    )
+    second_pair = second_sums.reshape(2, 8, width).sum(1)
 
     grad_branch_far = far_half(grad_branch_b)
     grad_chunks = order.keep(
@@ -1098,7 +1234,7 @@
     dz = order.keep(other_part(order(theirs[1]), own[1][0], streams, gain_first, other, 1))
     sums_far = order.wait(sums_far)
     packed = jnp.concatenate(
-        [grad_mixer_first, sums + sums_far, grad_gain_second, grad_shift_second], axis=0
+        [grad_mixer_first, sums + sums_far, second_pair], axis=0
     )
     packed = packed.reshape(packed.shape[0], fsdp, ctx, piece)
     packed = jnp.stack(

time: 1000 us -> 984 us (0.984)
  waiting for transfers between devices: 425 us -> 391 us
  Pallas kernels: 347 us -> 367 us
  other arithmetic: 57.2 us -> 38.8 us
    all_gather x4, waiting for transfers between devices: 41.2 us -> 7.97 us  [gather_ctx(): return lax.all_gather(shard, 'ctx', axis=0, tiled=True)]
    pallas_call x0 -> x2, Pallas kernels: none -> 20.6 us  [the longest x1 12.6 us: final_stage(): pl.pallas_call(final_kernel, name='final', grid=(tokens // tile,), in_spe...]
    unnamed x146 -> x151, local copies, waits for them, and re-layouts: 19.9 us -> 23.1 us
  transfers between devices with their start and end apart: 82 -> 82, of which waited for: 32 -> 31; matrix products, arithmetic and copies ran while one was open for 8% -> 8% of each run, Pallas kernels for 34% -> 36%
where the time goes in v4:
time: 984 us; the launch traced here: 974 us
  waiting for transfers between devices  391 us (40%)
  Pallas kernels  367 us (37%)
  starting transfers between devices  92.7 us (9%)
  local copies, waits for them, and re-layouts  49.8 us (5%)
  other arithmetic  38.8 us (4%)
  between operations  25.6 us (3%)
    ppermute x18, waiting for transfers between devices, shift_ctx(): lax.ppermute(values, 'ctx', [(i, (i + step) % size) for i in range(size)])  162 us
    ppermute x8, waiting for transfers between devices, over_tp(): return lax.ppermute(values, 'tp', xor_pairs(lax.axis_size('tp'), 1))  124 us
    ppermute x41, waiting for transfers between devices, over_fsdp(): return lax.ppermute(values, 'fsdp', xor_pairs(lax.axis_size('fsdp'), mask))  86.5 us
    pallas_call x14, Pallas kernels, grad_blocks(): pl.pallas_call(partial(grad_kernel, count=len(chosen), rights=len(near),...  81.2 us
    ppermute x18, starting transfers between devices, shift_ctx(): lax.ppermute(values, 'ctx', [(i, (i + step) % size) for i in range(size)])  55.2 us
    pallas_call x4, Pallas kernels, to_width(): pl.pallas_call(partial(back_kernel, lefts=len(lefts), parts=parts, adds=l...  44.6 us
    pallas_call x2, Pallas kernels, other_part(): pl.pallas_call(partial(other_kernel, parts=parts), name='other', grid=(ki...  28.7 us
    pallas_call x2, Pallas kernels, own_part(): pl.pallas_call(partial(own_kernel, parts=parts), name='own', grid_spec=pl...  26.3 us
  transfers between devices with their start and end apart: 82, of which 31 were waited for; matrix products, arithmetic and copies ran while one was open for 8% of the time, Pallas kernels for 36%

profile of v4, /device:TPU:0, one launch (start us, length us, event | category | flops | bytes accessed | tf_op | source)
XLA Modules:
  0.0 973.6 jit_solution(10218713665410572426)
XLA Ops:
  39.9 21.0 %mix.1 = (bf16[3,512,2048]{2,1,0:T(8,128)(2,1)}, f32[4,512,2048]{2,1,0:T(8,128)}) custom-call(s32[4]{0:T(128)} %get-tuple-element.564.perm_ref, bf16[8,512,2048]{2,1,0:T(8,128)(2,1)} %bitcast.143, f32[16,256,4]{2,1,0:T(8,128)} %bitcast.150, f32[1,2048]{1,0:T(1,128)} %bitcast.181, f32[1,2048]{1,0:T(1,128)} %bitcast.191), custom_call_target="tpu_custom_call" | custom-call | flops 420000000 | bytes 1024 | tf_op jit(solution)/shard_map/mix/pallas_call | solution.py:182
  60.9 3.9 slice.130
  70.8 5.7 all-gather.5.cloned.1.call-done.refs_0_
  82.3 65.0 %collective-permute-done.9.refs_0_ = bf16[512,3072]{1,0:T(8,128)(2,1)} collective-permute-done((bf16[512,3072]{1,0:T(8,128)(2,1)}, bf16[512,3072]{1,0:T(8,128)(2,1)}, u32[]{:S(2)}, u32[]{:S(2)}) %collective-permute-start.9) | collective-permute-done | bytes 3145760 | tf_op jit(solution)/shard_map/ppermute | solution.py:49
  149.6 4.9 collective-permute-done.10.refs_3_
  154.5 18.6 %heads.2 = (bf16[3,512,256]{2,1,0:T(8,128)(2,1)}, bf16[3,512,256]{2,1,0:T(8,128)(2,1)}, bf16[3,512,256]{2,1,0:T(8,128)(2,1)}, bf16[3,512,256]{2,1,0:T(8,128)(2,1)}) custom-call(s32[4]{0:T(128)} %and_select_fusion.target_ref, s32[4]{0:T(128)} %get-tuple-element.564.perm_ref, bf16[3,512,2048]{2,1,0:T(8,128)(2,1)} %get-tuple-element.252.a_ref.refs_0_, ...), custom_call_target="tpu_custom_call" | custom-call | flops 720000000 | bytes 1024 | tf_op jit(solution)/shard_map/heads/pallas_call | solution.py:261
  180.8 18.5 %collective-permute-done.11.refs_1_ = bf16[3,512,256]{2,1,0:T(8,128)(2,1)S(1)} collective-permute-done((bf16[3,512,256]{2,1,0:T(8,128)(2,1)}, bf16[3,512,256]{2,1,0:T(8,128)(2,1)S(1)}, u32[]{:S(2)}, u32[]{:S(2)}) %collective-permute-start.11) | collective-permute-done | bytes 786464 | tf_op jit(solution)/shard_map/ppermute | solution.py:54
  199.4 32.5 %collective-permute-done.12.refs_2_ = bf16[3,512,256]{2,1,0:T(8,128)(2,1)S(1)} collective-permute-done((bf16[3,512,256]{2,1,0:T(8,128)(2,1)}, bf16[3,512,256]{2,1,0:T(8,128)(2,1)S(1)}, u32[]{:S(2)}, u32[]{:S(2)}) %collective-permute-start.12) | collective-permute-done | bytes 786464 | tf_op jit(solution)/shard_map/ppermute | solution.py:54
  233.0 11.5 %attend.1 = (bf16[1,512,256]{2,1,0:T(8,128)(2,1)}, bf16[1,512,256]{2,1,0:T(8,128)(2,1)}, bf16[1,512,256]{2,1,0:T(8,128)(2,1)}, bf16[1,512,256]{2,1,0:T(8,128)(2,1)}) custom-call(s32[4]{0:T(128)} %copy-done.38, s32[2]{0:T(128)} %length_ref.5, bf16[3,512,256]{2,1,0:T(8,128)(2,1)} %get-tuple-element.264.refs_0_, bf16[3,512,256]{2,1,0:T(8,128)(2,1)} %copy-done.22, ...), custom_call_target="tpu_custom_call" | custom-call | flops 360000000 | bytes 1024 | tf_op jit(solution)/shard_map/attend/pallas_call | solution.py:367
  246.8 16.4 %collective-permute-start.15 = (bf16[1,512,256]{2,1,0:T(8,128)(2,1)S(1)}, bf16[1,512,256]{2,1,0:T(8,128)(2,1)S(1)}, u32[]{:S(2)}, u32[]{:S(2)}) collective-permute-start(bf16[1,512,256]{2,1,0:T(8,128)(2,1)S(1)} %copy-done.69), channel_id=1, source_target_pairs={{0,6},{2,0},{4,2},{6,4},{1,7},{3,1},{5,3},{7,5},{8,14},{10,8},{12,... | collective-permute-start | bytes 786440 | tf_op jit(solution)/shard_map/ppermute | solution.py:54
  266.4 5.3 collective-permute-done.15.refs_1_
  271.7 38.8 %collective-permute-done.16.refs_2_ = bf16[1,512,256]{2,1,0:T(8,128)(2,1)S(1)} collective-permute-done((bf16[1,512,256]{2,1,0:T(8,128)(2,1)S(1)}, bf16[1,512,256]{2,1,0:T(8,128)(2,1)S(1)}, u32[]{:S(2)}, u32[]{:S(2)}) %collective-permute-start.16) | collective-permute-done | bytes 262176 | tf_op jit(solution)/shard_map/ppermute | solution.py:54
  324.0 6.1 to_width.4
  332.1 7.2 collective-permute-done.24.refs_3_.refs_5_.refs_9_
  339.3 32.1 %collective-permute-done.22.refs_2_.refs_1_ = bf16[512,2048]{1,0:T(8,128)(2,1)} collective-permute-done((bf16[512,2048]{1,0:T(8,128)(2,1)}, bf16[512,2048]{1,0:T(8,128)(2,1)}, u32[]{:S(2)}, u32[]{:S(2)}) %collective-permute-start.22) | collective-permute-done | bytes 2097184 | tf_op jit(solution)/shard_map/ppermute | solution.py:45
  371.9 5.9 collective-permute-done.21
  379.3 4.2 fusion.43
  387.6 11.3 %up.2 = (bf16[512,2048]{1,0:T(8,128)(2,1)}, f32[512,2048]{1,0:T(8,128)}) custom-call(s32[4]{0:T(128)} %get-tuple-element.564.perm_ref, bf16[512,2048]{1,0:T(8,128)(2,1)} %add_convert_fusion.a_ref, bf16[512,5120]{1,0:T(8,128)(2,1)} %all-gather.7.cloned.1.call-done.refs_0_.refs_2_.refs_6_, bf16[512,5120]{1,0:T(8,128)(2,1)} %collective-permute-done.18.refs_1_.refs_3_.refs_7_, ...), custom_call_target="tpu_custom_call" | custom-call | flops 307200000 | bytes 1024 | tf_op jit(solution)/shard_map/up/pallas_call | solution.py:463
  398.9 11.3 %up.3 = (bf16[512,2048]{1,0:T(8,128)(2,1)}, f32[512,2048]{1,0:T(8,128)}) custom-call(s32[4]{0:T(128)} %get-tuple-element.564.perm_ref, bf16[512,2048]{1,0:T(8,128)(2,1)} %add_convert_fusion.a_ref, bf16[512,5120]{1,0:T(8,128)(2,1)} %all-gather.7.cloned.1.call-done.refs_0_.refs_2_.refs_6_, bf16[512,5120]{1,0:T(8,128)(2,1)} %collective-permute-done.18.refs_1_.refs_3_.refs_7_, ...), custom_call_target="tpu_custom_call" | custom-call | flops 307200000 | bytes 1024 | tf_op jit(solution)/shard_map/up/pallas_call | solution.py:463
  410.2 11.3 %to_width.5.refs_5_ = f32[512,2048]{1,0:T(8,128)} custom-call(bf16[512,2048]{1,0:T(8,128)(2,1)} %get-tuple-element.309.refs_0_, bf16[512,2048]{1,0:T(8,128)(2,1)} %all-gather.9.cloned.1.call-done.refs_1_.refs_0_, bf16[512,2048]{1,0:T(8,128)(2,1)} %collective-permute-done.22.refs_2_.refs_1_, bf16[512,2048]{1,0:T(8,128)(2,1)} %collective-permute-done.28.refs_3_.refs_2_, ...), custom_call_target="tpu_custom_call" | custom-call | flops 240000000 | bytes 1024 | tf_op jit(solution)/shard_map/to_width/pallas_call | solution.py:538
  425.1 5.9 collective-permute-done.30.refs_3_.refs_2_
  432.3 10.8 %to_width.6.mine_ref = bf16[512,2048]{1,0:T(8,128)(2,1)} custom-call(bf16[512,2048]{1,0:T(8,128)(2,1)} %get-tuple-element.314.refs_0_, bf16[512,2048]{1,0:T(8,128)(2,1)} %all-gather.11.cloned.1.call-done.refs_1_.refs_0_, bf16[512,2048]{1,0:T(8,128)(2,1)} %copy-done.18, bf16[512,2048]{1,0:T(8,128)(2,1)} %copy-done.19, ...), custom_call_target="tpu_custom_call" | custom-call | flops 240000000 | bytes 1024 | tf_op jit(solution)/shard_map/to_width/pallas_call | solution.py:538
  453.6 37.5 %collective-permute-done.32.theirs_ref = bf16[512,2048]{1,0:T(8,128)(2,1)} collective-permute-done((bf16[512,2048]{1,0:T(8,128)(2,1)}, bf16[512,2048]{1,0:T(8,128)(2,1)}, u32[]{:S(2)}, u32[]{:S(2)}) %collective-permute-start.32) | collective-permute-done | bytes 2097184 | tf_op jit(solution)/shard_map/ppermute | solution.py:49
  491.1 12.6 %final.1 = (f32[512,2048]{1,0:T(8,128)}, f32[512,2048]{1,0:T(8,128)}, bf16[512,2048]{1,0:T(8,128)(2,1)}, bf16[512,1024]{1,0:T(8,128)(2,1)}) custom-call(f32[512,2048]{1,0:T(8,128)} %copy-done, bf16[512,2048]{1,0:T(8,128)(2,1)} %to_width.6.mine_ref, bf16[512,2048]{1,0:T(8,128)(2,1)} %collective-permute-done.32.theirs_ref, ...), custom_call_target="tpu_custom_call" | custom-call | flops 240000000 | bytes 1024 | tf_op jit(solution)/shard_map/final/pallas_call | solution.py:849
  508.6 6.1 grad.14
  516.1 6.1 grad.15
  522.2 10.4 %up_back.2.refs_0_ = bf16[512,2048]{1,0:T(8,128)(2,1)} custom-call(s32[4]{0:T(128)} %get-tuple-element.564.perm_ref, bf16[512,2048]{1,0:T(8,128)(2,1)} %get-tuple-element.332.a_ref, f32[512,2048]{1,0:T(8,128)} %get-tuple-element.301.slope_ref, bf16[512,2048]{1,0:T(8,128)(2,1)} %all-gather.9.cloned.1.call-done.refs_1_.refs_0_, ...), custom_call_target="tpu_custom_call" | custom-call | flops 15360000000 | bytes 1024 | tf_op jit(solution)/shard_map/up_back/pallas_call | solution.py:495
  532.7 10.5 %up_back.3.refs_1_ = bf16[512,2048]{1,0:T(8,128)(2,1)} custom-call(s32[4]{0:T(128)} %get-tuple-element.564.perm_ref, bf16[512,2048]{1,0:T(8,128)(2,1)} %get-tuple-element.332.a_ref, f32[512,2048]{1,0:T(8,128)} %get-tuple-element.304.slope_ref, bf16[512,2048]{1,0:T(8,128)(2,1)} %all-gather.11.cloned.1.call-done.refs_1_.refs_0_, bf16[512,2048]{1,0:T(8,128)(2,1)} %copy-done.18, ...), custom_call_target="tpu_custom_call" | custom-call | flops 15360000000 | bytes 1024 | tf_op jit(solution)/shard_map/up_back/pallas_call | solution.py:495
  543.7 16.5 %to_width.7.mine_ref = bf16[512,2048]{1,0:T(8,128)(2,1)} custom-call(bf16[512,2048]{1,0:T(8,128)(2,1)} %up_back.2.refs_0_, bf16[512,2048]{1,0:T(8,128)(2,1)} %up_back.3.refs_1_, bf16[512,5120]{1,0:T(8,128)(2,1)} %all-gather.7.cloned.1.call-done.refs_0_.refs_2_.refs_6_, bf16[512,5120]{1,0:T(8,128)(2,1)} %collective-permute-done.18.refs_1_.refs_3_.refs_7_, ...), custom_call_target="tpu_custom_call" | custom-call | flops 24000000000 | bytes 1024 | tf_op jit(solution)/shard_map/to_width/pallas_call | solution.py:538
  563.0 6.6 grad.16
  571.6 6.2 grad.17
  587.7 3.6 fusion
  593.0 15.2 %collective-permute-done.41.theirs_ref = bf16[512,2048]{1,0:T(8,128)(2,1)} collective-permute-done((bf16[512,2048]{1,0:T(8,128)(2,1)}, bf16[512,2048]{1,0:T(8,128)(2,1)}, u32[]{:S(2)}, u32[]{:S(2)}) %collective-permute-start.41) | collective-permute-done | bytes 2097184 | tf_op jit(solution)/shard_map/ppermute | solution.py:49
  608.2 8.0 second.1
  617.5 7.5 heads.3
  625.1 7.0 grad.18
  633.2 3.9 collective-permute-start.44
  637.1 6.1 grad.19
  643.9 3.8 grad.20
  647.8 7.8 collective-permute-done.47.refs_4_
  655.5 6.7 grad.21
  662.7 3.8 collective-permute-done.43.refs_6_
  667.9 11.4 %attend_back.2 = (bf16[3,256,256]{2,1,0:T(8,128)(2,1)}, bf16[3,256,256]{2,1,0:T(8,128)(2,1)}, bf16[3,256,256]{2,1,0:T(8,128)(2,1)}, bf16[3,256,256]{2,1,0:T(8,128)(2,1)}) custom-call(s32[4]{0:T(128)} %copy-done.38, s32[2]{0:T(128)} %length_ref.5, bf16[3,512,256]{2,1,0:T(8,128)(2,1)} %get-tuple-element.264.refs_0_, bf16[3,512,256]{2,1,0:T(8,128)(2,1)} %copy-done.22, ...), custom_call_target="tpu_custom_call" | custom-call | flops 17999998976 | bytes 1024 | tf_op jit(solution)/shard_map/attend_back/pallas_call | solution.py:430
  679.3 14.3 %collective-permute-start.48 = (bf16[3,256,256]{2,1,0:T(8,128)(2,1)}, bf16[3,256,256]{2,1,0:T(8,128)(2,1)S(1)}, u32[]{:S(2)}, u32[]{:S(2)}) collective-permute-start(bf16[3,256,256]{2,1,0:T(8,128)(2,1)} %get-tuple-element.372), channel_id=1, source_target_pairs={{0,6},{2,0},{4,2},{6,4},{1,7},{3,1},{5,3},{7,5},{8,14},{10,8},{12,... | collective-permute-start | bytes 1179656 | tf_op jit(solution)/shard_map/ppermute | solution.py:54
  693.6 6.3 collective-permute-start.49
  700.3 11.3 %attend_back.3 = (bf16[3,256,256]{2,1,0:T(8,128)(2,1)}, bf16[3,256,256]{2,1,0:T(8,128)(2,1)}, bf16[3,256,256]{2,1,0:T(8,128)(2,1)}, bf16[3,256,256]{2,1,0:T(8,128)(2,1)}) custom-call(s32[4]{0:T(128)} %copy-done.38, s32[2]{0:T(128)} %length_ref.5, bf16[3,512,256]{2,1,0:T(8,128)(2,1)} %get-tuple-element.264.refs_0_, bf16[3,512,256]{2,1,0:T(8,128)(2,1)} %copy-done.22, ...), custom_call_target="tpu_custom_call" | custom-call | flops 17999998976 | bytes 1024 | tf_op jit(solution)/shard_map/attend_back/pallas_call | solution.py:430
  713.8 47.7 %collective-permute-done.49.refs_2_ = bf16[3,256,256]{2,1,0:T(8,128)(2,1)S(1)} collective-permute-done((bf16[3,256,256]{2,1,0:T(8,128)(2,1)}, bf16[3,256,256]{2,1,0:T(8,128)(2,1)S(1)}, u32[]{:S(2)}, u32[]{:S(2)}) %collective-permute-start.49) | collective-permute-done | bytes 393248 | tf_op jit(solution)/shard_map/ppermute | solution.py:54
  763.0 3.8 join.4.grad_ref.refs_2_
  768.9 13.0 %own.2 = (f32[3,256,2048]{2,1,0:T(8,128)}, f32[3,16,2048]{2,1,0:T(8,128)}) custom-call(s32[4]{0:T(128)} %get-tuple-element.564.perm_ref, bf16[3,256,1024]{2,1,0:T(8,128)(2,1)} %join.4.grad_ref.refs_2_, f32[4,512,2048]{2,1,0:T(8,128)} %get-tuple-element.235.z_ref, bf16[512,3072]{1,0:T(8,128)(2,1)} %all-gather.5.cloned.1.call-done.refs_0_, ...), custom_call_target="tpu_custom_call" | custom-call | flops 17999998976 | bytes 1024 | tf_op jit(solution)/shard_map/own/pallas_call | solution.py:662
  784.0 15.2 %collective-permute-done.52.refs_2_ = bf16[3,256,256]{2,1,0:T(8,128)(2,1)S(1)} collective-permute-done((bf16[3,256,256]{2,1,0:T(8,128)(2,1)S(1)}, bf16[3,256,256]{2,1,0:T(8,128)(2,1)S(1)}, u32[]{:S(2)}, u32[]{:S(2)}) %collective-permute-start.52) | collective-permute-done | bytes 393248 | tf_op jit(solution)/shard_map/ppermute | solution.py:54
  800.7 3.9 join.5.refs_3_.grad_ref
  804.6 4.3 grad.22
  811.6 6.8 grad.23
  820.8 4.0 grad.24
  825.3 6.3 grad.25
  833.1 13.3 %own.3 = (f32[3,256,2048]{2,1,0:T(8,128)}, f32[3,16,2048]{2,1,0:T(8,128)}) custom-call(s32[4]{0:T(128)} %get-tuple-element.564.perm_ref, bf16[3,256,1024]{2,1,0:T(8,128)(2,1)} %join.5.refs_3_.grad_ref, f32[4,512,2048]{2,1,0:T(8,128)} %get-tuple-element.235.z_ref, bf16[512,3072]{1,0:T(8,128)(2,1)} %all-gather.5.cloned.1.call-done.refs_0_, ...), custom_call_target="tpu_custom_call" | custom-call | flops 17999998976 | bytes 1024 | tf_op jit(solution)/shard_map/own/pallas_call | solution.py:662
  851.2 4.2 grad.26
  855.4 14.3 %other.2.dz_ref = bf16[3,256,2048]{2,1,0:T(8,128)(2,1)} custom-call(bf16[3,256,1024]{2,1,0:T(8,128)(2,1)} %collective-permute-done.56.grad_ref, f32[3,256,2048]{2,1,0:T(8,128)} %get-tuple-element.393.part_ref, f32[4,512,2048]{2,1,0:T(8,128)} %get-tuple-element.235.z_ref, f32[1,2048]{1,0:T(1,128)} %bitcast.182, ...), custom_call_target="tpu_custom_call" | custom-call | flops 20999999488 | bytes 1024 | tf_op jit(solution)/shard_map/other/pallas_call | solution.py:711
  869.7 13.0 %last.2 = (bf16[8,512,2048]{2,1,0:T(8,128)(2,1)}, f32[16,256,128]{2,1,0:T(8,128)}) custom-call(s32[4]{0:T(128)} %get-tuple-element.564.perm_ref, bf16[8,512,2048]{2,1,0:T(8,128)(2,1)} %bitcast.144, f32[16,256,4]{2,1,0:T(8,128)} %bitcast.151, bf16[3,256,2048]{2,1,0:T(8,128)(2,1)} %other.2.dz_ref, bf16[512,2048]{1,0:T(8,128)(2,1)} %get-tuple-element.349.dr_ref), custom_call_target="tpu_custom_call" | custom-call | flops 17999998976 | bytes 1024 | tf_op jit(solution)/shard_map/last/pallas_call | solution.py:767
  882.7 11.9 %collective-permute-done.61.refs_6_ = bf16[1,512,2048]{2,1,0:T(8,128)(2,1)} collective-permute-done((bf16[1,512,2048]{2,1,0:T(8,128)(2,1)}, bf16[1,512,2048]{2,1,0:T(8,128)(2,1)}, u32[]{:S(2)}, u32[]{:S(2)}) %collective-permute-start.61) | collective-permute-done | bytes 2097184 | tf_op jit(solution)/shard_map/ppermute | solution.py:45
  894.6 6.9 grad.27
  904.1 14.5 %other.3.dz_ref = bf16[3,256,2048]{2,1,0:T(8,128)(2,1)} custom-call(bf16[3,256,1024]{2,1,0:T(8,128)(2,1)} %collective-permute-done.54.grad_ref, f32[3,256,2048]{2,1,0:T(8,128)} %get-tuple-element.418.part_ref, f32[4,512,2048]{2,1,0:T(8,128)} %get-tuple-element.235.z_ref, f32[1,2048]{1,0:T(1,128)} %bitcast.183, ...), custom_call_target="tpu_custom_call" | custom-call | flops 420000000 | bytes 1024 | tf_op jit(solution)/shard_map/other/pallas_call | solution.py:711
  923.5 10.2 %collective-permute-done.64 = f32[37,128]{1,0:T(8,128)S(1)} collective-permute-done((f32[37,128]{1,0:T(8,128)S(1)}, f32[37,128]{1,0:T(8,128)S(1)}, u32[]{:S(2)}, u32[]{:S(2)}) %collective-permute-start.64) | collective-permute-done | bytes 18976 | tf_op jit(solution)/shard_map/ppermute | solution.py:1255
  936.9 13.0 %last.3 = (bf16[8,512,2048]{2,1,0:T(8,128)(2,1)}, f32[16,256,128]{2,1,0:T(8,128)}) custom-call(s32[4]{0:T(128)} %get-tuple-element.564.perm_ref, bf16[8,512,2048]{2,1,0:T(8,128)(2,1)} %bitcast.145, f32[16,256,4]{2,1,0:T(8,128)} %bitcast.152, bf16[3,256,2048]{2,1,0:T(8,128)(2,1)} %other.3.dz_ref, ...), custom_call_target="tpu_custom_call", output_to_operand_aliasing={{0}: (5, {}), {1}: (6, {})} | custom-call | flops 360000000 | bytes 1024 | tf_op jit(solution)/shard_map/last/pallas_call | solution.py:767
  (410 shorter events, 164.4 us)
Async XLA Ops:
  7.2 69.2 %all-gather.5.cloned.1.call-start = ((), (), s32[]{:S(2)}) async-start(), calls=%async_computation.7 | async-start | bytes 3932160 | tf_op jit(solution)/shard_map/all_gather | solution.py:88
  9.4 166.0 %all-gather.7.cloned.1.call-start = ((), (), s32[]{:S(2)}) async-start(), calls=%async_computation.8 | async-start | bytes 6553600 | tf_op jit(solution)/shard_map/all_gather | solution.py:88
  9.5 19.6 %collective-permute-start = (bf16[40,128]{1,0:T(8,128)(2,1)S(1)}, bf16[40,128]{1,0:T(8,128)(2,1)S(1)}, u32[]{:S(2)}, u32[]{:S(2)}) collective-permute-start(bf16[40,128]{1,0:T(8,128)(2,1)S(1)} %concatenate.45), channel_id=1, source_target_pairs={{0,2},{2,4},{4,6},{6,0},{1,3},{3,5},{5,7},{7,1},{8,10},{10,12},{12... | collective-permute-start | bytes 30728 | tf_op jit(solution)/shard_map/ppermute | solution.py:54
  12.6 16.6 %collective-permute-start.1 = (bf16[40,128]{1,0:T(8,128)(2,1)S(1)}, bf16[40,128]{1,0:T(8,128)(2,1)S(1)}, u32[]{:S(2)}, u32[]{:S(2)}) collective-permute-start(bf16[40,128]{1,0:T(8,128)(2,1)S(1)} %concatenate.45), channel_id=1, source_target_pairs={{0,4},{2,6},{4,0},{6,2},{1,5},{3,7},{5,1},{7,3},{8,12},{10,14},{12... | collective-permute-start | bytes 30728 | tf_op jit(solution)/shard_map/ppermute | solution.py:54
  15.2 14.0 %collective-permute-start.2 = (bf16[40,128]{1,0:T(8,128)(2,1)S(1)}, bf16[40,128]{1,0:T(8,128)(2,1)S(1)}, u32[]{:S(2)}, u32[]{:S(2)}) collective-permute-start(bf16[40,128]{1,0:T(8,128)(2,1)S(1)} %concatenate.45), channel_id=1, source_target_pairs={{0,6},{2,0},{4,2},{6,4},{1,7},{3,1},{5,3},{7,5},{8,14},{10,8},{12,... | collective-permute-start | bytes 30728 | tf_op jit(solution)/shard_map/ppermute | solution.py:54
  68.8 254.0 %all-gather.9.cloned.1.call-start = ((), (), s32[]{:S(2)}) async-start(), calls=%async_computation.9 | async-start | bytes 2621440 | tf_op jit(solution)/shard_map/all_gather | solution.py:88
  76.5 70.8 %collective-permute-start.9 = (bf16[512,3072]{1,0:T(8,128)(2,1)}, bf16[512,3072]{1,0:T(8,128)(2,1)}, u32[]{:S(2)}, u32[]{:S(2)}) collective-permute-start(bf16[512,3072]{1,0:T(8,128)(2,1)} %all-gather.5.cloned.1.call-done.refs_0_), channel_id=1, source_target_pairs={{0,1},{1,0},{2,3},{3,2},{4,5},{5,4},{6,7},{7,6},{8,9},{9,8},{10,11... | collective-permute-start | bytes 9437192 | tf_op jit(solution)/shard_map/ppermute | solution.py:49
  77.9 70.5 %collective-permute-start.8 = (bf16[512,3072]{1,0:T(8,128)(2,1)}, bf16[512,3072]{1,0:T(8,128)(2,1)}, u32[]{:S(2)}, u32[]{:S(2)}) collective-permute-start(bf16[512,3072]{1,0:T(8,128)(2,1)} %all-gather.5.cloned.1.call-done.refs_0_), channel_id=1, source_target_pairs={{0,16},{8,24},{16,0},{24,8},{1,17},{9,25},{17,1},{25,9},{2,18},{10... | collective-permute-start | bytes 9437192 | tf_op jit(solution)/shard_map/ppermute | solution.py:45
  149.0 82.9 %collective-permute-start.14 = (bf16[512,3072]{1,0:T(8,128)(2,1)}, bf16[512,3072]{1,0:T(8,128)(2,1)}, u32[]{:S(2)}, u32[]{:S(2)}) collective-permute-start(bf16[512,3072]{1,0:T(8,128)(2,1)} %collective-permute-done.8.refs_1_), channel_id=1, source_target_pairs={{0,1},{1,0},{2,3},{3,2},{4,5},{5,4},{6,7},{7,6},{8,9},{9,8},{10,11... | collective-permute-start | bytes 9437192 | tf_op jit(solution)/shard_map/ppermute | solution.py:49
  175.3 140.1 %collective-permute-start.18 = (bf16[512,5120]{1,0:T(8,128)(2,1)}, bf16[512,5120]{1,0:T(8,128)(2,1)}, u32[]{:S(2)}, u32[]{:S(2)}) collective-permute-start(bf16[512,5120]{1,0:T(8,128)(2,1)} %all-gather.7.cloned.1.call-done.refs_0_.refs_2_.refs_6_), channel_id=1, source_target_pairs={{0,16},{8,24},{16,0},{24,8},{1,17},{9,25},{17,1},{25,9},{2,18},{10... | collective-permute-start | bytes 15728648 | tf_op jit(solution)/shard_map/ppermute | solution.py:45
  176.8 22.6 %collective-permute-start.11 = (bf16[3,512,256]{2,1,0:T(8,128)(2,1)}, bf16[3,512,256]{2,1,0:T(8,128)(2,1)S(1)}, u32[]{:S(2)}, u32[]{:S(2)}) collective-permute-start(bf16[3,512,256]{2,1,0:T(8,128)(2,1)} %get-tuple-element.254), channel_id=1, source_target_pairs={{0,2},{2,4},{4,6},{6,0},{1,3},{3,5},{5,7},{7,1},{8,10},{10,12},{12... | collective-permute-start | bytes 2359304 | tf_op jit(solution)/shard_map/ppermute | solution.py:54
  176.8 55.0 %collective-permute-start.12 = (bf16[3,512,256]{2,1,0:T(8,128)(2,1)}, bf16[3,512,256]{2,1,0:T(8,128)(2,1)S(1)}, u32[]{:S(2)}, u32[]{:S(2)}) collective-permute-start(bf16[3,512,256]{2,1,0:T(8,128)(2,1)} %get-tuple-element.255), channel_id=1, source_target_pairs={{0,4},{2,6},{4,0},{6,2},{1,5},{3,7},{5,1},{7,3},{8,12},{10,14},{12... | collective-permute-start | bytes 2359304 | tf_op jit(solution)/shard_map/ppermute | solution.py:54
  178.1 53.8 %collective-permute-start.13 = (bf16[3,512,256]{2,1,0:T(8,128)(2,1)}, bf16[3,512,256]{2,1,0:T(8,128)(2,1)S(1)}, u32[]{:S(2)}, u32[]{:S(2)}) collective-permute-start(bf16[3,512,256]{2,1,0:T(8,128)(2,1)} %get-tuple-element.256), channel_id=1, source_target_pairs={{0,6},{2,0},{4,2},{6,4},{1,7},{3,1},{5,3},{7,5},{8,14},{10,8},{12,... | collective-permute-start | bytes 2359304 | tf_op jit(solution)/shard_map/ppermute | solution.py:54
  246.7 125.2 %all-gather.11.cloned.1.call-start = ((), (), s32[]{:S(2)}) async-start(), calls=%async_computation.10 | async-start | bytes 2621440 | tf_op jit(solution)/shard_map/all_gather | solution.py:88
  246.8 24.9 %collective-permute-start.15 = (bf16[1,512,256]{2,1,0:T(8,128)(2,1)S(1)}, bf16[1,512,256]{2,1,0:T(8,128)(2,1)S(1)}, u32[]{:S(2)}, u32[]{:S(2)}) collective-permute-start(bf16[1,512,256]{2,1,0:T(8,128)(2,1)S(1)} %copy-done.69), channel_id=1, source_target_pairs={{0,6},{2,0},{4,2},{6,4},{1,7},{3,1},{5,3},{7,5},{8,14},{10,8},{12,... | collective-permute-start | bytes 786440 | tf_op jit(solution)/shard_map/ppermute | solution.py:54
  263.2 47.3 %collective-permute-start.16 = (bf16[1,512,256]{2,1,0:T(8,128)(2,1)S(1)}, bf16[1,512,256]{2,1,0:T(8,128)(2,1)S(1)}, u32[]{:S(2)}, u32[]{:S(2)}) collective-permute-start(bf16[1,512,256]{2,1,0:T(8,128)(2,1)S(1)} %copy-done.68), channel_id=1, source_target_pairs={{0,4},{2,6},{4,0},{6,2},{1,5},{3,7},{5,1},{7,3},{8,12},{10,14},{12... | collective-permute-start | bytes 786440 | tf_op jit(solution)/shard_map/ppermute | solution.py:54
  264.3 46.1 %collective-permute-start.17 = (bf16[1,512,256]{2,1,0:T(8,128)(2,1)S(1)}, bf16[1,512,256]{2,1,0:T(8,128)(2,1)S(1)}, u32[]{:S(2)}, u32[]{:S(2)}) collective-permute-start(bf16[1,512,256]{2,1,0:T(8,128)(2,1)S(1)} %copy-done.67), channel_id=1, source_target_pairs={{0,2},{2,4},{4,6},{6,0},{1,3},{3,5},{5,7},{7,1},{8,10},{10,12},{12... | collective-permute-start | bytes 786440 | tf_op jit(solution)/shard_map/ppermute | solution.py:54
  322.9 16.4 %collective-permute-start.24 = (bf16[512,5120]{1,0:T(8,128)(2,1)}, bf16[512,5120]{1,0:T(8,128)(2,1)}, u32[]{:S(2)}, u32[]{:S(2)}) collective-permute-start(bf16[512,5120]{1,0:T(8,128)(2,1)} %collective-permute-done.18.refs_1_.refs_3_.refs_7_), channel_id=1, source_target_pairs={{0,8},{8,0},{16,24},{24,16},{1,9},{9,1},{17,25},{25,17},{2,10},{10... | collective-permute-start | bytes 15728648 | tf_op jit(solution)/shard_map/ppermute | solution.py:45
  323.3 388.3 %reduce-scatter.8.cloned.1.call-start = ((), (), s32[]{:S(2)}) async-start(), calls=%async_computation.11 | async-start | bytes 2621440 | tf_op jit(solution)/shard_map/reduce_scatter | solution.py:135
  323.4 48.1 %collective-permute-start.22 = (bf16[512,2048]{1,0:T(8,128)(2,1)}, bf16[512,2048]{1,0:T(8,128)(2,1)}, u32[]{:S(2)}, u32[]{:S(2)}) collective-permute-start(bf16[512,2048]{1,0:T(8,128)(2,1)} %all-gather.9.cloned.1.call-done.refs_1_.refs_0_), channel_id=1, source_target_pairs={{0,16},{8,24},{16,0},{24,8},{1,17},{9,25},{17,1},{25,9},{2,18},{10... | collective-permute-start | bytes 6291464 | tf_op jit(solution)/shard_map/ppermute | solution.py:45
  330.1 47.7 %collective-permute-start.21 = (bf16[512,2048]{1,0:T(8,128)(2,1)}, bf16[512,2048]{1,0:T(8,128)(2,1)}, u32[]{:S(2)}, u32[]{:S(2)}) collective-permute-start(bf16[512,2048]{1,0:T(8,128)(2,1)} %to_width.4), channel_id=1, source_target_pairs={{0,1},{1,0},{2,3},{3,2},{4,5},{5,4},{6,7},{7,6},{8,9},{9,8},{10,11... | collective-permute-start | bytes 6291464 | tf_op jit(solution)/shard_map/ppermute | solution.py:49
  331.6 78.6 %collective-permute-start.26 = (bf16[512,3072]{1,0:T(8,128)(2,1)}, bf16[512,3072]{1,0:T(8,128)(2,1)S(1)}, u32[]{:S(2)}, u32[]{:S(2)}) collective-permute-start(bf16[512,3072]{1,0:T(8,128)(2,1)} %collective-permute-done.9.refs_0_), channel_id=1, source_target_pairs={{0,8},{8,0},{16,24},{24,16},{1,9},{9,1},{17,25},{25,17},{2,10},{10... | collective-permute-start | bytes 9437192 | tf_op jit(solution)/shard_map/ppermute | solution.py:45
  331.8 78.5 %collective-permute-start.27 = (bf16[512,3072]{1,0:T(8,128)(2,1)}, bf16[512,3072]{1,0:T(8,128)(2,1)}, u32[]{:S(2)}, u32[]{:S(2)}) collective-permute-start(bf16[512,3072]{1,0:T(8,128)(2,1)} %collective-permute-done.14.refs_1_), channel_id=1, source_target_pairs={{0,8},{8,0},{16,24},{24,16},{1,9},{9,1},{17,25},{25,17},{2,10},{10... | collective-permute-start | bytes 9437192 | tf_op jit(solution)/shard_map/ppermute | solution.py:45
  371.4 38.8 %collective-permute-start.28 = (bf16[512,2048]{1,0:T(8,128)(2,1)}, bf16[512,2048]{1,0:T(8,128)(2,1)}, u32[]{:S(2)}, u32[]{:S(2)}) collective-permute-start(bf16[512,2048]{1,0:T(8,128)(2,1)} %all-gather.9.cloned.1.call-done.refs_1_.refs_0_), channel_id=1, source_target_pairs={{0,8},{8,0},{16,24},{24,16},{1,9},{9,1},{17,25},{25,17},{2,10},{10... | collective-permute-start | bytes 6291464 | tf_op jit(solution)/shard_map/ppermute | solution.py:45
  371.4 38.8 %collective-permute-start.29 = (bf16[512,2048]{1,0:T(8,128)(2,1)}, bf16[512,2048]{1,0:T(8,128)(2,1)}, u32[]{:S(2)}, u32[]{:S(2)}) collective-permute-start(bf16[512,2048]{1,0:T(8,128)(2,1)} %collective-permute-done.22.refs_2_.refs_1_), channel_id=1, source_target_pairs={{0,8},{8,0},{16,24},{24,16},{1,9},{9,1},{17,25},{25,17},{2,10},{10... | collective-permute-start | bytes 6291464 | tf_op jit(solution)/shard_map/ppermute | solution.py:45
  377.8 46.7 %collective-permute-start.25 = (bf16[512,2048]{1,0:T(8,128)(2,1)}, bf16[512,2048]{1,0:T(8,128)(2,1)S(1)}, u32[]{:S(2)}, u32[]{:S(2)}) collective-permute-start(bf16[512,2048]{1,0:T(8,128)(2,1)} %all-gather.11.cloned.1.call-done.refs_1_.refs_0_), channel_id=1, source_target_pairs={{0,16},{8,24},{16,0},{24,8},{1,17},{9,25},{17,1},{25,9},{2,18},{10... | collective-permute-start | bytes 6291464 | tf_op jit(solution)/shard_map/ppermute | solution.py:45
  443.1 48.0 %collective-permute-start.32 = (bf16[512,2048]{1,0:T(8,128)(2,1)}, bf16[512,2048]{1,0:T(8,128)(2,1)}, u32[]{:S(2)}, u32[]{:S(2)}) collective-permute-start(bf16[512,2048]{1,0:T(8,128)(2,1)} %to_width.6.mine_ref), channel_id=1, source_target_pairs={{0,1},{1,0},{2,3},{3,2},{4,5},{5,4},{6,7},{7,6},{8,9},{9,8},{10,11... | collective-permute-start | bytes 6291464 | tf_op jit(solution)/shard_map/ppermute | solution.py:49
  444.5 63.1 %collective-permute-start.34 = (bf16[512,2048]{1,0:T(8,128)(2,1)}, bf16[512,2048]{1,0:T(8,128)(2,1)}, u32[]{:S(2)}, u32[]{:S(2)}) collective-permute-start(bf16[512,2048]{1,0:T(8,128)(2,1)} %get-tuple-element.314.refs_0_), channel_id=1, source_target_pairs={{0,8},{8,0},{16,24},{24,16},{1,9},{9,1},{17,25},{25,17},{2,10},{10... | collective-permute-start | bytes 6291464 | tf_op jit(solution)/shard_map/ppermute | solution.py:45
  444.5 63.1 %collective-permute-start.33 = (bf16[512,2048]{1,0:T(8,128)(2,1)}, bf16[512,2048]{1,0:T(8,128)(2,1)}, u32[]{:S(2)}, u32[]{:S(2)}) collective-permute-start(bf16[512,2048]{1,0:T(8,128)(2,1)} %get-tuple-element.309.refs_0_), channel_id=1, source_target_pairs={{0,8},{8,0},{16,24},{24,16},{1,9},{9,1},{17,25},{25,17},{2,10},{10... | collective-permute-start | bytes 6291464 | tf_op jit(solution)/shard_map/ppermute | solution.py:45
  451.3 56.3 %collective-permute-start.36 = (bf16[512,1024]{1,0:T(8,128)(2,1)S(1)}, bf16[512,1024]{1,0:T(8,128)(2,1)}, u32[]{:S(2)}, u32[]{:S(2)}) collective-permute-start(bf16[512,1024]{1,0:T(8,128)(2,1)S(1)} %bitcast.159), channel_id=1, source_target_pairs={{0,8},{8,0},{16,24},{24,16},{1,9},{9,1},{17,25},{25,17},{2,10},{10... | collective-permute-start | bytes 3145736 | tf_op jit(solution)/shard_map/ppermute | solution.py:45
  452.4 55.2 %collective-permute-start.35 = (bf16[512,1024]{1,0:T(8,128)(2,1)}, bf16[512,1024]{1,0:T(8,128)(2,1)S(1)}, u32[]{:S(2)}, u32[]{:S(2)}) collective-permute-start(bf16[512,1024]{1,0:T(8,128)(2,1)} %slice.137), channel_id=1, source_target_pairs={{0,8},{8,0},{16,24},{24,16},{1,9},{9,1},{17,25},{25,17},{2,10},{10... | collective-permute-start | bytes 3145736 | tf_op jit(solution)/shard_map/ppermute | solution.py:45
  514.7 48.3 %collective-permute-start.40 = (bf16[1,512,2048]{2,1,0:T(8,128)(2,1)}, bf16[1,512,2048]{2,1,0:T(8,128)(2,1)}, u32[]{:S(2)}, u32[]{:S(2)}) collective-permute-start(bf16[1,512,2048]{2,1,0:T(8,128)(2,1)} %grad.14), channel_id=1, source_target_pairs={{0,16},{8,24},{16,0},{24,8},{1,17},{9,25},{17,1},{25,9},{2,18},{10... | collective-permute-start | bytes 6291464 | tf_op jit(solution)/shard_map/ppermute | solution.py:45
  543.2 26.4 %collective-permute-start.39 = (bf16[512,2048]{1,0:T(8,128)(2,1)}, bf16[512,2048]{1,0:T(8,128)(2,1)S(1)}, u32[]{:S(2)}, u32[]{:S(2)}) collective-permute-start(bf16[512,2048]{1,0:T(8,128)(2,1)} %up_back.3.refs_1_), channel_id=1, source_target_pairs={{0,8},{8,0},{16,24},{24,16},{1,9},{9,1},{17,25},{25,17},{2,10},{10... | collective-permute-start | bytes 6291464 | tf_op jit(solution)/shard_map/ppermute | solution.py:45
  543.4 26.3 %collective-permute-start.38 = (bf16[512,2048]{1,0:T(8,128)(2,1)S(1)}, bf16[512,2048]{1,0:T(8,128)(2,1)S(1)}, u32[]{:S(2)}, u32[]{:S(2)}) collective-permute-start(bf16[512,2048]{1,0:T(8,128)(2,1)S(1)} %copy-done.47), channel_id=1, source_target_pairs={{0,8},{8,0},{16,24},{24,16},{1,9},{9,1},{17,25},{25,17},{2,10},{10... | collective-permute-start | bytes 6291464 | tf_op jit(solution)/shard_map/ppermute | solution.py:45
  560.2 48.0 %collective-permute-start.41 = (bf16[512,2048]{1,0:T(8,128)(2,1)}, bf16[512,2048]{1,0:T(8,128)(2,1)}, u32[]{:S(2)}, u32[]{:S(2)}) collective-permute-start(bf16[512,2048]{1,0:T(8,128)(2,1)} %to_width.7.mine_ref), channel_id=1, source_target_pairs={{0,1},{1,0},{2,3},{3,2},{4,5},{5,4},{6,7},{7,6},{8,9},{9,8},{10,11... | collective-permute-start | bytes 6291464 | tf_op jit(solution)/shard_map/ppermute | solution.py:49
  561.8 63.3 %collective-permute-start.46 = (bf16[1,512,2048]{2,1,0:T(8,128)(2,1)}, bf16[1,512,2048]{2,1,0:T(8,128)(2,1)}, u32[]{:S(2)}, u32[]{:S(2)}) collective-permute-start(bf16[1,512,2048]{2,1,0:T(8,128)(2,1)} %grad.15), channel_id=1, source_target_pairs={{0,16},{8,24},{16,0},{24,8},{1,17},{9,25},{17,1},{25,9},{2,18},{10... | collective-permute-start | bytes 6291464 | tf_op jit(solution)/shard_map/ppermute | solution.py:45
  577.8 77.7 %collective-permute-start.47 = (bf16[1,512,2048]{2,1,0:T(8,128)(2,1)}, bf16[1,512,2048]{2,1,0:T(8,128)(2,1)}, u32[]{:S(2)}, u32[]{:S(2)}) collective-permute-start(bf16[1,512,2048]{2,1,0:T(8,128)(2,1)} %grad.17), channel_id=1, source_target_pairs={{0,16},{8,24},{16,0},{24,8},{1,17},{9,25},{17,1},{25,9},{2,18},{10... | collective-permute-start | bytes 6291464 | tf_op jit(solution)/shard_map/ppermute | solution.py:45
  579.9 202.0 %reduce-scatter.10.cloned.1.call-start = ((), (), s32[]{:S(2)}) async-start(), calls=%async_computation.12 | async-start | bytes 2621440 | tf_op jit(solution)/shard_map/reduce_scatter | solution.py:135
  632.1 186.6 %reduce-scatter.14.cloned.1.call-start = ((), (), s32[]{:S(2)}) async-start(), calls=%async_computation.14 | async-start | bytes 2621440 | tf_op jit(solution)/shard_map/reduce_scatter | solution.py:135
  633.0 29.7 %collective-permute-start.42 = (bf16[1,512,256]{2,1,0:T(8,128)(2,1)S(1)}, bf16[1,512,256]{2,1,0:T(8,128)(2,1)S(1)}, u32[]{:S(2)}, u32[]{:S(2)}) collective-permute-start(bf16[1,512,256]{2,1,0:T(8,128)(2,1)S(1)} %copy-done.66), channel_id=1, source_target_pairs={{0,2},{2,4},{4,6},{6,0},{1,3},{3,5},{5,7},{7,1},{8,10},{10,12},{12... | collective-permute-start | bytes 786440 | tf_op jit(solution)/shard_map/ppermute | solution.py:54
  633.1 33.4 %collective-permute-start.43 = (bf16[1,512,256]{2,1,0:T(8,128)(2,1)S(1)}, bf16[1,512,256]{2,1,0:T(8,128)(2,1)S(1)}, u32[]{:S(2)}, u32[]{:S(2)}) collective-permute-start(bf16[1,512,256]{2,1,0:T(8,128)(2,1)S(1)} %copy-done.65), channel_id=1, source_target_pairs={{0,4},{2,6},{4,0},{6,2},{1,5},{3,7},{5,1},{7,3},{8,12},{10,14},{12... | collective-permute-start | bytes 786440 | tf_op jit(solution)/shard_map/ppermute | solution.py:54
  633.2 33.3 %collective-permute-start.44 = (bf16[1,512,256]{2,1,0:T(8,128)(2,1)S(1)}, bf16[1,512,256]{2,1,0:T(8,128)(2,1)S(1)}, u32[]{:S(2)}, u32[]{:S(2)}) collective-permute-start(bf16[1,512,256]{2,1,0:T(8,128)(2,1)S(1)} %copy-done.64), channel_id=1, source_target_pairs={{0,6},{2,0},{4,2},{6,4},{1,7},{3,1},{5,3},{7,5},{8,14},{10,8},{12,... | collective-permute-start | bytes 786440 | tf_op jit(solution)/shard_map/ppermute | solution.py:54
  643.2 168.4 %collective-permute-start.59 = (bf16[1,512,2048]{2,1,0:T(8,128)(2,1)}, bf16[1,512,2048]{2,1,0:T(8,128)(2,1)}, u32[]{:S(2)}, u32[]{:S(2)}) collective-permute-start(bf16[1,512,2048]{2,1,0:T(8,128)(2,1)} %grad.19), channel_id=1, source_target_pairs={{0,16},{8,24},{16,0},{24,8},{1,17},{9,25},{17,1},{25,9},{2,18},{10... | collective-permute-start | bytes 6291464 | tf_op jit(solution)/shard_map/ppermute | solution.py:45
  662.2 142.4 %collective-permute-start.55 = (bf16[1,512,1024]{2,1,0:T(8,128)(2,1)}, bf16[1,512,1024]{2,1,0:T(8,128)(2,1)}, u32[]{:S(2)}, u32[]{:S(2)}) collective-permute-start(bf16[1,512,1024]{2,1,0:T(8,128)(2,1)} %grad.20), channel_id=1, source_target_pairs={{0,16},{8,24},{16,0},{24,8},{1,17},{9,25},{17,1},{25,9},{2,18},{10... | collective-permute-start | bytes 3145736 | tf_op jit(solution)/shard_map/ppermute | solution.py:45
  679.3 34.5 %collective-permute-start.48 = (bf16[3,256,256]{2,1,0:T(8,128)(2,1)}, bf16[3,256,256]{2,1,0:T(8,128)(2,1)S(1)}, u32[]{:S(2)}, u32[]{:S(2)}) collective-permute-start(bf16[3,256,256]{2,1,0:T(8,128)(2,1)} %get-tuple-element.372), channel_id=1, source_target_pairs={{0,6},{2,0},{4,2},{6,4},{1,7},{3,1},{5,3},{7,5},{8,14},{10,8},{12,... | collective-permute-start | bytes 1179656 | tf_op jit(solution)/shard_map/ppermute | solution.py:54
  693.6 68.0 %collective-permute-start.49 = (bf16[3,256,256]{2,1,0:T(8,128)(2,1)}, bf16[3,256,256]{2,1,0:T(8,128)(2,1)S(1)}, u32[]{:S(2)}, u32[]{:S(2)}) collective-permute-start(bf16[3,256,256]{2,1,0:T(8,128)(2,1)} %get-tuple-element.373), channel_id=1, source_target_pairs={{0,4},{2,6},{4,0},{6,2},{1,5},{3,7},{5,1},{7,3},{8,12},{10,14},{12... | collective-permute-start | bytes 1179656 | tf_op jit(solution)/shard_map/ppermute | solution.py:54
  699.8 61.7 %collective-permute-start.50 = (bf16[3,256,256]{2,1,0:T(8,128)(2,1)}, bf16[3,256,256]{2,1,0:T(8,128)(2,1)S(1)}, u32[]{:S(2)}, u32[]{:S(2)}) collective-permute-start(bf16[3,256,256]{2,1,0:T(8,128)(2,1)} %get-tuple-element.374), channel_id=1, source_target_pairs={{0,2},{2,4},{4,6},{6,0},{1,3},{3,5},{5,7},{7,1},{8,10},{10,12},{12... | collective-permute-start | bytes 1179656 | tf_op jit(solution)/shard_map/ppermute | solution.py:54
  699.8 148.3 %reduce-scatter.12.cloned.1.call-start = ((), (), s32[]{:S(2)}) async-start(), calls=%async_computation.13 | async-start | bytes 1310720 | tf_op jit(solution)/shard_map/reduce_scatter | solution.py:135
  766.8 17.2 %collective-permute-start.51 = (bf16[3,256,256]{2,1,0:T(8,128)(2,1)S(1)}, bf16[3,256,256]{2,1,0:T(8,128)(2,1)S(1)}, u32[]{:S(2)}, u32[]{:S(2)}) collective-permute-start(bf16[3,256,256]{2,1,0:T(8,128)(2,1)S(1)} %copy-done.54), channel_id=1, source_target_pairs={{0,6},{2,0},{4,2},{6,4},{1,7},{3,1},{5,3},{7,5},{8,14},{10,8},{12,... | collective-permute-start | bytes 1179656 | tf_op jit(solution)/shard_map/ppermute | solution.py:54
  766.8 32.4 %collective-permute-start.52 = (bf16[3,256,256]{2,1,0:T(8,128)(2,1)S(1)}, bf16[3,256,256]{2,1,0:T(8,128)(2,1)S(1)}, u32[]{:S(2)}, u32[]{:S(2)}) collective-permute-start(bf16[3,256,256]{2,1,0:T(8,128)(2,1)S(1)} %copy-done.53), channel_id=1, source_target_pairs={{0,4},{2,6},{4,0},{6,2},{1,5},{3,7},{5,1},{7,3},{8,12},{10,14},{12... | collective-permute-start | bytes 1179656 | tf_op jit(solution)/shard_map/ppermute | solution.py:54
  766.9 32.3 %collective-permute-start.53 = (bf16[3,256,256]{2,1,0:T(8,128)(2,1)S(1)}, bf16[3,256,256]{2,1,0:T(8,128)(2,1)S(1)}, u32[]{:S(2)}, u32[]{:S(2)}) collective-permute-start(bf16[3,256,256]{2,1,0:T(8,128)(2,1)S(1)} %copy-done.52), channel_id=1, source_target_pairs={{0,2},{2,4},{4,6},{6,0},{1,3},{3,5},{5,7},{7,1},{8,10},{10,12},{12... | collective-permute-start | bytes 1179656 | tf_op jit(solution)/shard_map/ppermute | solution.py:54
  809.0 112.4 %reduce-scatter.16.cloned.1.call-start = ((), (), s32[]{:S(2)}) async-start(), calls=%async_computation.15 | async-start | bytes 2621440 | tf_op jit(solution)/shard_map/reduce_scatter | solution.py:135
  809.0 11.8 %collective-permute-start.57 = (bf16[3,256,1024]{2,1,0:T(8,128)(2,1)S(1)}, bf16[3,256,1024]{2,1,0:T(8,128)(2,1)}, u32[]{:S(2)}, u32[]{:S(2)}) collective-permute-start(bf16[3,256,1024]{2,1,0:T(8,128)(2,1)S(1)} %copy-done.6), channel_id=1, source_target_pairs={{0,8},{8,0},{16,24},{24,16},{1,9},{9,1},{17,25},{25,17},{2,10},{10... | collective-permute-start | bytes 4718600 | tf_op jit(solution)/shard_map/ppermute | solution.py:45
  809.6 37.4 %collective-permute-start.56 = (bf16[3,256,1024]{2,1,0:T(8,128)(2,1)S(1)}, bf16[3,256,1024]{2,1,0:T(8,128)(2,1)}, u32[]{:S(2)}, u32[]{:S(2)}) collective-permute-start(bf16[3,256,1024]{2,1,0:T(8,128)(2,1)S(1)} %copy-done.6), channel_id=1, source_target_pairs={{0,1},{1,0},{2,3},{3,2},{4,5},{5,4},{6,7},{7,6},{8,9},{9,8},{10,11... | collective-permute-start | bytes 4718600 | tf_op jit(solution)/shard_map/ppermute | solution.py:49
  811.2 71.5 %collective-permute-start.54 = (bf16[3,256,1024]{2,1,0:T(8,128)(2,1)S(1)}, bf16[3,256,1024]{2,1,0:T(8,128)(2,1)}, u32[]{:S(2)}, u32[]{:S(2)}) collective-permute-start(bf16[3,256,1024]{2,1,0:T(8,128)(2,1)S(1)} %copy-done.7), channel_id=1, source_target_pairs={{0,1},{1,0},{2,3},{3,2},{4,5},{5,4},{6,7},{7,6},{8,9},{9,8},{10,11... | collective-permute-start | bytes 4718600 | tf_op jit(solution)/shard_map/ppermute | solution.py:49
  818.4 144.5 %reduce-scatter.18.cloned.1.call-start = ((), (), s32[]{:S(2)}) async-start(), calls=%async_computation.16 | async-start | bytes 1310720 | tf_op jit(solution)/shard_map/reduce_scatter | solution.py:135
  824.8 26.4 %collective-permute-start.60 = (bf16[1,512,1024]{2,1,0:T(8,128)(2,1)}, bf16[1,512,1024]{2,1,0:T(8,128)(2,1)}, u32[]{:S(2)}, u32[]{:S(2)}) collective-permute-start(bf16[1,512,1024]{2,1,0:T(8,128)(2,1)} %grad.24), channel_id=1, source_target_pairs={{0,16},{8,24},{16,0},{24,8},{1,17},{9,25},{17,1},{25,9},{2,18},{10... | collective-permute-start | bytes 3145736 | tf_op jit(solution)/shard_map/ppermute | solution.py:45
  831.6 63.0 %collective-permute-start.61 = (bf16[1,512,2048]{2,1,0:T(8,128)(2,1)}, bf16[1,512,2048]{2,1,0:T(8,128)(2,1)}, u32[]{:S(2)}, u32[]{:S(2)}) collective-permute-start(bf16[1,512,2048]{2,1,0:T(8,128)(2,1)} %grad.25), channel_id=1, source_target_pairs={{0,16},{8,24},{16,0},{24,8},{1,17},{9,25},{17,1},{25,9},{2,18},{10... | collective-permute-start | bytes 6291464 | tf_op jit(solution)/shard_map/ppermute | solution.py:45
  869.7 95.1 %reduce-scatter.20.cloned.1.call-start = ((), (), s32[]{:S(2)}) async-start(), calls=%async_computation.17 | async-start | bytes 2621440 | tf_op jit(solution)/shard_map/reduce_scatter | solution.py:135
  902.5 16.1 %collective-permute-start.62 = (f32[2,2048]{1,0:T(2,128)S(1)}, f32[2,2048]{1,0:T(2,128)S(1)}, u32[]{:S(2)}, u32[]{:S(2)}) collective-permute-start(f32[2,2048]{1,0:T(2,128)S(1)} %bitcast_reduce_fusion.1), channel_id=1, source_target_pairs={{0,1},{1,0},{2,3},{3,2},{4,5},{5,4},{6,7},{7,6},{8,9},{9,8},{10,11... | collective-permute-start | bytes 49160 | tf_op jit(solution)/shard_map/ppermute | solution.py:49
  919.3 14.5 %collective-permute-start.63 = (f32[2,4,40,128]{3,2,1,0:T(8,128)S(1)}, f32[2,4,40,128]{3,2,1,0:T(8,128)S(1)}, u32[]{:S(2)}, u32[]{:S(2)}) collective-permute-start(f32[2,4,40,128]{3,2,1,0:T(8,128)S(1)} %slice.140), channel_id=1, source_target_pairs={{0,2},{2,0},{4,6},{6,4},{1,3},{3,1},{5,7},{7,5},{8,10},{10,8},{12,... | collective-permute-start | bytes 491528 | tf_op jit(solution)/shard_map/ppermute | solution.py:1255
  919.4 14.4 %collective-permute-start.64 = (f32[37,128]{1,0:T(8,128)S(1)}, f32[37,128]{1,0:T(8,128)S(1)}, u32[]{:S(2)}, u32[]{:S(2)}) collective-permute-start(f32[37,128]{1,0:T(8,128)S(1)} %pad.22), channel_id=1, source_target_pairs={{0,2},{2,0},{4,6},{6,4},{1,3},{3,1},{5,7},{7,5},{8,10},{10,8},{12,... | collective-permute-start | bytes 56840 | tf_op jit(solution)/shard_map/ppermute | solution.py:1255
  933.8 16.1 %collective-permute-start.65 = (f32[1,4,40,128]{3,2,1,0:T(8,128)S(1)}, f32[1,4,40,128]{3,2,1,0:T(8,128)S(1)}, u32[]{:S(2)}, u32[]{:S(2)}) collective-permute-start(f32[1,4,40,128]{3,2,1,0:T(8,128)S(1)} %slice.165), channel_id=1, source_target_pairs={{0,4},{2,6},{4,0},{6,2},{1,5},{3,7},{5,1},{7,3},{8,12},{10,14},{12... | collective-permute-start | bytes 245768 | tf_op jit(solution)/shard_map/ppermute | solution.py:1255
  933.9 15.9 %collective-permute-start.66 = (f32[37,128]{1,0:T(8,128)S(1)}, f32[37,128]{1,0:T(8,128)S(1)}, u32[]{:S(2)}, u32[]{:S(2)}) collective-permute-start(f32[37,128]{1,0:T(8,128)S(1)} %add.235), channel_id=1, source_target_pairs={{0,4},{2,6},{4,0},{6,2},{1,5},{3,7},{5,1},{7,3},{8,12},{10,14},{12... | collective-permute-start | bytes 56840 | tf_op jit(solution)/shard_map/ppermute | solution.py:1255
  (90 other events, 1328.9 us)
Sparse Core Ops, SparseCore 0:
  10.2 66.2 all-gather.4
  78.6 96.6 all-gather.6
  246.8 74.0 all-gather.8
  323.4 43.4 all-gather.10
  580.0 41.5 reduce-scatter.7
  632.2 59.6 reduce-scatter.9
  700.0 64.8 reduce-scatter.13
  809.1 24.5 reduce-scatter.11
  836.0 42.4 reduce-scatter.15
  880.8 26.4 reduce-scatter.17
  909.5 48.5 reduce-scatter.19

commit v5 on v4

--- a/solution.py
+++ b/solution.py
@@ -1140,8 +1140,7 @@
         Scatter(order, grad_down_b[None], [a[None]], grad_down_far[None], [f[None]])
         for a, f in zip(active, active_far)
     ]
-    for d in down:
-        d.launch()
+    down[0].launch()
     grad_upward, upward_far = [], []
     for n in range(2):
         grad_upward.append(
@@ -1150,6 +1149,7 @@
         upward_far.append(over_fsdp(grad_upward[n], 1))
     normed_mine = order.keep(to_width(order(grad_upward), [blocks_up] * 2, width, (), BF16, (0, 1)))
     normed_theirs = over_tp(normed_mine)
+    down[1].launch()
     Pace.value = 3 * BACKWARD_PACE
     grad_down = [scatter_ctx(down[0].finish())]
     Pace.value = BACKWARD_PACE

time: 984 us -> 978 us (level)
  transfers between devices with their start and end apart: 82 -> 82, of which waited for: 31 -> 30; matrix products, arithmetic and copies ran while one was open for 8% -> 8% of each run, Pallas kernels for 36% -> 36%
where the time goes in v5:
time: 978 us; the launch traced here: 967 us
  waiting for transfers between devices  387 us (40%)
  Pallas kernels  368 us (38%)
  starting transfers between devices  90.4 us (9%)
  local copies, waits for them, and re-layouts  50 us (5%)
  other arithmetic  38.8 us (4%)
  between operations  25.6 us (3%)
    ppermute x18, waiting for transfers between devices, shift_ctx(): lax.ppermute(values, 'ctx', [(i, (i + step) % size) for i in range(size)])  158 us
    ppermute x8, waiting for transfers between devices, over_tp(): return lax.ppermute(values, 'tp', xor_pairs(lax.axis_size('tp'), 1))  118 us
    ppermute x41, waiting for transfers between devices, over_fsdp(): return lax.ppermute(values, 'fsdp', xor_pairs(lax.axis_size('fsdp'), mask))  92.5 us
    pallas_call x14, Pallas kernels, grad_blocks(): pl.pallas_call(partial(grad_kernel, count=len(chosen), rights=len(near),...  81.2 us
    ppermute x18, starting transfers between devices, shift_ctx(): lax.ppermute(values, 'ctx', [(i, (i + step) % size) for i in range(size)])  53 us
    pallas_call x4, Pallas kernels, to_width(): pl.pallas_call(partial(back_kernel, lefts=len(lefts), parts=parts, adds=l...  44.6 us
    pallas_call x2, Pallas kernels, other_part(): pl.pallas_call(partial(other_kernel, parts=parts), name='other', grid=(ki...  28.8 us
    pallas_call x2, Pallas kernels, own_part(): pl.pallas_call(partial(own_kernel, parts=parts), name='own', grid_spec=pl...  26.2 us
  transfers between devices with their start and end apart: 82, of which 30 were waited for; matrix products, arithmetic and copies ran while one was open for 8% of the time, Pallas kernels for 36%

profile of v5, /device:TPU:0, one launch (start us, length us, event | category | flops | bytes accessed | tf_op | source)
XLA Modules:
  0.0 967.4 jit_solution(11634561637823375834)
XLA Ops:
  39.8 21.0 %mix.1 = (bf16[3,512,2048]{2,1,0:T(8,128)(2,1)}, f32[4,512,2048]{2,1,0:T(8,128)}) custom-call(s32[4]{0:T(128)} %get-tuple-element.564.perm_ref, bf16[8,512,2048]{2,1,0:T(8,128)(2,1)} %bitcast.143, f32[16,256,4]{2,1,0:T(8,128)} %bitcast.150, f32[1,2048]{1,0:T(1,128)} %bitcast.181, f32[1,2048]{1,0:T(1,128)} %bitcast.191), custom_call_target="tpu_custom_call" | custom-call | flops 420000000 | bytes 1024 | tf_op jit(solution)/shard_map/mix/pallas_call | solution.py:182
  60.9 3.9 slice.130
  70.7 5.8 all-gather.5.cloned.1.call-done.refs_0_
  82.3 65.0 %collective-permute-done.9.refs_0_ = bf16[512,3072]{1,0:T(8,128)(2,1)} collective-permute-done((bf16[512,3072]{1,0:T(8,128)(2,1)}, bf16[512,3072]{1,0:T(8,128)(2,1)}, u32[]{:S(2)}, u32[]{:S(2)}) %collective-permute-start.9) | collective-permute-done | bytes 3145760 | tf_op jit(solution)/shard_map/ppermute | solution.py:49
  149.6 4.9 collective-permute-done.10.refs_3_
  154.5 18.6 %heads.2 = (bf16[3,512,256]{2,1,0:T(8,128)(2,1)}, bf16[3,512,256]{2,1,0:T(8,128)(2,1)}, bf16[3,512,256]{2,1,0:T(8,128)(2,1)}, bf16[3,512,256]{2,1,0:T(8,128)(2,1)}) custom-call(s32[4]{0:T(128)} %and_select_fusion.target_ref, s32[4]{0:T(128)} %get-tuple-element.564.perm_ref, bf16[3,512,2048]{2,1,0:T(8,128)(2,1)} %get-tuple-element.252.a_ref.refs_0_, ...), custom_call_target="tpu_custom_call" | custom-call | flops 720000000 | bytes 1024 | tf_op jit(solution)/shard_map/heads/pallas_call | solution.py:261
  180.8 18.5 %collective-permute-done.11.refs_1_ = bf16[3,512,256]{2,1,0:T(8,128)(2,1)S(1)} collective-permute-done((bf16[3,512,256]{2,1,0:T(8,128)(2,1)}, bf16[3,512,256]{2,1,0:T(8,128)(2,1)S(1)}, u32[]{:S(2)}, u32[]{:S(2)}) %collective-permute-start.11) | collective-permute-done | bytes 786464 | tf_op jit(solution)/shard_map/ppermute | solution.py:54
  199.4 32.5 %collective-permute-done.12.refs_2_ = bf16[3,512,256]{2,1,0:T(8,128)(2,1)S(1)} collective-permute-done((bf16[3,512,256]{2,1,0:T(8,128)(2,1)}, bf16[3,512,256]{2,1,0:T(8,128)(2,1)S(1)}, u32[]{:S(2)}, u32[]{:S(2)}) %collective-permute-start.12) | collective-permute-done | bytes 786464 | tf_op jit(solution)/shard_map/ppermute | solution.py:54
  233.0 11.5 %attend.1 = (bf16[1,512,256]{2,1,0:T(8,128)(2,1)}, bf16[1,512,256]{2,1,0:T(8,128)(2,1)}, bf16[1,512,256]{2,1,0:T(8,128)(2,1)}, bf16[1,512,256]{2,1,0:T(8,128)(2,1)}) custom-call(s32[4]{0:T(128)} %copy-done.38, s32[2]{0:T(128)} %length_ref.5, bf16[3,512,256]{2,1,0:T(8,128)(2,1)} %get-tuple-element.264.refs_0_, bf16[3,512,256]{2,1,0:T(8,128)(2,1)} %copy-done.22, ...), custom_call_target="tpu_custom_call" | custom-call | flops 360000000 | bytes 1024 | tf_op jit(solution)/shard_map/attend/pallas_call | solution.py:367
  246.8 16.4 %collective-permute-start.15 = (bf16[1,512,256]{2,1,0:T(8,128)(2,1)S(1)}, bf16[1,512,256]{2,1,0:T(8,128)(2,1)S(1)}, u32[]{:S(2)}, u32[]{:S(2)}) collective-permute-start(bf16[1,512,256]{2,1,0:T(8,128)(2,1)S(1)} %copy-done.69), channel_id=1, source_target_pairs={{0,6},{2,0},{4,2},{6,4},{1,7},{3,1},{5,3},{7,5},{8,14},{10,8},{12,... | collective-permute-start | bytes 786440 | tf_op jit(solution)/shard_map/ppermute | solution.py:54
  266.4 5.2 collective-permute-done.15.refs_1_
  271.6 38.8 %collective-permute-done.16.refs_2_ = bf16[1,512,256]{2,1,0:T(8,128)(2,1)S(1)} collective-permute-done((bf16[1,512,256]{2,1,0:T(8,128)(2,1)S(1)}, bf16[1,512,256]{2,1,0:T(8,128)(2,1)S(1)}, u32[]{:S(2)}, u32[]{:S(2)}) %collective-permute-start.16) | collective-permute-done | bytes 262176 | tf_op jit(solution)/shard_map/ppermute | solution.py:54
  311.9 3.5 join.3.refs_2_
  324.0 6.1 to_width.4
  332.1 7.2 collective-permute-done.24.refs_3_.refs_5_.refs_9_
  339.3 32.1 %collective-permute-done.22.refs_2_.refs_1_ = bf16[512,2048]{1,0:T(8,128)(2,1)} collective-permute-done((bf16[512,2048]{1,0:T(8,128)(2,1)}, bf16[512,2048]{1,0:T(8,128)(2,1)}, u32[]{:S(2)}, u32[]{:S(2)}) %collective-permute-start.22) | collective-permute-done | bytes 2097184 | tf_op jit(solution)/shard_map/ppermute | solution.py:45
  371.9 5.9 collective-permute-done.21
  379.3 4.2 fusion.43
  387.6 11.3 %up.2 = (bf16[512,2048]{1,0:T(8,128)(2,1)}, f32[512,2048]{1,0:T(8,128)}) custom-call(s32[4]{0:T(128)} %get-tuple-element.564.perm_ref, bf16[512,2048]{1,0:T(8,128)(2,1)} %add_convert_fusion.a_ref, bf16[512,5120]{1,0:T(8,128)(2,1)} %all-gather.7.cloned.1.call-done.refs_0_.refs_2_.refs_6_, bf16[512,5120]{1,0:T(8,128)(2,1)} %collective-permute-done.18.refs_1_.refs_3_.refs_7_, ...), custom_call_target="tpu_custom_call" | custom-call | flops 307200000 | bytes 1024 | tf_op jit(solution)/shard_map/up/pallas_call | solution.py:463
  398.9 11.3 %up.3 = (bf16[512,2048]{1,0:T(8,128)(2,1)}, f32[512,2048]{1,0:T(8,128)}) custom-call(s32[4]{0:T(128)} %get-tuple-element.564.perm_ref, bf16[512,2048]{1,0:T(8,128)(2,1)} %add_convert_fusion.a_ref, bf16[512,5120]{1,0:T(8,128)(2,1)} %all-gather.7.cloned.1.call-done.refs_0_.refs_2_.refs_6_, bf16[512,5120]{1,0:T(8,128)(2,1)} %collective-permute-done.18.refs_1_.refs_3_.refs_7_, ...), custom_call_target="tpu_custom_call" | custom-call | flops 307200000 | bytes 1024 | tf_op jit(solution)/shard_map/up/pallas_call | solution.py:463
  410.3 11.2 %to_width.5.refs_5_ = f32[512,2048]{1,0:T(8,128)} custom-call(bf16[512,2048]{1,0:T(8,128)(2,1)} %get-tuple-element.309.refs_0_, bf16[512,2048]{1,0:T(8,128)(2,1)} %all-gather.9.cloned.1.call-done.refs_1_.refs_0_, bf16[512,2048]{1,0:T(8,128)(2,1)} %collective-permute-done.22.refs_2_.refs_1_, bf16[512,2048]{1,0:T(8,128)(2,1)} %collective-permute-done.28.refs_3_.refs_2_, ...), custom_call_target="tpu_custom_call" | custom-call | flops 240000000 | bytes 1024 | tf_op jit(solution)/shard_map/to_width/pallas_call | solution.py:538
  425.1 5.9 collective-permute-done.30.refs_3_.refs_2_
  432.3 10.8 %to_width.6.mine_ref = bf16[512,2048]{1,0:T(8,128)(2,1)} custom-call(bf16[512,2048]{1,0:T(8,128)(2,1)} %get-tuple-element.314.refs_0_, bf16[512,2048]{1,0:T(8,128)(2,1)} %all-gather.11.cloned.1.call-done.refs_1_.refs_0_, bf16[512,2048]{1,0:T(8,128)(2,1)} %copy-done.18, bf16[512,2048]{1,0:T(8,128)(2,1)} %copy-done.19, ...), custom_call_target="tpu_custom_call" | custom-call | flops 240000000 | bytes 1024 | tf_op jit(solution)/shard_map/to_width/pallas_call | solution.py:538
  453.6 37.4 %collective-permute-done.32.theirs_ref = bf16[512,2048]{1,0:T(8,128)(2,1)} collective-permute-done((bf16[512,2048]{1,0:T(8,128)(2,1)}, bf16[512,2048]{1,0:T(8,128)(2,1)}, u32[]{:S(2)}, u32[]{:S(2)}) %collective-permute-start.32) | collective-permute-done | bytes 2097184 | tf_op jit(solution)/shard_map/ppermute | solution.py:49
  491.1 12.6 %final.1 = (f32[512,2048]{1,0:T(8,128)}, f32[512,2048]{1,0:T(8,128)}, bf16[512,2048]{1,0:T(8,128)(2,1)}, bf16[512,1024]{1,0:T(8,128)(2,1)}) custom-call(f32[512,2048]{1,0:T(8,128)} %copy-done, bf16[512,2048]{1,0:T(8,128)(2,1)} %to_width.6.mine_ref, bf16[512,2048]{1,0:T(8,128)(2,1)} %collective-permute-done.32.theirs_ref, ...), custom_call_target="tpu_custom_call" | custom-call | flops 240000000 | bytes 1024 | tf_op jit(solution)/shard_map/final/pallas_call | solution.py:849
  508.6 6.1 grad.14
  516.1 10.4 %up_back.2.refs_0_ = bf16[512,2048]{1,0:T(8,128)(2,1)} custom-call(s32[4]{0:T(128)} %get-tuple-element.564.perm_ref, bf16[512,2048]{1,0:T(8,128)(2,1)} %get-tuple-element.330.a_ref, f32[512,2048]{1,0:T(8,128)} %get-tuple-element.301.slope_ref, bf16[512,2048]{1,0:T(8,128)(2,1)} %all-gather.9.cloned.1.call-done.refs_1_.refs_0_, ...), custom_call_target="tpu_custom_call" | custom-call | flops 15360000000 | bytes 1024 | tf_op jit(solution)/shard_map/up_back/pallas_call | solution.py:495
  526.6 10.5 %up_back.3.refs_1_ = bf16[512,2048]{1,0:T(8,128)(2,1)} custom-call(s32[4]{0:T(128)} %get-tuple-element.564.perm_ref, bf16[512,2048]{1,0:T(8,128)(2,1)} %get-tuple-element.330.a_ref, f32[512,2048]{1,0:T(8,128)} %get-tuple-element.304.slope_ref, bf16[512,2048]{1,0:T(8,128)(2,1)} %all-gather.11.cloned.1.call-done.refs_1_.refs_0_, bf16[512,2048]{1,0:T(8,128)(2,1)} %copy-done.18, ...), custom_call_target="tpu_custom_call" | custom-call | flops 15360000000 | bytes 1024 | tf_op jit(solution)/shard_map/up_back/pallas_call | solution.py:495
  537.6 16.5 %to_width.7.mine_ref = bf16[512,2048]{1,0:T(8,128)(2,1)} custom-call(bf16[512,2048]{1,0:T(8,128)(2,1)} %up_back.2.refs_0_, bf16[512,2048]{1,0:T(8,128)(2,1)} %up_back.3.refs_1_, bf16[512,5120]{1,0:T(8,128)(2,1)} %all-gather.7.cloned.1.call-done.refs_0_.refs_2_.refs_6_, bf16[512,5120]{1,0:T(8,128)(2,1)} %collective-permute-done.18.refs_1_.refs_3_.refs_7_, ...), custom_call_target="tpu_custom_call" | custom-call | flops 24000000000 | bytes 1024 | tf_op jit(solution)/shard_map/to_width/pallas_call | solution.py:538
  555.6 6.1 grad.15
  563.0 6.6 grad.16
  571.6 6.3 grad.17
  587.8 3.6 fusion
  593.1 9.0 collective-permute-done.41.theirs_ref
  602.1 8.0 second.1
  611.4 7.5 heads.3
  619.0 7.0 grad.18
  627.1 3.9 collective-permute-start.44
  631.0 6.1 grad.19
  637.8 3.9 grad.20
  641.7 13.8 %collective-permute-done.47.refs_4_ = bf16[1,512,2048]{2,1,0:T(8,128)(2,1)} collective-permute-done((bf16[1,512,2048]{2,1,0:T(8,128)(2,1)}, bf16[1,512,2048]{2,1,0:T(8,128)(2,1)}, u32[]{:S(2)}, u32[]{:S(2)}) %collective-permute-start.47) | collective-permute-done | bytes 2097184 | tf_op jit(solution)/shard_map/ppermute | solution.py:45
  655.5 6.6 grad.21
  664.1 11.4 %attend_back.2 = (bf16[3,256,256]{2,1,0:T(8,128)(2,1)}, bf16[3,256,256]{2,1,0:T(8,128)(2,1)}, bf16[3,256,256]{2,1,0:T(8,128)(2,1)}, bf16[3,256,256]{2,1,0:T(8,128)(2,1)}) custom-call(s32[4]{0:T(128)} %copy-done.38, s32[2]{0:T(128)} %length_ref.5, bf16[3,512,256]{2,1,0:T(8,128)(2,1)} %get-tuple-element.264.refs_0_, bf16[3,512,256]{2,1,0:T(8,128)(2,1)} %copy-done.22, ...), custom_call_target="tpu_custom_call" | custom-call | flops 17999998976 | bytes 1024 | tf_op jit(solution)/shard_map/attend_back/pallas_call | solution.py:430
  675.5 12.0 %collective-permute-start.48 = (bf16[3,256,256]{2,1,0:T(8,128)(2,1)}, bf16[3,256,256]{2,1,0:T(8,128)(2,1)S(1)}, u32[]{:S(2)}, u32[]{:S(2)}) collective-permute-start(bf16[3,256,256]{2,1,0:T(8,128)(2,1)} %get-tuple-element.372), channel_id=1, source_target_pairs={{0,6},{2,0},{4,2},{6,4},{1,7},{3,1},{5,3},{7,5},{8,14},{10,8},{12,... | collective-permute-start | bytes 1179656 | tf_op jit(solution)/shard_map/ppermute | solution.py:54
  687.5 6.3 collective-permute-start.49
  694.2 11.3 %attend_back.3 = (bf16[3,256,256]{2,1,0:T(8,128)(2,1)}, bf16[3,256,256]{2,1,0:T(8,128)(2,1)}, bf16[3,256,256]{2,1,0:T(8,128)(2,1)}, bf16[3,256,256]{2,1,0:T(8,128)(2,1)}) custom-call(s32[4]{0:T(128)} %copy-done.38, s32[2]{0:T(128)} %length_ref.5, bf16[3,512,256]{2,1,0:T(8,128)(2,1)} %get-tuple-element.264.refs_0_, bf16[3,512,256]{2,1,0:T(8,128)(2,1)} %copy-done.22, ...), custom_call_target="tpu_custom_call" | custom-call | flops 17999998976 | bytes 1024 | tf_op jit(solution)/shard_map/attend_back/pallas_call | solution.py:430
  707.8 47.7 %collective-permute-done.49.refs_2_ = bf16[3,256,256]{2,1,0:T(8,128)(2,1)S(1)} collective-permute-done((bf16[3,256,256]{2,1,0:T(8,128)(2,1)}, bf16[3,256,256]{2,1,0:T(8,128)(2,1)S(1)}, u32[]{:S(2)}, u32[]{:S(2)}) %collective-permute-start.49) | collective-permute-done | bytes 393248 | tf_op jit(solution)/shard_map/ppermute | solution.py:54
  757.0 3.8 join.4.grad_ref.refs_2_
  762.9 13.0 %own.2 = (f32[3,256,2048]{2,1,0:T(8,128)}, f32[3,16,2048]{2,1,0:T(8,128)}) custom-call(s32[4]{0:T(128)} %get-tuple-element.564.perm_ref, bf16[3,256,1024]{2,1,0:T(8,128)(2,1)} %join.4.grad_ref.refs_2_, f32[4,512,2048]{2,1,0:T(8,128)} %get-tuple-element.235.z_ref, bf16[512,3072]{1,0:T(8,128)(2,1)} %all-gather.5.cloned.1.call-done.refs_0_, ...), custom_call_target="tpu_custom_call" | custom-call | flops 17999998976 | bytes 1024 | tf_op jit(solution)/shard_map/own/pallas_call | solution.py:662
  778.0 15.2 %collective-permute-done.52.refs_2_ = bf16[3,256,256]{2,1,0:T(8,128)(2,1)S(1)} collective-permute-done((bf16[3,256,256]{2,1,0:T(8,128)(2,1)S(1)}, bf16[3,256,256]{2,1,0:T(8,128)(2,1)S(1)}, u32[]{:S(2)}, u32[]{:S(2)}) %collective-permute-start.52) | collective-permute-done | bytes 393248 | tf_op jit(solution)/shard_map/ppermute | solution.py:54
  794.7 3.9 join.5.refs_3_.grad_ref
  798.6 4.3 grad.22
  805.6 6.8 grad.23
  814.7 4.0 grad.24
  819.2 6.3 grad.25
  827.1 13.3 %own.3 = (f32[3,256,2048]{2,1,0:T(8,128)}, f32[3,16,2048]{2,1,0:T(8,128)}) custom-call(s32[4]{0:T(128)} %get-tuple-element.564.perm_ref, bf16[3,256,1024]{2,1,0:T(8,128)(2,1)} %join.5.refs_3_.grad_ref, f32[4,512,2048]{2,1,0:T(8,128)} %get-tuple-element.235.z_ref, bf16[512,3072]{1,0:T(8,128)(2,1)} %all-gather.5.cloned.1.call-done.refs_0_, ...), custom_call_target="tpu_custom_call" | custom-call | flops 17999998976 | bytes 1024 | tf_op jit(solution)/shard_map/own/pallas_call | solution.py:662
  845.1 4.2 grad.26
  849.3 14.3 %other.2.dz_ref = bf16[3,256,2048]{2,1,0:T(8,128)(2,1)} custom-call(bf16[3,256,1024]{2,1,0:T(8,128)(2,1)} %collective-permute-done.56.grad_ref, f32[3,256,2048]{2,1,0:T(8,128)} %get-tuple-element.393.part_ref, f32[4,512,2048]{2,1,0:T(8,128)} %get-tuple-element.235.z_ref, f32[1,2048]{1,0:T(1,128)} %bitcast.182, ...), custom_call_target="tpu_custom_call" | custom-call | flops 20999999488 | bytes 1024 | tf_op jit(solution)/shard_map/other/pallas_call | solution.py:711
  863.7 13.0 %last.2 = (bf16[8,512,2048]{2,1,0:T(8,128)(2,1)}, f32[16,256,128]{2,1,0:T(8,128)}) custom-call(s32[4]{0:T(128)} %get-tuple-element.564.perm_ref, bf16[8,512,2048]{2,1,0:T(8,128)(2,1)} %bitcast.144, f32[16,256,4]{2,1,0:T(8,128)} %bitcast.151, bf16[3,256,2048]{2,1,0:T(8,128)(2,1)} %other.2.dz_ref, bf16[512,2048]{1,0:T(8,128)(2,1)} %get-tuple-element.349.dr_ref), custom_call_target="tpu_custom_call" | custom-call | flops 17999998976 | bytes 1024 | tf_op jit(solution)/shard_map/last/pallas_call | solution.py:767
  876.7 11.8 %collective-permute-done.61.refs_6_ = bf16[1,512,2048]{2,1,0:T(8,128)(2,1)} collective-permute-done((bf16[1,512,2048]{2,1,0:T(8,128)(2,1)}, bf16[1,512,2048]{2,1,0:T(8,128)(2,1)}, u32[]{:S(2)}, u32[]{:S(2)}) %collective-permute-start.61) | collective-permute-done | bytes 2097184 | tf_op jit(solution)/shard_map/ppermute | solution.py:45
  888.6 6.9 grad.27
  898.0 14.5 %other.3.dz_ref = bf16[3,256,2048]{2,1,0:T(8,128)(2,1)} custom-call(bf16[3,256,1024]{2,1,0:T(8,128)(2,1)} %collective-permute-done.54.grad_ref, f32[3,256,2048]{2,1,0:T(8,128)} %get-tuple-element.418.part_ref, f32[4,512,2048]{2,1,0:T(8,128)} %get-tuple-element.235.z_ref, f32[1,2048]{1,0:T(1,128)} %bitcast.183, ...), custom_call_target="tpu_custom_call" | custom-call | flops 420000000 | bytes 1024 | tf_op jit(solution)/shard_map/other/pallas_call | solution.py:711
  917.4 10.2 %collective-permute-done.64 = f32[37,128]{1,0:T(8,128)S(1)} collective-permute-done((f32[37,128]{1,0:T(8,128)S(1)}, f32[37,128]{1,0:T(8,128)S(1)}, u32[]{:S(2)}, u32[]{:S(2)}) %collective-permute-start.64) | collective-permute-done | bytes 18976 | tf_op jit(solution)/shard_map/ppermute | solution.py:1255
  930.8 13.0 %last.3 = (bf16[8,512,2048]{2,1,0:T(8,128)(2,1)}, f32[16,256,128]{2,1,0:T(8,128)}) custom-call(s32[4]{0:T(128)} %get-tuple-element.564.perm_ref, bf16[8,512,2048]{2,1,0:T(8,128)(2,1)} %bitcast.145, f32[16,256,4]{2,1,0:T(8,128)} %bitcast.152, bf16[3,256,2048]{2,1,0:T(8,128)(2,1)} %other.3.dz_ref, ...), custom_call_target="tpu_custom_call", output_to_operand_aliasing={{0}: (5, {}), {1}: (6, {})} | custom-call | flops 360000000 | bytes 1024 | tf_op jit(solution)/shard_map/last/pallas_call | solution.py:767
  (410 shorter events, 161.0 us)
Async XLA Ops:
  7.2 69.2 %all-gather.5.cloned.1.call-start = ((), (), s32[]{:S(2)}) async-start(), calls=%async_computation.7 | async-start | bytes 3932160 | tf_op jit(solution)/shard_map/all_gather | solution.py:88
  9.4 166.0 %all-gather.7.cloned.1.call-start = ((), (), s32[]{:S(2)}) async-start(), calls=%async_computation.8 | async-start | bytes 6553600 | tf_op jit(solution)/shard_map/all_gather | solution.py:88
  9.5 19.6 %collective-permute-start = (bf16[40,128]{1,0:T(8,128)(2,1)S(1)}, bf16[40,128]{1,0:T(8,128)(2,1)S(1)}, u32[]{:S(2)}, u32[]{:S(2)}) collective-permute-start(bf16[40,128]{1,0:T(8,128)(2,1)S(1)} %concatenate.45), channel_id=1, source_target_pairs={{0,2},{2,4},{4,6},{6,0},{1,3},{3,5},{5,7},{7,1},{8,10},{10,12},{12... | collective-permute-start | bytes 30728 | tf_op jit(solution)/shard_map/ppermute | solution.py:54
  12.6 16.5 %collective-permute-start.1 = (bf16[40,128]{1,0:T(8,128)(2,1)S(1)}, bf16[40,128]{1,0:T(8,128)(2,1)S(1)}, u32[]{:S(2)}, u32[]{:S(2)}) collective-permute-start(bf16[40,128]{1,0:T(8,128)(2,1)S(1)} %concatenate.45), channel_id=1, source_target_pairs={{0,4},{2,6},{4,0},{6,2},{1,5},{3,7},{5,1},{7,3},{8,12},{10,14},{12... | collective-permute-start | bytes 30728 | tf_op jit(solution)/shard_map/ppermute | solution.py:54
  15.2 14.0 %collective-permute-start.2 = (bf16[40,128]{1,0:T(8,128)(2,1)S(1)}, bf16[40,128]{1,0:T(8,128)(2,1)S(1)}, u32[]{:S(2)}, u32[]{:S(2)}) collective-permute-start(bf16[40,128]{1,0:T(8,128)(2,1)S(1)} %concatenate.45), channel_id=1, source_target_pairs={{0,6},{2,0},{4,2},{6,4},{1,7},{3,1},{5,3},{7,5},{8,14},{10,8},{12,... | collective-permute-start | bytes 30728 | tf_op jit(solution)/shard_map/ppermute | solution.py:54
  68.7 254.1 %all-gather.9.cloned.1.call-start = ((), (), s32[]{:S(2)}) async-start(), calls=%async_computation.9 | async-start | bytes 2621440 | tf_op jit(solution)/shard_map/all_gather | solution.py:88
  76.5 70.8 %collective-permute-start.9 = (bf16[512,3072]{1,0:T(8,128)(2,1)}, bf16[512,3072]{1,0:T(8,128)(2,1)}, u32[]{:S(2)}, u32[]{:S(2)}) collective-permute-start(bf16[512,3072]{1,0:T(8,128)(2,1)} %all-gather.5.cloned.1.call-done.refs_0_), channel_id=1, source_target_pairs={{0,1},{1,0},{2,3},{3,2},{4,5},{5,4},{6,7},{7,6},{8,9},{9,8},{10,11... | collective-permute-start | bytes 9437192 | tf_op jit(solution)/shard_map/ppermute | solution.py:49
  77.9 70.5 %collective-permute-start.8 = (bf16[512,3072]{1,0:T(8,128)(2,1)}, bf16[512,3072]{1,0:T(8,128)(2,1)}, u32[]{:S(2)}, u32[]{:S(2)}) collective-permute-start(bf16[512,3072]{1,0:T(8,128)(2,1)} %all-gather.5.cloned.1.call-done.refs_0_), channel_id=1, source_target_pairs={{0,16},{8,24},{16,0},{24,8},{1,17},{9,25},{17,1},{25,9},{2,18},{10... | collective-permute-start | bytes 9437192 | tf_op jit(solution)/shard_map/ppermute | solution.py:45
  149.0 82.9 %collective-permute-start.14 = (bf16[512,3072]{1,0:T(8,128)(2,1)}, bf16[512,3072]{1,0:T(8,128)(2,1)}, u32[]{:S(2)}, u32[]{:S(2)}) collective-permute-start(bf16[512,3072]{1,0:T(8,128)(2,1)} %collective-permute-done.8.refs_1_), channel_id=1, source_target_pairs={{0,1},{1,0},{2,3},{3,2},{4,5},{5,4},{6,7},{7,6},{8,9},{9,8},{10,11... | collective-permute-start | bytes 9437192 | tf_op jit(solution)/shard_map/ppermute | solution.py:49
  175.3 140.1 %collective-permute-start.18 = (bf16[512,5120]{1,0:T(8,128)(2,1)}, bf16[512,5120]{1,0:T(8,128)(2,1)}, u32[]{:S(2)}, u32[]{:S(2)}) collective-permute-start(bf16[512,5120]{1,0:T(8,128)(2,1)} %all-gather.7.cloned.1.call-done.refs_0_.refs_2_.refs_6_), channel_id=1, source_target_pairs={{0,16},{8,24},{16,0},{24,8},{1,17},{9,25},{17,1},{25,9},{2,18},{10... | collective-permute-start | bytes 15728648 | tf_op jit(solution)/shard_map/ppermute | solution.py:45
  176.8 22.6 %collective-permute-start.11 = (bf16[3,512,256]{2,1,0:T(8,128)(2,1)}, bf16[3,512,256]{2,1,0:T(8,128)(2,1)S(1)}, u32[]{:S(2)}, u32[]{:S(2)}) collective-permute-start(bf16[3,512,256]{2,1,0:T(8,128)(2,1)} %get-tuple-element.254), channel_id=1, source_target_pairs={{0,2},{2,4},{4,6},{6,0},{1,3},{3,5},{5,7},{7,1},{8,10},{10,12},{12... | collective-permute-start | bytes 2359304 | tf_op jit(solution)/shard_map/ppermute | solution.py:54
  176.8 55.0 %collective-permute-start.12 = (bf16[3,512,256]{2,1,0:T(8,128)(2,1)}, bf16[3,512,256]{2,1,0:T(8,128)(2,1)S(1)}, u32[]{:S(2)}, u32[]{:S(2)}) collective-permute-start(bf16[3,512,256]{2,1,0:T(8,128)(2,1)} %get-tuple-element.255), channel_id=1, source_target_pairs={{0,4},{2,6},{4,0},{6,2},{1,5},{3,7},{5,1},{7,3},{8,12},{10,14},{12... | collective-permute-start | bytes 2359304 | tf_op jit(solution)/shard_map/ppermute | solution.py:54
  178.1 53.8 %collective-permute-start.13 = (bf16[3,512,256]{2,1,0:T(8,128)(2,1)}, bf16[3,512,256]{2,1,0:T(8,128)(2,1)S(1)}, u32[]{:S(2)}, u32[]{:S(2)}) collective-permute-start(bf16[3,512,256]{2,1,0:T(8,128)(2,1)} %get-tuple-element.256), channel_id=1, source_target_pairs={{0,6},{2,0},{4,2},{6,4},{1,7},{3,1},{5,3},{7,5},{8,14},{10,8},{12,... | collective-permute-start | bytes 2359304 | tf_op jit(solution)/shard_map/ppermute | solution.py:54
  246.7 125.2 %all-gather.11.cloned.1.call-start = ((), (), s32[]{:S(2)}) async-start(), calls=%async_computation.10 | async-start | bytes 2621440 | tf_op jit(solution)/shard_map/all_gather | solution.py:88
  246.8 24.9 %collective-permute-start.15 = (bf16[1,512,256]{2,1,0:T(8,128)(2,1)S(1)}, bf16[1,512,256]{2,1,0:T(8,128)(2,1)S(1)}, u32[]{:S(2)}, u32[]{:S(2)}) collective-permute-start(bf16[1,512,256]{2,1,0:T(8,128)(2,1)S(1)} %copy-done.69), channel_id=1, source_target_pairs={{0,6},{2,0},{4,2},{6,4},{1,7},{3,1},{5,3},{7,5},{8,14},{10,8},{12,... | collective-permute-start | bytes 786440 | tf_op jit(solution)/shard_map/ppermute | solution.py:54
  263.1 47.3 %collective-permute-start.16 = (bf16[1,512,256]{2,1,0:T(8,128)(2,1)S(1)}, bf16[1,512,256]{2,1,0:T(8,128)(2,1)S(1)}, u32[]{:S(2)}, u32[]{:S(2)}) collective-permute-start(bf16[1,512,256]{2,1,0:T(8,128)(2,1)S(1)} %copy-done.68), channel_id=1, source_target_pairs={{0,4},{2,6},{4,0},{6,2},{1,5},{3,7},{5,1},{7,3},{8,12},{10,14},{12... | collective-permute-start | bytes 786440 | tf_op jit(solution)/shard_map/ppermute | solution.py:54
  264.4 46.1 %collective-permute-start.17 = (bf16[1,512,256]{2,1,0:T(8,128)(2,1)S(1)}, bf16[1,512,256]{2,1,0:T(8,128)(2,1)S(1)}, u32[]{:S(2)}, u32[]{:S(2)}) collective-permute-start(bf16[1,512,256]{2,1,0:T(8,128)(2,1)S(1)} %copy-done.67), channel_id=1, source_target_pairs={{0,2},{2,4},{4,6},{6,0},{1,3},{3,5},{5,7},{7,1},{8,10},{10,12},{12... | collective-permute-start | bytes 786440 | tf_op jit(solution)/shard_map/ppermute | solution.py:54
  322.9 16.4 %collective-permute-start.24 = (bf16[512,5120]{1,0:T(8,128)(2,1)}, bf16[512,5120]{1,0:T(8,128)(2,1)}, u32[]{:S(2)}, u32[]{:S(2)}) collective-permute-start(bf16[512,5120]{1,0:T(8,128)(2,1)} %collective-permute-done.18.refs_1_.refs_3_.refs_7_), channel_id=1, source_target_pairs={{0,8},{8,0},{16,24},{24,16},{1,9},{9,1},{17,25},{25,17},{2,10},{10... | collective-permute-start | bytes 15728648 | tf_op jit(solution)/shard_map/ppermute | solution.py:45
  323.3 382.3 %reduce-scatter.8.cloned.1.call-start = ((), (), s32[]{:S(2)}) async-start(), calls=%async_computation.11 | async-start | bytes 2621440 | tf_op jit(solution)/shard_map/reduce_scatter | solution.py:135
  323.4 48.1 %collective-permute-start.22 = (bf16[512,2048]{1,0:T(8,128)(2,1)}, bf16[512,2048]{1,0:T(8,128)(2,1)}, u32[]{:S(2)}, u32[]{:S(2)}) collective-permute-start(bf16[512,2048]{1,0:T(8,128)(2,1)} %all-gather.9.cloned.1.call-done.refs_1_.refs_0_), channel_id=1, source_target_pairs={{0,16},{8,24},{16,0},{24,8},{1,17},{9,25},{17,1},{25,9},{2,18},{10... | collective-permute-start | bytes 6291464 | tf_op jit(solution)/shard_map/ppermute | solution.py:45
  330.1 47.7 %collective-permute-start.21 = (bf16[512,2048]{1,0:T(8,128)(2,1)}, bf16[512,2048]{1,0:T(8,128)(2,1)}, u32[]{:S(2)}, u32[]{:S(2)}) collective-permute-start(bf16[512,2048]{1,0:T(8,128)(2,1)} %to_width.4), channel_id=1, source_target_pairs={{0,1},{1,0},{2,3},{3,2},{4,5},{5,4},{6,7},{7,6},{8,9},{9,8},{10,11... | collective-permute-start | bytes 6291464 | tf_op jit(solution)/shard_map/ppermute | solution.py:49
  331.6 78.7 %collective-permute-start.26 = (bf16[512,3072]{1,0:T(8,128)(2,1)}, bf16[512,3072]{1,0:T(8,128)(2,1)S(1)}, u32[]{:S(2)}, u32[]{:S(2)}) collective-permute-start(bf16[512,3072]{1,0:T(8,128)(2,1)} %collective-permute-done.9.refs_0_), channel_id=1, source_target_pairs={{0,8},{8,0},{16,24},{24,16},{1,9},{9,1},{17,25},{25,17},{2,10},{10... | collective-permute-start | bytes 9437192 | tf_op jit(solution)/shard_map/ppermute | solution.py:45
  331.8 78.5 %collective-permute-start.27 = (bf16[512,3072]{1,0:T(8,128)(2,1)}, bf16[512,3072]{1,0:T(8,128)(2,1)}, u32[]{:S(2)}, u32[]{:S(2)}) collective-permute-start(bf16[512,3072]{1,0:T(8,128)(2,1)} %collective-permute-done.14.refs_1_), channel_id=1, source_target_pairs={{0,8},{8,0},{16,24},{24,16},{1,9},{9,1},{17,25},{25,17},{2,10},{10... | collective-permute-start | bytes 9437192 | tf_op jit(solution)/shard_map/ppermute | solution.py:45
  371.4 38.8 %collective-permute-start.28 = (bf16[512,2048]{1,0:T(8,128)(2,1)}, bf16[512,2048]{1,0:T(8,128)(2,1)}, u32[]{:S(2)}, u32[]{:S(2)}) collective-permute-start(bf16[512,2048]{1,0:T(8,128)(2,1)} %all-gather.9.cloned.1.call-done.refs_1_.refs_0_), channel_id=1, source_target_pairs={{0,8},{8,0},{16,24},{24,16},{1,9},{9,1},{17,25},{25,17},{2,10},{10... | collective-permute-start | bytes 6291464 | tf_op jit(solution)/shard_map/ppermute | solution.py:45
  371.4 38.8 %collective-permute-start.29 = (bf16[512,2048]{1,0:T(8,128)(2,1)}, bf16[512,2048]{1,0:T(8,128)(2,1)}, u32[]{:S(2)}, u32[]{:S(2)}) collective-permute-start(bf16[512,2048]{1,0:T(8,128)(2,1)} %collective-permute-done.22.refs_2_.refs_1_), channel_id=1, source_target_pairs={{0,8},{8,0},{16,24},{24,16},{1,9},{9,1},{17,25},{25,17},{2,10},{10... | collective-permute-start | bytes 6291464 | tf_op jit(solution)/shard_map/ppermute | solution.py:45
  377.8 46.8 %collective-permute-start.25 = (bf16[512,2048]{1,0:T(8,128)(2,1)}, bf16[512,2048]{1,0:T(8,128)(2,1)S(1)}, u32[]{:S(2)}, u32[]{:S(2)}) collective-permute-start(bf16[512,2048]{1,0:T(8,128)(2,1)} %all-gather.11.cloned.1.call-done.refs_1_.refs_0_), channel_id=1, source_target_pairs={{0,16},{8,24},{16,0},{24,8},{1,17},{9,25},{17,1},{25,9},{2,18},{10... | collective-permute-start | bytes 6291464 | tf_op jit(solution)/shard_map/ppermute | solution.py:45
  443.1 48.0 %collective-permute-start.32 = (bf16[512,2048]{1,0:T(8,128)(2,1)}, bf16[512,2048]{1,0:T(8,128)(2,1)}, u32[]{:S(2)}, u32[]{:S(2)}) collective-permute-start(bf16[512,2048]{1,0:T(8,128)(2,1)} %to_width.6.mine_ref), channel_id=1, source_target_pairs={{0,1},{1,0},{2,3},{3,2},{4,5},{5,4},{6,7},{7,6},{8,9},{9,8},{10,11... | collective-permute-start | bytes 6291464 | tf_op jit(solution)/shard_map/ppermute | solution.py:49
  444.5 63.0 %collective-permute-start.34 = (bf16[512,2048]{1,0:T(8,128)(2,1)}, bf16[512,2048]{1,0:T(8,128)(2,1)}, u32[]{:S(2)}, u32[]{:S(2)}) collective-permute-start(bf16[512,2048]{1,0:T(8,128)(2,1)} %get-tuple-element.314.refs_0_), channel_id=1, source_target_pairs={{0,8},{8,0},{16,24},{24,16},{1,9},{9,1},{17,25},{25,17},{2,10},{10... | collective-permute-start | bytes 6291464 | tf_op jit(solution)/shard_map/ppermute | solution.py:45
  444.5 63.0 %collective-permute-start.33 = (bf16[512,2048]{1,0:T(8,128)(2,1)}, bf16[512,2048]{1,0:T(8,128)(2,1)}, u32[]{:S(2)}, u32[]{:S(2)}) collective-permute-start(bf16[512,2048]{1,0:T(8,128)(2,1)} %get-tuple-element.309.refs_0_), channel_id=1, source_target_pairs={{0,8},{8,0},{16,24},{24,16},{1,9},{9,1},{17,25},{25,17},{2,10},{10... | collective-permute-start | bytes 6291464 | tf_op jit(solution)/shard_map/ppermute | solution.py:45
  451.3 56.2 %collective-permute-start.36 = (bf16[512,1024]{1,0:T(8,128)(2,1)S(1)}, bf16[512,1024]{1,0:T(8,128)(2,1)}, u32[]{:S(2)}, u32[]{:S(2)}) collective-permute-start(bf16[512,1024]{1,0:T(8,128)(2,1)S(1)} %bitcast.159), channel_id=1, source_target_pairs={{0,8},{8,0},{16,24},{24,16},{1,9},{9,1},{17,25},{25,17},{2,10},{10... | collective-permute-start | bytes 3145736 | tf_op jit(solution)/shard_map/ppermute | solution.py:45
  452.4 55.1 %collective-permute-start.35 = (bf16[512,1024]{1,0:T(8,128)(2,1)}, bf16[512,1024]{1,0:T(8,128)(2,1)S(1)}, u32[]{:S(2)}, u32[]{:S(2)}) collective-permute-start(bf16[512,1024]{1,0:T(8,128)(2,1)} %slice.137), channel_id=1, source_target_pairs={{0,8},{8,0},{16,24},{24,16},{1,9},{9,1},{17,25},{25,17},{2,10},{10... | collective-permute-start | bytes 3145736 | tf_op jit(solution)/shard_map/ppermute | solution.py:45
  514.7 48.3 %collective-permute-start.40 = (bf16[1,512,2048]{2,1,0:T(8,128)(2,1)}, bf16[1,512,2048]{2,1,0:T(8,128)(2,1)}, u32[]{:S(2)}, u32[]{:S(2)}) collective-permute-start(bf16[1,512,2048]{2,1,0:T(8,128)(2,1)} %grad.14), channel_id=1, source_target_pairs={{0,16},{8,24},{16,0},{24,8},{1,17},{9,25},{17,1},{25,9},{2,18},{10... | collective-permute-start | bytes 6291464 | tf_op jit(solution)/shard_map/ppermute | solution.py:45
  537.1 32.5 %collective-permute-start.39 = (bf16[512,2048]{1,0:T(8,128)(2,1)}, bf16[512,2048]{1,0:T(8,128)(2,1)S(1)}, u32[]{:S(2)}, u32[]{:S(2)}) collective-permute-start(bf16[512,2048]{1,0:T(8,128)(2,1)} %up_back.3.refs_1_), channel_id=1, source_target_pairs={{0,8},{8,0},{16,24},{24,16},{1,9},{9,1},{17,25},{25,17},{2,10},{10... | collective-permute-start | bytes 6291464 | tf_op jit(solution)/shard_map/ppermute | solution.py:45
  537.3 32.3 %collective-permute-start.38 = (bf16[512,2048]{1,0:T(8,128)(2,1)S(1)}, bf16[512,2048]{1,0:T(8,128)(2,1)S(1)}, u32[]{:S(2)}, u32[]{:S(2)}) collective-permute-start(bf16[512,2048]{1,0:T(8,128)(2,1)S(1)} %copy-done.47), channel_id=1, source_target_pairs={{0,8},{8,0},{16,24},{24,16},{1,9},{9,1},{17,25},{25,17},{2,10},{10... | collective-permute-start | bytes 6291464 | tf_op jit(solution)/shard_map/ppermute | solution.py:45
  554.1 48.0 %collective-permute-start.41 = (bf16[512,2048]{1,0:T(8,128)(2,1)}, bf16[512,2048]{1,0:T(8,128)(2,1)}, u32[]{:S(2)}, u32[]{:S(2)}) collective-permute-start(bf16[512,2048]{1,0:T(8,128)(2,1)} %to_width.7.mine_ref), channel_id=1, source_target_pairs={{0,1},{1,0},{2,3},{3,2},{4,5},{5,4},{6,7},{7,6},{8,9},{9,8},{10,11... | collective-permute-start | bytes 6291464 | tf_op jit(solution)/shard_map/ppermute | solution.py:49
  561.7 57.3 %collective-permute-start.46 = (bf16[1,512,2048]{2,1,0:T(8,128)(2,1)}, bf16[1,512,2048]{2,1,0:T(8,128)(2,1)}, u32[]{:S(2)}, u32[]{:S(2)}) collective-permute-start(bf16[1,512,2048]{2,1,0:T(8,128)(2,1)} %grad.15), channel_id=1, source_target_pairs={{0,16},{8,24},{16,0},{24,8},{1,17},{9,25},{17,1},{25,9},{2,18},{10... | collective-permute-start | bytes 6291464 | tf_op jit(solution)/shard_map/ppermute | solution.py:45
  577.9 77.6 %collective-permute-start.47 = (bf16[1,512,2048]{2,1,0:T(8,128)(2,1)}, bf16[1,512,2048]{2,1,0:T(8,128)(2,1)}, u32[]{:S(2)}, u32[]{:S(2)}) collective-permute-start(bf16[1,512,2048]{2,1,0:T(8,128)(2,1)} %grad.17), channel_id=1, source_target_pairs={{0,16},{8,24},{16,0},{24,8},{1,17},{9,25},{17,1},{25,9},{2,18},{10... | collective-permute-start | bytes 6291464 | tf_op jit(solution)/shard_map/ppermute | solution.py:45
  579.9 195.9 %reduce-scatter.10.cloned.1.call-start = ((), (), s32[]{:S(2)}) async-start(), calls=%async_computation.12 | async-start | bytes 2621440 | tf_op jit(solution)/shard_map/reduce_scatter | solution.py:135
  626.0 186.6 %reduce-scatter.14.cloned.1.call-start = ((), (), s32[]{:S(2)}) async-start(), calls=%async_computation.14 | async-start | bytes 2621440 | tf_op jit(solution)/shard_map/reduce_scatter | solution.py:135
  626.9 35.7 %collective-permute-start.42 = (bf16[1,512,256]{2,1,0:T(8,128)(2,1)S(1)}, bf16[1,512,256]{2,1,0:T(8,128)(2,1)S(1)}, u32[]{:S(2)}, u32[]{:S(2)}) collective-permute-start(bf16[1,512,256]{2,1,0:T(8,128)(2,1)S(1)} %copy-done.66), channel_id=1, source_target_pairs={{0,2},{2,4},{4,6},{6,0},{1,3},{3,5},{5,7},{7,1},{8,10},{10,12},{12... | collective-permute-start | bytes 786440 | tf_op jit(solution)/shard_map/ppermute | solution.py:54
  627.0 35.6 %collective-permute-start.43 = (bf16[1,512,256]{2,1,0:T(8,128)(2,1)S(1)}, bf16[1,512,256]{2,1,0:T(8,128)(2,1)S(1)}, u32[]{:S(2)}, u32[]{:S(2)}) collective-permute-start(bf16[1,512,256]{2,1,0:T(8,128)(2,1)S(1)} %copy-done.65), channel_id=1, source_target_pairs={{0,4},{2,6},{4,0},{6,2},{1,5},{3,7},{5,1},{7,3},{8,12},{10,14},{12... | collective-permute-start | bytes 786440 | tf_op jit(solution)/shard_map/ppermute | solution.py:54
  627.1 35.5 %collective-permute-start.44 = (bf16[1,512,256]{2,1,0:T(8,128)(2,1)S(1)}, bf16[1,512,256]{2,1,0:T(8,128)(2,1)S(1)}, u32[]{:S(2)}, u32[]{:S(2)}) collective-permute-start(bf16[1,512,256]{2,1,0:T(8,128)(2,1)S(1)} %copy-done.64), channel_id=1, source_target_pairs={{0,6},{2,0},{4,2},{6,4},{1,7},{3,1},{5,3},{7,5},{8,14},{10,8},{12,... | collective-permute-start | bytes 786440 | tf_op jit(solution)/shard_map/ppermute | solution.py:54
  637.2 168.4 %collective-permute-start.59 = (bf16[1,512,2048]{2,1,0:T(8,128)(2,1)}, bf16[1,512,2048]{2,1,0:T(8,128)(2,1)}, u32[]{:S(2)}, u32[]{:S(2)}) collective-permute-start(bf16[1,512,2048]{2,1,0:T(8,128)(2,1)} %grad.19), channel_id=1, source_target_pairs={{0,16},{8,24},{16,0},{24,8},{1,17},{9,25},{17,1},{25,9},{2,18},{10... | collective-permute-start | bytes 6291464 | tf_op jit(solution)/shard_map/ppermute | solution.py:45
  662.1 136.4 %collective-permute-start.55 = (bf16[1,512,1024]{2,1,0:T(8,128)(2,1)}, bf16[1,512,1024]{2,1,0:T(8,128)(2,1)}, u32[]{:S(2)}, u32[]{:S(2)}) collective-permute-start(bf16[1,512,1024]{2,1,0:T(8,128)(2,1)} %grad.20), channel_id=1, source_target_pairs={{0,16},{8,24},{16,0},{24,8},{1,17},{9,25},{17,1},{25,9},{2,18},{10... | collective-permute-start | bytes 3145736 | tf_op jit(solution)/shard_map/ppermute | solution.py:45
  675.5 32.2 %collective-permute-start.48 = (bf16[3,256,256]{2,1,0:T(8,128)(2,1)}, bf16[3,256,256]{2,1,0:T(8,128)(2,1)S(1)}, u32[]{:S(2)}, u32[]{:S(2)}) collective-permute-start(bf16[3,256,256]{2,1,0:T(8,128)(2,1)} %get-tuple-element.372), channel_id=1, source_target_pairs={{0,6},{2,0},{4,2},{6,4},{1,7},{3,1},{5,3},{7,5},{8,14},{10,8},{12,... | collective-permute-start | bytes 1179656 | tf_op jit(solution)/shard_map/ppermute | solution.py:54
  687.5 68.0 %collective-permute-start.49 = (bf16[3,256,256]{2,1,0:T(8,128)(2,1)}, bf16[3,256,256]{2,1,0:T(8,128)(2,1)S(1)}, u32[]{:S(2)}, u32[]{:S(2)}) collective-permute-start(bf16[3,256,256]{2,1,0:T(8,128)(2,1)} %get-tuple-element.373), channel_id=1, source_target_pairs={{0,4},{2,6},{4,0},{6,2},{1,5},{3,7},{5,1},{7,3},{8,12},{10,14},{12... | collective-permute-start | bytes 1179656 | tf_op jit(solution)/shard_map/ppermute | solution.py:54
  693.8 61.7 %collective-permute-start.50 = (bf16[3,256,256]{2,1,0:T(8,128)(2,1)}, bf16[3,256,256]{2,1,0:T(8,128)(2,1)S(1)}, u32[]{:S(2)}, u32[]{:S(2)}) collective-permute-start(bf16[3,256,256]{2,1,0:T(8,128)(2,1)} %get-tuple-element.374), channel_id=1, source_target_pairs={{0,2},{2,4},{4,6},{6,0},{1,3},{3,5},{5,7},{7,1},{8,10},{10,12},{12... | collective-permute-start | bytes 1179656 | tf_op jit(solution)/shard_map/ppermute | solution.py:54
  693.8 148.3 %reduce-scatter.12.cloned.1.call-start = ((), (), s32[]{:S(2)}) async-start(), calls=%async_computation.13 | async-start | bytes 1310720 | tf_op jit(solution)/shard_map/reduce_scatter | solution.py:135
  760.8 17.2 %collective-permute-start.51 = (bf16[3,256,256]{2,1,0:T(8,128)(2,1)S(1)}, bf16[3,256,256]{2,1,0:T(8,128)(2,1)S(1)}, u32[]{:S(2)}, u32[]{:S(2)}) collective-permute-start(bf16[3,256,256]{2,1,0:T(8,128)(2,1)S(1)} %copy-done.54), channel_id=1, source_target_pairs={{0,6},{2,0},{4,2},{6,4},{1,7},{3,1},{5,3},{7,5},{8,14},{10,8},{12,... | collective-permute-start | bytes 1179656 | tf_op jit(solution)/shard_map/ppermute | solution.py:54
  760.8 32.4 %collective-permute-start.52 = (bf16[3,256,256]{2,1,0:T(8,128)(2,1)S(1)}, bf16[3,256,256]{2,1,0:T(8,128)(2,1)S(1)}, u32[]{:S(2)}, u32[]{:S(2)}) collective-permute-start(bf16[3,256,256]{2,1,0:T(8,128)(2,1)S(1)} %copy-done.53), channel_id=1, source_target_pairs={{0,4},{2,6},{4,0},{6,2},{1,5},{3,7},{5,1},{7,3},{8,12},{10,14},{12... | collective-permute-start | bytes 1179656 | tf_op jit(solution)/shard_map/ppermute | solution.py:54
  760.9 32.3 %collective-permute-start.53 = (bf16[3,256,256]{2,1,0:T(8,128)(2,1)S(1)}, bf16[3,256,256]{2,1,0:T(8,128)(2,1)S(1)}, u32[]{:S(2)}, u32[]{:S(2)}) collective-permute-start(bf16[3,256,256]{2,1,0:T(8,128)(2,1)S(1)} %copy-done.52), channel_id=1, source_target_pairs={{0,2},{2,4},{4,6},{6,0},{1,3},{3,5},{5,7},{7,1},{8,10},{10,12},{12... | collective-permute-start | bytes 1179656 | tf_op jit(solution)/shard_map/ppermute | solution.py:54
  802.9 112.4 %reduce-scatter.16.cloned.1.call-start = ((), (), s32[]{:S(2)}) async-start(), calls=%async_computation.15 | async-start | bytes 2621440 | tf_op jit(solution)/shard_map/reduce_scatter | solution.py:135
  803.0 11.7 %collective-permute-start.57 = (bf16[3,256,1024]{2,1,0:T(8,128)(2,1)S(1)}, bf16[3,256,1024]{2,1,0:T(8,128)(2,1)}, u32[]{:S(2)}, u32[]{:S(2)}) collective-permute-start(bf16[3,256,1024]{2,1,0:T(8,128)(2,1)S(1)} %copy-done.6), channel_id=1, source_target_pairs={{0,8},{8,0},{16,24},{24,16},{1,9},{9,1},{17,25},{25,17},{2,10},{10... | collective-permute-start | bytes 4718600 | tf_op jit(solution)/shard_map/ppermute | solution.py:45
  803.6 37.4 %collective-permute-start.56 = (bf16[3,256,1024]{2,1,0:T(8,128)(2,1)S(1)}, bf16[3,256,1024]{2,1,0:T(8,128)(2,1)}, u32[]{:S(2)}, u32[]{:S(2)}) collective-permute-start(bf16[3,256,1024]{2,1,0:T(8,128)(2,1)S(1)} %copy-done.6), channel_id=1, source_target_pairs={{0,1},{1,0},{2,3},{3,2},{4,5},{5,4},{6,7},{7,6},{8,9},{9,8},{10,11... | collective-permute-start | bytes 4718600 | tf_op jit(solution)/shard_map/ppermute | solution.py:49
  805.1 71.6 %collective-permute-start.54 = (bf16[3,256,1024]{2,1,0:T(8,128)(2,1)S(1)}, bf16[3,256,1024]{2,1,0:T(8,128)(2,1)}, u32[]{:S(2)}, u32[]{:S(2)}) collective-permute-start(bf16[3,256,1024]{2,1,0:T(8,128)(2,1)S(1)} %copy-done.7), channel_id=1, source_target_pairs={{0,1},{1,0},{2,3},{3,2},{4,5},{5,4},{6,7},{7,6},{8,9},{9,8},{10,11... | collective-permute-start | bytes 4718600 | tf_op jit(solution)/shard_map/ppermute | solution.py:49
  812.4 144.4 %reduce-scatter.18.cloned.1.call-start = ((), (), s32[]{:S(2)}) async-start(), calls=%async_computation.16 | async-start | bytes 1310720 | tf_op jit(solution)/shard_map/reduce_scatter | solution.py:135
  818.7 26.4 %collective-permute-start.60 = (bf16[1,512,1024]{2,1,0:T(8,128)(2,1)}, bf16[1,512,1024]{2,1,0:T(8,128)(2,1)}, u32[]{:S(2)}, u32[]{:S(2)}) collective-permute-start(bf16[1,512,1024]{2,1,0:T(8,128)(2,1)} %grad.24), channel_id=1, source_target_pairs={{0,16},{8,24},{16,0},{24,8},{1,17},{9,25},{17,1},{25,9},{2,18},{10... | collective-permute-start | bytes 3145736 | tf_op jit(solution)/shard_map/ppermute | solution.py:45
  825.5 63.0 %collective-permute-start.61 = (bf16[1,512,2048]{2,1,0:T(8,128)(2,1)}, bf16[1,512,2048]{2,1,0:T(8,128)(2,1)}, u32[]{:S(2)}, u32[]{:S(2)}) collective-permute-start(bf16[1,512,2048]{2,1,0:T(8,128)(2,1)} %grad.25), channel_id=1, source_target_pairs={{0,16},{8,24},{16,0},{24,8},{1,17},{9,25},{17,1},{25,9},{2,18},{10... | collective-permute-start | bytes 6291464 | tf_op jit(solution)/shard_map/ppermute | solution.py:45
  863.7 95.0 %reduce-scatter.20.cloned.1.call-start = ((), (), s32[]{:S(2)}) async-start(), calls=%async_computation.17 | async-start | bytes 2621440 | tf_op jit(solution)/shard_map/reduce_scatter | solution.py:135
  896.4 16.0 %collective-permute-start.62 = (f32[2,2048]{1,0:T(2,128)S(1)}, f32[2,2048]{1,0:T(2,128)S(1)}, u32[]{:S(2)}, u32[]{:S(2)}) collective-permute-start(f32[2,2048]{1,0:T(2,128)S(1)} %bitcast_reduce_fusion.1), channel_id=1, source_target_pairs={{0,1},{1,0},{2,3},{3,2},{4,5},{5,4},{6,7},{7,6},{8,9},{9,8},{10,11... | collective-permute-start | bytes 49160 | tf_op jit(solution)/shard_map/ppermute | solution.py:49
  913.2 14.4 %collective-permute-start.63 = (f32[2,4,40,128]{3,2,1,0:T(8,128)S(1)}, f32[2,4,40,128]{3,2,1,0:T(8,128)S(1)}, u32[]{:S(2)}, u32[]{:S(2)}) collective-permute-start(f32[2,4,40,128]{3,2,1,0:T(8,128)S(1)} %slice.140), channel_id=1, source_target_pairs={{0,2},{2,0},{4,6},{6,4},{1,3},{3,1},{5,7},{7,5},{8,10},{10,8},{12,... | collective-permute-start | bytes 491528 | tf_op jit(solution)/shard_map/ppermute | solution.py:1255
  913.3 14.4 %collective-permute-start.64 = (f32[37,128]{1,0:T(8,128)S(1)}, f32[37,128]{1,0:T(8,128)S(1)}, u32[]{:S(2)}, u32[]{:S(2)}) collective-permute-start(f32[37,128]{1,0:T(8,128)S(1)} %pad.22), channel_id=1, source_target_pairs={{0,2},{2,0},{4,6},{6,4},{1,3},{3,1},{5,7},{7,5},{8,10},{10,8},{12,... | collective-permute-start | bytes 56840 | tf_op jit(solution)/shard_map/ppermute | solution.py:1255
  927.7 16.1 %collective-permute-start.65 = (f32[1,4,40,128]{3,2,1,0:T(8,128)S(1)}, f32[1,4,40,128]{3,2,1,0:T(8,128)S(1)}, u32[]{:S(2)}, u32[]{:S(2)}) collective-permute-start(f32[1,4,40,128]{3,2,1,0:T(8,128)S(1)} %slice.165), channel_id=1, source_target_pairs={{0,4},{2,6},{4,0},{6,2},{1,5},{3,7},{5,1},{7,3},{8,12},{10,14},{12... | collective-permute-start | bytes 245768 | tf_op jit(solution)/shard_map/ppermute | solution.py:1255
  927.8 15.9 %collective-permute-start.66 = (f32[37,128]{1,0:T(8,128)S(1)}, f32[37,128]{1,0:T(8,128)S(1)}, u32[]{:S(2)}, u32[]{:S(2)}) collective-permute-start(f32[37,128]{1,0:T(8,128)S(1)} %add.235), channel_id=1, source_target_pairs={{0,4},{2,6},{4,0},{6,2},{1,5},{3,7},{5,1},{7,3},{8,12},{10,14},{12... | collective-permute-start | bytes 56840 | tf_op jit(solution)/shard_map/ppermute | solution.py:1255
  (90 other events, 1325.8 us)
Sparse Core Ops, SparseCore 0:
  10.2 66.1 all-gather.4
  78.6 96.7 all-gather.6
  246.8 73.9 all-gather.8
  323.4 43.4 all-gather.10
  580.0 41.4 reduce-scatter.7
  626.1 59.6 reduce-scatter.9
  693.9 65.0 reduce-scatter.13
  803.1 24.4 reduce-scatter.11
  829.9 42.5 reduce-scatter.15
  874.7 26.4 reduce-scatter.17
  903.5 48.4 reduce-scatter.19

commit v6 on v5

--- a/solution.py
+++ b/solution.py
@@ -20,7 +20,7 @@
 BF16 = jnp.bfloat16
 GROUP = 32
 FORWARD_PACE = 3.0e7
-BACKWARD_PACE = 1.5e9
+BACKWARD_PACE = 2.2e9
 
 
 def params(grid_rank):
@@ -1187,13 +1187,13 @@
         order, grad_branch_b[None], [attended[None]], grad_branch_far[None], [attended_far[None]]
     )
     made_proj = proj.make(1)
-    grad_up = [scatter_ctx(up[0].finish())]
     proj.launch(0, None, order(made_proj))
     grad_pieces = order.wait(grad_pieces)
     back = [
         order.keep(attend_back(source, lengths, pieces, order(grad_pieces), tables_all, 0))
     ]
-    sent = [to_slots(back[0])]
+    grad_up = [scatter_ctx(up[0].finish())]
+    sent = [to_slots(order(back[0]))]
     back.append(
         order.keep(attend_back(source, lengths, pieces, order(grad_pieces), tables_all, 1))
     )
@@ -1205,6 +1205,7 @@
     sent.append(to_slots(order(back[1])))
     own.append(order.keep(own_part(perm, order(mine[0]), streams, blocks_qkv, 0)))
     grad_down[1] = order.wait(grad_down[1])
+    grad_up[0] = order.wait(grad_up[0])
     sent[1] = order.wait(sent[1])
     mine.append(order.keep(join(target, sent[1])))
     theirs.append(over_tp(mine[1]))
@@ -1216,7 +1217,6 @@
     qkv.launch(0, 1)
     qkv.launch(1, 2)
     own.append(order.keep(own_part(perm, order(mine[1]), streams, blocks_qkv, 1)))
-    grad_up[0] = order.wait(grad_up[0])
     theirs[0] = order.wait(theirs[0])
     grad_query = scatter_ctx(qkv.finish(0, 1))
     sums = (own[0][1] + own[1][1]).sum(0).reshape(2, 8, width).sum(1)

time: 978 us -> 972 us (level)
  waiting for transfers between devices: 387 us -> 376 us
    ppermute x41, waiting for transfers between devices: 92.5 us -> 76.3 us  [over_fsdp(): return lax.ppermute(values, 'fsdp', xor_pairs(lax.axis_size('fsdp'), mask))]
  transfers between devices with their start and end apart: 82 -> 82, of which waited for: 30 -> 29; matrix products, arithmetic and copies ran while one was open for 8% -> 8% of each run, Pallas kernels for 36% -> 36%
where the time goes in v6:
time: 972 us; the launch traced here: 962 us
  waiting for transfers between devices  376 us (39%)
  Pallas kernels  367 us (38%)
  starting transfers between devices  95.2 us (10%)
  local copies, waits for them, and re-layouts  49.1 us (5%)
  other arithmetic  38.9 us (4%)
  between operations  25.6 us (3%)
  matrix products  10.5 us (1%)
    ppermute x18, waiting for transfers between devices, shift_ctx(): lax.ppermute(values, 'ctx', [(i, (i + step) % size) for i in range(size)])  162 us
    ppermute x8, waiting for transfers between devices, over_tp(): return lax.ppermute(values, 'tp', xor_pairs(lax.axis_size('tp'), 1))  118 us
    pallas_call x14, Pallas kernels, grad_blocks(): pl.pallas_call(partial(grad_kernel, count=len(chosen), rights=len(near),...  81 us
    ppermute x41, waiting for transfers between devices, over_fsdp(): return lax.ppermute(values, 'fsdp', xor_pairs(lax.axis_size('fsdp'), mask))  76.3 us
    ppermute x18, starting transfers between devices, shift_ctx(): lax.ppermute(values, 'ctx', [(i, (i + step) % size) for i in range(size)])  57.8 us
    pallas_call x4, Pallas kernels, to_width(): pl.pallas_call(partial(back_kernel, lefts=len(lefts), parts=parts, adds=l...  44.7 us
    pallas_call x2, Pallas kernels, other_part(): pl.pallas_call(partial(other_kernel, parts=parts), name='other', grid=(ki...  28.5 us
    pallas_call x2, Pallas kernels, to_chunks(): pl.pallas_call(partial(heads_kernel, parts=parts, turned=turned), name='h...  26.1 us
  transfers between devices with their start and end apart: 82, of which 29 were waited for; matrix products, arithmetic and copies ran while one was open for 8% of the time, Pallas kernels for 36%

profile of v6, /device:TPU:0, one launch (start us, length us, event | category | flops | bytes accessed | tf_op | source)
XLA Modules:
  0.0 961.7 jit_solution(6272971152954975363)
XLA Ops:
  39.8 21.0 %mix.1 = (bf16[3,512,2048]{2,1,0:T(8,128)(2,1)}, f32[4,512,2048]{2,1,0:T(8,128)}) custom-call(s32[4]{0:T(128)} %get-tuple-element.572.perm_ref, bf16[8,512,2048]{2,1,0:T(8,128)(2,1)} %bitcast.143, f32[16,256,4]{2,1,0:T(8,128)} %bitcast.150, f32[1,2048]{1,0:T(1,128)} %bitcast.181, f32[1,2048]{1,0:T(1,128)} %bitcast.191), custom_call_target="tpu_custom_call" | custom-call | flops 420000000 | bytes 1024 | tf_op jit(solution)/shard_map/mix/pallas_call | solution.py:182
  60.9 3.9 slice.130
  70.7 5.8 all-gather.5.cloned.1.call-done.refs_0_
  82.3 65.0 %collective-permute-done.9.refs_0_ = bf16[512,3072]{1,0:T(8,128)(2,1)} collective-permute-done((bf16[512,3072]{1,0:T(8,128)(2,1)}, bf16[512,3072]{1,0:T(8,128)(2,1)}, u32[]{:S(2)}, u32[]{:S(2)}) %collective-permute-start.9) | collective-permute-done | bytes 3145760 | tf_op jit(solution)/shard_map/ppermute | solution.py:49
  149.6 4.9 collective-permute-done.10.refs_3_
  154.5 18.6 %heads.2 = (bf16[3,512,256]{2,1,0:T(8,128)(2,1)}, bf16[3,512,256]{2,1,0:T(8,128)(2,1)}, bf16[3,512,256]{2,1,0:T(8,128)(2,1)}, bf16[3,512,256]{2,1,0:T(8,128)(2,1)}) custom-call(s32[4]{0:T(128)} %and_select_fusion.target_ref, s32[4]{0:T(128)} %get-tuple-element.572.perm_ref, bf16[3,512,2048]{2,1,0:T(8,128)(2,1)} %get-tuple-element.256.a_ref.refs_0_, ...), custom_call_target="tpu_custom_call" | custom-call | flops 720000000 | bytes 1024 | tf_op jit(solution)/shard_map/heads/pallas_call | solution.py:261
  180.8 18.5 %collective-permute-done.11.refs_1_ = bf16[3,512,256]{2,1,0:T(8,128)(2,1)S(1)} collective-permute-done((bf16[3,512,256]{2,1,0:T(8,128)(2,1)}, bf16[3,512,256]{2,1,0:T(8,128)(2,1)S(1)}, u32[]{:S(2)}, u32[]{:S(2)}) %collective-permute-start.11) | collective-permute-done | bytes 786464 | tf_op jit(solution)/shard_map/ppermute | solution.py:54
  199.4 32.5 %collective-permute-done.12.refs_2_ = bf16[3,512,256]{2,1,0:T(8,128)(2,1)S(1)} collective-permute-done((bf16[3,512,256]{2,1,0:T(8,128)(2,1)}, bf16[3,512,256]{2,1,0:T(8,128)(2,1)S(1)}, u32[]{:S(2)}, u32[]{:S(2)}) %collective-permute-start.12) | collective-permute-done | bytes 786464 | tf_op jit(solution)/shard_map/ppermute | solution.py:54
  233.0 11.5 %attend.1 = (bf16[1,512,256]{2,1,0:T(8,128)(2,1)}, bf16[1,512,256]{2,1,0:T(8,128)(2,1)}, bf16[1,512,256]{2,1,0:T(8,128)(2,1)}, bf16[1,512,256]{2,1,0:T(8,128)(2,1)}) custom-call(s32[4]{0:T(128)} %copy-done.38, s32[2]{0:T(128)} %length_ref.5, bf16[3,512,256]{2,1,0:T(8,128)(2,1)} %get-tuple-element.268.refs_0_, bf16[3,512,256]{2,1,0:T(8,128)(2,1)} %copy-done.22, ...), custom_call_target="tpu_custom_call" | custom-call | flops 360000000 | bytes 1024 | tf_op jit(solution)/shard_map/attend/pallas_call | solution.py:367
  246.8 16.4 %collective-permute-start.15 = (bf16[1,512,256]{2,1,0:T(8,128)(2,1)S(1)}, bf16[1,512,256]{2,1,0:T(8,128)(2,1)S(1)}, u32[]{:S(2)}, u32[]{:S(2)}) collective-permute-start(bf16[1,512,256]{2,1,0:T(8,128)(2,1)S(1)} %copy-done.69), channel_id=1, source_target_pairs={{0,6},{2,0},{4,2},{6,4},{1,7},{3,1},{5,3},{7,5},{8,14},{10,8},{12,... | collective-permute-start | bytes 786440 | tf_op jit(solution)/shard_map/ppermute | solution.py:54
  266.4 5.2 collective-permute-done.15.refs_1_
  271.6 38.8 %collective-permute-done.16.refs_2_ = bf16[1,512,256]{2,1,0:T(8,128)(2,1)S(1)} collective-permute-done((bf16[1,512,256]{2,1,0:T(8,128)(2,1)S(1)}, bf16[1,512,256]{2,1,0:T(8,128)(2,1)S(1)}, u32[]{:S(2)}, u32[]{:S(2)}) %collective-permute-start.16) | collective-permute-done | bytes 262176 | tf_op jit(solution)/shard_map/ppermute | solution.py:54
  311.9 3.5 join.3.refs_2_
  324.0 6.1 to_width.4
  332.1 7.2 collective-permute-done.24.refs_3_.refs_5_.refs_9_
  339.3 32.1 %collective-permute-done.22.refs_2_.refs_1_ = bf16[512,2048]{1,0:T(8,128)(2,1)} collective-permute-done((bf16[512,2048]{1,0:T(8,128)(2,1)}, bf16[512,2048]{1,0:T(8,128)(2,1)}, u32[]{:S(2)}, u32[]{:S(2)}) %collective-permute-start.22) | collective-permute-done | bytes 2097184 | tf_op jit(solution)/shard_map/ppermute | solution.py:45
  371.9 5.9 collective-permute-done.21
  379.3 4.2 fusion.43
  387.6 11.3 %up.2 = (bf16[512,2048]{1,0:T(8,128)(2,1)}, f32[512,2048]{1,0:T(8,128)}) custom-call(s32[4]{0:T(128)} %get-tuple-element.572.perm_ref, bf16[512,2048]{1,0:T(8,128)(2,1)} %add_convert_fusion.a_ref, bf16[512,5120]{1,0:T(8,128)(2,1)} %all-gather.7.cloned.1.call-done.refs_0_.refs_2_.refs_6_, bf16[512,5120]{1,0:T(8,128)(2,1)} %collective-permute-done.18.refs_1_.refs_3_.refs_7_, ...), custom_call_target="tpu_custom_call" | custom-call | flops 307200000 | bytes 1024 | tf_op jit(solution)/shard_map/up/pallas_call | solution.py:463
  398.9 11.3 %up.3 = (bf16[512,2048]{1,0:T(8,128)(2,1)}, f32[512,2048]{1,0:T(8,128)}) custom-call(s32[4]{0:T(128)} %get-tuple-element.572.perm_ref, bf16[512,2048]{1,0:T(8,128)(2,1)} %add_convert_fusion.a_ref, bf16[512,5120]{1,0:T(8,128)(2,1)} %all-gather.7.cloned.1.call-done.refs_0_.refs_2_.refs_6_, bf16[512,5120]{1,0:T(8,128)(2,1)} %collective-permute-done.18.refs_1_.refs_3_.refs_7_, ...), custom_call_target="tpu_custom_call" | custom-call | flops 307200000 | bytes 1024 | tf_op jit(solution)/shard_map/up/pallas_call | solution.py:463
  410.3 11.2 %to_width.5.refs_5_ = f32[512,2048]{1,0:T(8,128)} custom-call(bf16[512,2048]{1,0:T(8,128)(2,1)} %get-tuple-element.313.refs_0_, bf16[512,2048]{1,0:T(8,128)(2,1)} %all-gather.9.cloned.1.call-done.refs_1_.refs_0_, bf16[512,2048]{1,0:T(8,128)(2,1)} %collective-permute-done.22.refs_2_.refs_1_, bf16[512,2048]{1,0:T(8,128)(2,1)} %collective-permute-done.28.refs_3_.refs_2_, ...), custom_call_target="tpu_custom_call" | custom-call | flops 240000000 | bytes 1024 | tf_op jit(solution)/shard_map/to_width/pallas_call | solution.py:538
  425.1 5.9 collective-permute-done.30.refs_3_.refs_2_
  432.3 10.9 %to_width.6.mine_ref = bf16[512,2048]{1,0:T(8,128)(2,1)} custom-call(bf16[512,2048]{1,0:T(8,128)(2,1)} %get-tuple-element.318.refs_0_, bf16[512,2048]{1,0:T(8,128)(2,1)} %all-gather.11.cloned.1.call-done.refs_1_.refs_0_, bf16[512,2048]{1,0:T(8,128)(2,1)} %copy-done.18, bf16[512,2048]{1,0:T(8,128)(2,1)} %copy-done.19, ...), custom_call_target="tpu_custom_call" | custom-call | flops 240000000 | bytes 1024 | tf_op jit(solution)/shard_map/to_width/pallas_call | solution.py:538
  453.8 37.4 %collective-permute-done.32.theirs_ref = bf16[512,2048]{1,0:T(8,128)(2,1)} collective-permute-done((bf16[512,2048]{1,0:T(8,128)(2,1)}, bf16[512,2048]{1,0:T(8,128)(2,1)}, u32[]{:S(2)}, u32[]{:S(2)}) %collective-permute-start.32) | collective-permute-done | bytes 2097184 | tf_op jit(solution)/shard_map/ppermute | solution.py:49
  491.2 12.6 %final.1 = (f32[512,2048]{1,0:T(8,128)}, f32[512,2048]{1,0:T(8,128)}, bf16[512,2048]{1,0:T(8,128)(2,1)}, bf16[512,1024]{1,0:T(8,128)(2,1)}) custom-call(f32[512,2048]{1,0:T(8,128)} %copy-done, bf16[512,2048]{1,0:T(8,128)(2,1)} %to_width.6.mine_ref, bf16[512,2048]{1,0:T(8,128)(2,1)} %collective-permute-done.32.theirs_ref, ...), custom_call_target="tpu_custom_call" | custom-call | flops 240000000 | bytes 1024 | tf_op jit(solution)/shard_map/final/pallas_call | solution.py:849
  508.7 6.1 grad.14
  516.3 10.5 %up_back.2.refs_0_ = bf16[512,2048]{1,0:T(8,128)(2,1)} custom-call(s32[4]{0:T(128)} %get-tuple-element.572.perm_ref, bf16[512,2048]{1,0:T(8,128)(2,1)} %get-tuple-element.334.a_ref, f32[512,2048]{1,0:T(8,128)} %get-tuple-element.305.slope_ref, bf16[512,2048]{1,0:T(8,128)(2,1)} %all-gather.9.cloned.1.call-done.refs_1_.refs_0_, ...), custom_call_target="tpu_custom_call" | custom-call | flops 22528000000 | bytes 1024 | tf_op jit(solution)/shard_map/up_back/pallas_call | solution.py:495
  526.7 10.5 %up_back.3.refs_1_ = bf16[512,2048]{1,0:T(8,128)(2,1)} custom-call(s32[4]{0:T(128)} %get-tuple-element.572.perm_ref, bf16[512,2048]{1,0:T(8,128)(2,1)} %get-tuple-element.334.a_ref, f32[512,2048]{1,0:T(8,128)} %get-tuple-element.308.slope_ref, bf16[512,2048]{1,0:T(8,128)(2,1)} %all-gather.11.cloned.1.call-done.refs_1_.refs_0_, bf16[512,2048]{1,0:T(8,128)(2,1)} %copy-done.18, ...), custom_call_target="tpu_custom_call" | custom-call | flops 22528000000 | bytes 1024 | tf_op jit(solution)/shard_map/up_back/pallas_call | solution.py:495
  537.8 16.5 %to_width.7.mine_ref = bf16[512,2048]{1,0:T(8,128)(2,1)} custom-call(bf16[512,2048]{1,0:T(8,128)(2,1)} %up_back.2.refs_0_, bf16[512,2048]{1,0:T(8,128)(2,1)} %up_back.3.refs_1_, bf16[512,5120]{1,0:T(8,128)(2,1)} %all-gather.7.cloned.1.call-done.refs_0_.refs_2_.refs_6_, bf16[512,5120]{1,0:T(8,128)(2,1)} %collective-permute-done.18.refs_1_.refs_3_.refs_7_, ...), custom_call_target="tpu_custom_call" | custom-call | flops 35200000000 | bytes 1024 | tf_op jit(solution)/shard_map/to_width/pallas_call | solution.py:538
  555.8 6.1 grad.15
  563.1 6.6 grad.16
  571.8 6.2 grad.17
  589.7 5.9 fusion
  595.6 6.8 collective-permute-done.41.theirs_ref
  602.3 8.0 second.1
  611.7 7.5 heads.3
  619.3 3.7 collective-permute-start.44
  623.1 6.7 grad.18
  630.0 6.2 grad.19
  636.7 3.9 grad.20
  640.6 6.1 collective-permute-done.43.refs_6_
  648.0 11.3 %attend_back.2 = (bf16[3,256,256]{2,1,0:T(8,128)(2,1)}, bf16[3,256,256]{2,1,0:T(8,128)(2,1)}, bf16[3,256,256]{2,1,0:T(8,128)(2,1)}, bf16[3,256,256]{2,1,0:T(8,128)(2,1)}) custom-call(s32[4]{0:T(128)} %copy-done.38, s32[2]{0:T(128)} %length_ref.5, bf16[3,512,256]{2,1,0:T(8,128)(2,1)} %get-tuple-element.268.refs_0_, bf16[3,512,256]{2,1,0:T(8,128)(2,1)} %copy-done.22, ...), custom_call_target="tpu_custom_call" | custom-call | flops 26400000000 | bytes 1024 | tf_op jit(solution)/shard_map/attend_back/pallas_call | solution.py:430
  659.5 6.7 grad.21
  666.2 12.6 %collective-permute-start.48 = (bf16[3,256,256]{2,1,0:T(8,128)(2,1)S(1)}, bf16[3,256,256]{2,1,0:T(8,128)(2,1)S(1)}, u32[]{:S(2)}, u32[]{:S(2)}) collective-permute-start(bf16[3,256,256]{2,1,0:T(8,128)(2,1)S(1)} %copy-done.57), channel_id=1, source_target_pairs={{0,6},{2,0},{4,2},{6,4},{1,7},{3,1},{5,3},{7,5},{8,14},{10,8},{12,... | collective-permute-start | bytes 1179656 | tf_op jit(solution)/shard_map/ppermute | solution.py:54
  678.8 10.7 %collective-permute-start.49 = (bf16[3,256,256]{2,1,0:T(8,128)(2,1)S(1)}, bf16[3,256,256]{2,1,0:T(8,128)(2,1)S(1)}, u32[]{:S(2)}, u32[]{:S(2)}) collective-permute-start(bf16[3,256,256]{2,1,0:T(8,128)(2,1)S(1)} %copy-done.56), channel_id=1, source_target_pairs={{0,4},{2,6},{4,0},{6,2},{1,5},{3,7},{5,1},{7,3},{8,12},{10,14},{12... | collective-permute-start | bytes 1179656 | tf_op jit(solution)/shard_map/ppermute | solution.py:54
  690.0 11.3 %attend_back.3 = (bf16[3,256,256]{2,1,0:T(8,128)(2,1)}, bf16[3,256,256]{2,1,0:T(8,128)(2,1)}, bf16[3,256,256]{2,1,0:T(8,128)(2,1)}, bf16[3,256,256]{2,1,0:T(8,128)(2,1)}) custom-call(s32[4]{0:T(128)} %copy-done.38, s32[2]{0:T(128)} %length_ref.5, bf16[3,512,256]{2,1,0:T(8,128)(2,1)} %get-tuple-element.268.refs_0_, bf16[3,512,256]{2,1,0:T(8,128)(2,1)} %copy-done.22, ...), custom_call_target="tpu_custom_call" | custom-call | flops 26400000000 | bytes 1024 | tf_op jit(solution)/shard_map/attend_back/pallas_call | solution.py:430
  703.5 49.7 %collective-permute-done.49.refs_2_ = bf16[3,256,256]{2,1,0:T(8,128)(2,1)S(1)} collective-permute-done((bf16[3,256,256]{2,1,0:T(8,128)(2,1)S(1)}, bf16[3,256,256]{2,1,0:T(8,128)(2,1)S(1)}, u32[]{:S(2)}, u32[]{:S(2)}) %collective-permute-start.49) | collective-permute-done | bytes 393248 | tf_op jit(solution)/shard_map/ppermute | solution.py:54
  754.7 3.8 join.4.grad_ref.refs_2_
  760.6 13.0 %own.2 = (f32[3,256,2048]{2,1,0:T(8,128)}, f32[3,16,2048]{2,1,0:T(8,128)}) custom-call(s32[4]{0:T(128)} %get-tuple-element.572.perm_ref, bf16[3,256,1024]{2,1,0:T(8,128)(2,1)} %join.4.grad_ref.refs_2_, f32[4,512,2048]{2,1,0:T(8,128)} %get-tuple-element.239.z_ref, bf16[512,3072]{1,0:T(8,128)(2,1)} %all-gather.5.cloned.1.call-done.refs_0_, ...), custom_call_target="tpu_custom_call" | custom-call | flops 26400000000 | bytes 1024 | tf_op jit(solution)/shard_map/own/pallas_call | solution.py:662
  777.8 10.9 %collective-permute-done.52.refs_2_ = bf16[3,256,256]{2,1,0:T(8,128)(2,1)S(1)} collective-permute-done((bf16[3,256,256]{2,1,0:T(8,128)(2,1)S(1)}, bf16[3,256,256]{2,1,0:T(8,128)(2,1)S(1)}, u32[]{:S(2)}, u32[]{:S(2)}) %collective-permute-start.52) | collective-permute-done | bytes 393248 | tf_op jit(solution)/shard_map/ppermute | solution.py:54
  790.2 3.9 join.5.refs_3_.grad_ref
  794.1 4.4 grad.22
  801.1 6.6 grad.23
  808.0 4.0 grad.24
  813.6 6.4 grad.25
  820.5 13.0 %own.3 = (f32[3,256,2048]{2,1,0:T(8,128)}, f32[3,16,2048]{2,1,0:T(8,128)}) custom-call(s32[4]{0:T(128)} %get-tuple-element.572.perm_ref, bf16[3,256,1024]{2,1,0:T(8,128)(2,1)} %join.5.refs_3_.grad_ref, f32[4,512,2048]{2,1,0:T(8,128)} %get-tuple-element.239.z_ref, bf16[512,3072]{1,0:T(8,128)(2,1)} %all-gather.5.cloned.1.call-done.refs_0_, ...), custom_call_target="tpu_custom_call" | custom-call | flops 26400000000 | bytes 1024 | tf_op jit(solution)/shard_map/own/pallas_call | solution.py:662
  839.4 4.2 grad.26
  843.6 14.3 %other.2.dz_ref = bf16[3,256,2048]{2,1,0:T(8,128)(2,1)} custom-call(bf16[3,256,1024]{2,1,0:T(8,128)(2,1)} %collective-permute-done.56.grad_ref, f32[3,256,2048]{2,1,0:T(8,128)} %get-tuple-element.401.part_ref, f32[4,512,2048]{2,1,0:T(8,128)} %get-tuple-element.239.z_ref, f32[1,2048]{1,0:T(1,128)} %bitcast.182, ...), custom_call_target="tpu_custom_call" | custom-call | flops 30799998976 | bytes 1024 | tf_op jit(solution)/shard_map/other/pallas_call | solution.py:711
  858.0 13.0 %last.2 = (bf16[8,512,2048]{2,1,0:T(8,128)(2,1)}, f32[16,256,128]{2,1,0:T(8,128)}) custom-call(s32[4]{0:T(128)} %get-tuple-element.572.perm_ref, bf16[8,512,2048]{2,1,0:T(8,128)(2,1)} %bitcast.144, f32[16,256,4]{2,1,0:T(8,128)} %bitcast.151, bf16[3,256,2048]{2,1,0:T(8,128)(2,1)} %other.2.dz_ref, bf16[512,2048]{1,0:T(8,128)(2,1)} %get-tuple-element.353.dr_ref), custom_call_target="tpu_custom_call" | custom-call | flops 26400000000 | bytes 1024 | tf_op jit(solution)/shard_map/last/pallas_call | solution.py:767
  871.0 10.8 %collective-permute-done.61.refs_6_ = bf16[1,512,2048]{2,1,0:T(8,128)(2,1)} collective-permute-done((bf16[1,512,2048]{2,1,0:T(8,128)(2,1)}, bf16[1,512,2048]{2,1,0:T(8,128)(2,1)}, u32[]{:S(2)}, u32[]{:S(2)}) %collective-permute-start.61) | collective-permute-done | bytes 2097184 | tf_op jit(solution)/shard_map/ppermute | solution.py:45
  881.8 6.9 grad.27
  891.4 14.2 %other.3.dz_ref = bf16[3,256,2048]{2,1,0:T(8,128)(2,1)} custom-call(bf16[3,256,1024]{2,1,0:T(8,128)(2,1)} %collective-permute-done.54.grad_ref, f32[3,256,2048]{2,1,0:T(8,128)} %get-tuple-element.427.part_ref, f32[4,512,2048]{2,1,0:T(8,128)} %get-tuple-element.239.z_ref, f32[1,2048]{1,0:T(1,128)} %bitcast.183, ...), custom_call_target="tpu_custom_call" | custom-call | flops 420000000 | bytes 1024 | tf_op jit(solution)/shard_map/other/pallas_call | solution.py:711
  910.6 11.3 %collective-permute-done.64 = f32[37,128]{1,0:T(8,128)S(1)} collective-permute-done((f32[37,128]{1,0:T(8,128)S(1)}, f32[37,128]{1,0:T(8,128)S(1)}, u32[]{:S(2)}, u32[]{:S(2)}) %collective-permute-start.64) | collective-permute-done | bytes 18976 | tf_op jit(solution)/shard_map/ppermute | solution.py:1255
  925.0 13.0 %last.3 = (bf16[8,512,2048]{2,1,0:T(8,128)(2,1)}, f32[16,256,128]{2,1,0:T(8,128)}) custom-call(s32[4]{0:T(128)} %get-tuple-element.572.perm_ref, bf16[8,512,2048]{2,1,0:T(8,128)(2,1)} %bitcast.145, f32[16,256,4]{2,1,0:T(8,128)} %bitcast.152, bf16[3,256,2048]{2,1,0:T(8,128)(2,1)} %other.3.dz_ref, ...), custom_call_target="tpu_custom_call", output_to_operand_aliasing={{0}: (5, {}), {1}: (6, {})} | custom-call | flops 360000000 | bytes 1024 | tf_op jit(solution)/shard_map/last/pallas_call | solution.py:767
  (410 shorter events, 161.2 us)
Async XLA Ops:
  7.2 69.2 %all-gather.5.cloned.1.call-start = ((), (), s32[]{:S(2)}) async-start(), calls=%async_computation.7 | async-start | bytes 3932160 | tf_op jit(solution)/shard_map/all_gather | solution.py:88
  9.4 166.0 %all-gather.7.cloned.1.call-start = ((), (), s32[]{:S(2)}) async-start(), calls=%async_computation.8 | async-start | bytes 6553600 | tf_op jit(solution)/shard_map/all_gather | solution.py:88
  9.5 19.6 %collective-permute-start = (bf16[40,128]{1,0:T(8,128)(2,1)S(1)}, bf16[40,128]{1,0:T(8,128)(2,1)S(1)}, u32[]{:S(2)}, u32[]{:S(2)}) collective-permute-start(bf16[40,128]{1,0:T(8,128)(2,1)S(1)} %concatenate.45), channel_id=1, source_target_pairs={{0,2},{2,4},{4,6},{6,0},{1,3},{3,5},{5,7},{7,1},{8,10},{10,12},{12... | collective-permute-start | bytes 30728 | tf_op jit(solution)/shard_map/ppermute | solution.py:54
  12.6 16.5 %collective-permute-start.1 = (bf16[40,128]{1,0:T(8,128)(2,1)S(1)}, bf16[40,128]{1,0:T(8,128)(2,1)S(1)}, u32[]{:S(2)}, u32[]{:S(2)}) collective-permute-start(bf16[40,128]{1,0:T(8,128)(2,1)S(1)} %concatenate.45), channel_id=1, source_target_pairs={{0,4},{2,6},{4,0},{6,2},{1,5},{3,7},{5,1},{7,3},{8,12},{10,14},{12... | collective-permute-start | bytes 30728 | tf_op jit(solution)/shard_map/ppermute | solution.py:54
  15.2 14.0 %collective-permute-start.2 = (bf16[40,128]{1,0:T(8,128)(2,1)S(1)}, bf16[40,128]{1,0:T(8,128)(2,1)S(1)}, u32[]{:S(2)}, u32[]{:S(2)}) collective-permute-start(bf16[40,128]{1,0:T(8,128)(2,1)S(1)} %concatenate.45), channel_id=1, source_target_pairs={{0,6},{2,0},{4,2},{6,4},{1,7},{3,1},{5,3},{7,5},{8,14},{10,8},{12,... | collective-permute-start | bytes 30728 | tf_op jit(solution)/shard_map/ppermute | solution.py:54
  68.7 254.1 %all-gather.9.cloned.1.call-start = ((), (), s32[]{:S(2)}) async-start(), calls=%async_computation.9 | async-start | bytes 2621440 | tf_op jit(solution)/shard_map/all_gather | solution.py:88
  76.5 70.8 %collective-permute-start.9 = (bf16[512,3072]{1,0:T(8,128)(2,1)}, bf16[512,3072]{1,0:T(8,128)(2,1)}, u32[]{:S(2)}, u32[]{:S(2)}) collective-permute-start(bf16[512,3072]{1,0:T(8,128)(2,1)} %all-gather.5.cloned.1.call-done.refs_0_), channel_id=1, source_target_pairs={{0,1},{1,0},{2,3},{3,2},{4,5},{5,4},{6,7},{7,6},{8,9},{9,8},{10,11... | collective-permute-start | bytes 9437192 | tf_op jit(solution)/shard_map/ppermute | solution.py:49
  77.9 70.5 %collective-permute-start.8 = (bf16[512,3072]{1,0:T(8,128)(2,1)}, bf16[512,3072]{1,0:T(8,128)(2,1)}, u32[]{:S(2)}, u32[]{:S(2)}) collective-permute-start(bf16[512,3072]{1,0:T(8,128)(2,1)} %all-gather.5.cloned.1.call-done.refs_0_), channel_id=1, source_target_pairs={{0,16},{8,24},{16,0},{24,8},{1,17},{9,25},{17,1},{25,9},{2,18},{10... | collective-permute-start | bytes 9437192 | tf_op jit(solution)/shard_map/ppermute | solution.py:45
  149.0 82.9 %collective-permute-start.14 = (bf16[512,3072]{1,0:T(8,128)(2,1)}, bf16[512,3072]{1,0:T(8,128)(2,1)}, u32[]{:S(2)}, u32[]{:S(2)}) collective-permute-start(bf16[512,3072]{1,0:T(8,128)(2,1)} %collective-permute-done.8.refs_1_), channel_id=1, source_target_pairs={{0,1},{1,0},{2,3},{3,2},{4,5},{5,4},{6,7},{7,6},{8,9},{9,8},{10,11... | collective-permute-start | bytes 9437192 | tf_op jit(solution)/shard_map/ppermute | solution.py:49
  175.3 140.1 %collective-permute-start.18 = (bf16[512,5120]{1,0:T(8,128)(2,1)}, bf16[512,5120]{1,0:T(8,128)(2,1)}, u32[]{:S(2)}, u32[]{:S(2)}) collective-permute-start(bf16[512,5120]{1,0:T(8,128)(2,1)} %all-gather.7.cloned.1.call-done.refs_0_.refs_2_.refs_6_), channel_id=1, source_target_pairs={{0,16},{8,24},{16,0},{24,8},{1,17},{9,25},{17,1},{25,9},{2,18},{10... | collective-permute-start | bytes 15728648 | tf_op jit(solution)/shard_map/ppermute | solution.py:45
  176.8 22.6 %collective-permute-start.11 = (bf16[3,512,256]{2,1,0:T(8,128)(2,1)}, bf16[3,512,256]{2,1,0:T(8,128)(2,1)S(1)}, u32[]{:S(2)}, u32[]{:S(2)}) collective-permute-start(bf16[3,512,256]{2,1,0:T(8,128)(2,1)} %get-tuple-element.258), channel_id=1, source_target_pairs={{0,2},{2,4},{4,6},{6,0},{1,3},{3,5},{5,7},{7,1},{8,10},{10,12},{12... | collective-permute-start | bytes 2359304 | tf_op jit(solution)/shard_map/ppermute | solution.py:54
  176.8 55.0 %collective-permute-start.12 = (bf16[3,512,256]{2,1,0:T(8,128)(2,1)}, bf16[3,512,256]{2,1,0:T(8,128)(2,1)S(1)}, u32[]{:S(2)}, u32[]{:S(2)}) collective-permute-start(bf16[3,512,256]{2,1,0:T(8,128)(2,1)} %get-tuple-element.259), channel_id=1, source_target_pairs={{0,4},{2,6},{4,0},{6,2},{1,5},{3,7},{5,1},{7,3},{8,12},{10,14},{12... | collective-permute-start | bytes 2359304 | tf_op jit(solution)/shard_map/ppermute | solution.py:54
  178.1 53.8 %collective-permute-start.13 = (bf16[3,512,256]{2,1,0:T(8,128)(2,1)}, bf16[3,512,256]{2,1,0:T(8,128)(2,1)S(1)}, u32[]{:S(2)}, u32[]{:S(2)}) collective-permute-start(bf16[3,512,256]{2,1,0:T(8,128)(2,1)} %get-tuple-element.260), channel_id=1, source_target_pairs={{0,6},{2,0},{4,2},{6,4},{1,7},{3,1},{5,3},{7,5},{8,14},{10,8},{12,... | collective-permute-start | bytes 2359304 | tf_op jit(solution)/shard_map/ppermute | solution.py:54
  246.7 125.2 %all-gather.11.cloned.1.call-start = ((), (), s32[]{:S(2)}) async-start(), calls=%async_computation.10 | async-start | bytes 2621440 | tf_op jit(solution)/shard_map/all_gather | solution.py:88
  246.8 24.9 %collective-permute-start.15 = (bf16[1,512,256]{2,1,0:T(8,128)(2,1)S(1)}, bf16[1,512,256]{2,1,0:T(8,128)(2,1)S(1)}, u32[]{:S(2)}, u32[]{:S(2)}) collective-permute-start(bf16[1,512,256]{2,1,0:T(8,128)(2,1)S(1)} %copy-done.69), channel_id=1, source_target_pairs={{0,6},{2,0},{4,2},{6,4},{1,7},{3,1},{5,3},{7,5},{8,14},{10,8},{12,... | collective-permute-start | bytes 786440 | tf_op jit(solution)/shard_map/ppermute | solution.py:54
  263.1 47.3 %collective-permute-start.16 = (bf16[1,512,256]{2,1,0:T(8,128)(2,1)S(1)}, bf16[1,512,256]{2,1,0:T(8,128)(2,1)S(1)}, u32[]{:S(2)}, u32[]{:S(2)}) collective-permute-start(bf16[1,512,256]{2,1,0:T(8,128)(2,1)S(1)} %copy-done.68), channel_id=1, source_target_pairs={{0,4},{2,6},{4,0},{6,2},{1,5},{3,7},{5,1},{7,3},{8,12},{10,14},{12... | collective-permute-start | bytes 786440 | tf_op jit(solution)/shard_map/ppermute | solution.py:54
  264.4 46.1 %collective-permute-start.17 = (bf16[1,512,256]{2,1,0:T(8,128)(2,1)S(1)}, bf16[1,512,256]{2,1,0:T(8,128)(2,1)S(1)}, u32[]{:S(2)}, u32[]{:S(2)}) collective-permute-start(bf16[1,512,256]{2,1,0:T(8,128)(2,1)S(1)} %copy-done.67), channel_id=1, source_target_pairs={{0,2},{2,4},{4,6},{6,0},{1,3},{3,5},{5,7},{7,1},{8,10},{10,12},{12... | collective-permute-start | bytes 786440 | tf_op jit(solution)/shard_map/ppermute | solution.py:54
  322.9 16.4 %collective-permute-start.24 = (bf16[512,5120]{1,0:T(8,128)(2,1)}, bf16[512,5120]{1,0:T(8,128)(2,1)}, u32[]{:S(2)}, u32[]{:S(2)}) collective-permute-start(bf16[512,5120]{1,0:T(8,128)(2,1)} %collective-permute-done.18.refs_1_.refs_3_.refs_7_), channel_id=1, source_target_pairs={{0,8},{8,0},{16,24},{24,16},{1,9},{9,1},{17,25},{25,17},{2,10},{10... | collective-permute-start | bytes 15728648 | tf_op jit(solution)/shard_map/ppermute | solution.py:45
  323.3 378.0 %reduce-scatter.8.cloned.1.call-start = ((), (), s32[]{:S(2)}) async-start(), calls=%async_computation.11 | async-start | bytes 2621440 | tf_op jit(solution)/shard_map/reduce_scatter | solution.py:135
  323.4 48.1 %collective-permute-start.22 = (bf16[512,2048]{1,0:T(8,128)(2,1)}, bf16[512,2048]{1,0:T(8,128)(2,1)}, u32[]{:S(2)}, u32[]{:S(2)}) collective-permute-start(bf16[512,2048]{1,0:T(8,128)(2,1)} %all-gather.9.cloned.1.call-done.refs_1_.refs_0_), channel_id=1, source_target_pairs={{0,16},{8,24},{16,0},{24,8},{1,17},{9,25},{17,1},{25,9},{2,18},{10... | collective-permute-start | bytes 6291464 | tf_op jit(solution)/shard_map/ppermute | solution.py:45
  330.1 47.7 %collective-permute-start.21 = (bf16[512,2048]{1,0:T(8,128)(2,1)}, bf16[512,2048]{1,0:T(8,128)(2,1)}, u32[]{:S(2)}, u32[]{:S(2)}) collective-permute-start(bf16[512,2048]{1,0:T(8,128)(2,1)} %to_width.4), channel_id=1, source_target_pairs={{0,1},{1,0},{2,3},{3,2},{4,5},{5,4},{6,7},{7,6},{8,9},{9,8},{10,11... | collective-permute-start | bytes 6291464 | tf_op jit(solution)/shard_map/ppermute | solution.py:49
  331.6 78.7 %collective-permute-start.26 = (bf16[512,3072]{1,0:T(8,128)(2,1)}, bf16[512,3072]{1,0:T(8,128)(2,1)S(1)}, u32[]{:S(2)}, u32[]{:S(2)}) collective-permute-start(bf16[512,3072]{1,0:T(8,128)(2,1)} %collective-permute-done.9.refs_0_), channel_id=1, source_target_pairs={{0,8},{8,0},{16,24},{24,16},{1,9},{9,1},{17,25},{25,17},{2,10},{10... | collective-permute-start | bytes 9437192 | tf_op jit(solution)/shard_map/ppermute | solution.py:45
  331.8 78.5 %collective-permute-start.27 = (bf16[512,3072]{1,0:T(8,128)(2,1)}, bf16[512,3072]{1,0:T(8,128)(2,1)}, u32[]{:S(2)}, u32[]{:S(2)}) collective-permute-start(bf16[512,3072]{1,0:T(8,128)(2,1)} %collective-permute-done.14.refs_1_), channel_id=1, source_target_pairs={{0,8},{8,0},{16,24},{24,16},{1,9},{9,1},{17,25},{25,17},{2,10},{10... | collective-permute-start | bytes 9437192 | tf_op jit(solution)/shard_map/ppermute | solution.py:45
  371.4 38.8 %collective-permute-start.28 = (bf16[512,2048]{1,0:T(8,128)(2,1)}, bf16[512,2048]{1,0:T(8,128)(2,1)}, u32[]{:S(2)}, u32[]{:S(2)}) collective-permute-start(bf16[512,2048]{1,0:T(8,128)(2,1)} %all-gather.9.cloned.1.call-done.refs_1_.refs_0_), channel_id=1, source_target_pairs={{0,8},{8,0},{16,24},{24,16},{1,9},{9,1},{17,25},{25,17},{2,10},{10... | collective-permute-start | bytes 6291464 | tf_op jit(solution)/shard_map/ppermute | solution.py:45
  371.4 38.8 %collective-permute-start.29 = (bf16[512,2048]{1,0:T(8,128)(2,1)}, bf16[512,2048]{1,0:T(8,128)(2,1)}, u32[]{:S(2)}, u32[]{:S(2)}) collective-permute-start(bf16[512,2048]{1,0:T(8,128)(2,1)} %collective-permute-done.22.refs_2_.refs_1_), channel_id=1, source_target_pairs={{0,8},{8,0},{16,24},{24,16},{1,9},{9,1},{17,25},{25,17},{2,10},{10... | collective-permute-start | bytes 6291464 | tf_op jit(solution)/shard_map/ppermute | solution.py:45
  377.8 46.8 %collective-permute-start.25 = (bf16[512,2048]{1,0:T(8,128)(2,1)}, bf16[512,2048]{1,0:T(8,128)(2,1)S(1)}, u32[]{:S(2)}, u32[]{:S(2)}) collective-permute-start(bf16[512,2048]{1,0:T(8,128)(2,1)} %all-gather.11.cloned.1.call-done.refs_1_.refs_0_), channel_id=1, source_target_pairs={{0,16},{8,24},{16,0},{24,8},{1,17},{9,25},{17,1},{25,9},{2,18},{10... | collective-permute-start | bytes 6291464 | tf_op jit(solution)/shard_map/ppermute | solution.py:45
  443.2 48.0 %collective-permute-start.32 = (bf16[512,2048]{1,0:T(8,128)(2,1)}, bf16[512,2048]{1,0:T(8,128)(2,1)}, u32[]{:S(2)}, u32[]{:S(2)}) collective-permute-start(bf16[512,2048]{1,0:T(8,128)(2,1)} %to_width.6.mine_ref), channel_id=1, source_target_pairs={{0,1},{1,0},{2,3},{3,2},{4,5},{5,4},{6,7},{7,6},{8,9},{9,8},{10,11... | collective-permute-start | bytes 6291464 | tf_op jit(solution)/shard_map/ppermute | solution.py:49
  444.7 63.0 %collective-permute-start.34 = (bf16[512,2048]{1,0:T(8,128)(2,1)}, bf16[512,2048]{1,0:T(8,128)(2,1)}, u32[]{:S(2)}, u32[]{:S(2)}) collective-permute-start(bf16[512,2048]{1,0:T(8,128)(2,1)} %get-tuple-element.318.refs_0_), channel_id=1, source_target_pairs={{0,8},{8,0},{16,24},{24,16},{1,9},{9,1},{17,25},{25,17},{2,10},{10... | collective-permute-start | bytes 6291464 | tf_op jit(solution)/shard_map/ppermute | solution.py:45
  444.7 63.0 %collective-permute-start.33 = (bf16[512,2048]{1,0:T(8,128)(2,1)}, bf16[512,2048]{1,0:T(8,128)(2,1)}, u32[]{:S(2)}, u32[]{:S(2)}) collective-permute-start(bf16[512,2048]{1,0:T(8,128)(2,1)} %get-tuple-element.313.refs_0_), channel_id=1, source_target_pairs={{0,8},{8,0},{16,24},{24,16},{1,9},{9,1},{17,25},{25,17},{2,10},{10... | collective-permute-start | bytes 6291464 | tf_op jit(solution)/shard_map/ppermute | solution.py:45
  451.4 56.2 %collective-permute-start.36 = (bf16[512,1024]{1,0:T(8,128)(2,1)S(1)}, bf16[512,1024]{1,0:T(8,128)(2,1)}, u32[]{:S(2)}, u32[]{:S(2)}) collective-permute-start(bf16[512,1024]{1,0:T(8,128)(2,1)S(1)} %bitcast.159), channel_id=1, source_target_pairs={{0,8},{8,0},{16,24},{24,16},{1,9},{9,1},{17,25},{25,17},{2,10},{10... | collective-permute-start | bytes 3145736 | tf_op jit(solution)/shard_map/ppermute | solution.py:45
  452.6 55.1 %collective-permute-start.35 = (bf16[512,1024]{1,0:T(8,128)(2,1)}, bf16[512,1024]{1,0:T(8,128)(2,1)S(1)}, u32[]{:S(2)}, u32[]{:S(2)}) collective-permute-start(bf16[512,1024]{1,0:T(8,128)(2,1)} %slice.137), channel_id=1, source_target_pairs={{0,8},{8,0},{16,24},{24,16},{1,9},{9,1},{17,25},{25,17},{2,10},{10... | collective-permute-start | bytes 3145736 | tf_op jit(solution)/shard_map/ppermute | solution.py:45
  514.8 48.3 %collective-permute-start.40 = (bf16[1,512,2048]{2,1,0:T(8,128)(2,1)}, bf16[1,512,2048]{2,1,0:T(8,128)(2,1)}, u32[]{:S(2)}, u32[]{:S(2)}) collective-permute-start(bf16[1,512,2048]{2,1,0:T(8,128)(2,1)} %grad.14), channel_id=1, source_target_pairs={{0,16},{8,24},{16,0},{24,8},{1,17},{9,25},{17,1},{25,9},{2,18},{10... | collective-permute-start | bytes 6291464 | tf_op jit(solution)/shard_map/ppermute | solution.py:45
  537.3 32.5 %collective-permute-start.39 = (bf16[512,2048]{1,0:T(8,128)(2,1)}, bf16[512,2048]{1,0:T(8,128)(2,1)S(1)}, u32[]{:S(2)}, u32[]{:S(2)}) collective-permute-start(bf16[512,2048]{1,0:T(8,128)(2,1)} %up_back.3.refs_1_), channel_id=1, source_target_pairs={{0,8},{8,0},{16,24},{24,16},{1,9},{9,1},{17,25},{25,17},{2,10},{10... | collective-permute-start | bytes 6291464 | tf_op jit(solution)/shard_map/ppermute | solution.py:45
  537.5 32.3 %collective-permute-start.38 = (bf16[512,2048]{1,0:T(8,128)(2,1)S(1)}, bf16[512,2048]{1,0:T(8,128)(2,1)S(1)}, u32[]{:S(2)}, u32[]{:S(2)}) collective-permute-start(bf16[512,2048]{1,0:T(8,128)(2,1)S(1)} %copy-done.47), channel_id=1, source_target_pairs={{0,8},{8,0},{16,24},{24,16},{1,9},{9,1},{17,25},{25,17},{2,10},{10... | collective-permute-start | bytes 6291464 | tf_op jit(solution)/shard_map/ppermute | solution.py:45
  554.3 48.0 %collective-permute-start.41 = (bf16[512,2048]{1,0:T(8,128)(2,1)}, bf16[512,2048]{1,0:T(8,128)(2,1)}, u32[]{:S(2)}, u32[]{:S(2)}) collective-permute-start(bf16[512,2048]{1,0:T(8,128)(2,1)} %to_width.7.mine_ref), channel_id=1, source_target_pairs={{0,1},{1,0},{2,3},{3,2},{4,5},{5,4},{6,7},{7,6},{8,9},{9,8},{10,11... | collective-permute-start | bytes 6291464 | tf_op jit(solution)/shard_map/ppermute | solution.py:49
  561.9 61.1 %collective-permute-start.46 = (bf16[1,512,2048]{2,1,0:T(8,128)(2,1)}, bf16[1,512,2048]{2,1,0:T(8,128)(2,1)}, u32[]{:S(2)}, u32[]{:S(2)}) collective-permute-start(bf16[1,512,2048]{2,1,0:T(8,128)(2,1)} %grad.15), channel_id=1, source_target_pairs={{0,16},{8,24},{16,0},{24,8},{1,17},{9,25},{17,1},{25,9},{2,18},{10... | collective-permute-start | bytes 6291464 | tf_op jit(solution)/shard_map/ppermute | solution.py:45
  578.1 81.4 %collective-permute-start.47 = (bf16[1,512,2048]{2,1,0:T(8,128)(2,1)}, bf16[1,512,2048]{2,1,0:T(8,128)(2,1)}, u32[]{:S(2)}, u32[]{:S(2)}) collective-permute-start(bf16[1,512,2048]{2,1,0:T(8,128)(2,1)} %grad.17), channel_id=1, source_target_pairs={{0,16},{8,24},{16,0},{24,8},{1,17},{9,25},{17,1},{25,9},{2,18},{10... | collective-permute-start | bytes 6291464 | tf_op jit(solution)/shard_map/ppermute | solution.py:45
  580.1 193.4 %reduce-scatter.12.cloned.1.call-start = ((), (), s32[]{:S(2)}) async-start(), calls=%async_computation.13 | async-start | bytes 2621440 | tf_op jit(solution)/shard_map/reduce_scatter | solution.py:135
  619.2 21.4 %collective-permute-start.42 = (bf16[1,512,256]{2,1,0:T(8,128)(2,1)}, bf16[1,512,256]{2,1,0:T(8,128)(2,1)S(1)}, u32[]{:S(2)}, u32[]{:S(2)}) collective-permute-start(bf16[1,512,256]{2,1,0:T(8,128)(2,1)} %get-tuple-element.355), channel_id=1, source_target_pairs={{0,2},{2,4},{4,6},{6,0},{1,3},{3,5},{5,7},{7,1},{8,10},{10,12},{12... | collective-permute-start | bytes 786440 | tf_op jit(solution)/shard_map/ppermute | solution.py:54
  619.2 27.5 %collective-permute-start.43 = (bf16[1,512,256]{2,1,0:T(8,128)(2,1)}, bf16[1,512,256]{2,1,0:T(8,128)(2,1)S(1)}, u32[]{:S(2)}, u32[]{:S(2)}) collective-permute-start(bf16[1,512,256]{2,1,0:T(8,128)(2,1)} %get-tuple-element.356), channel_id=1, source_target_pairs={{0,4},{2,6},{4,0},{6,2},{1,5},{3,7},{5,1},{7,3},{8,12},{10,14},{12... | collective-permute-start | bytes 786440 | tf_op jit(solution)/shard_map/ppermute | solution.py:54
  619.3 27.3 %collective-permute-start.44 = (bf16[1,512,256]{2,1,0:T(8,128)(2,1)}, bf16[1,512,256]{2,1,0:T(8,128)(2,1)S(1)}, u32[]{:S(2)}, u32[]{:S(2)}) collective-permute-start(bf16[1,512,256]{2,1,0:T(8,128)(2,1)} %get-tuple-element.357), channel_id=1, source_target_pairs={{0,6},{2,0},{4,2},{6,4},{1,7},{3,1},{5,3},{7,5},{8,14},{10,8},{12,... | collective-permute-start | bytes 786440 | tf_op jit(solution)/shard_map/ppermute | solution.py:54
  629.7 145.9 %reduce-scatter.10.cloned.1.call-start = ((), (), s32[]{:S(2)}) async-start(), calls=%async_computation.12 | async-start | bytes 2621440 | tf_op jit(solution)/shard_map/reduce_scatter | solution.py:135
  636.2 165.0 %collective-permute-start.59 = (bf16[1,512,2048]{2,1,0:T(8,128)(2,1)}, bf16[1,512,2048]{2,1,0:T(8,128)(2,1)}, u32[]{:S(2)}, u32[]{:S(2)}) collective-permute-start(bf16[1,512,2048]{2,1,0:T(8,128)(2,1)} %grad.19), channel_id=1, source_target_pairs={{0,16},{8,24},{16,0},{24,8},{1,17},{9,25},{17,1},{25,9},{2,18},{10... | collective-permute-start | bytes 6291464 | tf_op jit(solution)/shard_map/ppermute | solution.py:45
  659.4 134.7 %collective-permute-start.55 = (bf16[1,512,1024]{2,1,0:T(8,128)(2,1)}, bf16[1,512,1024]{2,1,0:T(8,128)(2,1)}, u32[]{:S(2)}, u32[]{:S(2)}) collective-permute-start(bf16[1,512,1024]{2,1,0:T(8,128)(2,1)} %grad.20), channel_id=1, source_target_pairs={{0,16},{8,24},{16,0},{24,8},{1,17},{9,25},{17,1},{25,9},{2,18},{10... | collective-permute-start | bytes 3145736 | tf_op jit(solution)/shard_map/ppermute | solution.py:45
  666.2 37.2 %collective-permute-start.48 = (bf16[3,256,256]{2,1,0:T(8,128)(2,1)S(1)}, bf16[3,256,256]{2,1,0:T(8,128)(2,1)S(1)}, u32[]{:S(2)}, u32[]{:S(2)}) collective-permute-start(bf16[3,256,256]{2,1,0:T(8,128)(2,1)S(1)} %copy-done.57), channel_id=1, source_target_pairs={{0,6},{2,0},{4,2},{6,4},{1,7},{3,1},{5,3},{7,5},{8,14},{10,8},{12,... | collective-permute-start | bytes 1179656 | tf_op jit(solution)/shard_map/ppermute | solution.py:54
  678.8 74.4 %collective-permute-start.49 = (bf16[3,256,256]{2,1,0:T(8,128)(2,1)S(1)}, bf16[3,256,256]{2,1,0:T(8,128)(2,1)S(1)}, u32[]{:S(2)}, u32[]{:S(2)}) collective-permute-start(bf16[3,256,256]{2,1,0:T(8,128)(2,1)S(1)} %copy-done.56), channel_id=1, source_target_pairs={{0,4},{2,6},{4,0},{6,2},{1,5},{3,7},{5,1},{7,3},{8,12},{10,14},{12... | collective-permute-start | bytes 1179656 | tf_op jit(solution)/shard_map/ppermute | solution.py:54
  689.5 63.7 %collective-permute-start.50 = (bf16[3,256,256]{2,1,0:T(8,128)(2,1)S(1)}, bf16[3,256,256]{2,1,0:T(8,128)(2,1)S(1)}, u32[]{:S(2)}, u32[]{:S(2)}) collective-permute-start(bf16[3,256,256]{2,1,0:T(8,128)(2,1)S(1)} %copy-done.54), channel_id=1, source_target_pairs={{0,2},{2,4},{4,6},{6,0},{1,3},{3,5},{5,7},{7,1},{8,10},{10,12},{12... | collective-permute-start | bytes 1179656 | tf_op jit(solution)/shard_map/ppermute | solution.py:54
  689.5 148.1 %reduce-scatter.14.cloned.1.call-start = ((), (), s32[]{:S(2)}) async-start(), calls=%async_computation.14 | async-start | bytes 1310720 | tf_op jit(solution)/shard_map/reduce_scatter | solution.py:135
  758.5 19.3 %collective-permute-start.51 = (bf16[3,256,256]{2,1,0:T(8,128)(2,1)S(1)}, bf16[3,256,256]{2,1,0:T(8,128)(2,1)S(1)}, u32[]{:S(2)}, u32[]{:S(2)}) collective-permute-start(bf16[3,256,256]{2,1,0:T(8,128)(2,1)S(1)} %copy-done.55), channel_id=1, source_target_pairs={{0,6},{2,0},{4,2},{6,4},{1,7},{3,1},{5,3},{7,5},{8,14},{10,8},{12,... | collective-permute-start | bytes 1179656 | tf_op jit(solution)/shard_map/ppermute | solution.py:54
  758.5 30.2 %collective-permute-start.52 = (bf16[3,256,256]{2,1,0:T(8,128)(2,1)S(1)}, bf16[3,256,256]{2,1,0:T(8,128)(2,1)S(1)}, u32[]{:S(2)}, u32[]{:S(2)}) collective-permute-start(bf16[3,256,256]{2,1,0:T(8,128)(2,1)S(1)} %copy-done.53), channel_id=1, source_target_pairs={{0,4},{2,6},{4,0},{6,2},{1,5},{3,7},{5,1},{7,3},{8,12},{10,14},{12... | collective-permute-start | bytes 1179656 | tf_op jit(solution)/shard_map/ppermute | solution.py:54
  758.6 30.1 %collective-permute-start.53 = (bf16[3,256,256]{2,1,0:T(8,128)(2,1)S(1)}, bf16[3,256,256]{2,1,0:T(8,128)(2,1)S(1)}, u32[]{:S(2)}, u32[]{:S(2)}) collective-permute-start(bf16[3,256,256]{2,1,0:T(8,128)(2,1)S(1)} %copy-done.52), channel_id=1, source_target_pairs={{0,2},{2,4},{4,6},{6,0},{1,3},{3,5},{5,7},{7,1},{8,10},{10,12},{12... | collective-permute-start | bytes 1179656 | tf_op jit(solution)/shard_map/ppermute | solution.py:54
  798.5 110.0 %reduce-scatter.16.cloned.1.call-start = ((), (), s32[]{:S(2)}) async-start(), calls=%async_computation.15 | async-start | bytes 2621440 | tf_op jit(solution)/shard_map/reduce_scatter | solution.py:135
  798.5 9.5 collective-permute-start.57
  799.1 37.4 %collective-permute-start.56 = (bf16[3,256,1024]{2,1,0:T(8,128)(2,1)S(1)}, bf16[3,256,1024]{2,1,0:T(8,128)(2,1)}, u32[]{:S(2)}, u32[]{:S(2)}) collective-permute-start(bf16[3,256,1024]{2,1,0:T(8,128)(2,1)S(1)} %copy-done.6), channel_id=1, source_target_pairs={{0,1},{1,0},{2,3},{3,2},{4,5},{5,4},{6,7},{7,6},{8,9},{9,8},{10,11... | collective-permute-start | bytes 4718600 | tf_op jit(solution)/shard_map/ppermute | solution.py:49
  800.8 70.2 %collective-permute-start.54 = (bf16[3,256,1024]{2,1,0:T(8,128)(2,1)S(1)}, bf16[3,256,1024]{2,1,0:T(8,128)(2,1)}, u32[]{:S(2)}, u32[]{:S(2)}) collective-permute-start(bf16[3,256,1024]{2,1,0:T(8,128)(2,1)S(1)} %copy-done.7), channel_id=1, source_target_pairs={{0,1},{1,0},{2,3},{3,2},{4,5},{5,4},{6,7},{7,6},{8,9},{9,8},{10,11... | collective-permute-start | bytes 4718600 | tf_op jit(solution)/shard_map/ppermute | solution.py:49
  807.8 143.3 %reduce-scatter.18.cloned.1.call-start = ((), (), s32[]{:S(2)}) async-start(), calls=%async_computation.16 | async-start | bytes 1310720 | tf_op jit(solution)/shard_map/reduce_scatter | solution.py:135
  812.0 27.4 %collective-permute-start.60 = (bf16[1,512,1024]{2,1,0:T(8,128)(2,1)}, bf16[1,512,1024]{2,1,0:T(8,128)(2,1)}, u32[]{:S(2)}, u32[]{:S(2)}) collective-permute-start(bf16[1,512,1024]{2,1,0:T(8,128)(2,1)} %grad.24), channel_id=1, source_target_pairs={{0,16},{8,24},{16,0},{24,8},{1,17},{9,25},{17,1},{25,9},{2,18},{10... | collective-permute-start | bytes 3145736 | tf_op jit(solution)/shard_map/ppermute | solution.py:45
  820.0 61.8 %collective-permute-start.61 = (bf16[1,512,2048]{2,1,0:T(8,128)(2,1)}, bf16[1,512,2048]{2,1,0:T(8,128)(2,1)}, u32[]{:S(2)}, u32[]{:S(2)}) collective-permute-start(bf16[1,512,2048]{2,1,0:T(8,128)(2,1)} %grad.25), channel_id=1, source_target_pairs={{0,16},{8,24},{16,0},{24,8},{1,17},{9,25},{17,1},{25,9},{2,18},{10... | collective-permute-start | bytes 6291464 | tf_op jit(solution)/shard_map/ppermute | solution.py:45
  857.9 95.0 %reduce-scatter.20.cloned.1.call-start = ((), (), s32[]{:S(2)}) async-start(), calls=%async_computation.17 | async-start | bytes 2621440 | tf_op jit(solution)/shard_map/reduce_scatter | solution.py:135
  889.7 15.9 %collective-permute-start.62 = (f32[2,2048]{1,0:T(2,128)S(1)}, f32[2,2048]{1,0:T(2,128)S(1)}, u32[]{:S(2)}, u32[]{:S(2)}) collective-permute-start(f32[2,2048]{1,0:T(2,128)S(1)} %bitcast_reduce_fusion.1), channel_id=1, source_target_pairs={{0,1},{1,0},{2,3},{3,2},{4,5},{5,4},{6,7},{7,6},{8,9},{9,8},{10,11... | collective-permute-start | bytes 49160 | tf_op jit(solution)/shard_map/ppermute | solution.py:49
  906.3 15.6 %collective-permute-start.63 = (f32[2,4,40,128]{3,2,1,0:T(8,128)S(1)}, f32[2,4,40,128]{3,2,1,0:T(8,128)S(1)}, u32[]{:S(2)}, u32[]{:S(2)}) collective-permute-start(f32[2,4,40,128]{3,2,1,0:T(8,128)S(1)} %slice.140), channel_id=1, source_target_pairs={{0,2},{2,0},{4,6},{6,4},{1,3},{3,1},{5,7},{7,5},{8,10},{10,8},{12,... | collective-permute-start | bytes 491528 | tf_op jit(solution)/shard_map/ppermute | solution.py:1255
  906.4 15.5 %collective-permute-start.64 = (f32[37,128]{1,0:T(8,128)S(1)}, f32[37,128]{1,0:T(8,128)S(1)}, u32[]{:S(2)}, u32[]{:S(2)}) collective-permute-start(f32[37,128]{1,0:T(8,128)S(1)} %pad.22), channel_id=1, source_target_pairs={{0,2},{2,0},{4,6},{6,4},{1,3},{3,1},{5,7},{7,5},{8,10},{10,8},{12,... | collective-permute-start | bytes 56840 | tf_op jit(solution)/shard_map/ppermute | solution.py:1255
  921.9 16.1 %collective-permute-start.65 = (f32[1,4,40,128]{3,2,1,0:T(8,128)S(1)}, f32[1,4,40,128]{3,2,1,0:T(8,128)S(1)}, u32[]{:S(2)}, u32[]{:S(2)}) collective-permute-start(f32[1,4,40,128]{3,2,1,0:T(8,128)S(1)} %slice.165), channel_id=1, source_target_pairs={{0,4},{2,6},{4,0},{6,2},{1,5},{3,7},{5,1},{7,3},{8,12},{10,14},{12... | collective-permute-start | bytes 245768 | tf_op jit(solution)/shard_map/ppermute | solution.py:1255
  922.0 15.9 %collective-permute-start.66 = (f32[37,128]{1,0:T(8,128)S(1)}, f32[37,128]{1,0:T(8,128)S(1)}, u32[]{:S(2)}, u32[]{:S(2)}) collective-permute-start(f32[37,128]{1,0:T(8,128)S(1)} %add.235), channel_id=1, source_target_pairs={{0,4},{2,6},{4,0},{6,2},{1,5},{3,7},{5,1},{7,3},{8,12},{10,14},{12... | collective-permute-start | bytes 56840 | tf_op jit(solution)/shard_map/ppermute | solution.py:1255
  (90 other events, 1387.7 us)
Sparse Core Ops, SparseCore 0:
  10.2 66.1 all-gather.4
  78.6 96.7 all-gather.6
  246.8 73.9 all-gather.8
  323.4 43.4 all-gather.10
  580.3 41.4 reduce-scatter.7
  629.9 47.9 reduce-scatter.11
  689.6 63.9 reduce-scatter.9
  798.6 25.6 reduce-scatter.13
  826.5 42.4 reduce-scatter.15
  871.3 26.5 reduce-scatter.17
  900.2 47.5 reduce-scatter.19
